TPU v7x, 32 devices: a whole 2x2x4 slice. The times are simulated.
32 devices in a mesh: pass: 8 (over z, x), head: 4 (over y, core).
Axes of the slice: x: 2, y: 2, z: 4, core: 2. Of those that a mesh axis runs over, the one named last changes fastest.
Arguments:
- queries: bfloat16 [3072, 8192], P('pass', 'head'), may hold values from -4.5 to 4.5
- own_kv: bfloat16 [3072, 8, 256], P('pass', 'head'), may hold values from -4.5 to 4.5
- passage_cache: bfloat16 [128, 512, 8, 256], P('pass', None, 'head'), may hold values from -4.5 to 4.5
- out_weight: bfloat16 [8192, 4096], P('head', 'pass'), may hold values from -3.5 to 3.5
- lists: int32 [24, 8], replicated, may hold values from 0 to 127, as said below
- passage_slot: int32 [128], replicated, may hold values from 0 to 127, as said below
- question_slot: int32 [24], replicated, may hold values from 0 to 23, as said below
Outputs:
- attended: bfloat16 [3072, 4096], P('pass', 'head')
Inputs may be any that keep to these rules, and one draw needn't show every extreme that they name: Each question lists 8 different passages. The listed passages of the 3 questions at slots d * 3 to d * 3 + 2 are all different, and at most 3 of them have their cache rows in one aligned block of 16 rows; some block holds exactly 3 of them. `passage_slot`: A permutation. `question_slot`: A permutation.
All inputs are finite; a program needn't handle non-finite values.
Results may differ from a plain program's by a relative error of at most 0.014.
Values may be sent and summed in bfloat16 or wider, within the bound.
A program may use at most 192 MiB of HBM per device.

v0:
```python
import functools
import math

import jax
import jax.numpy as jnp
from jax import lax
from jax.experimental import pallas as pl
from jax.experimental.pallas import tpu as pltpu
from jax.sharding import PartitionSpec as P


H = 64
KVH = 8
HD = 128
LQ = 128
GROUP = H // KVH
COEF = HD ** (-0.5) * math.log2(math.e)
NEG = -1e30
ROWS = 256


def round_of(a, b, n):
    if n & (n - 1) == 0:
        return a ^ b
    return lax.rem(b - a + n, n)


def pairs_of(k, n):
    if n & (n - 1) == 0:
        return [(p, p ^ k) for p in range(n)]
    return [(p, (p + k) % n) for p in range(n)]


def order_of(n):
    rest = range(1, n)
    return sorted(rest, key=lambda k: (bin(k).count("1"), k))


def gather_kernel(n, most, per_device, order, lists_ref, pslot_ref, qslot_ref, cache_ref, *refs):
    recv_ref, own_row_ref = refs[0], refs[1]
    outs = refs[2 : 2 + len(order)]
    send_row, send_cnt, recv_cnt, buf, in_sem, out_sem = refs[2 + len(order) :]
    me = lax.axis_index("pass")
    pass_dev = cache_ref.shape[0]
    topp, nq = lists_ref.shape
    for k in range(n):
        send_cnt[k] = 0
        recv_cnt[k] = 0
    for i in range(n * most):
        recv_ref[i] = -1
        send_row[i] = 0

    def question(q, carry):
        slot = qslot_ref[q]
        dest = slot // per_device
        local = slot - dest * per_device
        k_send = round_of(me, dest, n)
        for t in range(topp):
            row = pslot_ref[lists_ref[t, q]]
            owner = row // pass_dev

            @pl.when(owner == me)
            def _():
                count = send_cnt[k_send]
                send_row[k_send * most + count] = row - owner * pass_dev
                send_cnt[k_send] = count + 1

            @pl.when(dest == me)
            def _():
                k = round_of(owner, me, n)
                count = recv_cnt[k]
                recv_ref[k * most + count] = local
                recv_cnt[k] = count + 1

        return carry

    lax.fori_loop(0, nq, question, 0)
    for r in range(most):
        own_row_ref[r] = send_row[r]
    copies = []
    for j, k in enumerate(order):
        for r in range(most):
            i = j * most + r
            get = pltpu.make_async_copy(
                cache_ref.at[send_row[k * most + r]], buf.at[i], in_sem.at[i]
            )
            get.start()
            copies.append((get, pltpu.make_async_copy(buf.at[i], outs[j].at[r], out_sem.at[i])))
    for get, put in copies:
        get.wait()
        put.start()
    for get, put in copies:
        put.wait()


def gather(lists, passage_slot, question_slot, cache, n, most, per_device, order):
    item = cache.shape[1:]
    slots = (n - 1) * most
    smem = pl.BlockSpec(memory_space=pltpu.SMEM)
    anyspace = pl.BlockSpec(memory_space=pl.ANY)
    return pl.pallas_call(
        functools.partial(gather_kernel, n, most, per_device, order),
        out_shape=[
            jax.ShapeDtypeStruct((n * most,), jnp.int32),
            jax.ShapeDtypeStruct((most,), jnp.int32),
        ]
        + [jax.ShapeDtypeStruct((most,) + item, cache.dtype)] * len(order),
        in_specs=[smem, smem, smem, anyspace],
        out_specs=[smem, smem] + [anyspace] * len(order),
        scratch_shapes=[
            pltpu.SMEM((n * most,), jnp.int32),
            pltpu.SMEM((n,), jnp.int32),
            pltpu.SMEM((n,), jnp.int32),
            pltpu.VMEM((slots,) + item, cache.dtype),
            pltpu.SemaphoreType.DMA((slots,)),
            pltpu.SemaphoreType.DMA((slots,)),
        ],
        name="gather_items",
        cost_estimate=pl.CostEstimate(
            flops=0, bytes_accessed=2 * slots * math.prod(item) * 2, transcendentals=0
        ),
    )(lists.T, passage_slot, question_slot, cache)


def block_step(q_ref, m_ref, l_ref, acc_ref, question, head, keys, values, causal):
    rows = q_ref.shape[2]
    step = min(ROWS, rows)
    width = keys.shape[0]
    ones = jnp.ones(values.shape, values.dtype)
    extended = jnp.concatenate([values, ones], axis=1)
    for start in range(0, rows, step):
        part = pl.ds(start, step)
        q = q_ref[question, head, part, :]
        scores = (
            lax.dot_general(q, keys, (((1,), (1,)), ((), ())), preferred_element_type=jnp.float32)
            * COEF
        )
        if causal:
            token = lax.broadcasted_iota(jnp.int32, scores.shape, 0) % LQ
            column = lax.broadcasted_iota(jnp.int32, scores.shape, 1)
            scores = jnp.where(column <= token, scores, NEG)
        old = m_ref[question, head, part, :]
        new = jnp.maximum(old, jnp.max(scores, axis=1, keepdims=True))
        weights = jnp.exp2(scores - jnp.concatenate([new] * (width // HD), axis=1))
        mixed = jnp.dot(
            weights.astype(jnp.bfloat16), extended, preferred_element_type=jnp.float32
        )
        alpha = jnp.exp2(old - new)
        m_ref[question, head, part, :] = new
        l_ref[question, head, part, :] = l_ref[question, head, part, :] * alpha + mixed[:, HD:]
        acc_ref[question, head, part, :] = (
            acc_ref[question, head, part, :] * alpha + mixed[:, :HD]
        )


def attend_kernel(first, last, rounds, most, *refs):
    refs = list(refs)
    recv_ref, q_ref = refs.pop(0), refs.pop(0)
    if first:
        row_ref, own_ref, cache_ref = refs.pop(0), refs.pop(0), refs.pop(0)
        sources = None
        entries = most
    else:
        state_in = [refs.pop(0) for _ in range(3)]
        sources = [refs.pop(0) for _ in rounds]
        entries = len(rounds) * most
    if last:
        out_ref = refs.pop(0)
        m_ref, l_ref, acc_ref = [refs.pop(0) for _ in range(3)]
    else:
        m_ref, l_ref, acc_ref = [refs.pop(0) for _ in range(3)]
    buf, sem = refs
    per_device, heads = q_ref.shape[0], q_ref.shape[1]

    def fetch(i, slot):
        if first:
            pltpu.make_async_copy(cache_ref.at[row_ref[i]], buf.at[slot], sem.at[slot]).start()
            return
        for j in range(len(rounds)):

            @pl.when(i // most == j)
            def _():
                pltpu.make_async_copy(
                    sources[j].at[i - j * most], buf.at[slot], sem.at[slot]
                ).start()

    def tag_of(i):
        if first:
            return recv_ref[i]
        k = jnp.int32(0)
        for j, value in enumerate(rounds):
            k = jnp.where(i // most == j, value, k)
        return recv_ref[k * most + lax.rem(i, most)]

    fetch(jnp.int32(0), 0)
    if first:
        m_ref[...] = jnp.full(m_ref.shape, NEG, jnp.float32)
        l_ref[...] = jnp.zeros(l_ref.shape, jnp.float32)
        acc_ref[...] = jnp.zeros(acc_ref.shape, jnp.float32)

        def own_block(question, carry):
            for head in range(heads):
                block = own_ref[question, head]
                block_step(
                    q_ref, m_ref, l_ref, acc_ref, question, head, block[:, :HD], block[:, HD:], True
                )
            return carry

        lax.fori_loop(0, per_device, own_block, 0)
    else:
        m_ref[...] = state_in[0][...]
        l_ref[...] = state_in[1][...]
        acc_ref[...] = state_in[2][...]

    def item(i, carry):
        slot = lax.rem(i, 2)
        pltpu.make_async_copy(buf.at[slot], buf.at[slot], sem.at[slot]).wait()

        @pl.when(i + 1 < entries)
        def _():
            fetch(i + 1, lax.rem(i + 1, 2))

        tag = tag_of(i)

        @pl.when(tag >= 0)
        def _():
            for head in range(heads):
                block_step(
                    q_ref,
                    m_ref,
                    l_ref,
                    acc_ref,
                    tag,
                    head,
                    buf[slot, head, :, :HD],
                    buf[slot, head, :, HD:],
                    False,
                )

        return carry

    lax.fori_loop(0, entries, item, 0)
    if last:
        for question in range(per_device):
            for head in range(heads):
                for g in range(GROUP):
                    part = pl.ds(g * LQ, LQ)
                    column = (head * GROUP + g) * HD
                    out_ref[pl.ds(question * LQ, LQ), pl.ds(column, HD)] = (
                        acc_ref[question, head, part, :] / l_ref[question, head, part, :]
                    ).astype(out_ref.dtype)


def attend_call(first, last, rounds, most, recv, q, rest, item):
    per_device, heads, rows, _ = q.shape
    state = jax.ShapeDtypeStruct(q.shape, jnp.float32)
    smem = pl.BlockSpec(memory_space=pltpu.SMEM)
    vmem = pl.BlockSpec(memory_space=pltpu.VMEM)
    anyspace = pl.BlockSpec(memory_space=pl.ANY)
    if first:
        in_specs = [smem, vmem, smem, vmem, anyspace]
        entries = most
    else:
        in_specs = [smem, vmem] + [vmem] * 3 + [anyspace] * len(rounds)
        entries = most * len(rounds)
    scratch = [pltpu.VMEM((2,) + item, q.dtype), pltpu.SemaphoreType.DMA((2,))]
    if last:
        out_shape = jax.ShapeDtypeStruct((per_device * LQ, heads * GROUP * HD), q.dtype)
        out_specs = vmem
        scratch = [pltpu.VMEM(q.shape, jnp.float32)] * 3 + scratch
    else:
        out_shape = [state] * 3
        out_specs = [vmem] * 3
    weights = entries * heads * rows * item[1]
    return pl.pallas_call(
        functools.partial(attend_kernel, first, last, rounds, most),
        out_shape=out_shape,
        in_specs=in_specs,
        out_specs=out_specs,
        scratch_shapes=scratch,
        name="attend_first" if first else ("attend_last" if last else "attend_more"),
        cost_estimate=pl.CostEstimate(
            flops=weights * HD * 4,
            bytes_accessed=entries * math.prod(item) * 2,
            transcendentals=weights,
        ),
    )(recv, q, *rest)


def weight_blocks(own, n):
    if n & (n - 1):
        return [lax.all_gather(own, "pass", axis=1, tiled=True)]
    have = {0: own}
    bit = n // 2
    while bit:
        for k in list(have):
            have[k ^ bit] = lax.ppermute(have[k], "pass", pairs_of(bit, n))
        bit //= 2
    return [have[k] for k in range(n)]


def project(context, weights):
    parts = [
        jnp.dot(context, weight, preferred_element_type=jnp.float32).astype(jnp.bfloat16)
        for weight in weights
    ]
    me = lax.axis_index("pass")
    bit = len(parts) // 2
    while bit:
        swap = (me & bit) != 0
        parts = [jnp.where(swap, parts[k ^ bit], parts[k]) for k in range(len(parts))]
        bit //= 2
    return jnp.concatenate(parts, axis=1)


def body(queries, own_kv, passage_cache, out_weight, lists, passage_slot, question_slot):
    n = lax.axis_size("pass")
    per_device = queries.shape[0] // LQ
    heads = own_kv.shape[1]
    entries = per_device * lists.shape[1]
    most = (entries + n - 1) // n
    order = order_of(n)
    cache = jnp.transpose(passage_cache, (0, 2, 1, 3))
    recv, own_row, *items = gather(
        lists, passage_slot, question_slot, cache, n, most, per_device, order
    )
    arrived = [
        lax.ppermute(item, "pass", pairs_of(k, n)) for k, item in zip(order, items)
    ]
    weights = weight_blocks(out_weight, n)
    q = (
        queries.reshape(per_device, LQ, heads, GROUP, HD)
        .transpose(0, 2, 3, 1, 4)
        .reshape(per_device, heads, GROUP * LQ, HD)
    )
    own = own_kv.reshape(per_device, LQ, heads, 2 * HD).transpose(0, 2, 1, 3)
    item = cache.shape[1:]
    state = attend_call(True, False, (0,), most, recv, q, (own_row, own, cache), item)
    calls = 3
    bounds = [len(order) * i // calls for i in range(calls + 1)]
    for i in range(calls):
        rounds = tuple(order[bounds[i] : bounds[i + 1]])
        rest = tuple(state) + tuple(arrived[bounds[i] : bounds[i + 1]])
        state = attend_call(False, i == calls - 1, rounds, most, recv, q, rest, item)
    context = state
    return lax.psum_scatter(project(context, weights), "head", scatter_dimension=1, tiled=True)


LINE = 4
EXTRA = 16


def mirror(k, ends=None):
    pairs = [(p, p ^ int(2 * k)) for p in range(2 * LINE)]
    if ends is None:
        return pairs
    return [(p, d) for p, d in pairs if (p // 2 in (0, LINE - 1)) == (ends == "outer")]


def is_inner():
    z = lax.axis_index("pass") // 2
    return jnp.logical_and(z > 0, z < LINE - 1)


def sort_kernel(most, per_device, lists_ref, pslot_ref, qslot_ref, cache_ref, *refs):
    row_ref, tag_ref, far_tag_ref = refs[:3]
    outs = refs[3 : 3 + LINE]
    send_row, near_cnt, send_cnt, far_cnt, buf, in_sem, out_sem = refs[3 + LINE :]
    me = lax.axis_index("pass")
    z, x = me // 2, me % 2
    pass_dev = cache_ref.shape[0]
    topp, nq = lists_ref.shape
    for k in range(LINE):
        near_cnt[k] = 0
        send_cnt[k] = 0
        far_cnt[k] = 0

    def question(q, carry):
        slot = qslot_ref[q]
        dest = slot // per_device
        local = slot - dest * per_device
        k = (dest // 2) ^ z
        same = dest % 2 == x
        for t in range(topp):
            row = pslot_ref[lists_ref[t, q]]
            owner = row // pass_dev
            mine = owner == me

            @pl.when(jnp.logical_and(mine, same))
            def _():
                at = k * most + near_cnt[k]
                row_ref[at] = row - owner * pass_dev
                tag_ref[at] = local
                near_cnt[k] = near_cnt[k] + 1

            @pl.when(jnp.logical_and(mine, jnp.logical_not(same)))
            def _():
                send_row[k * most + send_cnt[k]] = row - owner * pass_dev
                send_cnt[k] = send_cnt[k] + 1

            @pl.when(jnp.logical_and(owner == (me ^ 1), same))
            def _():
                far_tag_ref[k * most + far_cnt[k]] = local
                far_cnt[k] = far_cnt[k] + 1

        return carry

    lax.fori_loop(0, nq, question, 0)
    copies = []
    for k in (1, 2, 3, 0):
        for r in range(most):
            i = k * most + r
            get = pltpu.make_async_copy(cache_ref.at[send_row[i]], buf.at[i], in_sem.at[i])
            get.start()
            copies.append((get, pltpu.make_async_copy(buf.at[i], outs[k].at[r], out_sem.at[i])))
    for get, put in copies:
        get.wait()
        put.start()
    for get, put in copies:
        put.wait()


def sort_items(lists, passage_slot, question_slot, cache, most, per_device):
    item = cache.shape[1:]
    slots = LINE * most
    smem = pl.BlockSpec(memory_space=pltpu.SMEM)
    anyspace = pl.BlockSpec(memory_space=pl.ANY)
    return pl.pallas_call(
        functools.partial(sort_kernel, most, per_device),
        out_shape=[jax.ShapeDtypeStruct((slots,), jnp.int32)] * 3
        + [jax.ShapeDtypeStruct((most,) + item, cache.dtype)] * LINE,
        in_specs=[smem, smem, smem, anyspace],
        out_specs=[smem] * 3 + [anyspace] * LINE,
        scratch_shapes=[
            pltpu.SMEM((slots,), jnp.int32),
            pltpu.SMEM((LINE,), jnp.int32),
            pltpu.SMEM((LINE,), jnp.int32),
            pltpu.SMEM((LINE,), jnp.int32),
            pltpu.VMEM((slots,) + item, cache.dtype),
            pltpu.SemaphoreType.DMA((slots,)),
            pltpu.SemaphoreType.DMA((slots,)),
        ],
        name="sort_items",
        cost_estimate=pl.CostEstimate(
            flops=0, bytes_accessed=2 * slots * math.prod(item) * 2, transcendentals=0
        ),
    )(lists.T, passage_slot, question_slot, cache)


def unit():
    r = lax.broadcasted_iota(jnp.int32, (LQ, LQ), 0)
    c = lax.broadcasted_iota(jnp.int32, (LQ, LQ), 1)
    return r == c


def part_step(q_ref, m_ref, l_ref, acc_ref, question, head, keys, values, causal):
    rows = GROUP * LQ
    width = keys.shape[0]
    ones = jnp.ones(values.shape, values.dtype)
    extended = jnp.concatenate([values, ones], axis=1)
    tokens = pl.ds(pl.multiple_of(question * LQ, LQ), LQ)
    for start in range(0, rows, ROWS):
        part = pl.ds(start, ROWS)
        q = jnp.concatenate(
            [
                q_ref[tokens, pl.ds(pl.multiple_of((head * GROUP + g) * HD, HD), HD)]
                for g in range(start // LQ, (start + ROWS) // LQ)
            ],
            axis=0,
        )
        scores = (
            lax.dot_general(q, keys, (((1,), (1,)), ((), ())), preferred_element_type=jnp.float32)
            * COEF
        )
        if causal:
            token = lax.broadcasted_iota(jnp.int32, scores.shape, 0) % LQ
            column = lax.broadcasted_iota(jnp.int32, scores.shape, 1)
            scores = jnp.where(column <= token, scores, NEG)
        old = m_ref[question, head, part, :]
        new = jnp.maximum(old, jnp.max(scores, axis=1, keepdims=True))
        weights = jnp.exp2(scores - jnp.concatenate([new] * (width // HD), axis=1))
        mixed = jnp.dot(
            weights.astype(jnp.bfloat16), extended, preferred_element_type=jnp.float32
        )
        alpha = jnp.exp2(old - new)
        m_ref[question, head, part, :] = new
        l_ref[question, head, part, :] = l_ref[question, head, part, :] * alpha + mixed[:, HD:]
        acc_ref[question, head, part, :] = (
            acc_ref[question, head, part, :] * alpha + mixed[:, :HD]
        )


def part_kernel(k, most, heads, *refs):
    refs = list(refs)
    row_ref, tag_ref, far_tag_ref = refs.pop(0), refs.pop(0), refs.pop(0)
    own_ref = refs.pop(0) if k == 0 else None
    questions = [refs.pop(0) for _ in range(2 if k > 1 else 1)]
    cache_ref, items_ref, out_ref, q_ref, m_ref, l_ref, acc_ref, buf, sem, q_sem = refs
    per_device = q_ref.shape[0] // LQ
    entries = 2 * most

    def fetch(i, slot):
        @pl.when(i < most)
        def _():
            row = row_ref[k * most + jnp.minimum(i, most - 1)]
            pltpu.make_async_copy(cache_ref.at[row], buf.at[slot], sem.at[slot]).start()

        @pl.when(i >= most)
        def _():
            pltpu.make_async_copy(
                items_ref.at[jnp.maximum(i - most, 0)], buf.at[slot], sem.at[slot]
            ).start()

    if len(questions) == 1:
        pltpu.make_async_copy(questions[0], q_ref, q_sem).start()
    else:
        inner = is_inner()

        @pl.when(inner)
        def _():
            pltpu.make_async_copy(questions[0], q_ref, q_sem).start()

        @pl.when(jnp.logical_not(inner))
        def _():
            pltpu.make_async_copy(questions[1], q_ref, q_sem).start()

    fetch(jnp.int32(0), 0)
    m_ref[...] = jnp.full(m_ref.shape, NEG, jnp.float32)
    l_ref[...] = jnp.zeros(l_ref.shape, jnp.float32)
    acc_ref[...] = jnp.zeros(acc_ref.shape, jnp.float32)
    pltpu.make_async_copy(q_ref, q_ref, q_sem).wait()
    if k == 0:

        def own_block(i, carry):
            question, head = i // heads, lax.rem(i, heads)
            part_step(
                q_ref,
                m_ref,
                l_ref,
                acc_ref,
                question,
                head,
                own_ref[question, head, :, :HD],
                own_ref[question, head, :, HD:],
                True,
            )
            return carry

        lax.fori_loop(0, per_device * heads, own_block, 0)

    def item(i, carry):
        slot = lax.rem(i, 2)
        pltpu.make_async_copy(buf.at[slot], buf.at[slot], sem.at[slot]).wait()

        @pl.when(i + 1 < entries)
        def _():
            fetch(i + 1, lax.rem(i + 1, 2))

        at = k * most + lax.rem(i, most)
        tag = jnp.where(i < most, tag_ref[at], far_tag_ref[at])

        def one_head(head, carry):
            part_step(
                q_ref,
                m_ref,
                l_ref,
                acc_ref,
                tag,
                head,
                buf[slot, head, :, :HD],
                buf[slot, head, :, HD:],
                False,
            )
            return carry

        return lax.fori_loop(0, heads, one_head, carry)

    lax.fori_loop(0, entries, item, 0)
    eye = unit()
    row_of = lax.broadcasted_iota(jnp.int32, (8, LQ), 0)

    def close(c, carry):
        head, g = c // GROUP, lax.rem(c, GROUP)
        columns = pl.ds(pl.multiple_of(c * HD, HD), HD)
        part = pl.ds(pl.multiple_of(g * LQ, LQ), LQ)
        tile = jnp.full((8, LQ), NEG, jnp.float32)
        for question in range(per_device):
            total = l_ref[question, head, part, :]
            some = total > 0.0
            safe = jnp.where(some, total, 1.0)
            out_ref[pl.ds(question * LQ, LQ), columns] = (
                acc_ref[question, head, part, :] / safe
            ).astype(out_ref.dtype)
            level = jnp.where(some, m_ref[question, head, part, :] + jnp.log2(safe), NEG)
            line = jnp.sum(jnp.where(eye, level, 0.0), axis=0, keepdims=True)
            tile = jnp.where(row_of == question, line, tile)
        store_level(out_ref, columns, tile)
        return carry

    lax.fori_loop(0, heads * GROUP, close, 0)


def store_level(out_ref, columns, tile):
    high = tile.astype(jnp.bfloat16).astype(jnp.float32)
    both = jnp.concatenate([high, tile - high], axis=0)
    out_ref[pl.ds(out_ref.shape[0] - EXTRA, EXTRA), columns] = both.astype(out_ref.dtype)


def load_level(ref, columns):
    both = ref[pl.ds(ref.shape[0] - EXTRA, EXTRA), columns].astype(jnp.float32)
    return both[:8] + both[8:]


def part_call(k, most, tables, own, questions, cache, items):
    tokens, columns = questions[0].shape
    heads, item = cache.shape[1], cache.shape[1:]
    state = (tokens // LQ, heads, GROUP * LQ, HD)
    smem = pl.BlockSpec(memory_space=pltpu.SMEM)
    vmem = pl.BlockSpec(memory_space=pltpu.VMEM)
    anyspace = pl.BlockSpec(memory_space=pl.ANY)
    owned = [own] if k == 0 else []
    weights = 2 * most * heads * GROUP * LQ * item[1]
    return pl.pallas_call(
        functools.partial(part_kernel, k, most, heads),
        out_shape=jax.ShapeDtypeStruct((tokens + EXTRA, columns), cache.dtype),
        in_specs=[smem] * 3 + [vmem] * len(owned) + [anyspace] * (len(questions) + 2),
        out_specs=vmem,
        scratch_shapes=[
            pltpu.VMEM((tokens, columns), cache.dtype),
            pltpu.VMEM(state, jnp.float32),
            pltpu.VMEM(state, jnp.float32),
            pltpu.VMEM(state, jnp.float32),
            pltpu.VMEM((2,) + item, cache.dtype),
            pltpu.SemaphoreType.DMA((2,)),
            pltpu.SemaphoreType.DMA,
        ],
        cost_estimate=pl.CostEstimate(
            flops=weights * HD * 4,
            bytes_accessed=2 * most * math.prod(item) * 2,
            transcendentals=weights,
        ),
    )(*tables, *owned, *questions, cache, items)


def merge_into(a_ref, b_ref, out_ref, out_rows, leveled):
    rows = a_ref.shape[0] - EXTRA
    eye = unit()
    ones = jnp.ones((2 * LQ, LQ), jnp.bfloat16)

    def tile(c, carry):
        columns = pl.ds(pl.multiple_of(c * HD, HD), HD)
        one, two = load_level(a_ref, columns), load_level(b_ref, columns)
        top = jnp.maximum(one, two)
        first, second = jnp.exp2(one - top), jnp.exp2(two - top)
        total = first + second
        share = first / total
        high = share.astype(jnp.bfloat16).astype(jnp.float32)
        low = share - high
        for question in range(rows // LQ):
            at = slice(question, question + 1)
            spread = jnp.concatenate(
                [
                    jnp.where(eye, jnp.broadcast_to(v[at, :], (LQ, LQ)), 0.0).astype(jnp.bfloat16)
                    for v in (high, low)
                ],
                axis=1,
            )
            column = jnp.dot(spread, ones, preferred_element_type=jnp.float32)
            tokens = pl.ds(question * LQ, LQ)
            a = a_ref[tokens, columns].astype(jnp.float32)
            b = b_ref[tokens, columns].astype(jnp.float32)
            out_ref[pl.ds(out_rows + question * LQ, LQ), columns] = (
                b + (a - b) * column
            ).astype(out_ref.dtype)
        if leveled:
            store_level(out_ref, columns, top + jnp.log2(total))
        return carry

    lax.fori_loop(0, a_ref.shape[1] // HD, tile, 0)


def merge_kernel(a_ref, b_ref, out_ref):
    inner = is_inner()

    @pl.when(inner)
    def _():
        merge_into(a_ref, b_ref, out_ref, 0, True)

    @pl.when(jnp.logical_not(inner))
    def _():
        out_ref[...] = a_ref[...]


def merge(a, b):
    vmem = pl.BlockSpec(memory_space=pltpu.VMEM)
    return pl.pallas_call(
        merge_kernel,
        out_shape=jax.ShapeDtypeStruct(a.shape, a.dtype),
        in_specs=[vmem, vmem],
        out_specs=vmem,
        cost_estimate=pl.CostEstimate(
            flops=a.size * 8, bytes_accessed=a.size * 6, transcendentals=0
        ),
    )(a, b)


def finish_kernel(a_ref, b_ref, c_ref, d_ref, out_ref):
    rows = a_ref.shape[0] - EXTRA
    merge_into(a_ref, b_ref, out_ref, 0, False)
    merge_into(c_ref, d_ref, out_ref, rows, False)


def finish(a, b, c, d):
    vmem = pl.BlockSpec(memory_space=pltpu.VMEM)
    return pl.pallas_call(
        finish_kernel,
        out_shape=jax.ShapeDtypeStruct((2 * (a.shape[0] - EXTRA), a.shape[1]), a.dtype),
        in_specs=[vmem] * 4,
        out_specs=vmem,
        name="finish_context",
        cost_estimate=pl.CostEstimate(
            flops=a.size * 16, bytes_accessed=a.size * 12, transcendentals=0
        ),
    )(a, b, c, d)


def line_steps(queries, own_kv, passage_cache, out_weight, lists, passage_slot, question_slot):
    per_device = queries.shape[0] // LQ
    heads = own_kv.shape[1]
    most = per_device * lists.shape[1] // (2 * LINE)
    half = out_weight.shape[0] // 2

    def send(value, pairs):
        return lax.ppermute(value, "pass", pairs)

    def part(k, *args):
        return part_call(k, most, tables, own if k == 0 else None, *args)

    across = [(p, p ^ 1) for p in range(2 * LINE)]
    inner_across = [(p, d) for p, d in across if p // 2 in (1, 2)]
    outer_across = [(p, d) for p, d in across if p // 2 not in (1, 2)]
    near, middle = mirror(1), mirror(3, "inner")
    inward, outward = mirror(1, "outer"), mirror(1, "inner")
    q_near = send(queries, near)
    q_mid = send(queries, middle)
    w_across0 = send(out_weight[:half], across)
    w_across1 = send(out_weight[half:], across)
    cache = jnp.transpose(passage_cache, (0, 2, 1, 3))
    row, tag, far_tag, *items = sort_items(
        lists, passage_slot, question_slot, cache, most, per_device
    )
    tables = (row, tag, far_tag)
    q_out = send(q_mid, outward)
    q_cross = send(q_near, middle)
    q_end = send(q_cross, outward)
    far = [send(items[k], across) for k in range(LINE)]
    own = own_kv.reshape(per_device, LQ, heads, 2 * HD).transpose(0, 2, 1, 3)
    part2 = part(2, [q_cross, q_out], cache, far[2])
    part3 = part(3, [q_mid, q_end], cache, far[3])
    part0 = part(0, [queries], cache, far[0])
    part1 = part(1, [q_near], cache, far[1])
    back2 = send(part2, inward)
    back3 = send(part3, inward)
    w_in = send(out_weight, mirror(2, "outer"))
    w_out = send(out_weight, mirror(2, "inner"))
    w_in_both = send(w_in, inner_across)
    w_out_both = send(w_out, outer_across)
    cross3 = send(merge(part3, back2), middle)
    cross2 = send(merge(part2, back3), middle)
    near0 = merge(part0, cross3)
    near1 = merge(part1, cross2)
    beside = send(near0, near)
    back1 = send(near1, near)
    context = finish(near0, back1, near1, beside)
    return project_call(
        context, out_weight, w_across0, w_across1, w_in, w_in_both, w_out, w_out_both
    )


MESH = pl.DeviceIdType.MESH


def project_kernel(context_ref, own_ref, a0_ref, a1_ref, *refs):
    in_ref, in2_ref, out1_ref, out2_ref = refs[:4]
    out_ref, w_ref, part_ref, core_ref, y_ref, ysend_ref, zsend_ref = refs[4:11]
    w_sem, send_sem, recv_sem = refs[11:]
    me, head = lax.axis_index("pass"), lax.axis_index("head")
    z, x, y, core = me // 2, me % 2, head // 2, head % 2
    rows, wide = out_ref.shape[0], w_ref.shape[3]
    half = a0_ref.shape[0]
    inner = is_inner()
    core_peer = (me, head ^ 1)
    y_peer = (me, head ^ 2)
    z_peer = (me ^ 2, head ^ 1)
    stays = core == z % 2

    loads = [
        pltpu.make_async_copy(own_ref, w_ref.at[0, x], w_sem.at[0]),
        pltpu.make_async_copy(a0_ref, w_ref.at[0, 1 - x, pl.ds(0, half)], w_sem.at[1]),
        pltpu.make_async_copy(a1_ref, w_ref.at[0, 1 - x, pl.ds(half, half)], w_sem.at[2]),
    ]
    for load in loads:
        load.start()
    inner_loads = [
        pltpu.make_async_copy(in_ref, w_ref.at[1, x], w_sem.at[3]),
        pltpu.make_async_copy(in2_ref, w_ref.at[1, 1 - x], w_sem.at[4]),
    ]
    outer_loads = [
        pltpu.make_async_copy(out1_ref, w_ref.at[1, x], w_sem.at[3]),
        pltpu.make_async_copy(out2_ref, w_ref.at[1, 1 - x], w_sem.at[4]),
    ]

    @pl.when(inner)
    def _():
        for load in inner_loads:
            load.start()

    @pl.when(jnp.logical_not(inner))
    def _():
        for load in outer_loads:
            load.start()

    barrier = pltpu.get_barrier_semaphore()
    for peer in (core_peer, y_peer, z_peer):
        pl.semaphore_signal(barrier, inc=1, device_id=peer, device_id_type=MESH)
    pl.semaphore_wait(barrier, 3)

    def remote(src, dst, i, peer):
        return pltpu.make_async_remote_copy(
            src_ref=src,
            dst_ref=dst,
            send_sem=send_sem.at[i],
            recv_sem=recv_sem.at[i],
            device_id=peer,
            device_id_type=MESH,
        )

    def columns(j):
        return pl.ds(j * wide, wide)

    core_copies = [
        [remote(part_ref.at[s, j], core_ref.at[s, j], s * 2 + j, core_peer) for j in range(2)]
        for s in range(2)
    ]
    y_copies = [remote(ysend_ref.at[j], y_ref.at[j], 4 + j, y_peer) for j in range(2)]
    z_copies = [remote(zsend_ref.at[j], out_ref.at[:, columns(j)], 6 + j, z_peer) for j in range(2)]

    for load in loads + inner_loads:
        load.wait()

    def product(to_y, to_core, j):
        start = pl.multiple_of(jnp.where(to_core == z % 2, 0, rows), LQ)
        here = jnp.where(to_y == z // 2, 0, 1)
        return jnp.dot(
            context_ref[pl.ds(start, rows), :],
            w_ref[here, j],
            preferred_element_type=jnp.float32,
        ).astype(jnp.bfloat16)

    for s, to_y in enumerate((1 - y, y)):
        for j in range(2):
            part_ref[s, j] = product(to_y, 1 - core, j)
            core_copies[s][j].start()
        for j in range(2):
            value = product(to_y, core, j).astype(jnp.float32)
            core_copies[s][j].wait_recv()
            value = value + core_ref[s, j].astype(jnp.float32)
            if s == 0:
                ysend_ref[j] = value.astype(jnp.bfloat16)
                y_copies[j].start()
            else:
                y_copies[j].wait_recv()
                total = (value + y_ref[j].astype(jnp.float32)).astype(jnp.bfloat16)

                @pl.when(stays)
                def _():
                    out_ref[:, columns(j)] = total

                @pl.when(jnp.logical_not(stays))
                def _():
                    zsend_ref[j] = total
                    z_copies[j].start()

    @pl.when(jnp.logical_not(stays))
    def _():
        for copy in z_copies:
            copy.wait()

    for copies in core_copies + [y_copies]:
        for copy in copies:
            copy.wait_send()


def project_call(context, own, a0, a1, *lines):
    rows, depth = context.shape[0] // 2, context.shape[1]
    wide = own.shape[1]
    dtype = context.dtype
    vmem = pl.BlockSpec(memory_space=pltpu.VMEM)
    anyspace = pl.BlockSpec(memory_space=pl.ANY)
    return pl.pallas_call(
        project_kernel,
        out_shape=jax.ShapeDtypeStruct((rows, 2 * wide), dtype),
        in_specs=[vmem] + [anyspace] * 7,
        out_specs=vmem,
        scratch_shapes=[
            pltpu.VMEM((2, 2, depth, wide), dtype),
            pltpu.VMEM((2, 2, rows, wide), dtype),
            pltpu.VMEM((2, 2, rows, wide), dtype),
            pltpu.VMEM((2, rows, wide), dtype),
            pltpu.VMEM((2, rows, wide), dtype),
            pltpu.VMEM((2, rows, wide), dtype),
            pltpu.SemaphoreType.DMA((5,)),
            pltpu.SemaphoreType.DMA((8,)),
            pltpu.SemaphoreType.DMA((8,)),
        ],
        compiler_params=pltpu.CompilerParams(collective_id=0, has_side_effects=True),
        name="project_sum",
        cost_estimate=pl.CostEstimate(
            flops=2 * 4 * 2 * rows * depth * wide,
            bytes_accessed=4 * depth * wide * 2,
            transcendentals=0,
        ),
    )(context, own, a0, a1, *lines)


def suits_line(mesh, queries, lists):
    passes, heads = mesh.shape["pass"], mesh.shape["head"]
    entries = queries.shape[0] // LQ // passes * lists.shape[1]
    return passes == 2 * LINE and heads == LINE and entries % passes == 0


def solution(mesh):
    in_specs = (
        P("pass", "head"),
        P("pass", "head", None),
        P("pass", None, "head", None),
        P("head", "pass"),
        P(),
        P(),
        P(),
    )
    out_specs = P("pass", "head")

    def run(*args):
        if not suits_line(mesh, args[0], args[4]):
            return jax.shard_map(
                body, mesh=mesh, in_specs=in_specs, out_specs=out_specs, check_vma=False
            )(*args)
        step = jax.shard_map(
            line_steps, mesh=mesh, in_specs=in_specs, out_specs=out_specs, check_vma=False
        )
        return step(*args)

    return run
```

profile of v0, /device:TPU:0, one launch (start us, length us, event | category | flops | bytes accessed | tf_op | source)
XLA Modules:
  0.0 402.3 jit_solution(5595322028281170828)
XLA Ops:
  0.0 3.1 collective-permute-start.2
  3.8 33.9 %collective-permute-done.2.refs_3_ = bf16[384,2048]{1,0:T(8,128)(2,1)} collective-permute-done((bf16[384,2048]{1,0:T(8,128)(2,1)}, bf16[384,2048]{1,0:T(8,128)(2,1)}, u32[]{:S(2)}, u32[]{:S(2)}) %collective-permute-start.2) | collective-permute-done | bytes 1572896 | tf_op jit(solution)/shard_map/ppermute | solution.py:734
  38.5 8.2 %copy.16 = bf16[16,512,2,256]{3,1,2,0:T(8,128)(2,1)} copy(bf16[16,512,2,256]{3,2,1,0:T(2,128)(2,1)} %param.9) | data formatting | bytes 16777216 | tf_op args[2]
  46.7 10.7 %sort_items.1 = (s32[12]{0:T(128)}, s32[12]{0:T(128)}, s32[12]{0:T(128)}, bf16[3,2,512,256]{3,2,1,0:T(8,128)(2,1)}, bf16[3,2,512,256]{3,2,1,0:T(8,128)(2,1)}, /*...) custom-call(s32[8,24]{1,0:T(8,128)} %bitcast.15, s32[128]{0:T(128)} %pslot_ref.1, s32[24]{0:T(128)} %qslot_ref.1, ...), custom_call_target="tpu_custom_call" | custom-call | bytes 12582912 | tf_op jit(solution)/shard_map/sort_items/pallas_call | solution.py:428
  62.1 32.8 %collective-permute-done.7.refs_6_ = bf16[3,2,512,256]{3,2,1,0:T(8,128)(2,1)S(1)} collective-permute-done((bf16[3,2,512,256]{3,2,1,0:T(8,128)(2,1)}, bf16[3,2,512,256]{3,2,1,0:T(8,128)(2,1)S(1)}, u32[]{:S(2)}, u32[]{:S(2)}) %collective-permute-start.7) | collective-permute-done | bytes 1572896 | tf_op jit(solution)/shard_map/ppermute | solution.py:734
  94.9 5.0 %collective-permute-done.6.refs_4_ = bf16[384,2048]{1,0:T(8,128)(2,1)S(1)} collective-permute-done((bf16[384,2048]{1,0:T(8,128)(2,1)S(1)}, bf16[384,2048]{1,0:T(8,128)(2,1)S(1)}, u32[]{:S(2)}, u32[]{:S(2)}) %collective-permute-start.6) | collective-permute-done | bytes 1572896 | tf_op jit(solution)/shard_map/ppermute | solution.py:734
  101.1 17.7 %shard_map.75.a_ref = bf16[400,2048]{1,0:T(8,128)(2,1)} custom-call(s32[12]{0:T(128)} %get-tuple-element.12.refs_0_, s32[12]{0:T(128)} %get-tuple-element.13.refs_1_, s32[12]{0:T(128)} %get-tuple-element.14.refs_2_, bf16[384,2048]{1,0:T(8,128)(2,1)} %copy-done.2, bf16[384,2048]{1,0:T(8,128)(2,1)} %copy-done.4, bf16[16,2,512,256]{3,2,1,0:T(8,128)(2,1)} %bitcast.9, ...), custom_call_target="tpu_custom_call" | custom-call | flops 3221225472 | bytes 3145728 | tf_op jit(solution)/shard_map/pallas_call | solution.py:623
  118.8 4.0 collective-permute-start.8
  122.8 4.2 %collective-permute-done.5.refs_6_ = bf16[3,2,512,256]{3,2,1,0:T(8,128)(2,1)} collective-permute-done((bf16[3,2,512,256]{3,2,1,0:T(8,128)(2,1)}, bf16[3,2,512,256]{3,2,1,0:T(8,128)(2,1)}, u32[]{:S(2)}, u32[]{:S(2)}) %collective-permute-start.5) | collective-permute-done | bytes 1572896 | tf_op jit(solution)/shard_map/ppermute | solution.py:734
  127.0 4.5 %collective-permute-done.4.refs_4_ = bf16[384,2048]{1,0:T(8,128)(2,1)} collective-permute-done((bf16[384,2048]{1,0:T(8,128)(2,1)S(1)}, bf16[384,2048]{1,0:T(8,128)(2,1)}, u32[]{:S(2)}, u32[]{:S(2)}) %collective-permute-start.4) | collective-permute-done | bytes 1572896 | tf_op jit(solution)/shard_map/ppermute | solution.py:734
  131.5 17.7 %shard_map.74.a_ref = bf16[400,2048]{1,0:T(8,128)(2,1)} custom-call(s32[12]{0:T(128)} %get-tuple-element.12.refs_0_, s32[12]{0:T(128)} %get-tuple-element.13.refs_1_, s32[12]{0:T(128)} %get-tuple-element.14.refs_2_, bf16[384,2048]{1,0:T(8,128)(2,1)} %copy-done.1, bf16[384,2048]{1,0:T(8,128)(2,1)} %collective-permute-done.4.refs_4_, ...), custom_call_target="tpu_custom_call" | custom-call | flops 3221225472 | bytes 3145728 | tf_op jit(solution)/shard_map/pallas_call | solution.py:623
  149.2 2.8 collective-permute-start.11
  153.3 3.1 collective-permute-done.8.b_ref
  156.3 3.2 shard_map.76
  159.5 1.8 collective-permute-start.9
  161.4 10.7 %collective-permute-start.17 = (bf16[2048,512]{1,0:T(8,128)(2,1)S(1)}, bf16[2048,512]{1,0:T(8,128)(2,1)}, u32[]{:S(2)}, u32[]{:S(2)}) collective-permute-start(bf16[2048,512]{1,0:T(8,128)(2,1)S(1)} %copy-done), channel_id=1, source_target_pairs={{0,16},{4,20},{24,8},{28,12},{1,17},{5,21},{25,9},{29,13},{2,18},{... | collective-permute-start | bytes 6291464 | tf_op jit(solution)/shard_map/ppermute | solution.py:734
  173.3 18.1 %collective-permute-done.11.b_ref = bf16[400,2048]{1,0:T(8,128)(2,1)} collective-permute-done((bf16[400,2048]{1,0:T(8,128)(2,1)}, bf16[400,2048]{1,0:T(8,128)(2,1)}, u32[]{:S(2)}, u32[]{:S(2)}) %collective-permute-start.11) | collective-permute-done | bytes 1638432 | tf_op jit(solution)/shard_map/ppermute | solution.py:734
  192.7 3.2 shard_map.79
  198.5 22.5 %shard_map.73.a_ref = bf16[400,2048]{1,0:T(8,128)(2,1)} custom-call(s32[12]{0:T(128)} %get-tuple-element.12.refs_0_, s32[12]{0:T(128)} %get-tuple-element.13.refs_1_, s32[12]{0:T(128)} %get-tuple-element.14.refs_2_, bf16[3,2,128,256]{3,2,1,0:T(8,128)(2,1)} %bitcast.13, bf16[384,2048]{1,0:T(8,128)(2,1)} %refs_4_.1, bf16[16,2,512,256]{3,2,1,0:T(8,128)(2,1)} %bitcast.11, ...), custom_call_target="tpu_custom_call" | custom-call | flops 3221225472 | bytes 3145728 | tf_op jit(solution)/shard_map/pallas_call | solution.py:623
  221.1 3.2 shard_map.77.a_ref
  224.3 33.5 %collective-permute-start.14 = (bf16[400,2048]{1,0:T(8,128)(2,1)}, bf16[400,2048]{1,0:T(8,128)(2,1)}, u32[]{:S(2)}, u32[]{:S(2)}) collective-permute-start(bf16[400,2048]{1,0:T(8,128)(2,1)} %shard_map.77.a_ref), channel_id=1, source_target_pairs={{0,8},{4,12},{8,0},{12,4},{16,24},{20,28},{24,16},{28,20},{1,9},{5... | collective-permute-start | bytes 4915208 | tf_op jit(solution)/shard_map/ppermute | solution.py:734
  257.7 2.0 collective-permute-start.18
  259.7 35.9 %collective-permute-done.19.refs_2_ = bf16[2048,512]{1,0:T(8,128)(2,1)} collective-permute-done((bf16[2048,512]{1,0:T(8,128)(2,1)S(1)}, bf16[2048,512]{1,0:T(8,128)(2,1)}, u32[]{:S(2)}, u32[]{:S(2)}) %collective-permute-start.19) | collective-permute-done | bytes 2097184 | tf_op jit(solution)/shard_map/ppermute | solution.py:734
  295.6 3.1 collective-permute-start.20
  298.8 17.7 %shard_map.78.a_ref = bf16[400,2048]{1,0:T(8,128)(2,1)} custom-call(s32[12]{0:T(128)} %get-tuple-element.12.refs_0_, s32[12]{0:T(128)} %get-tuple-element.13.refs_1_, s32[12]{0:T(128)} %get-tuple-element.14.refs_2_, bf16[384,2048]{1,0:T(8,128)(2,1)} %collective-permute-done.2.refs_3_, bf16[16,2,512,256]{3,2,1,0:T(8,128)(2,1)} %bitcast.12, ...), custom_call_target="tpu_custom_call" | custom-call | flops 3221225472 | bytes 3145728 | tf_op jit(solution)/shard_map/pallas_call | solution.py:623
  316.5 3.2 shard_map.80.c_ref
  319.7 8.5 %collective-permute-start.13 = (bf16[400,2048]{1,0:T(8,128)(2,1)}, bf16[400,2048]{1,0:T(8,128)(2,1)}, u32[]{:S(2)}, u32[]{:S(2)}) collective-permute-start(bf16[400,2048]{1,0:T(8,128)(2,1)} %shard_map.80.c_ref), channel_id=1, source_target_pairs={{0,8},{4,12},{8,0},{12,4},{16,24},{20,28},{24,16},{28,20},{1,9},{5... | collective-permute-start | bytes 4915208 | tf_op jit(solution)/shard_map/ppermute | solution.py:734
  331.3 23.4 %collective-permute-done.13.b_ref = bf16[400,2048]{1,0:T(8,128)(2,1)} collective-permute-done((bf16[400,2048]{1,0:T(8,128)(2,1)}, bf16[400,2048]{1,0:T(8,128)(2,1)}, u32[]{:S(2)}, u32[]{:S(2)}) %collective-permute-start.13) | collective-permute-done | bytes 1638432 | tf_op jit(solution)/shard_map/ppermute | solution.py:734
  354.7 11.4 %finish_context.1.context_ref = bf16[768,2048]{1,0:T(8,128)(2,1)} custom-call(bf16[400,2048]{1,0:T(8,128)(2,1)} %shard_map.77.a_ref, bf16[400,2048]{1,0:T(8,128)(2,1)} %collective-permute-done.13.b_ref, bf16[400,2048]{1,0:T(8,128)(2,1)} %shard_map.80.c_ref, bf16[400,2048]{1,0:T(8,128)(2,1)} %collective-permute-done.14.d_ref), custom_call_target="tpu_custom_call" | custom-call | flops 13107200 | bytes 9830400 | tf_op jit(solution)/shard_map/finish_context/pallas_call | solution.py:715
  366.2 4.4 %collective-permute-done.16.a1_ref = bf16[1024,512]{1,0:T(8,128)(2,1)S(1)} collective-permute-done((bf16[1024,512]{1,0:T(8,128)(2,1)S(1)}, bf16[1024,512]{1,0:T(8,128)(2,1)S(1)}, u32[]{:S(2)}, u32[]{:S(2)}) %collective-permute-start.16) | collective-permute-done | bytes 1048608 | tf_op jit(solution)/shard_map/ppermute | solution.py:734
  371.6 28.7 %project_sum.1 = bf16[384,1024]{1,0:T(8,128)(2,1)} custom-call(bf16[768,2048]{1,0:T(8,128)(2,1)} %finish_context.1.context_ref, bf16[2048,512]{1,0:T(8,128)(2,1)} %own_ref.1, bf16[1024,512]{1,0:T(8,128)(2,1)} %copy-done.6, bf16[1024,512]{1,0:T(8,128)(2,1)} %copy-done.7, bf16[2048,512]{1,0:T(8,128)(2,1)} %collective-permute-done.17.refs_0_, ...), custom_call_target="tpu_custom_call" | custom-call | flops 6442450944 | bytes 8388608 | tf_op jit(solution)/shard_map/project_sum/pallas_call | solution.py:900
  400.3 2.1 copy.19
  (41 shorter events, 17.9 us)
Async XLA Ops:
  0.0 37.8 %collective-permute-start.2 = (bf16[384,2048]{1,0:T(8,128)(2,1)}, bf16[384,2048]{1,0:T(8,128)(2,1)}, u32[]{:S(2)}, u32[]{:S(2)}) collective-permute-start(bf16[384,2048]{1,0:T(8,128)(2,1)} %refs_4_.1), channel_id=1, source_target_pairs={{0,8},{4,12},{8,0},{12,4},{16,24},{20,28},{24,16},{28,20},{1,9},{5... | collective-permute-start | bytes 4718600 | tf_op jit(solution)/shard_map/ppermute | solution.py:734
  3.1 56.2 %collective-permute-start.1 = (bf16[384,2048]{1,0:T(8,128)(2,1)}, bf16[384,2048]{1,0:T(8,128)(2,1)S(1)}, u32[]{:S(2)}, u32[]{:S(2)}) collective-permute-start(bf16[384,2048]{1,0:T(8,128)(2,1)} %refs_4_.1), channel_id=1, source_target_pairs={{8,16},{12,20},{16,8},{20,12},{9,17},{13,21},{17,9},{21,13},{10,18... | collective-permute-start | bytes 4718600 | tf_op jit(solution)/shard_map/ppermute | solution.py:734
  37.8 23.1 %collective-permute-start.3 = (bf16[384,2048]{1,0:T(8,128)(2,1)}, bf16[384,2048]{1,0:T(8,128)(2,1)S(1)}, u32[]{:S(2)}, u32[]{:S(2)}) collective-permute-start(bf16[384,2048]{1,0:T(8,128)(2,1)} %collective-permute-done.2.refs_3_), channel_id=1, source_target_pairs={{8,16},{12,20},{16,8},{20,12},{9,17},{13,21},{17,9},{21,13},{10,18... | collective-permute-start | bytes 4718600 | tf_op jit(solution)/shard_map/ppermute | solution.py:734
  57.4 37.5 %collective-permute-start.7 = (bf16[3,2,512,256]{3,2,1,0:T(8,128)(2,1)}, bf16[3,2,512,256]{3,2,1,0:T(8,128)(2,1)S(1)}, u32[]{:S(2)}, u32[]{:S(2)}) collective-permute-start(bf16[3,2,512,256]{3,2,1,0:T(8,128)(2,1)} %get-tuple-element.17), channel_id=1, source_target_pairs={{0,4},{4,0},{8,12},{12,8},{16,20},{20,16},{24,28},{28,24},{1,5},{5... | collective-permute-start | bytes 4718600 | tf_op jit(solution)/shard_map/ppermute | solution.py:734
  59.2 59.6 %copy-start.1 = (bf16[384,2048]{1,0:T(8,128)(2,1)}, bf16[384,2048]{1,0:T(8,128)(2,1)S(1)}, u32[]{:S(2)}) copy-start(bf16[384,2048]{1,0:T(8,128)(2,1)S(1)} %collective-permute-done.1.refs_3_) | copy-start | bytes 4718596
  59.2 40.7 %collective-permute-start.6 = (bf16[384,2048]{1,0:T(8,128)(2,1)S(1)}, bf16[384,2048]{1,0:T(8,128)(2,1)S(1)}, u32[]{:S(2)}, u32[]{:S(2)}) collective-permute-start(bf16[384,2048]{1,0:T(8,128)(2,1)S(1)} %collective-permute-done.1.refs_3_), channel_id=1, source_target_pairs={{8,0},{12,4},{16,24},{20,28},{9,1},{13,5},{17,25},{21,29},{10,2},{... | collective-permute-start | bytes 4718600 | tf_op jit(solution)/shard_map/ppermute | solution.py:734
  60.5 66.5 %collective-permute-start.5 = (bf16[3,2,512,256]{3,2,1,0:T(8,128)(2,1)}, bf16[3,2,512,256]{3,2,1,0:T(8,128)(2,1)}, u32[]{:S(2)}, u32[]{:S(2)}) collective-permute-start(bf16[3,2,512,256]{3,2,1,0:T(8,128)(2,1)} %get-tuple-element.16), channel_id=1, source_target_pairs={{0,4},{4,0},{8,12},{12,8},{16,20},{20,16},{24,28},{28,24},{1,5},{5... | collective-permute-start | bytes 4718600 | tf_op jit(solution)/shard_map/ppermute | solution.py:734
  60.9 40.3 %copy-start.2 = (bf16[384,2048]{1,0:T(8,128)(2,1)}, bf16[384,2048]{1,0:T(8,128)(2,1)S(1)}, u32[]{:S(2)}) copy-start(bf16[384,2048]{1,0:T(8,128)(2,1)S(1)} %collective-permute-done.3.refs_3_) | copy-start | bytes 4718596
  60.9 70.7 %collective-permute-start.4 = (bf16[384,2048]{1,0:T(8,128)(2,1)S(1)}, bf16[384,2048]{1,0:T(8,128)(2,1)}, u32[]{:S(2)}, u32[]{:S(2)}) collective-permute-start(bf16[384,2048]{1,0:T(8,128)(2,1)S(1)} %collective-permute-done.3.refs_3_), channel_id=1, source_target_pairs={{8,0},{12,4},{16,24},{20,28},{9,1},{13,5},{17,25},{21,29},{10,2},{... | collective-permute-start | bytes 4718600 | tf_op jit(solution)/shard_map/ppermute | solution.py:734
  94.9 5.0 %copy-start.3 = (bf16[3,2,512,256]{3,2,1,0:T(8,128)(2,1)}, bf16[3,2,512,256]{3,2,1,0:T(8,128)(2,1)S(1)}, u32[]{:S(2)}) copy-start(bf16[3,2,512,256]{3,2,1,0:T(8,128)(2,1)S(1)} %collective-permute-done.7.refs_6_) | copy-start | bytes 4718596
  100.0 1.1 copy-start.4
  118.8 37.5 %collective-permute-start.8 = (bf16[400,2048]{1,0:T(8,128)(2,1)}, bf16[400,2048]{1,0:T(8,128)(2,1)}, u32[]{:S(2)}, u32[]{:S(2)}) collective-permute-start(bf16[400,2048]{1,0:T(8,128)(2,1)} %shard_map.75.a_ref), channel_id=1, source_target_pairs={{0,8},{4,12},{24,16},{28,20},{1,9},{5,13},{25,17},{29,21},{2,10},{... | collective-permute-start | bytes 4915208 | tf_op jit(solution)/shard_map/ppermute | solution.py:734
  149.2 42.2 %collective-permute-start.11 = (bf16[400,2048]{1,0:T(8,128)(2,1)}, bf16[400,2048]{1,0:T(8,128)(2,1)}, u32[]{:S(2)}, u32[]{:S(2)}) collective-permute-start(bf16[400,2048]{1,0:T(8,128)(2,1)} %shard_map.74.a_ref), channel_id=1, source_target_pairs={{0,8},{4,12},{24,16},{28,20},{1,9},{5,13},{25,17},{29,21},{2,10},{... | collective-permute-start | bytes 4915208 | tf_op jit(solution)/shard_map/ppermute | solution.py:734
  152.0 9.4 %copy-start = (bf16[2048,512]{1,0:T(8,128)(2,1)S(1)}, bf16[2048,512]{1,0:T(8,128)(2,1)}, u32[]{:S(2)}) copy-start(bf16[2048,512]{1,0:T(8,128)(2,1)} %own_ref.1) | copy-start | bytes 6291460
  152.0 43.9 %collective-permute-start = (bf16[3,2,512,256]{3,2,1,0:T(8,128)(2,1)}, bf16[3,2,512,256]{3,2,1,0:T(8,128)(2,1)}, u32[]{:S(2)}, u32[]{:S(2)}) collective-permute-start(bf16[3,2,512,256]{3,2,1,0:T(8,128)(2,1)} %get-tuple-element.15), channel_id=1, source_target_pairs={{0,4},{4,0},{8,12},{12,8},{16,20},{20,16},{24,28},{28,24},{1,5},{5... | collective-permute-start | bytes 4718600 | tf_op jit(solution)/shard_map/ppermute | solution.py:734
  159.5 61.5 %collective-permute-start.9 = (bf16[400,2048]{1,0:T(8,128)(2,1)}, bf16[400,2048]{1,0:T(8,128)(2,1)}, u32[]{:S(2)}, u32[]{:S(2)}) collective-permute-start(bf16[400,2048]{1,0:T(8,128)(2,1)} %shard_map.76), channel_id=1, source_target_pairs={{8,16},{12,20},{16,8},{20,12},{9,17},{13,21},{17,9},{21,13},{10,18... | collective-permute-start | bytes 4915208 | tf_op jit(solution)/shard_map/ppermute | solution.py:734
  161.4 96.4 %collective-permute-start.17 = (bf16[2048,512]{1,0:T(8,128)(2,1)S(1)}, bf16[2048,512]{1,0:T(8,128)(2,1)}, u32[]{:S(2)}, u32[]{:S(2)}) collective-permute-start(bf16[2048,512]{1,0:T(8,128)(2,1)S(1)} %copy-done), channel_id=1, source_target_pairs={{0,16},{4,20},{24,8},{28,12},{1,17},{5,21},{25,9},{29,13},{2,18},{... | collective-permute-start | bytes 6291464 | tf_op jit(solution)/shard_map/ppermute | solution.py:734
  172.0 123.6 %collective-permute-start.19 = (bf16[2048,512]{1,0:T(8,128)(2,1)S(1)}, bf16[2048,512]{1,0:T(8,128)(2,1)}, u32[]{:S(2)}, u32[]{:S(2)}) collective-permute-start(bf16[2048,512]{1,0:T(8,128)(2,1)S(1)} %copy-done), channel_id=1, source_target_pairs={{8,24},{12,28},{16,0},{20,4},{9,25},{13,29},{17,1},{21,5},{10,26},... | collective-permute-start | bytes 6291464 | tf_op jit(solution)/shard_map/ppermute | solution.py:734
  191.4 6.3 %copy-start.5 = (bf16[384,2,256]{2,1,0:T(2,128)(2,1)S(1)}, bf16[384,2,256]{2,1,0:T(2,128)(2,1)}, u32[]{:S(2)}) copy-start(bf16[384,2,256]{2,1,0:T(2,128)(2,1)} %param.8) | copy-start | bytes 1179652
  191.4 107.3 %collective-permute-start.10 = (bf16[3,2,512,256]{3,2,1,0:T(8,128)(2,1)}, bf16[3,2,512,256]{3,2,1,0:T(8,128)(2,1)}, u32[]{:S(2)}, u32[]{:S(2)}) collective-permute-start(bf16[3,2,512,256]{3,2,1,0:T(8,128)(2,1)} %get-tuple-element.18), channel_id=1, source_target_pairs={{0,4},{4,0},{8,12},{12,8},{16,20},{20,16},{24,28},{28,24},{1,5},{5... | collective-permute-start | bytes 4718600 | tf_op jit(solution)/shard_map/ppermute | solution.py:734
  195.9 120.6 %collective-permute-start.12 = (bf16[400,2048]{1,0:T(8,128)(2,1)}, bf16[400,2048]{1,0:T(8,128)(2,1)}, u32[]{:S(2)}, u32[]{:S(2)}) collective-permute-start(bf16[400,2048]{1,0:T(8,128)(2,1)} %shard_map.79), channel_id=1, source_target_pairs={{8,16},{12,20},{16,8},{20,12},{9,17},{13,21},{17,9},{21,13},{10,18... | collective-permute-start | bytes 4915208 | tf_op jit(solution)/shard_map/ppermute | solution.py:734
  224.3 106.3 %collective-permute-start.14 = (bf16[400,2048]{1,0:T(8,128)(2,1)}, bf16[400,2048]{1,0:T(8,128)(2,1)}, u32[]{:S(2)}, u32[]{:S(2)}) collective-permute-start(bf16[400,2048]{1,0:T(8,128)(2,1)} %shard_map.77.a_ref), channel_id=1, source_target_pairs={{0,8},{4,12},{8,0},{12,4},{16,24},{20,28},{24,16},{28,20},{1,9},{5... | collective-permute-start | bytes 4915208 | tf_op jit(solution)/shard_map/ppermute | solution.py:734
  257.7 112.8 %collective-permute-start.18 = (bf16[2048,512]{1,0:T(8,128)(2,1)}, bf16[2048,512]{1,0:T(8,128)(2,1)}, u32[]{:S(2)}, u32[]{:S(2)}) collective-permute-start(bf16[2048,512]{1,0:T(8,128)(2,1)} %collective-permute-done.17.refs_0_), channel_id=1, source_target_pairs={{8,12},{12,8},{16,20},{20,16},{9,13},{13,9},{17,21},{21,17},{10,14... | collective-permute-start | bytes 6291464 | tf_op jit(solution)/shard_map/ppermute | solution.py:734
  295.6 75.0 %collective-permute-start.20 = (bf16[2048,512]{1,0:T(8,128)(2,1)}, bf16[2048,512]{1,0:T(8,128)(2,1)}, u32[]{:S(2)}, u32[]{:S(2)}) collective-permute-start(bf16[2048,512]{1,0:T(8,128)(2,1)} %collective-permute-done.19.refs_2_), channel_id=1, source_target_pairs={{0,4},{4,0},{24,28},{28,24},{1,5},{5,1},{25,29},{29,25},{2,6},{6,2... | collective-permute-start | bytes 6291464 | tf_op jit(solution)/shard_map/ppermute | solution.py:734
  319.7 35.0 %collective-permute-start.13 = (bf16[400,2048]{1,0:T(8,128)(2,1)}, bf16[400,2048]{1,0:T(8,128)(2,1)}, u32[]{:S(2)}, u32[]{:S(2)}) collective-permute-start(bf16[400,2048]{1,0:T(8,128)(2,1)} %shard_map.80.c_ref), channel_id=1, source_target_pairs={{0,8},{4,12},{8,0},{12,4},{16,24},{20,28},{24,16},{28,20},{1,9},{5... | collective-permute-start | bytes 4915208 | tf_op jit(solution)/shard_map/ppermute | solution.py:734
  329.3 36.9 %collective-permute-start.15 = (bf16[1024,512]{1,0:T(8,128)(2,1)}, bf16[1024,512]{1,0:T(8,128)(2,1)S(1)}, u32[]{:S(2)}, u32[]{:S(2)}) collective-permute-start(bf16[1024,512]{1,0:T(8,128)(2,1)} %get-tuple-element.20), channel_id=1, source_target_pairs={{0,4},{4,0},{8,12},{12,8},{16,20},{20,16},{24,28},{28,24},{1,5},{5... | collective-permute-start | bytes 3145736 | tf_op jit(solution)/shard_map/ppermute | solution.py:734
  330.5 40.0 %collective-permute-start.16 = (bf16[1024,512]{1,0:T(8,128)(2,1)S(1)}, bf16[1024,512]{1,0:T(8,128)(2,1)S(1)}, u32[]{:S(2)}, u32[]{:S(2)}) collective-permute-start(bf16[1024,512]{1,0:T(8,128)(2,1)S(1)} %get-tuple-element.19), channel_id=1, source_target_pairs={{0,4},{4,0},{8,12},{12,8},{16,20},{20,16},{24,28},{28,24},{1,5},{5... | collective-permute-start | bytes 3145736 | tf_op jit(solution)/shard_map/ppermute | solution.py:734
  366.2 4.4 %copy-start.6 = (bf16[1024,512]{1,0:T(8,128)(2,1)}, bf16[1024,512]{1,0:T(8,128)(2,1)S(1)}, u32[]{:S(2)}) copy-start(bf16[1024,512]{1,0:T(8,128)(2,1)S(1)} %collective-permute-done.15.a0_ref) | copy-start | bytes 3145732
  370.6 1.0 copy-start.7
where the time goes:
time: 407 us; the launch traced here: 402 us
  waiting for transfers between devices  165 us (41%)
  Pallas kernels  139 us (34%)
  starting transfers between devices  83.2 us (20%)
  local copies, waits for them, and re-layouts  14.3 us (4%)
    ppermute x21, waiting for transfers between devices, send(): return lax.ppermute(value, 'pass', pairs)  165 us
    ppermute x21, starting transfers between devices, send(): return lax.ppermute(value, 'pass', pairs)  83.2 us
    pallas_call x4, Pallas kernels, part_call(): pl.pallas_call(functools.partial(part_kernel, k, most, heads), out_shape=...  75.7 us
    pallas_call x1, Pallas kernels, project_call(): pl.pallas_call(project_kernel, out_shape=jax.ShapeDtypeStruct((rows, 2 *...  28.7 us
    pallas_call x4, Pallas kernels, merge(): pl.pallas_call(merge_kernel, out_shape=jax.ShapeDtypeStruct(a.shape, a.dt...  12.9 us
    unnamed x18, local copies, waits for them, and re-layouts  12.4 us
    pallas_call x1, Pallas kernels, finish(): pl.pallas_call(finish_kernel, out_shape=jax.ShapeDtypeStruct((2 * (a.shap...  11.4 us
    pallas_call x1, Pallas kernels, sort_items(): pl.pallas_call(functools.partial(sort_kernel, most, per_device), out_shap...  10.7 us
  transfers between devices with their start and end apart: 21, of which 10 were waited for; matrix products, arithmetic and copies ran while one was open for 3% of the time, Pallas kernels for 28%

commit v1 on v0

--- a/solution.py
+++ b/solution.py
@@ -559,7 +559,7 @@
         at = k * most + lax.rem(i, most)
         tag = jnp.where(i < most, tag_ref[at], far_tag_ref[at])
 
-        def one_head(head, carry):
+        for head in range(heads):
             part_step(
                 q_ref,
                 m_ref,
@@ -571,44 +571,35 @@
                 buf[slot, head, :, HD:],
                 False,
             )
-            return carry
-
-        return lax.fori_loop(0, heads, one_head, carry)
+        return carry
 
     lax.fori_loop(0, entries, item, 0)
     eye = unit()
-    row_of = lax.broadcasted_iota(jnp.int32, (8, LQ), 0)
 
     def close(c, carry):
         head, g = c // GROUP, lax.rem(c, GROUP)
         columns = pl.ds(pl.multiple_of(c * HD, HD), HD)
         part = pl.ds(pl.multiple_of(g * LQ, LQ), LQ)
-        tile = jnp.full((8, LQ), NEG, jnp.float32)
         for question in range(per_device):
             total = l_ref[question, head, part, :]
             some = total > 0.0
             safe = jnp.where(some, total, 1.0)
-            out_ref[pl.ds(question * LQ, LQ), columns] = (
+            out_ref[question, :LQ, columns] = (
                 acc_ref[question, head, part, :] / safe
             ).astype(out_ref.dtype)
             level = jnp.where(some, m_ref[question, head, part, :] + jnp.log2(safe), NEG)
             line = jnp.sum(jnp.where(eye, level, 0.0), axis=0, keepdims=True)
-            tile = jnp.where(row_of == question, line, tile)
-        store_level(out_ref, columns, tile)
+            store_level(out_ref, question, columns, line)
         return carry
 
     lax.fori_loop(0, heads * GROUP, close, 0)
 
 
-def store_level(out_ref, columns, tile):
-    high = tile.astype(jnp.bfloat16).astype(jnp.float32)
-    both = jnp.concatenate([high, tile - high], axis=0)
-    out_ref[pl.ds(out_ref.shape[0] - EXTRA, EXTRA), columns] = both.astype(out_ref.dtype)
-
-
-def load_level(ref, columns):
-    both = ref[pl.ds(ref.shape[0] - EXTRA, EXTRA), columns].astype(jnp.float32)
-    return both[:8] + both[8:]
+def store_level(out_ref, question, columns, line):
+    row_of = lax.broadcasted_iota(jnp.int32, (EXTRA, line.shape[1]), 0)
+    high = line.astype(jnp.bfloat16).astype(jnp.float32)
+    both = jnp.where(row_of == 0, high, jnp.where(row_of == EXTRA // 2, line - high, 0.0))
+    out_ref[question, LQ:, columns] = both.astype(out_ref.dtype)
 
 
 def part_call(k, most, tables, own, questions, cache, items):
@@ -622,7 +613,7 @@
     weights = 2 * most * heads * GROUP * LQ * item[1]
     return pl.pallas_call(
         functools.partial(part_kernel, k, most, heads),
-        out_shape=jax.ShapeDtypeStruct((tokens + EXTRA, columns), cache.dtype),
+        out_shape=jax.ShapeDtypeStruct((tokens // LQ, LQ + EXTRA, columns), cache.dtype),
         in_specs=[smem] * 3 + [vmem] * len(owned) + [anyspace] * (len(questions) + 2),
         out_specs=vmem,
         scratch_shapes=[
@@ -642,41 +633,40 @@
     )(*tables, *owned, *questions, cache, items)
 
 
-def merge_into(a_ref, b_ref, out_ref, out_rows, leveled):
-    rows = a_ref.shape[0] - EXTRA
+def blend(a_ref, b_ref, out_ref, leveled):
     eye = unit()
     ones = jnp.ones((2 * LQ, LQ), jnp.bfloat16)
 
-    def tile(c, carry):
-        columns = pl.ds(pl.multiple_of(c * HD, HD), HD)
-        one, two = load_level(a_ref, columns), load_level(b_ref, columns)
-        top = jnp.maximum(one, two)
-        first, second = jnp.exp2(one - top), jnp.exp2(two - top)
-        total = first + second
-        share = first / total
-        high = share.astype(jnp.bfloat16).astype(jnp.float32)
-        low = share - high
-        for question in range(rows // LQ):
-            at = slice(question, question + 1)
-            spread = jnp.concatenate(
-                [
-                    jnp.where(eye, jnp.broadcast_to(v[at, :], (LQ, LQ)), 0.0).astype(jnp.bfloat16)
-                    for v in (high, low)
-                ],
-                axis=1,
-            )
-            column = jnp.dot(spread, ones, preferred_element_type=jnp.float32)
-            tokens = pl.ds(question * LQ, LQ)
-            a = a_ref[tokens, columns].astype(jnp.float32)
-            b = b_ref[tokens, columns].astype(jnp.float32)
-            out_ref[pl.ds(out_rows + question * LQ, LQ), columns] = (
-                b + (a - b) * column
-            ).astype(out_ref.dtype)
+    def level_of(ref):
+        both = ref[0, LQ:, :].astype(jnp.float32)
+        return both[:1] + both[EXTRA // 2 : EXTRA // 2 + 1]
+
+    one, two = level_of(a_ref), level_of(b_ref)
+    top = jnp.maximum(one, two)
+    first, second = jnp.exp2(one - top), jnp.exp2(two - top)
+    total = first + second
+    share = first / total
+    high = share.astype(jnp.bfloat16).astype(jnp.float32)
+    low = share - high
+    for c in range(share.shape[1] // HD):
+        columns = slice(c * HD, (c + 1) * HD)
+        spread = jnp.concatenate(
+            [
+                jnp.where(eye, jnp.broadcast_to(v[:, columns], (LQ, LQ)), 0.0).astype(jnp.bfloat16)
+                for v in (high, low)
+            ],
+            axis=1,
+        )
+        column = jnp.dot(spread, ones, preferred_element_type=jnp.float32)
+        a = a_ref[0, :LQ, columns].astype(jnp.float32)
+        b = b_ref[0, :LQ, columns].astype(jnp.float32)
+        value = (b + (a - b) * column).astype(out_ref.dtype)
         if leveled:
-            store_level(out_ref, columns, top + jnp.log2(total))
-        return carry
-
-    lax.fori_loop(0, a_ref.shape[1] // HD, tile, 0)
+            out_ref[0, :LQ, columns] = value
+        else:
+            out_ref[:, columns] = value
+    if leveled:
+        store_level(out_ref, 0, slice(None), top + jnp.log2(total))
 
 
 def merge_kernel(a_ref, b_ref, out_ref):
@@ -684,44 +674,44 @@
 
     @pl.when(inner)
     def _():
-        merge_into(a_ref, b_ref, out_ref, 0, True)
+        blend(a_ref, b_ref, out_ref, True)
 
     @pl.when(jnp.logical_not(inner))
     def _():
         out_ref[...] = a_ref[...]
 
 
-def merge(a, b):
-    vmem = pl.BlockSpec(memory_space=pltpu.VMEM)
+def finish_kernel(a_ref, b_ref, out_ref):
+    blend(a_ref, b_ref, out_ref, False)
+
+
+def question_spec(value, at):
+    shape = (1,) + value.shape[1:]
+    if value.shape[0] == 1:
+        return pl.BlockSpec(shape, lambda q: (0, 0, 0))
+    if at is None:
+        return pl.BlockSpec(shape, lambda q: (q, 0, 0))
+    return pl.BlockSpec(shape, lambda q: (at, 0, 0))
+
+
+def join_call(a, b, at, leveled):
+    questions = a.shape[0] if at is None else 1
+    columns = a.shape[2]
+    if leveled:
+        shape, block = (questions,) + a.shape[1:], (1,) + a.shape[1:]
+        out_spec = pl.BlockSpec(block, lambda q: (q, 0, 0))
+    else:
+        shape = (questions * LQ, columns)
+        out_spec = pl.BlockSpec((LQ, columns), lambda q: (q, 0))
+    size = questions * LQ * columns
     return pl.pallas_call(
-        merge_kernel,
-        out_shape=jax.ShapeDtypeStruct(a.shape, a.dtype),
-        in_specs=[vmem, vmem],
-        out_specs=vmem,
-        cost_estimate=pl.CostEstimate(
-            flops=a.size * 8, bytes_accessed=a.size * 6, transcendentals=0
-        ),
+        merge_kernel if leveled else finish_kernel,
+        out_shape=jax.ShapeDtypeStruct(shape, a.dtype),
+        grid=(questions,),
+        in_specs=[question_spec(a, at), question_spec(b, at)],
+        out_specs=out_spec,
+        cost_estimate=pl.CostEstimate(flops=size * 8, bytes_accessed=size * 6, transcendentals=0),
     )(a, b)
-
-
-def finish_kernel(a_ref, b_ref, c_ref, d_ref, out_ref):
-    rows = a_ref.shape[0] - EXTRA
-    merge_into(a_ref, b_ref, out_ref, 0, False)
-    merge_into(c_ref, d_ref, out_ref, rows, False)
-
-
-def finish(a, b, c, d):
-    vmem = pl.BlockSpec(memory_space=pltpu.VMEM)
-    return pl.pallas_call(
-        finish_kernel,
-        out_shape=jax.ShapeDtypeStruct((2 * (a.shape[0] - EXTRA), a.shape[1]), a.dtype),
-        in_specs=[vmem] * 4,
-        out_specs=vmem,
-        name="finish_context",
-        cost_estimate=pl.CostEstimate(
-            flops=a.size * 16, bytes_accessed=a.size * 12, transcendentals=0
-        ),
-    )(a, b, c, d)
 
 
 def line_steps(queries, own_kv, passage_cache, out_weight, lists, passage_slot, question_slot):
@@ -735,6 +725,9 @@
 
     def part(k, *args):
         return part_call(k, most, tables, own if k == 0 else None, *args)
+
+    def join(a, b, at=None, leveled=True):
+        return join_call(a, b, at, leveled)
 
     across = [(p, p ^ 1) for p in range(2 * LINE)]
     inner_across = [(p, d) for p, d in across if p // 2 in (1, 2)]
@@ -760,30 +753,42 @@
     part0 = part(0, [queries], cache, far[0])
     part1 = part(1, [q_near], cache, far[1])
     back2 = send(part2, inward)
-    back3 = send(part3, inward)
     w_in = send(out_weight, mirror(2, "outer"))
     w_out = send(out_weight, mirror(2, "inner"))
+    back3 = send(part3, inward)
     w_in_both = send(w_in, inner_across)
     w_out_both = send(w_out, outer_across)
-    cross3 = send(merge(part3, back2), middle)
-    cross2 = send(merge(part2, back3), middle)
-    near0 = merge(part0, cross3)
-    near1 = merge(part1, cross2)
+    cross3 = send(join(part3, back2), middle)
+    near0 = join(part0, cross3)
     beside = send(near0, near)
-    back1 = send(near1, near)
-    context = finish(near0, back1, near1, beside)
+    own_rows, near_rows = [], []
+    for q in range(per_device):
+        cross2 = send(join(part2, back3, q), middle)
+        near1 = join(part1, cross2, q)
+        back1 = send(near1, near)
+        near_rows.append(join(near1, beside, q, False))
+        own_rows.append(join(near0, back1, q, False))
     return project_call(
-        context, out_weight, w_across0, w_across1, w_in, w_in_both, w_out, w_out_both
+        own_rows + near_rows,
+        out_weight,
+        w_across0,
+        w_across1,
+        w_in,
+        w_in_both,
+        w_out,
+        w_out_both,
     )
 
 
 MESH = pl.DeviceIdType.MESH
 
 
-def project_kernel(context_ref, own_ref, a0_ref, a1_ref, *refs):
-    in_ref, in2_ref, out1_ref, out2_ref = refs[:4]
-    out_ref, w_ref, part_ref, core_ref, y_ref, ysend_ref, zsend_ref = refs[4:11]
-    w_sem, send_sem, recv_sem = refs[11:]
+def project_kernel(pieces, *refs):
+    rows_refs = refs[:pieces]
+    own_ref, a0_ref, a1_ref, in_ref, in2_ref, out1_ref, out2_ref = refs[pieces : pieces + 7]
+    refs = refs[pieces + 7 :]
+    out_ref, context_ref, w_ref, part_ref, core_ref, y_ref, ysend_ref, zsend_ref = refs[:8]
+    row_sem, w_sem, send_sem, recv_sem = refs[8:]
     me, head = lax.axis_index("pass"), lax.axis_index("head")
     z, x, y, core = me // 2, me % 2, head // 2, head % 2
     rows, wide = out_ref.shape[0], w_ref.shape[3]
@@ -794,32 +799,32 @@
     z_peer = (me ^ 2, head ^ 1)
     stays = core == z % 2
 
-    loads = [
-        pltpu.make_async_copy(own_ref, w_ref.at[0, x], w_sem.at[0]),
-        pltpu.make_async_copy(a0_ref, w_ref.at[0, 1 - x, pl.ds(0, half)], w_sem.at[1]),
-        pltpu.make_async_copy(a1_ref, w_ref.at[0, 1 - x, pl.ds(half, half)], w_sem.at[2]),
+    row_loads = [
+        pltpu.make_async_copy(ref, context_ref.at[pl.ds(i * LQ, LQ)], row_sem.at[i])
+        for i, ref in enumerate(rows_refs)
     ]
-    for load in loads:
+    for load in row_loads:
         load.start()
-    inner_loads = [
-        pltpu.make_async_copy(in_ref, w_ref.at[1, x], w_sem.at[3]),
-        pltpu.make_async_copy(in2_ref, w_ref.at[1, 1 - x], w_sem.at[4]),
-    ]
-    outer_loads = [
-        pltpu.make_async_copy(out1_ref, w_ref.at[1, x], w_sem.at[3]),
-        pltpu.make_async_copy(out2_ref, w_ref.at[1, 1 - x], w_sem.at[4]),
-    ]
-
-    @pl.when(inner)
-    def _():
-        for load in inner_loads:
-            load.start()
-
-    @pl.when(jnp.logical_not(inner))
-    def _():
-        for load in outer_loads:
-            load.start()
-
+
+    def load_here():
+        pltpu.make_async_copy(own_ref, w_ref.at[0, x], w_sem.at[0, x]).start()
+        low, high = w_ref.at[0, 1 - x, pl.ds(0, half)], w_ref.at[0, 1 - x, pl.ds(half, half)]
+        pltpu.make_async_copy(a0_ref, low, w_sem.at[0, 1 - x]).start()
+        pltpu.make_async_copy(a1_ref, high, w_sem.at[0, 1 - x]).start()
+
+    def load_there():
+        for which, (one, two) in (
+            (inner, (in_ref, in2_ref)),
+            (jnp.logical_not(inner), (out1_ref, out2_ref)),
+        ):
+
+            @pl.when(which)
+            def _():
+                pltpu.make_async_copy(one, w_ref.at[1, x], w_sem.at[1, x]).start()
+                pltpu.make_async_copy(two, w_ref.at[1, 1 - x], w_sem.at[1, 1 - x]).start()
+
+    load_here()
+    load_there()
     barrier = pltpu.get_barrier_semaphore()
     for peer in (core_peer, y_peer, z_peer):
         pl.semaphore_signal(barrier, inc=1, device_id=peer, device_id_type=MESH)
@@ -845,7 +850,7 @@
     y_copies = [remote(ysend_ref.at[j], y_ref.at[j], 4 + j, y_peer) for j in range(2)]
     z_copies = [remote(zsend_ref.at[j], out_ref.at[:, columns(j)], 6 + j, z_peer) for j in range(2)]
 
-    for load in loads + inner_loads:
+    for load in row_loads:
         load.wait()
 
     def product(to_y, to_core, j):
@@ -858,10 +863,12 @@
         ).astype(jnp.bfloat16)
 
     for s, to_y in enumerate((1 - y, y)):
+        here = jnp.where(to_y == z // 2, 0, 1)
         for j in range(2):
+            block = w_ref.at[here, j]
+            pltpu.make_async_copy(block, block, w_sem.at[here, j]).wait()
             part_ref[s, j] = product(to_y, 1 - core, j)
             core_copies[s][j].start()
-        for j in range(2):
             value = product(to_y, core, j).astype(jnp.float32)
             core_copies[s][j].wait_recv()
             value = value + core_ref[s, j].astype(jnp.float32)
@@ -891,25 +898,26 @@
             copy.wait_send()
 
 
-def project_call(context, own, a0, a1, *lines):
-    rows, depth = context.shape[0] // 2, context.shape[1]
+def project_call(pieces, own, a0, a1, *lines):
+    rows, depth = len(pieces) // 2 * LQ, own.shape[0]
     wide = own.shape[1]
-    dtype = context.dtype
-    vmem = pl.BlockSpec(memory_space=pltpu.VMEM)
+    dtype = own.dtype
     anyspace = pl.BlockSpec(memory_space=pl.ANY)
     return pl.pallas_call(
-        project_kernel,
+        functools.partial(project_kernel, len(pieces)),
         out_shape=jax.ShapeDtypeStruct((rows, 2 * wide), dtype),
-        in_specs=[vmem] + [anyspace] * 7,
-        out_specs=vmem,
+        in_specs=[anyspace] * (len(pieces) + 7),
+        out_specs=pl.BlockSpec(memory_space=pltpu.VMEM),
         scratch_shapes=[
+            pltpu.VMEM((2 * rows, depth), dtype),
             pltpu.VMEM((2, 2, depth, wide), dtype),
             pltpu.VMEM((2, 2, rows, wide), dtype),
             pltpu.VMEM((2, 2, rows, wide), dtype),
             pltpu.VMEM((2, rows, wide), dtype),
             pltpu.VMEM((2, rows, wide), dtype),
             pltpu.VMEM((2, rows, wide), dtype),
-            pltpu.SemaphoreType.DMA((5,)),
+            pltpu.SemaphoreType.DMA((len(pieces),)),
+            pltpu.SemaphoreType.DMA((2, 2)),
             pltpu.SemaphoreType.DMA((8,)),
             pltpu.SemaphoreType.DMA((8,)),
         ],
@@ -920,7 +928,7 @@
             bytes_accessed=4 * depth * wide * 2,
             transcendentals=0,
         ),
-    )(context, own, a0, a1, *lines)
+    )(*pieces, own, a0, a1, *lines)
 
 
 def suits_line(mesh, queries, lists):

time: 407 us -> 460 us (1.13)
  waiting for transfers between devices: 165 us -> 193 us
  starting transfers between devices: 83.2 us -> 102 us
    ppermute x21 -> x25, waiting for transfers between devices: 165 us -> 193 us  [send(): return lax.ppermute(value, 'pass', pairs)]
    ppermute x21 -> x25, starting transfers between devices: 83.2 us -> 102 us  [send(): return lax.ppermute(value, 'pass', pairs)]
    pallas_call x6 -> x15, Pallas kernels: 53 us -> 62.5 us  [the longest x14 35.7 us: join_call(): pl.pallas_call(merge_kernel if leveled else finish_kernel, out_shape=jax....]
    pallas_call x4, Pallas kernels: 75.7 us -> 67 us  [part_call(): pl.pallas_call(functools.partial(part_kernel, k, most, heads), out_shape=...]
    unnamed x18 -> x24, local copies, waits for them, and re-layouts: 12.4 us -> 13.9 us
  transfers between devices with their start and end apart: 21 -> 25, of which waited for: 10 -> 11; matrix products, arithmetic and copies ran while one was open for 3% -> 3% of each run, Pallas kernels for 28% -> 25%
where the time goes in v1:
time: 460 us; the launch traced here: 452 us
  waiting for transfers between devices  193 us (42%)
  Pallas kernels  140 us (30%)
  starting transfers between devices  102 us (22%)
  local copies, waits for them, and re-layouts  17.4 us (4%)
    ppermute x25, waiting for transfers between devices, send(): return lax.ppermute(value, 'pass', pairs)  193 us
    ppermute x25, starting transfers between devices, send(): return lax.ppermute(value, 'pass', pairs)  102 us
    pallas_call x4, Pallas kernels, part_call(): pl.pallas_call(functools.partial(part_kernel, k, most, heads), out_shape=...  67 us
    pallas_call x14, Pallas kernels, join_call(): pl.pallas_call(merge_kernel if leveled else finish_kernel, out_shape=jax....  35.7 us
    pallas_call x1, Pallas kernels, project_call(): pl.pallas_call(functools.partial(project_kernel, len(pieces)), out_shape=...  26.8 us
    unnamed x24, local copies, waits for them, and re-layouts  13.9 us
    pallas_call x1, Pallas kernels, sort_items(): pl.pallas_call(functools.partial(sort_kernel, most, per_device), out_shap...  10.7 us
  transfers between devices with their start and end apart: 25, of which 11 were waited for; matrix products, arithmetic and copies ran while one was open for 3% of the time, Pallas kernels for 25%

profile of v1, /device:TPU:0, one launch (start us, length us, event | category | flops | bytes accessed | tf_op | source)
XLA Modules:
  0.0 452.2 jit_solution(2980377595837385173)
XLA Ops:
  0.0 3.1 collective-permute-start.2
  3.8 33.9 %collective-permute-done.2.refs_3_ = bf16[384,2048]{1,0:T(8,128)(2,1)} collective-permute-done((bf16[384,2048]{1,0:T(8,128)(2,1)}, bf16[384,2048]{1,0:T(8,128)(2,1)}, u32[]{:S(2)}, u32[]{:S(2)}) %collective-permute-start.2) | collective-permute-done | bytes 1572896 | tf_op jit(solution)/shard_map/ppermute | solution.py:724
  39.7 8.2 %copy.16 = bf16[16,512,2,256]{3,1,2,0:T(8,128)(2,1)} copy(bf16[16,512,2,256]{3,2,1,0:T(2,128)(2,1)} %param.9) | data formatting | bytes 16777216 | tf_op args[2]
  47.9 10.7 %sort_items.1 = (s32[12]{0:T(128)}, s32[12]{0:T(128)}, s32[12]{0:T(128)}, bf16[3,2,512,256]{3,2,1,0:T(8,128)(2,1)}, bf16[3,2,512,256]{3,2,1,0:T(8,128)(2,1)}, /*...) custom-call(s32[8,24]{1,0:T(8,128)} %bitcast.15, s32[128]{0:T(128)} %pslot_ref.1, s32[24]{0:T(128)} %qslot_ref.1, ...), custom_call_target="tpu_custom_call" | custom-call | bytes 12582912 | tf_op jit(solution)/shard_map/sort_items/pallas_call | solution.py:428
  63.3 32.8 %collective-permute-done.7.refs_6_ = bf16[3,2,512,256]{3,2,1,0:T(8,128)(2,1)S(1)} collective-permute-done((bf16[3,2,512,256]{3,2,1,0:T(8,128)(2,1)}, bf16[3,2,512,256]{3,2,1,0:T(8,128)(2,1)S(1)}, u32[]{:S(2)}, u32[]{:S(2)}) %collective-permute-start.7) | collective-permute-done | bytes 1572896 | tf_op jit(solution)/shard_map/ppermute | solution.py:724
  96.1 3.9 collective-permute-done.6.refs_4_
  101.2 15.6 %shard_map.75.a_ref = bf16[3,144,2048]{2,1,0:T(8,128)(2,1)} custom-call(s32[12]{0:T(128)} %get-tuple-element.12.refs_0_, s32[12]{0:T(128)} %get-tuple-element.13.refs_1_, s32[12]{0:T(128)} %get-tuple-element.14.refs_2_, bf16[384,2048]{1,0:T(8,128)(2,1)} %collective-permute-done.3.refs_3_, bf16[384,2048]{1,0:T(8,128)(2,1)} %copy-done.6, ...), custom_call_target="tpu_custom_call" | custom-call | flops 3221225472 | bytes 3145728 | tf_op jit(solution)/shard_map/pallas_call | solution.py:614
  118.9 9.3 %collective-permute-done.5.refs_6_ = bf16[3,2,512,256]{3,2,1,0:T(8,128)(2,1)} collective-permute-done((bf16[3,2,512,256]{3,2,1,0:T(8,128)(2,1)}, bf16[3,2,512,256]{3,2,1,0:T(8,128)(2,1)}, u32[]{:S(2)}, u32[]{:S(2)}) %collective-permute-start.5) | collective-permute-done | bytes 1572896 | tf_op jit(solution)/shard_map/ppermute | solution.py:724
  128.2 3.4 collective-permute-done.4.refs_4_
  131.5 15.6 %shard_map.74.a_ref = bf16[3,144,2048]{2,1,0:T(8,128)(2,1)} custom-call(s32[12]{0:T(128)} %get-tuple-element.12.refs_0_, s32[12]{0:T(128)} %get-tuple-element.13.refs_1_, s32[12]{0:T(128)} %get-tuple-element.14.refs_2_, bf16[384,2048]{1,0:T(8,128)(2,1)} %copy-done.4, bf16[384,2048]{1,0:T(8,128)(2,1)} %collective-permute-done.4.refs_4_, ...), custom_call_target="tpu_custom_call" | custom-call | flops 3221225472 | bytes 3145728 | tf_op jit(solution)/shard_map/pallas_call | solution.py:614
  150.2 3.2 collective-permute-start.21
  154.7 3.4 collective-permute-done.8.b_ref
  159.4 3.9 shard_map.76
  163.3 32.7 %collective-permute-done.11.b_ref = bf16[3,144,2048]{2,1,0:T(8,128)(2,1)S(1)} collective-permute-done((bf16[3,144,2048]{2,1,0:T(8,128)(2,1)}, bf16[3,144,2048]{2,1,0:T(8,128)(2,1)S(1)}, u32[]{:S(2)}, u32[]{:S(2)}) %collective-permute-start.11) | collective-permute-done | bytes 1769504 | tf_op jit(solution)/shard_map/ppermute | solution.py:724
  202.2 14.6 %collective-permute-done.refs_6_ = bf16[3,2,512,256]{3,2,1,0:T(8,128)(2,1)} collective-permute-done((bf16[3,2,512,256]{3,2,1,0:T(8,128)(2,1)}, bf16[3,2,512,256]{3,2,1,0:T(8,128)(2,1)}, u32[]{:S(2)}, u32[]{:S(2)}) %collective-permute-start) | collective-permute-done | bytes 1572896 | tf_op jit(solution)/shard_map/ppermute | solution.py:724
  218.3 15.5 %shard_map.78.a_ref = bf16[3,144,2048]{2,1,0:T(8,128)(2,1)} custom-call(s32[12]{0:T(128)} %get-tuple-element.12.refs_0_, s32[12]{0:T(128)} %get-tuple-element.13.refs_1_, s32[12]{0:T(128)} %get-tuple-element.14.refs_2_, bf16[384,2048]{1,0:T(8,128)(2,1)} %collective-permute-done.2.refs_3_, bf16[16,2,512,256]{3,2,1,0:T(8,128)(2,1)} %bitcast.11, ...), custom_call_target="tpu_custom_call" | custom-call | flops 3221225472 | bytes 3145728 | tf_op jit(solution)/shard_map/pallas_call | solution.py:614
  239.6 66.6 %collective-permute-start.17 = (bf16[1,144,2048]{2,1,0:T(8,128)(2,1)}, bf16[1,144,2048]{2,1,0:T(8,128)(2,1)}, u32[]{:S(2)}, u32[]{:S(2)}) collective-permute-start(bf16[1,144,2048]{2,1,0:T(8,128)(2,1)} %shard_map.86.a_ref), channel_id=1, source_target_pairs={{0,8},{4,12},{8,0},{12,4},{16,24},{20,28},{24,16},{28,20},{1,9},{5... | collective-permute-start | bytes 1769480 | tf_op jit(solution)/shard_map/ppermute | solution.py:724
  308.2 3.3 collective-permute-start.24
  312.4 20.3 %shard_map.73.a_ref = bf16[3,144,2048]{2,1,0:T(8,128)(2,1)} custom-call(s32[12]{0:T(128)} %get-tuple-element.12.refs_0_, s32[12]{0:T(128)} %get-tuple-element.13.refs_1_, s32[12]{0:T(128)} %get-tuple-element.14.refs_2_, bf16[3,2,128,256]{3,2,1,0:T(8,128)(2,1)} %bitcast.13, bf16[384,2048]{1,0:T(8,128)(2,1)} %refs_4_.1, bf16[16,2,512,256]{3,2,1,0:T(8,128)(2,1)} %bitcast.12, ...), custom_call_target="tpu_custom_call" | custom-call | flops 3221225472 | bytes 3145728 | tf_op jit(solution)/shard_map/pallas_call | solution.py:614
  332.7 3.9 shard_map.77.a_ref
  341.2 2.3 shard_map.80.a_ref
  344.3 2.7 fusion
  346.9 41.6 %collective-permute-done.15.b_ref = bf16[1,144,2048]{2,1,0:T(8,128)(2,1)S(1)} collective-permute-done((bf16[1,144,2048]{2,1,0:T(8,128)(2,1)}, bf16[1,144,2048]{2,1,0:T(8,128)(2,1)S(1)}, u32[]{:S(2)}, u32[]{:S(2)}) %collective-permute-start.15) | collective-permute-done | bytes 589856 | tf_op jit(solution)/shard_map/ppermute | solution.py:724
  388.9 5.9 %collective-permute-done.13.b_ref = bf16[1,144,2048]{2,1,0:T(8,128)(2,1)S(1)} collective-permute-done((bf16[1,144,2048]{2,1,0:T(8,128)(2,1)}, bf16[1,144,2048]{2,1,0:T(8,128)(2,1)S(1)}, u32[]{:S(2)}, u32[]{:S(2)}) %collective-permute-start.13) | collective-permute-done | bytes 589856 | tf_op jit(solution)/shard_map/ppermute | solution.py:724
  396.0 2.5 shard_map.87.refs_2_
  398.5 2.5 shard_map.84.refs_1_
  401.1 2.5 shard_map.81.refs_0_
  404.8 2.5 shard_map.90.refs_5_
  407.3 2.5 shard_map.89.refs_4_
  409.8 2.5 shard_map.88.refs_3_
  412.2 11.1 %collective-permute-done.20.refs_8_ = bf16[1024,512]{1,0:T(8,128)(2,1)} collective-permute-done((bf16[1024,512]{1,0:T(8,128)(2,1)S(1)}, bf16[1024,512]{1,0:T(8,128)(2,1)}, u32[]{:S(2)}, u32[]{:S(2)}) %collective-permute-start.20) | collective-permute-done | bytes 1048608 | tf_op jit(solution)/shard_map/ppermute | solution.py:724
  423.3 26.8 %project_sum.1 = bf16[384,1024]{1,0:T(8,128)(2,1)} custom-call(bf16[128,2048]{1,0:T(8,128)(2,1)} %shard_map.81.refs_0_, bf16[128,2048]{1,0:T(8,128)(2,1)} %shard_map.84.refs_1_, bf16[128,2048]{1,0:T(8,128)(2,1)} %shard_map.87.refs_2_, bf16[128,2048]{1,0:T(8,128)(2,1)} %shard_map.88.refs_3_, bf16[128,2048]{1,0:T(8,128)(2,1)} %shard_map.89.refs_4_, ...), custom_call_target="tpu_custom_call" | custom-call | flops 6442450944 | bytes 8388608 | tf_op jit(solution)/shard_map/project_sum/pallas_call | solution.py:906
  (64 shorter events, 42.8 us)
Async XLA Ops:
  0.0 37.8 %collective-permute-start.2 = (bf16[384,2048]{1,0:T(8,128)(2,1)}, bf16[384,2048]{1,0:T(8,128)(2,1)}, u32[]{:S(2)}, u32[]{:S(2)}) collective-permute-start(bf16[384,2048]{1,0:T(8,128)(2,1)} %refs_4_.1), channel_id=1, source_target_pairs={{0,8},{4,12},{8,0},{12,4},{16,24},{20,28},{24,16},{28,20},{1,9},{5... | collective-permute-start | bytes 4718600 | tf_op jit(solution)/shard_map/ppermute | solution.py:724
  3.1 57.4 %collective-permute-start.1 = (bf16[384,2048]{1,0:T(8,128)(2,1)}, bf16[384,2048]{1,0:T(8,128)(2,1)S(1)}, u32[]{:S(2)}, u32[]{:S(2)}) collective-permute-start(bf16[384,2048]{1,0:T(8,128)(2,1)} %refs_4_.1), channel_id=1, source_target_pairs={{8,16},{12,20},{16,8},{20,12},{9,17},{13,21},{17,9},{21,13},{10,18... | collective-permute-start | bytes 4718600 | tf_op jit(solution)/shard_map/ppermute | solution.py:724
  37.8 24.2 %collective-permute-start.3 = (bf16[384,2048]{1,0:T(8,128)(2,1)}, bf16[384,2048]{1,0:T(8,128)(2,1)}, u32[]{:S(2)}, u32[]{:S(2)}) collective-permute-start(bf16[384,2048]{1,0:T(8,128)(2,1)} %collective-permute-done.2.refs_3_), channel_id=1, source_target_pairs={{8,16},{12,20},{16,8},{20,12},{9,17},{13,21},{17,9},{21,13},{10,18... | collective-permute-start | bytes 4718600 | tf_op jit(solution)/shard_map/ppermute | solution.py:724
  58.5 37.5 %collective-permute-start.7 = (bf16[3,2,512,256]{3,2,1,0:T(8,128)(2,1)}, bf16[3,2,512,256]{3,2,1,0:T(8,128)(2,1)S(1)}, u32[]{:S(2)}, u32[]{:S(2)}) collective-permute-start(bf16[3,2,512,256]{3,2,1,0:T(8,128)(2,1)} %get-tuple-element.17), channel_id=1, source_target_pairs={{0,4},{4,0},{8,12},{12,8},{16,20},{20,16},{24,28},{28,24},{1,5},{5... | collective-permute-start | bytes 4718600 | tf_op jit(solution)/shard_map/ppermute | solution.py:724
  60.4 56.3 %copy-start.4 = (bf16[384,2048]{1,0:T(8,128)(2,1)}, bf16[384,2048]{1,0:T(8,128)(2,1)S(1)}, u32[]{:S(2)}) copy-start(bf16[384,2048]{1,0:T(8,128)(2,1)S(1)} %collective-permute-done.1.refs_3_) | copy-start | bytes 4718596
  60.4 39.6 %collective-permute-start.6 = (bf16[384,2048]{1,0:T(8,128)(2,1)S(1)}, bf16[384,2048]{1,0:T(8,128)(2,1)S(1)}, u32[]{:S(2)}, u32[]{:S(2)}) collective-permute-start(bf16[384,2048]{1,0:T(8,128)(2,1)S(1)} %collective-permute-done.1.refs_3_), channel_id=1, source_target_pairs={{8,0},{12,4},{16,24},{20,28},{9,1},{13,5},{17,25},{21,29},{10,2},{... | collective-permute-start | bytes 4718600 | tf_op jit(solution)/shard_map/ppermute | solution.py:724
  61.7 66.5 %collective-permute-start.5 = (bf16[3,2,512,256]{3,2,1,0:T(8,128)(2,1)}, bf16[3,2,512,256]{3,2,1,0:T(8,128)(2,1)}, u32[]{:S(2)}, u32[]{:S(2)}) collective-permute-start(bf16[3,2,512,256]{3,2,1,0:T(8,128)(2,1)} %get-tuple-element.16), channel_id=1, source_target_pairs={{0,4},{4,0},{8,12},{12,8},{16,20},{20,16},{24,28},{28,24},{1,5},{5... | collective-permute-start | bytes 4718600 | tf_op jit(solution)/shard_map/ppermute | solution.py:724
  62.0 69.5 %collective-permute-start.4 = (bf16[384,2048]{1,0:T(8,128)(2,1)}, bf16[384,2048]{1,0:T(8,128)(2,1)}, u32[]{:S(2)}, u32[]{:S(2)}) collective-permute-start(bf16[384,2048]{1,0:T(8,128)(2,1)} %collective-permute-done.3.refs_3_), channel_id=1, source_target_pairs={{8,0},{12,4},{16,24},{20,28},{9,1},{13,5},{17,25},{21,29},{10,2},{... | collective-permute-start | bytes 4718600 | tf_op jit(solution)/shard_map/ppermute | solution.py:724
  96.1 5.1 %copy-start.5 = (bf16[3,2,512,256]{3,2,1,0:T(8,128)(2,1)}, bf16[3,2,512,256]{3,2,1,0:T(8,128)(2,1)S(1)}, u32[]{:S(2)}) copy-start(bf16[3,2,512,256]{3,2,1,0:T(8,128)(2,1)S(1)} %collective-permute-done.7.refs_6_) | copy-start | bytes 4718596
  116.7 41.4 %collective-permute-start.8 = (bf16[3,144,2048]{2,1,0:T(8,128)(2,1)}, bf16[3,144,2048]{2,1,0:T(8,128)(2,1)S(1)}, u32[]{:S(2)}, u32[]{:S(2)}) collective-permute-start(bf16[3,144,2048]{2,1,0:T(8,128)(2,1)} %shard_map.75.a_ref), channel_id=1, source_target_pairs={{0,8},{4,12},{24,16},{28,20},{1,9},{5,13},{25,17},{29,21},{2,10},{... | collective-permute-start | bytes 5308424 | tf_op jit(solution)/shard_map/ppermute | solution.py:724
  147.2 48.9 %collective-permute-start.11 = (bf16[3,144,2048]{2,1,0:T(8,128)(2,1)}, bf16[3,144,2048]{2,1,0:T(8,128)(2,1)S(1)}, u32[]{:S(2)}, u32[]{:S(2)}) collective-permute-start(bf16[3,144,2048]{2,1,0:T(8,128)(2,1)} %shard_map.74.a_ref), channel_id=1, source_target_pairs={{0,8},{4,12},{24,16},{28,20},{1,9},{5,13},{25,17},{29,21},{2,10},{... | collective-permute-start | bytes 5308424 | tf_op jit(solution)/shard_map/ppermute | solution.py:724
  148.8 50.5 %collective-permute-start.10 = (bf16[3,2,512,256]{3,2,1,0:T(8,128)(2,1)}, bf16[3,2,512,256]{3,2,1,0:T(8,128)(2,1)}, u32[]{:S(2)}, u32[]{:S(2)}) collective-permute-start(bf16[3,2,512,256]{3,2,1,0:T(8,128)(2,1)} %get-tuple-element.18), channel_id=1, source_target_pairs={{0,4},{4,0},{8,12},{12,8},{16,20},{20,16},{24,28},{28,24},{1,5},{5... | collective-permute-start | bytes 4718600 | tf_op jit(solution)/shard_map/ppermute | solution.py:724
  150.2 89.4 %collective-permute-start.21 = (bf16[2048,512]{1,0:T(8,128)(2,1)}, bf16[2048,512]{1,0:T(8,128)(2,1)}, u32[]{:S(2)}, u32[]{:S(2)}) collective-permute-start(bf16[2048,512]{1,0:T(8,128)(2,1)} %refs_6_.1), channel_id=1, source_target_pairs={{0,16},{4,20},{24,8},{28,12},{1,17},{5,21},{25,9},{29,13},{2,18},{... | collective-permute-start | bytes 6291464 | tf_op jit(solution)/shard_map/ppermute | solution.py:724
  153.4 152.8 %collective-permute-start.23 = (bf16[2048,512]{1,0:T(8,128)(2,1)}, bf16[2048,512]{1,0:T(8,128)(2,1)}, u32[]{:S(2)}, u32[]{:S(2)}) collective-permute-start(bf16[2048,512]{1,0:T(8,128)(2,1)} %refs_6_.1), channel_id=1, source_target_pairs={{8,24},{12,28},{16,0},{20,4},{9,25},{13,29},{17,1},{21,5},{10,26},... | collective-permute-start | bytes 6291464 | tf_op jit(solution)/shard_map/ppermute | solution.py:724
  158.1 1.3 copy-start.3
  158.1 58.7 %collective-permute-start = (bf16[3,2,512,256]{3,2,1,0:T(8,128)(2,1)}, bf16[3,2,512,256]{3,2,1,0:T(8,128)(2,1)}, u32[]{:S(2)}, u32[]{:S(2)}) collective-permute-start(bf16[3,2,512,256]{3,2,1,0:T(8,128)(2,1)} %get-tuple-element.15), channel_id=1, source_target_pairs={{0,4},{4,0},{8,12},{12,8},{16,20},{20,16},{24,28},{28,24},{1,5},{5... | collective-permute-start | bytes 4718600 | tf_op jit(solution)/shard_map/ppermute | solution.py:724
  196.0 112.2 %collective-permute-start.9 = (bf16[3,144,2048]{2,1,0:T(8,128)(2,1)}, bf16[3,144,2048]{2,1,0:T(8,128)(2,1)S(1)}, u32[]{:S(2)}, u32[]{:S(2)}) collective-permute-start(bf16[3,144,2048]{2,1,0:T(8,128)(2,1)} %shard_map.76), channel_id=1, source_target_pairs={{8,16},{12,20},{16,8},{20,12},{9,17},{13,21},{17,9},{21,13},{10,18... | collective-permute-start | bytes 5308424 | tf_op jit(solution)/shard_map/ppermute | solution.py:724
  199.3 36.6 %collective-permute-start.16 = (bf16[1,144,2048]{2,1,0:T(8,128)(2,1)}, bf16[1,144,2048]{2,1,0:T(8,128)(2,1)S(1)}, u32[]{:S(2)}, u32[]{:S(2)}) collective-permute-start(bf16[1,144,2048]{2,1,0:T(8,128)(2,1)} %shard_map.85), channel_id=1, source_target_pairs={{8,16},{12,20},{16,8},{20,12},{9,17},{13,21},{17,9},{21,13},{10,18... | collective-permute-start | bytes 1769480 | tf_op jit(solution)/shard_map/ppermute | solution.py:724
  216.8 119.9 %collective-permute-start.14 = (bf16[1,144,2048]{2,1,0:T(8,128)(2,1)}, bf16[1,144,2048]{2,1,0:T(8,128)(2,1)}, u32[]{:S(2)}, u32[]{:S(2)}) collective-permute-start(bf16[1,144,2048]{2,1,0:T(8,128)(2,1)} %shard_map.82), channel_id=1, source_target_pairs={{8,16},{12,20},{16,8},{20,12},{9,17},{13,21},{17,9},{21,13},{10,18... | collective-permute-start | bytes 1769480 | tf_op jit(solution)/shard_map/ppermute | solution.py:724
  235.9 75.6 %copy-start.10 = (bf16[384,2,256]{2,1,0:T(2,128)(2,1)S(1)}, bf16[384,2,256]{2,1,0:T(2,128)(2,1)}, u32[]{:S(2)}) copy-start(bf16[384,2,256]{2,1,0:T(2,128)(2,1)} %param.8) | copy-start | bytes 1179652
  235.9 1.6 copy-start.8
  235.9 103.6 %collective-permute-start.12 = (bf16[1,144,2048]{2,1,0:T(8,128)(2,1)}, bf16[1,144,2048]{2,1,0:T(8,128)(2,1)}, u32[]{:S(2)}, u32[]{:S(2)}) collective-permute-start(bf16[1,144,2048]{2,1,0:T(8,128)(2,1)} %shard_map.79), channel_id=1, source_target_pairs={{8,16},{12,20},{16,8},{20,12},{9,17},{13,21},{17,9},{21,13},{10,18... | collective-permute-start | bytes 1769480 | tf_op jit(solution)/shard_map/ppermute | solution.py:724
  239.6 103.9 %collective-permute-start.17 = (bf16[1,144,2048]{2,1,0:T(8,128)(2,1)}, bf16[1,144,2048]{2,1,0:T(8,128)(2,1)}, u32[]{:S(2)}, u32[]{:S(2)}) collective-permute-start(bf16[1,144,2048]{2,1,0:T(8,128)(2,1)} %shard_map.86.a_ref), channel_id=1, source_target_pairs={{0,8},{4,12},{8,0},{12,4},{16,24},{20,28},{24,16},{28,20},{1,9},{5... | collective-permute-start | bytes 1769480 | tf_op jit(solution)/shard_map/ppermute | solution.py:724
  306.2 117.1 %collective-permute-start.22 = (bf16[2048,512]{1,0:T(8,128)(2,1)}, bf16[2048,512]{1,0:T(8,128)(2,1)}, u32[]{:S(2)}, u32[]{:S(2)}) collective-permute-start(bf16[2048,512]{1,0:T(8,128)(2,1)} %collective-permute-done.21.refs_9_), channel_id=1, source_target_pairs={{8,12},{12,8},{16,20},{20,16},{9,13},{13,9},{17,21},{21,17},{10,14... | collective-permute-start | bytes 6291464 | tf_op jit(solution)/shard_map/ppermute | solution.py:724
  308.2 24.5 %copy-start.2 = (bf16[3,144,2048]{2,1,0:T(8,128)(2,1)}, bf16[3,144,2048]{2,1,0:T(8,128)(2,1)S(1)}, u32[]{:S(2)}) copy-start(bf16[3,144,2048]{2,1,0:T(8,128)(2,1)S(1)} %collective-permute-done.9.b_ref) | copy-start | bytes 5308420
  308.2 115.1 %collective-permute-start.24 = (bf16[2048,512]{1,0:T(8,128)(2,1)}, bf16[2048,512]{1,0:T(8,128)(2,1)}, u32[]{:S(2)}, u32[]{:S(2)}) collective-permute-start(bf16[2048,512]{1,0:T(8,128)(2,1)} %collective-permute-done.23.refs_11_), channel_id=1, source_target_pairs={{0,4},{4,0},{24,28},{28,24},{1,5},{5,1},{25,29},{29,25},{2,6},{6,2... | collective-permute-start | bytes 6291464 | tf_op jit(solution)/shard_map/ppermute | solution.py:724
  336.6 66.9 %collective-permute-start.18 = (bf16[3,144,2048]{2,1,0:T(8,128)(2,1)}, bf16[3,144,2048]{2,1,0:T(8,128)(2,1)S(1)}, u32[]{:S(2)}, u32[]{:S(2)}) collective-permute-start(bf16[3,144,2048]{2,1,0:T(8,128)(2,1)} %shard_map.77.a_ref), channel_id=1, source_target_pairs={{0,8},{4,12},{8,0},{12,4},{16,24},{20,28},{24,16},{28,20},{1,9},{5... | collective-permute-start | bytes 5308424 | tf_op jit(solution)/shard_map/ppermute | solution.py:724
  339.5 49.0 %collective-permute-start.15 = (bf16[1,144,2048]{2,1,0:T(8,128)(2,1)}, bf16[1,144,2048]{2,1,0:T(8,128)(2,1)S(1)}, u32[]{:S(2)}, u32[]{:S(2)}) collective-permute-start(bf16[1,144,2048]{2,1,0:T(8,128)(2,1)} %shard_map.83.a_ref), channel_id=1, source_target_pairs={{0,8},{4,12},{8,0},{12,4},{16,24},{20,28},{24,16},{28,20},{1,9},{5... | collective-permute-start | bytes 1769480 | tf_op jit(solution)/shard_map/ppermute | solution.py:724
  343.5 51.3 %collective-permute-start.13 = (bf16[1,144,2048]{2,1,0:T(8,128)(2,1)}, bf16[1,144,2048]{2,1,0:T(8,128)(2,1)S(1)}, u32[]{:S(2)}, u32[]{:S(2)}) collective-permute-start(bf16[1,144,2048]{2,1,0:T(8,128)(2,1)} %shard_map.80.a_ref), channel_id=1, source_target_pairs={{0,8},{4,12},{8,0},{12,4},{16,24},{20,28},{24,16},{28,20},{1,9},{5... | collective-permute-start | bytes 1769480 | tf_op jit(solution)/shard_map/ppermute | solution.py:724
  388.5 10.1 %copy-start.7 = (bf16[1,144,2048]{2,1,0:T(8,128)(2,1)}, bf16[1,144,2048]{2,1,0:T(8,128)(2,1)S(1)}, u32[]{:S(2)}) copy-start(bf16[1,144,2048]{2,1,0:T(8,128)(2,1)S(1)} %collective-permute-done.15.b_ref) | copy-start | bytes 1769476
  388.5 23.8 %collective-permute-start.19 = (bf16[1024,512]{1,0:T(8,128)(2,1)}, bf16[1024,512]{1,0:T(8,128)(2,1)}, u32[]{:S(2)}, u32[]{:S(2)}) collective-permute-start(bf16[1024,512]{1,0:T(8,128)(2,1)} %get-tuple-element.20), channel_id=1, source_target_pairs={{0,4},{4,0},{8,12},{12,8},{16,20},{20,16},{24,28},{28,24},{1,5},{5... | collective-permute-start | bytes 3145736 | tf_op jit(solution)/shard_map/ppermute | solution.py:724
  395.6 27.7 %collective-permute-start.20 = (bf16[1024,512]{1,0:T(8,128)(2,1)S(1)}, bf16[1024,512]{1,0:T(8,128)(2,1)}, u32[]{:S(2)}, u32[]{:S(2)}) collective-permute-start(bf16[1024,512]{1,0:T(8,128)(2,1)S(1)} %get-tuple-element.19), channel_id=1, source_target_pairs={{0,4},{4,0},{8,12},{12,8},{16,20},{20,16},{24,28},{28,24},{1,5},{5... | collective-permute-start | bytes 3145736 | tf_op jit(solution)/shard_map/ppermute | solution.py:724
  (4 other events, 4.4 us)

commit v2 on v1

--- a/solution.py
+++ b/solution.py
@@ -347,7 +347,8 @@
 
 
 LINE = 4
-EXTRA = 16
+EXTRA = 8
+VMEM_BYTES = 67043328
 
 
 def mirror(k, ends=None):
@@ -440,6 +441,7 @@
             pltpu.SemaphoreType.DMA((slots,)),
             pltpu.SemaphoreType.DMA((slots,)),
         ],
+        compiler_params=pltpu.CompilerParams(vmem_limit_bytes=VMEM_BYTES),
         name="sort_items",
         cost_estimate=pl.CostEstimate(
             flops=0, bytes_accessed=2 * slots * math.prod(item) * 2, transcendentals=0
@@ -598,7 +600,7 @@
 def store_level(out_ref, question, columns, line):
     row_of = lax.broadcasted_iota(jnp.int32, (EXTRA, line.shape[1]), 0)
     high = line.astype(jnp.bfloat16).astype(jnp.float32)
-    both = jnp.where(row_of == 0, high, jnp.where(row_of == EXTRA // 2, line - high, 0.0))
+    both = jnp.where(row_of == 0, high, jnp.where(row_of == 1, line - high, 0.0))
     out_ref[question, LQ:, columns] = both.astype(out_ref.dtype)
 
 
@@ -625,6 +627,7 @@
             pltpu.SemaphoreType.DMA((2,)),
             pltpu.SemaphoreType.DMA,
         ],
+        compiler_params=pltpu.CompilerParams(vmem_limit_bytes=VMEM_BYTES),
         cost_estimate=pl.CostEstimate(
             flops=weights * HD * 4,
             bytes_accessed=2 * most * math.prod(item) * 2,
@@ -639,7 +642,7 @@
 
     def level_of(ref):
         both = ref[0, LQ:, :].astype(jnp.float32)
-        return both[:1] + both[EXTRA // 2 : EXTRA // 2 + 1]
+        return both[:1] + both[1:2]
 
     one, two = level_of(a_ref), level_of(b_ref)
     top = jnp.maximum(one, two)
@@ -710,6 +713,7 @@
         grid=(questions,),
         in_specs=[question_spec(a, at), question_spec(b, at)],
         out_specs=out_spec,
+        compiler_params=pltpu.CompilerParams(vmem_limit_bytes=VMEM_BYTES),
         cost_estimate=pl.CostEstimate(flops=size * 8, bytes_accessed=size * 6, transcendentals=0),
     )(a, b)
 
@@ -758,11 +762,11 @@
     back3 = send(part3, inward)
     w_in_both = send(w_in, inner_across)
     w_out_both = send(w_out, outer_across)
-    cross3 = send(join(part3, back2), middle)
-    near0 = join(part0, cross3)
-    beside = send(near0, near)
     own_rows, near_rows = [], []
     for q in range(per_device):
+        cross3 = send(join(part3, back2, q), middle)
+        near0 = join(part0, cross3, q)
+        beside = send(near0, near)
         cross2 = send(join(part2, back3, q), middle)
         near1 = join(part1, cross2, q)
         back1 = send(near1, near)
@@ -921,7 +925,9 @@
             pltpu.SemaphoreType.DMA((8,)),
             pltpu.SemaphoreType.DMA((8,)),
         ],
-        compiler_params=pltpu.CompilerParams(collective_id=0, has_side_effects=True),
+        compiler_params=pltpu.CompilerParams(
+            collective_id=0, has_side_effects=True, vmem_limit_bytes=VMEM_BYTES
+        ),
         name="project_sum",
         cost_estimate=pl.CostEstimate(
             flops=2 * 4 * 2 * rows * depth * wide,

time: 460 us -> 388 us (0.84)
  the two profiles are of different devices: /device:TPU:0 before, /device:TPU:1 now
where the time goes in v2:
time: 388 us; the launch traced here: 387 us
  Pallas kernels  160 us (41%)
  starting transfers between devices  114 us (29%)
  waiting for transfers between devices  97.7 us (25%)
  local copies, waits for them, and re-layouts  15 us (4%)
    ppermute x29, starting transfers between devices, send(): return lax.ppermute(value, 'pass', pairs)  114 us
    ppermute x29, waiting for transfers between devices, send(): return lax.ppermute(value, 'pass', pairs)  97.7 us
    pallas_call x4, Pallas kernels, part_call(): pl.pallas_call(functools.partial(part_kernel, k, most, heads), out_shape=...  66.8 us
    pallas_call x1, Pallas kernels, project_call(): pl.pallas_call(functools.partial(project_kernel, len(pieces)), out_shape=...  43.1 us
    pallas_call x18, Pallas kernels, join_call(): pl.pallas_call(merge_kernel if leveled else finish_kernel, out_shape=jax....  39.9 us
    pallas_call x1, Pallas kernels, sort_items(): pl.pallas_call(functools.partial(sort_kernel, most, per_device), out_shap...  10.6 us
    unnamed x2, local copies, waits for them, and re-layouts  10.3 us
  transfers between devices with their start and end apart: 29, of which 13 were waited for; matrix products, arithmetic and copies ran while one was open for 3% of the time, Pallas kernels for 30%

profile of v2, /device:TPU:1, one launch (start us, length us, event | category | flops | bytes accessed | tf_op | source)
XLA Modules:
  0.0 387.1 jit_solution(18171040269693319201)
XLA Ops:
  0.0 2.1 collective-permute-start.2
  3.9 8.2 %copy.16 = bf16[16,512,2,256]{3,1,2,0:T(8,128)(2,1)} copy(bf16[16,512,2,256]{3,2,1,0:T(2,128)(2,1)} %param.9) | data formatting | bytes 16777216 | tf_op args[2]
  12.1 10.6 %sort_items.1 = (s32[12]{0:T(128)}, s32[12]{0:T(128)}, s32[12]{0:T(128)}, bf16[3,2,512,256]{3,2,1,0:T(8,128)(2,1)}, bf16[3,2,512,256]{3,2,1,0:T(8,128)(2,1)}, /*...) custom-call(s32[8,24]{1,0:T(8,128)} %bitcast.15, s32[128]{0:T(128)} %pslot_ref.1, s32[24]{0:T(128)} %qslot_ref.1, ...), custom_call_target="tpu_custom_call" | custom-call | bytes 12582912 | tf_op jit(solution)/shard_map/sort_items/pallas_call | solution.py:429
  22.7 13.8 %collective-permute-done.2.refs_3_ = bf16[384,2048]{1,0:T(8,128)(2,1)} collective-permute-done((bf16[384,2048]{1,0:T(8,128)(2,1)}, bf16[384,2048]{1,0:T(8,128)(2,1)}, u32[]{:S(2)}, u32[]{:S(2)}) %collective-permute-start.2) | collective-permute-done | bytes 1572896 | tf_op jit(solution)/shard_map/ppermute | solution.py:728
  42.5 30.9 %collective-permute-done.7.refs_6_ = bf16[3,2,512,256]{3,2,1,0:T(8,128)(2,1)} collective-permute-done((bf16[3,2,512,256]{3,2,1,0:T(8,128)(2,1)}, bf16[3,2,512,256]{3,2,1,0:T(8,128)(2,1)}, u32[]{:S(2)}, u32[]{:S(2)}) %collective-permute-start.7) | collective-permute-done | bytes 1572896 | tf_op jit(solution)/shard_map/ppermute | solution.py:728
  73.4 3.1 collective-permute-done.6.refs_4_
  76.5 15.5 %shard_map.75.a_ref = bf16[3,136,2048]{2,1,0:T(8,128)(2,1)} custom-call(s32[12]{0:T(128)} %get-tuple-element.12.refs_0_, s32[12]{0:T(128)} %get-tuple-element.13.refs_1_, s32[12]{0:T(128)} %get-tuple-element.14.refs_2_, bf16[384,2048]{1,0:T(8,128)(2,1)} %collective-permute-done.3.refs_3_, bf16[384,2048]{1,0:T(8,128)(2,1)} %collective-permute-done.6.refs_4_, ...), custom_call_target="tpu_custom_call" | custom-call | flops 3221225472 | bytes 3145728 | tf_op jit(solution)/shard_map/pallas_call | solution.py:616
  92.0 3.5 collective-permute-start.8
  96.7 2.7 collective-permute-start.25
  99.4 7.7 %collective-permute-done.5.refs_6_ = bf16[3,2,512,256]{3,2,1,0:T(8,128)(2,1)} collective-permute-done((bf16[3,2,512,256]{3,2,1,0:T(8,128)(2,1)}, bf16[3,2,512,256]{3,2,1,0:T(8,128)(2,1)}, u32[]{:S(2)}, u32[]{:S(2)}) %collective-permute-start.5) | collective-permute-done | bytes 1572896 | tf_op jit(solution)/shard_map/ppermute | solution.py:728
  108.4 2.5 collective-permute-done.4.refs_4_
  110.9 15.5 %shard_map.74.a_ref = bf16[3,136,2048]{2,1,0:T(8,128)(2,1)} custom-call(s32[12]{0:T(128)} %get-tuple-element.12.refs_0_, s32[12]{0:T(128)} %get-tuple-element.13.refs_1_, s32[12]{0:T(128)} %get-tuple-element.14.refs_2_, bf16[384,2048]{1,0:T(8,128)(2,1)} %collective-permute-done.1.refs_3_, bf16[384,2048]{1,0:T(8,128)(2,1)} %collective-permute-done.4.refs_4_, ...), custom_call_target="tpu_custom_call" | custom-call | flops 3221225472 | bytes 3145728 | tf_op jit(solution)/shard_map/pallas_call | solution.py:616
  127.0 6.4 %collective-permute-start.11 = (bf16[3,136,2048]{2,1,0:T(8,128)(2,1)}, bf16[3,136,2048]{2,1,0:T(8,128)(2,1)}, u32[]{:S(2)}, u32[]{:S(2)}) collective-permute-start(bf16[3,136,2048]{2,1,0:T(8,128)(2,1)} %shard_map.74.a_ref), channel_id=1, source_target_pairs={{0,8},{4,12},{24,16},{28,20},{1,9},{5,13},{25,17},{29,21},{2,10},{... | collective-permute-start | bytes 5013512 | tf_op jit(solution)/shard_map/ppermute | solution.py:728
  135.5 5.3 %collective-permute-done.refs_6_ = bf16[3,2,512,256]{3,2,1,0:T(8,128)(2,1)} collective-permute-done((bf16[3,2,512,256]{3,2,1,0:T(8,128)(2,1)}, bf16[3,2,512,256]{3,2,1,0:T(8,128)(2,1)}, u32[]{:S(2)}, u32[]{:S(2)}) %collective-permute-start) | collective-permute-done | bytes 1572896 | tf_op jit(solution)/shard_map/ppermute | solution.py:728
  147.6 20.3 %shard_map.73.a_ref = bf16[3,136,2048]{2,1,0:T(8,128)(2,1)} custom-call(s32[12]{0:T(128)} %get-tuple-element.12.refs_0_, s32[12]{0:T(128)} %get-tuple-element.13.refs_1_, s32[12]{0:T(128)} %get-tuple-element.14.refs_2_, bf16[3,2,128,256]{3,2,1,0:T(8,128)(2,1)} %bitcast.13, bf16[384,2048]{1,0:T(8,128)(2,1)} %refs_4_.1, bf16[16,2,512,256]{3,2,1,0:T(8,128)(2,1)} %bitcast.11, ...), custom_call_target="tpu_custom_call" | custom-call | flops 3221225472 | bytes 3145728 | tf_op jit(solution)/shard_map/pallas_call | solution.py:616
  172.1 2.4 collective-permute-done.10.refs_5_
  176.0 67.1 %collective-permute-start.20 = (bf16[1,136,2048]{2,1,0:T(8,128)(2,1)}, bf16[1,136,2048]{2,1,0:T(8,128)(2,1)}, u32[]{:S(2)}, u32[]{:S(2)}) collective-permute-start(bf16[1,136,2048]{2,1,0:T(8,128)(2,1)} %shard_map.77.a_ref), channel_id=1, source_target_pairs={{0,8},{4,12},{8,0},{12,4},{16,24},{20,28},{24,16},{28,20},{1,9},{5... | collective-permute-start | bytes 1671176 | tf_op jit(solution)/shard_map/ppermute | solution.py:728
  254.8 3.1 collective-permute-start.28
  260.0 2.9 collective-permute-done.21.b_ref
  264.7 15.4 %shard_map.78.a_ref = bf16[3,136,2048]{2,1,0:T(8,128)(2,1)} custom-call(s32[12]{0:T(128)} %get-tuple-element.12.refs_0_, s32[12]{0:T(128)} %get-tuple-element.13.refs_1_, s32[12]{0:T(128)} %get-tuple-element.14.refs_2_, bf16[384,2048]{1,0:T(8,128)(2,1)} %collective-permute-done.2.refs_3_, bf16[16,2,512,256]{3,2,1,0:T(8,128)(2,1)} %bitcast.12, ...), custom_call_target="tpu_custom_call" | custom-call | flops 3221225472 | bytes 3145728 | tf_op jit(solution)/shard_map/pallas_call | solution.py:616
  285.7 2.7 collective-permute-start.13
  290.9 3.0 fusion
  296.6 2.3 shard_map.90.a_ref
  298.9 6.2 %collective-permute-done.16.b_ref = bf16[1,136,2048]{2,1,0:T(8,128)(2,1)} collective-permute-done((bf16[1,136,2048]{2,1,0:T(8,128)(2,1)}, bf16[1,136,2048]{2,1,0:T(8,128)(2,1)}, u32[]{:S(2)}, u32[]{:S(2)}) %collective-permute-start.16) | collective-permute-done | bytes 557088 | tf_op jit(solution)/shard_map/ppermute | solution.py:728
  306.2 2.5 shard_map.92.refs_3_
  308.7 2.5 shard_map.93.refs_4_
  311.1 2.5 shard_map.94.refs_5_
  313.6 2.5 shard_map.81.refs_0_
  316.1 2.5 shard_map.86.refs_1_
  319.9 2.5 shard_map.91.refs_2_
  322.3 19.6 %collective-permute-done.24.refs_8_ = bf16[1024,512]{1,0:T(8,128)(2,1)} collective-permute-done((bf16[1024,512]{1,0:T(8,128)(2,1)}, bf16[1024,512]{1,0:T(8,128)(2,1)}, u32[]{:S(2)}, u32[]{:S(2)}) %collective-permute-start.24) | collective-permute-done | bytes 1048608 | tf_op jit(solution)/shard_map/ppermute | solution.py:728
  341.9 43.1 %project_sum.1 = bf16[384,1024]{1,0:T(8,128)(2,1)} custom-call(bf16[128,2048]{1,0:T(8,128)(2,1)} %shard_map.81.refs_0_, bf16[128,2048]{1,0:T(8,128)(2,1)} %shard_map.86.refs_1_, bf16[128,2048]{1,0:T(8,128)(2,1)} %shard_map.91.refs_2_, bf16[128,2048]{1,0:T(8,128)(2,1)} %shard_map.92.refs_3_, bf16[128,2048]{1,0:T(8,128)(2,1)} %shard_map.93.refs_4_, ...), custom_call_target="tpu_custom_call" | custom-call | flops 6442450944 | bytes 8388608 | tf_op jit(solution)/shard_map/project_sum/pallas_call | solution.py:910
  (54 shorter events, 56.2 us)
Async XLA Ops:
  0.0 36.5 %collective-permute-start.2 = (bf16[384,2048]{1,0:T(8,128)(2,1)}, bf16[384,2048]{1,0:T(8,128)(2,1)}, u32[]{:S(2)}, u32[]{:S(2)}) collective-permute-start(bf16[384,2048]{1,0:T(8,128)(2,1)} %refs_4_.1), channel_id=1, source_target_pairs={{0,8},{4,12},{8,0},{12,4},{16,24},{20,28},{24,16},{28,20},{1,9},{5... | collective-permute-start | bytes 4718600 | tf_op jit(solution)/shard_map/ppermute | solution.py:728
  2.1 37.3 %collective-permute-start.1 = (bf16[384,2048]{1,0:T(8,128)(2,1)}, bf16[384,2048]{1,0:T(8,128)(2,1)}, u32[]{:S(2)}, u32[]{:S(2)}) collective-permute-start(bf16[384,2048]{1,0:T(8,128)(2,1)} %refs_4_.1), channel_id=1, source_target_pairs={{8,16},{12,20},{16,8},{20,12},{9,17},{13,21},{17,9},{21,13},{10,18... | collective-permute-start | bytes 4718600 | tf_op jit(solution)/shard_map/ppermute | solution.py:728
  36.5 4.6 %collective-permute-start.3 = (bf16[384,2048]{1,0:T(8,128)(2,1)}, bf16[384,2048]{1,0:T(8,128)(2,1)}, u32[]{:S(2)}, u32[]{:S(2)}) collective-permute-start(bf16[384,2048]{1,0:T(8,128)(2,1)} %collective-permute-done.2.refs_3_), channel_id=1, source_target_pairs={{8,16},{12,20},{16,8},{20,12},{9,17},{13,21},{17,9},{21,13},{10,18... | collective-permute-start | bytes 4718600 | tf_op jit(solution)/shard_map/ppermute | solution.py:728
  38.3 35.0 %collective-permute-start.7 = (bf16[3,2,512,256]{3,2,1,0:T(8,128)(2,1)}, bf16[3,2,512,256]{3,2,1,0:T(8,128)(2,1)}, u32[]{:S(2)}, u32[]{:S(2)}) collective-permute-start(bf16[3,2,512,256]{3,2,1,0:T(8,128)(2,1)} %get-tuple-element.17), channel_id=1, source_target_pairs={{0,4},{4,0},{8,12},{12,8},{16,20},{20,16},{24,28},{28,24},{1,5},{5... | collective-permute-start | bytes 4718600 | tf_op jit(solution)/shard_map/ppermute | solution.py:728
  39.4 37.0 %collective-permute-start.6 = (bf16[384,2048]{1,0:T(8,128)(2,1)}, bf16[384,2048]{1,0:T(8,128)(2,1)}, u32[]{:S(2)}, u32[]{:S(2)}) collective-permute-start(bf16[384,2048]{1,0:T(8,128)(2,1)} %collective-permute-done.1.refs_3_), channel_id=1, source_target_pairs={{8,0},{12,4},{16,24},{20,28},{9,1},{13,5},{17,25},{21,29},{10,2},{... | collective-permute-start | bytes 4718600 | tf_op jit(solution)/shard_map/ppermute | solution.py:728
  40.7 66.3 %collective-permute-start.5 = (bf16[3,2,512,256]{3,2,1,0:T(8,128)(2,1)}, bf16[3,2,512,256]{3,2,1,0:T(8,128)(2,1)}, u32[]{:S(2)}, u32[]{:S(2)}) collective-permute-start(bf16[3,2,512,256]{3,2,1,0:T(8,128)(2,1)} %get-tuple-element.16), channel_id=1, source_target_pairs={{0,4},{4,0},{8,12},{12,8},{16,20},{20,16},{24,28},{28,24},{1,5},{5... | collective-permute-start | bytes 4718600 | tf_op jit(solution)/shard_map/ppermute | solution.py:728
  41.2 69.7 %collective-permute-start.4 = (bf16[384,2048]{1,0:T(8,128)(2,1)}, bf16[384,2048]{1,0:T(8,128)(2,1)}, u32[]{:S(2)}, u32[]{:S(2)}) collective-permute-start(bf16[384,2048]{1,0:T(8,128)(2,1)} %collective-permute-done.3.refs_3_), channel_id=1, source_target_pairs={{8,0},{12,4},{16,24},{20,28},{9,1},{13,5},{17,25},{21,29},{10,2},{... | collective-permute-start | bytes 4718600 | tf_op jit(solution)/shard_map/ppermute | solution.py:728
  92.0 35.0 %collective-permute-start.8 = (bf16[3,136,2048]{2,1,0:T(8,128)(2,1)}, bf16[3,136,2048]{2,1,0:T(8,128)(2,1)}, u32[]{:S(2)}, u32[]{:S(2)}) collective-permute-start(bf16[3,136,2048]{2,1,0:T(8,128)(2,1)} %shard_map.75.a_ref), channel_id=1, source_target_pairs={{0,8},{4,12},{24,16},{28,20},{1,9},{5,13},{25,17},{29,21},{2,10},{... | collective-permute-start | bytes 5013512 | tf_op jit(solution)/shard_map/ppermute | solution.py:728
  95.5 45.2 %collective-permute-start = (bf16[3,2,512,256]{3,2,1,0:T(8,128)(2,1)}, bf16[3,2,512,256]{3,2,1,0:T(8,128)(2,1)}, u32[]{:S(2)}, u32[]{:S(2)}) collective-permute-start(bf16[3,2,512,256]{3,2,1,0:T(8,128)(2,1)} %get-tuple-element.15), channel_id=1, source_target_pairs={{0,4},{4,0},{8,12},{12,8},{16,20},{20,16},{24,28},{28,24},{1,5},{5... | collective-permute-start | bytes 4718600 | tf_op jit(solution)/shard_map/ppermute | solution.py:728
  96.7 151.0 %collective-permute-start.25 = (bf16[2048,512]{1,0:T(8,128)(2,1)}, bf16[2048,512]{1,0:T(8,128)(2,1)}, u32[]{:S(2)}, u32[]{:S(2)}) collective-permute-start(bf16[2048,512]{1,0:T(8,128)(2,1)} %refs_6_.1), channel_id=1, source_target_pairs={{0,16},{4,20},{24,8},{28,12},{1,17},{5,21},{25,9},{29,13},{2,18},{... | collective-permute-start | bytes 6291464 | tf_op jit(solution)/shard_map/ppermute | solution.py:728
  107.1 144.3 %collective-permute-start.27 = (bf16[2048,512]{1,0:T(8,128)(2,1)}, bf16[2048,512]{1,0:T(8,128)(2,1)}, u32[]{:S(2)}, u32[]{:S(2)}) collective-permute-start(bf16[2048,512]{1,0:T(8,128)(2,1)} %refs_6_.1), channel_id=1, source_target_pairs={{8,24},{12,28},{16,0},{20,4},{9,25},{13,29},{17,1},{21,5},{10,26},... | collective-permute-start | bytes 6291464 | tf_op jit(solution)/shard_map/ppermute | solution.py:728
  110.9 63.6 %collective-permute-start.10 = (bf16[3,2,512,256]{3,2,1,0:T(8,128)(2,1)}, bf16[3,2,512,256]{3,2,1,0:T(8,128)(2,1)}, u32[]{:S(2)}, u32[]{:S(2)}) collective-permute-start(bf16[3,2,512,256]{3,2,1,0:T(8,128)(2,1)} %get-tuple-element.18), channel_id=1, source_target_pairs={{0,4},{4,0},{8,12},{12,8},{16,20},{20,16},{24,28},{28,24},{1,5},{5... | collective-permute-start | bytes 4718600 | tf_op jit(solution)/shard_map/ppermute | solution.py:728
  127.0 118.2 %collective-permute-start.11 = (bf16[3,136,2048]{2,1,0:T(8,128)(2,1)}, bf16[3,136,2048]{2,1,0:T(8,128)(2,1)}, u32[]{:S(2)}, u32[]{:S(2)}) collective-permute-start(bf16[3,136,2048]{2,1,0:T(8,128)(2,1)} %shard_map.74.a_ref), channel_id=1, source_target_pairs={{0,8},{4,12},{24,16},{28,20},{1,9},{5,13},{25,17},{29,21},{2,10},{... | collective-permute-start | bytes 5013512 | tf_op jit(solution)/shard_map/ppermute | solution.py:728
  140.8 3.6 collective-permute-start.9
  144.4 31.6 %collective-permute-start.14 = (bf16[1,136,2048]{2,1,0:T(8,128)(2,1)}, bf16[1,136,2048]{2,1,0:T(8,128)(2,1)}, u32[]{:S(2)}, u32[]{:S(2)}) collective-permute-start(bf16[1,136,2048]{2,1,0:T(8,128)(2,1)} %shard_map.82), channel_id=1, source_target_pairs={{8,16},{12,20},{16,8},{20,12},{9,17},{13,21},{17,9},{21,13},{10,18... | collective-permute-start | bytes 1671176 | tf_op jit(solution)/shard_map/ppermute | solution.py:728
  174.5 78.3 %collective-permute-start.17 = (bf16[1,136,2048]{2,1,0:T(8,128)(2,1)}, bf16[1,136,2048]{2,1,0:T(8,128)(2,1)}, u32[]{:S(2)}, u32[]{:S(2)}) collective-permute-start(bf16[1,136,2048]{2,1,0:T(8,128)(2,1)} %shard_map.87), channel_id=1, source_target_pairs={{8,16},{12,20},{16,8},{20,12},{9,17},{13,21},{17,9},{21,13},{10,18... | collective-permute-start | bytes 1671176 | tf_op jit(solution)/shard_map/ppermute | solution.py:728
  176.0 78.8 %collective-permute-start.20 = (bf16[1,136,2048]{2,1,0:T(8,128)(2,1)}, bf16[1,136,2048]{2,1,0:T(8,128)(2,1)}, u32[]{:S(2)}, u32[]{:S(2)}) collective-permute-start(bf16[1,136,2048]{2,1,0:T(8,128)(2,1)} %shard_map.77.a_ref), channel_id=1, source_target_pairs={{0,8},{4,12},{8,0},{12,4},{16,24},{20,28},{24,16},{28,20},{1,9},{5... | collective-permute-start | bytes 1671176 | tf_op jit(solution)/shard_map/ppermute | solution.py:728
  245.2 17.6 %collective-permute-start.21 = (bf16[1,136,2048]{2,1,0:T(8,128)(2,1)}, bf16[1,136,2048]{2,1,0:T(8,128)(2,1)}, u32[]{:S(2)}, u32[]{:S(2)}) collective-permute-start(bf16[1,136,2048]{2,1,0:T(8,128)(2,1)} %shard_map.83.a_ref), channel_id=1, source_target_pairs={{0,8},{4,12},{8,0},{12,4},{16,24},{20,28},{24,16},{28,20},{1,9},{5... | collective-permute-start | bytes 1671176 | tf_op jit(solution)/shard_map/ppermute | solution.py:728
  247.8 34.4 %collective-permute-start.12 = (bf16[1,136,2048]{2,1,0:T(8,128)(2,1)}, bf16[1,136,2048]{2,1,0:T(8,128)(2,1)}, u32[]{:S(2)}, u32[]{:S(2)}) collective-permute-start(bf16[1,136,2048]{2,1,0:T(8,128)(2,1)} %shard_map.79), channel_id=1, source_target_pairs={{8,16},{12,20},{16,8},{20,12},{9,17},{13,21},{17,9},{21,13},{10,18... | collective-permute-start | bytes 1671176 | tf_op jit(solution)/shard_map/ppermute | solution.py:728
  251.4 34.4 %collective-permute-start.15 = (bf16[1,136,2048]{2,1,0:T(8,128)(2,1)}, bf16[1,136,2048]{2,1,0:T(8,128)(2,1)}, u32[]{:S(2)}, u32[]{:S(2)}) collective-permute-start(bf16[1,136,2048]{2,1,0:T(8,128)(2,1)} %shard_map.84), channel_id=1, source_target_pairs={{8,16},{12,20},{16,8},{20,12},{9,17},{13,21},{17,9},{21,13},{10,18... | collective-permute-start | bytes 1671176 | tf_op jit(solution)/shard_map/ppermute | solution.py:728
  252.8 89.1 %collective-permute-start.26 = (bf16[2048,512]{1,0:T(8,128)(2,1)}, bf16[2048,512]{1,0:T(8,128)(2,1)}, u32[]{:S(2)}, u32[]{:S(2)}) collective-permute-start(bf16[2048,512]{1,0:T(8,128)(2,1)} %collective-permute-done.25.refs_9_), channel_id=1, source_target_pairs={{8,12},{12,8},{16,20},{20,16},{9,13},{13,9},{17,21},{21,17},{10,14... | collective-permute-start | bytes 6291464 | tf_op jit(solution)/shard_map/ppermute | solution.py:728
  254.8 87.1 %collective-permute-start.28 = (bf16[2048,512]{1,0:T(8,128)(2,1)}, bf16[2048,512]{1,0:T(8,128)(2,1)}, u32[]{:S(2)}, u32[]{:S(2)}) collective-permute-start(bf16[2048,512]{1,0:T(8,128)(2,1)} %collective-permute-done.27.refs_11_), channel_id=1, source_target_pairs={{0,4},{4,0},{24,28},{28,24},{1,5},{5,1},{25,29},{29,25},{2,6},{6,2... | collective-permute-start | bytes 6291464 | tf_op jit(solution)/shard_map/ppermute | solution.py:728
  262.9 27.6 %collective-permute-start.22 = (bf16[1,136,2048]{2,1,0:T(8,128)(2,1)}, bf16[1,136,2048]{2,1,0:T(8,128)(2,1)}, u32[]{:S(2)}, u32[]{:S(2)}) collective-permute-start(bf16[1,136,2048]{2,1,0:T(8,128)(2,1)} %shard_map.88.a_ref), channel_id=1, source_target_pairs={{0,8},{4,12},{8,0},{12,4},{16,24},{20,28},{24,16},{28,20},{1,9},{5... | collective-permute-start | bytes 1671176 | tf_op jit(solution)/shard_map/ppermute | solution.py:728
  282.2 11.7 %collective-permute-start.18 = (bf16[1,136,2048]{2,1,0:T(8,128)(2,1)}, bf16[1,136,2048]{2,1,0:T(8,128)(2,1)}, u32[]{:S(2)}, u32[]{:S(2)}) collective-permute-start(bf16[1,136,2048]{2,1,0:T(8,128)(2,1)} %shard_map.89), channel_id=1, source_target_pairs={{8,16},{12,20},{16,8},{20,12},{9,17},{13,21},{17,9},{21,13},{10,18... | collective-permute-start | bytes 1671176 | tf_op jit(solution)/shard_map/ppermute | solution.py:728
  285.7 10.2 %collective-permute-start.13 = (bf16[1,136,2048]{2,1,0:T(8,128)(2,1)}, bf16[1,136,2048]{2,1,0:T(8,128)(2,1)}, u32[]{:S(2)}, u32[]{:S(2)}) collective-permute-start(bf16[1,136,2048]{2,1,0:T(8,128)(2,1)} %shard_map.80.a_ref), channel_id=1, source_target_pairs={{0,8},{4,12},{8,0},{12,4},{16,24},{20,28},{24,16},{28,20},{1,9},{5... | collective-permute-start | bytes 1671176 | tf_op jit(solution)/shard_map/ppermute | solution.py:728
  290.5 14.5 %collective-permute-start.16 = (bf16[1,136,2048]{2,1,0:T(8,128)(2,1)}, bf16[1,136,2048]{2,1,0:T(8,128)(2,1)}, u32[]{:S(2)}, u32[]{:S(2)}) collective-permute-start(bf16[1,136,2048]{2,1,0:T(8,128)(2,1)} %shard_map.85.a_ref), channel_id=1, source_target_pairs={{0,8},{4,12},{8,0},{12,4},{16,24},{20,28},{24,16},{28,20},{1,9},{5... | collective-permute-start | bytes 1671176 | tf_op jit(solution)/shard_map/ppermute | solution.py:728
  293.9 28.4 %collective-permute-start.23 = (bf16[1024,512]{1,0:T(8,128)(2,1)}, bf16[1024,512]{1,0:T(8,128)(2,1)}, u32[]{:S(2)}, u32[]{:S(2)}) collective-permute-start(bf16[1024,512]{1,0:T(8,128)(2,1)} %get-tuple-element.20), channel_id=1, source_target_pairs={{0,4},{4,0},{8,12},{12,8},{16,20},{20,16},{24,28},{28,24},{1,5},{5... | collective-permute-start | bytes 3145736 | tf_op jit(solution)/shard_map/ppermute | solution.py:728
  296.0 45.9 %collective-permute-start.24 = (bf16[1024,512]{1,0:T(8,128)(2,1)}, bf16[1024,512]{1,0:T(8,128)(2,1)}, u32[]{:S(2)}, u32[]{:S(2)}) collective-permute-start(bf16[1024,512]{1,0:T(8,128)(2,1)} %get-tuple-element.19), channel_id=1, source_target_pairs={{0,4},{4,0},{8,12},{12,8},{16,20},{20,16},{24,28},{28,24},{1,5},{5... | collective-permute-start | bytes 3145736 | tf_op jit(solution)/shard_map/ppermute | solution.py:728
  305.0 14.8 %collective-permute-start.19 = (bf16[1,136,2048]{2,1,0:T(8,128)(2,1)}, bf16[1,136,2048]{2,1,0:T(8,128)(2,1)}, u32[]{:S(2)}, u32[]{:S(2)}) collective-permute-start(bf16[1,136,2048]{2,1,0:T(8,128)(2,1)} %shard_map.90.a_ref), channel_id=1, source_target_pairs={{0,8},{4,12},{8,0},{12,4},{16,24},{20,28},{24,16},{28,20},{1,9},{5... | collective-permute-start | bytes 1671176 | tf_op jit(solution)/shard_map/ppermute | solution.py:728

commit v3 on v2

--- a/solution.py
+++ b/solution.py
@@ -772,36 +772,34 @@
         back1 = send(near1, near)
         near_rows.append(join(near1, beside, q, False))
         own_rows.append(join(near0, back1, q, False))
-    return project_call(
-        own_rows + near_rows,
-        out_weight,
-        w_across0,
-        w_across1,
-        w_in,
-        w_in_both,
-        w_out,
-        w_out_both,
-    )
+    weights = (out_weight, w_across0, w_across1, w_in, w_in_both, w_out, w_out_both)
+    far_out = project_call(near_rows, weights, True)
+    home_out = project_call(own_rows, weights, False)
+    return jnp.where(at_home(), home_out, far_out)
 
 
 MESH = pl.DeviceIdType.MESH
 
 
-def project_kernel(pieces, *refs):
+def at_home():
+    return lax.axis_index("head") % 2 == lax.axis_index("pass") // 2 % 2
+
+
+def project_kernel(pieces, hops, *refs):
     rows_refs = refs[:pieces]
     own_ref, a0_ref, a1_ref, in_ref, in2_ref, out1_ref, out2_ref = refs[pieces : pieces + 7]
     refs = refs[pieces + 7 :]
     out_ref, context_ref, w_ref, part_ref, core_ref, y_ref, ysend_ref, zsend_ref = refs[:8]
     row_sem, w_sem, send_sem, recv_sem = refs[8:]
     me, head = lax.axis_index("pass"), lax.axis_index("head")
-    z, x, y, core = me // 2, me % 2, head // 2, head % 2
-    rows, wide = out_ref.shape[0], w_ref.shape[3]
+    z, x, y = me // 2, me % 2, head // 2
+    wide = w_ref.shape[3]
     half = a0_ref.shape[0]
     inner = is_inner()
     core_peer = (me, head ^ 1)
     y_peer = (me, head ^ 2)
     z_peer = (me ^ 2, head ^ 1)
-    stays = core == z % 2
+    sums = jnp.logical_not(at_home()) if hops else at_home()
 
     row_loads = [
         pltpu.make_async_copy(ref, context_ref.at[pl.ds(i * LQ, LQ)], row_sem.at[i])
@@ -827,8 +825,18 @@
                 pltpu.make_async_copy(one, w_ref.at[1, x], w_sem.at[1, x]).start()
                 pltpu.make_async_copy(two, w_ref.at[1, 1 - x], w_sem.at[1, 1 - x]).start()
 
-    load_here()
-    load_there()
+    here_first = y != z // 2
+
+    @pl.when(here_first)
+    def _():
+        load_here()
+        load_there()
+
+    @pl.when(jnp.logical_not(here_first))
+    def _():
+        load_there()
+        load_here()
+
     barrier = pltpu.get_barrier_semaphore()
     for peer in (core_peer, y_peer, z_peer):
         pl.semaphore_signal(barrier, inc=1, device_id=peer, device_id_type=MESH)
@@ -857,63 +865,61 @@
     for load in row_loads:
         load.wait()
 
-    def product(to_y, to_core, j):
-        start = pl.multiple_of(jnp.where(to_core == z % 2, 0, rows), LQ)
-        here = jnp.where(to_y == z // 2, 0, 1)
-        return jnp.dot(
-            context_ref[pl.ds(start, rows), :],
-            w_ref[here, j],
-            preferred_element_type=jnp.float32,
-        ).astype(jnp.bfloat16)
-
     for s, to_y in enumerate((1 - y, y)):
         here = jnp.where(to_y == z // 2, 0, 1)
         for j in range(2):
             block = w_ref.at[here, j]
             pltpu.make_async_copy(block, block, w_sem.at[here, j]).wait()
-            part_ref[s, j] = product(to_y, 1 - core, j)
-            core_copies[s][j].start()
-            value = product(to_y, core, j).astype(jnp.float32)
-            core_copies[s][j].wait_recv()
-            value = value + core_ref[s, j].astype(jnp.float32)
-            if s == 0:
-                ysend_ref[j] = value.astype(jnp.bfloat16)
-                y_copies[j].start()
-            else:
-                y_copies[j].wait_recv()
-                total = (value + y_ref[j].astype(jnp.float32)).astype(jnp.bfloat16)
-
-                @pl.when(stays)
-                def _():
-                    out_ref[:, columns(j)] = total
-
-                @pl.when(jnp.logical_not(stays))
-                def _():
-                    zsend_ref[j] = total
-                    z_copies[j].start()
-
-    @pl.when(jnp.logical_not(stays))
+            part_ref[s, j] = jnp.dot(
+                context_ref[...], w_ref[here, j], preferred_element_type=jnp.float32
+            ).astype(part_ref.dtype)
+
+            @pl.when(jnp.logical_not(sums))
+            def _():
+                core_copies[s][j].start()
+
+            @pl.when(sums)
+            def _():
+                core_copies[s][j].wait_recv()
+                value = part_ref[s, j].astype(jnp.float32) + core_ref[s, j].astype(jnp.float32)
+                if s == 0:
+                    ysend_ref[j] = value.astype(ysend_ref.dtype)
+                    y_copies[j].start()
+                else:
+                    y_copies[j].wait_recv()
+                    total = (value + y_ref[j].astype(jnp.float32)).astype(out_ref.dtype)
+                    if hops:
+                        zsend_ref[j] = total
+                        z_copies[j].start()
+                    else:
+                        out_ref[:, columns(j)] = total
+
+    @pl.when(sums)
     def _():
-        for copy in z_copies:
-            copy.wait()
-
-    for copies in core_copies + [y_copies]:
-        for copy in copies:
+        for copy in y_copies:
             copy.wait_send()
-
-
-def project_call(pieces, own, a0, a1, *lines):
-    rows, depth = len(pieces) // 2 * LQ, own.shape[0]
-    wide = own.shape[1]
+        if hops:
+            for copy in z_copies:
+                copy.wait()
+
+    @pl.when(jnp.logical_not(sums))
+    def _():
+        for copies in core_copies:
+            for copy in copies:
+                copy.wait_send()
+
+
+def project_call(pieces, weights, hops):
+    own = weights[0]
+    rows, (depth, wide) = len(pieces) * LQ, own.shape
     dtype = own.dtype
-    anyspace = pl.BlockSpec(memory_space=pl.ANY)
     return pl.pallas_call(
-        functools.partial(project_kernel, len(pieces)),
+        functools.partial(project_kernel, len(pieces), hops),
         out_shape=jax.ShapeDtypeStruct((rows, 2 * wide), dtype),
-        in_specs=[anyspace] * (len(pieces) + 7),
+        in_specs=[pl.BlockSpec(memory_space=pl.ANY)] * (len(pieces) + len(weights)),
         out_specs=pl.BlockSpec(memory_space=pltpu.VMEM),
         scratch_shapes=[
-            pltpu.VMEM((2 * rows, depth), dtype),
+            pltpu.VMEM((rows, depth), dtype),
             pltpu.VMEM((2, 2, depth, wide), dtype),
             pltpu.VMEM((2, 2, rows, wide), dtype),
             pltpu.VMEM((2, 2, rows, wide), dtype),
@@ -926,15 +932,15 @@
             pltpu.SemaphoreType.DMA((8,)),
         ],
         compiler_params=pltpu.CompilerParams(
-            collective_id=0, has_side_effects=True, vmem_limit_bytes=VMEM_BYTES
+            collective_id=int(hops), has_side_effects=True, vmem_limit_bytes=VMEM_BYTES
         ),
-        name="project_sum",
+        name="project_far" if hops else "project_home",
         cost_estimate=pl.CostEstimate(
-            flops=2 * 4 * 2 * rows * depth * wide,
+            flops=2 * 4 * rows * depth * wide,
             bytes_accessed=4 * depth * wide * 2,
             transcendentals=0,
         ),
-    )(*pieces, own, a0, a1, *lines)
+    )(*pieces, *weights)
 
 
 def suits_line(mesh, queries, lists):

time: 388 us -> 389 us (level)
  the two profiles are of different devices: /device:TPU:1 before, /device:TPU:0 now
where the time goes in v3:
time: 389 us; the launch traced here: 388 us
  Pallas kernels  158 us (41%)
  waiting for transfers between devices  152 us (39%)
  starting transfers between devices  62.9 us (16%)
  local copies, waits for them, and re-layouts  13 us (3%)
    ppermute x29, waiting for transfers between devices, send(): return lax.ppermute(value, 'pass', pairs)  152 us
    pallas_call x4, Pallas kernels, part_call(): pl.pallas_call(functools.partial(part_kernel, k, most, heads), out_shape=...  66.8 us
    ppermute x29, starting transfers between devices, send(): return lax.ppermute(value, 'pass', pairs)  62.9 us
    pallas_call x2, Pallas kernels, project_call(): pl.pallas_call(functools.partial(project_kernel, len(pieces), hops), out_...  40.8 us
    pallas_call x18, Pallas kernels, join_call(): pl.pallas_call(merge_kernel if leveled else finish_kernel, out_shape=jax....  39.9 us
    pallas_call x1, Pallas kernels, sort_items(): pl.pallas_call(functools.partial(sort_kernel, most, per_device), out_shap...  10.6 us
    unnamed x1, local copies, waits for them, and re-layouts  8.19 us
  transfers between devices with their start and end apart: 29, of which 12 were waited for; matrix products, arithmetic and copies ran while one was open for 3% of the time, Pallas kernels for 32%

profile of v3, /device:TPU:0, one launch (start us, length us, event | category | flops | bytes accessed | tf_op | source)
XLA Modules:
  0.0 388.2 jit_solution(461188984541166094)
XLA Ops:
  0.0 3.1 collective-permute-start.2
  4.9 8.2 %copy.16 = bf16[16,512,2,256]{3,1,2,0:T(8,128)(2,1)} copy(bf16[16,512,2,256]{3,2,1,0:T(2,128)(2,1)} %param.9) | data formatting | bytes 16777216 | tf_op args[2]
  13.1 10.6 %sort_items.1 = (s32[12]{0:T(128)}, s32[12]{0:T(128)}, s32[12]{0:T(128)}, bf16[3,2,512,256]{3,2,1,0:T(8,128)(2,1)}, bf16[3,2,512,256]{3,2,1,0:T(8,128)(2,1)}, /*...) custom-call(s32[8,24]{1,0:T(8,128)} %bitcast.15, s32[128]{0:T(128)} %pslot_ref.1, s32[24]{0:T(128)} %qslot_ref.1, ...), custom_call_target="tpu_custom_call" | custom-call | bytes 12582912 | tf_op jit(solution)/shard_map/sort_items/pallas_call | solution.py:429
  25.4 12.4 %collective-permute-done.2.refs_3_ = bf16[384,2048]{1,0:T(8,128)(2,1)} collective-permute-done((bf16[384,2048]{1,0:T(8,128)(2,1)}, bf16[384,2048]{1,0:T(8,128)(2,1)}, u32[]{:S(2)}, u32[]{:S(2)}) %collective-permute-start.2) | collective-permute-done | bytes 1572896 | tf_op jit(solution)/shard_map/ppermute | solution.py:728
  42.6 3.0 fusion
  45.9 15.4 %collective-permute-done.7.refs_6_ = bf16[3,2,512,256]{3,2,1,0:T(8,128)(2,1)} collective-permute-done((bf16[3,2,512,256]{3,2,1,0:T(8,128)(2,1)}, bf16[3,2,512,256]{3,2,1,0:T(8,128)(2,1)}, u32[]{:S(2)}, u32[]{:S(2)}) %collective-permute-start.7) | collective-permute-done | bytes 1572896 | tf_op jit(solution)/shard_map/ppermute | solution.py:728
  64.2 13.9 %collective-permute-done.6.refs_4_ = bf16[384,2048]{1,0:T(8,128)(2,1)} collective-permute-done((bf16[384,2048]{1,0:T(8,128)(2,1)}, bf16[384,2048]{1,0:T(8,128)(2,1)}, u32[]{:S(2)}, u32[]{:S(2)}) %collective-permute-start.6) | collective-permute-done | bytes 1572896 | tf_op jit(solution)/shard_map/ppermute | solution.py:728
  78.2 15.5 %shard_map.75.a_ref = bf16[3,136,2048]{2,1,0:T(8,128)(2,1)} custom-call(s32[12]{0:T(128)} %get-tuple-element.12.refs_0_, s32[12]{0:T(128)} %get-tuple-element.13.refs_1_, s32[12]{0:T(128)} %get-tuple-element.14.refs_2_, bf16[384,2048]{1,0:T(8,128)(2,1)} %collective-permute-done.3.refs_3_, bf16[384,2048]{1,0:T(8,128)(2,1)} %collective-permute-done.6.refs_4_, ...), custom_call_target="tpu_custom_call" | custom-call | flops 3221225472 | bytes 3145728 | tf_op jit(solution)/shard_map/pallas_call | solution.py:616
  93.7 4.4 %collective-permute-start.8 = (bf16[3,136,2048]{2,1,0:T(8,128)(2,1)}, bf16[3,136,2048]{2,1,0:T(8,128)(2,1)}, u32[]{:S(2)}, u32[]{:S(2)}) collective-permute-start(bf16[3,136,2048]{2,1,0:T(8,128)(2,1)} %shard_map.75.a_ref), channel_id=1, source_target_pairs={{0,8},{4,12},{24,16},{28,20},{1,9},{5,13},{25,17},{29,21},{2,10},{... | collective-permute-start | bytes 5013512 | tf_op jit(solution)/shard_map/ppermute | solution.py:728
  98.1 19.4 %collective-permute-done.20.refs_4_ = bf16[1024,512]{1,0:T(8,128)(2,1)} collective-permute-done((bf16[1024,512]{1,0:T(8,128)(2,1)}, bf16[1024,512]{1,0:T(8,128)(2,1)}, u32[]{:S(2)}, u32[]{:S(2)}) %collective-permute-start.20) | collective-permute-done | bytes 1048608 | tf_op jit(solution)/shard_map/ppermute | solution.py:728
  117.5 6.1 %collective-permute-start.22 = (bf16[2048,512]{1,0:T(8,128)(2,1)}, bf16[2048,512]{1,0:T(8,128)(2,1)}, u32[]{:S(2)}, u32[]{:S(2)}) collective-permute-start(bf16[2048,512]{1,0:T(8,128)(2,1)} %refs_3_.3), channel_id=1, source_target_pairs={{0,16},{4,20},{24,8},{28,12},{1,17},{5,21},{25,9},{29,13},{2,18},{... | collective-permute-start | bytes 6291464 | tf_op jit(solution)/shard_map/ppermute | solution.py:728
  123.7 14.9 %collective-permute-done.21.refs_5_ = bf16[1024,512]{1,0:T(8,128)(2,1)} collective-permute-done((bf16[1024,512]{1,0:T(8,128)(2,1)}, bf16[1024,512]{1,0:T(8,128)(2,1)}, u32[]{:S(2)}, u32[]{:S(2)}) %collective-permute-start.21) | collective-permute-done | bytes 1048608 | tf_op jit(solution)/shard_map/ppermute | solution.py:728
  142.0 15.5 %shard_map.74.a_ref = bf16[3,136,2048]{2,1,0:T(8,128)(2,1)} custom-call(s32[12]{0:T(128)} %get-tuple-element.12.refs_0_, s32[12]{0:T(128)} %get-tuple-element.13.refs_1_, s32[12]{0:T(128)} %get-tuple-element.14.refs_2_, bf16[384,2048]{1,0:T(8,128)(2,1)} %collective-permute-done.1.refs_3_, bf16[384,2048]{1,0:T(8,128)(2,1)} %collective-permute-done.4.refs_4_, ...), custom_call_target="tpu_custom_call" | custom-call | flops 3221225472 | bytes 3145728 | tf_op jit(solution)/shard_map/pallas_call | solution.py:616
  157.5 7.8 %collective-permute-start.11 = (bf16[3,136,2048]{2,1,0:T(8,128)(2,1)}, bf16[3,136,2048]{2,1,0:T(8,128)(2,1)}, u32[]{:S(2)}, u32[]{:S(2)}) collective-permute-start(bf16[3,136,2048]{2,1,0:T(8,128)(2,1)} %shard_map.74.a_ref), channel_id=1, source_target_pairs={{0,8},{4,12},{24,16},{28,20},{1,9},{5,13},{25,17},{29,21},{2,10},{... | collective-permute-start | bytes 5013512 | tf_op jit(solution)/shard_map/ppermute | solution.py:728
  167.4 10.1 %collective-permute-done.refs_6_ = bf16[3,2,512,256]{3,2,1,0:T(8,128)(2,1)} collective-permute-done((bf16[3,2,512,256]{3,2,1,0:T(8,128)(2,1)}, bf16[3,2,512,256]{3,2,1,0:T(8,128)(2,1)}, u32[]{:S(2)}, u32[]{:S(2)}) %collective-permute-start) | collective-permute-done | bytes 1572896 | tf_op jit(solution)/shard_map/ppermute | solution.py:728
  181.0 43.1 %collective-permute-done.24.refs_8_ = bf16[2048,512]{1,0:T(8,128)(2,1)} collective-permute-done((bf16[2048,512]{1,0:T(8,128)(2,1)}, bf16[2048,512]{1,0:T(8,128)(2,1)}, u32[]{:S(2)}, u32[]{:S(2)}) %collective-permute-start.24) | collective-permute-done | bytes 2097184 | tf_op jit(solution)/shard_map/ppermute | solution.py:728
  224.1 3.4 collective-permute-start.25
  236.4 20.3 %shard_map.73.a_ref = bf16[3,136,2048]{2,1,0:T(8,128)(2,1)} custom-call(s32[12]{0:T(128)} %get-tuple-element.12.refs_0_, s32[12]{0:T(128)} %get-tuple-element.13.refs_1_, s32[12]{0:T(128)} %get-tuple-element.14.refs_2_, bf16[3,2,128,256]{3,2,1,0:T(8,128)(2,1)} %bitcast.13, bf16[384,2048]{1,0:T(8,128)(2,1)} %refs_4_.1, bf16[16,2,512,256]{3,2,1,0:T(8,128)(2,1)} %bitcast.11, ...), custom_call_target="tpu_custom_call" | custom-call | flops 3221225472 | bytes 3145728 | tf_op jit(solution)/shard_map/pallas_call | solution.py:616
  258.8 5.0 %collective-permute-start.26 = (bf16[1,136,2048]{2,1,0:T(8,128)(2,1)}, bf16[1,136,2048]{2,1,0:T(8,128)(2,1)}, u32[]{:S(2)}, u32[]{:S(2)}) collective-permute-start(bf16[1,136,2048]{2,1,0:T(8,128)(2,1)} %shard_map.77.a_ref), channel_id=1, source_target_pairs={{0,8},{4,12},{8,0},{12,4},{16,24},{20,28},{24,16},{28,20},{1,9},{5... | collective-permute-start | bytes 1671176 | tf_op jit(solution)/shard_map/ppermute | solution.py:728
  271.9 5.6 %collective-permute-done.26.b_ref = bf16[1,136,2048]{2,1,0:T(8,128)(2,1)} collective-permute-done((bf16[1,136,2048]{2,1,0:T(8,128)(2,1)}, bf16[1,136,2048]{2,1,0:T(8,128)(2,1)}, u32[]{:S(2)}, u32[]{:S(2)}) %collective-permute-start.26) | collective-permute-done | bytes 557088 | tf_op jit(solution)/shard_map/ppermute | solution.py:728
  281.1 7.3 %collective-permute-done.27.b_ref = bf16[1,136,2048]{2,1,0:T(8,128)(2,1)} collective-permute-done((bf16[1,136,2048]{2,1,0:T(8,128)(2,1)}, bf16[1,136,2048]{2,1,0:T(8,128)(2,1)}, u32[]{:S(2)}, u32[]{:S(2)}) %collective-permute-start.27) | collective-permute-done | bytes 557088 | tf_op jit(solution)/shard_map/ppermute | solution.py:728
  291.9 4.2 %collective-permute-start.28 = (bf16[1,136,2048]{2,1,0:T(8,128)(2,1)}, bf16[1,136,2048]{2,1,0:T(8,128)(2,1)}, u32[]{:S(2)}, u32[]{:S(2)}) collective-permute-start(bf16[1,136,2048]{2,1,0:T(8,128)(2,1)} %shard_map.88.a_ref), channel_id=1, source_target_pairs={{0,8},{4,12},{8,0},{12,4},{16,24},{20,28},{24,16},{28,20},{1,9},{5... | collective-permute-start | bytes 1671176 | tf_op jit(solution)/shard_map/ppermute | solution.py:728
  296.1 15.5 %shard_map.78.a_ref = bf16[3,136,2048]{2,1,0:T(8,128)(2,1)} custom-call(s32[12]{0:T(128)} %get-tuple-element.12.refs_0_, s32[12]{0:T(128)} %get-tuple-element.13.refs_1_, s32[12]{0:T(128)} %get-tuple-element.14.refs_2_, bf16[384,2048]{1,0:T(8,128)(2,1)} %collective-permute-done.2.refs_3_, bf16[16,2,512,256]{3,2,1,0:T(8,128)(2,1)} %bitcast.12, ...), custom_call_target="tpu_custom_call" | custom-call | flops 3221225472 | bytes 3145728 | tf_op jit(solution)/shard_map/pallas_call | solution.py:616
  320.9 2.5 shard_map.92.refs_0_
  323.4 2.5 shard_map.93.refs_1_
  325.8 2.5 shard_map.94.refs_2_
  328.3 8.5 %project_far.1 = bf16[384,1024]{1,0:T(8,128)(2,1)} custom-call(bf16[128,2048]{1,0:T(8,128)(2,1)} %shard_map.92.refs_0_, bf16[128,2048]{1,0:T(8,128)(2,1)} %shard_map.93.refs_1_, bf16[128,2048]{1,0:T(8,128)(2,1)} %shard_map.94.refs_2_, bf16[2048,512]{1,0:T(8,128)(2,1)} %refs_3_.3, bf16[1024,512]{1,0:T(8,128)(2,1)} %collective-permute-done.20.refs_4_, ...), custom_call_target="tpu_custom_call" | custom-call | flops 3221225472 | bytes 8388608 | tf_op jit(solution)/shard_map/project_far/pallas_call | solution.py:916
  336.8 2.5 shard_map.81.refs_0_
  341.4 2.5 shard_map.86.refs_1_
  343.9 7.4 %collective-permute-done.19.b_ref = bf16[1,136,2048]{2,1,0:T(8,128)(2,1)} collective-permute-done((bf16[1,136,2048]{2,1,0:T(8,128)(2,1)}, bf16[1,136,2048]{2,1,0:T(8,128)(2,1)}, u32[]{:S(2)}, u32[]{:S(2)}) %collective-permute-start.19) | collective-permute-done | bytes 557088 | tf_op jit(solution)/shard_map/ppermute | solution.py:728
  351.3 2.5 shard_map.91.refs_2_
  353.8 32.3 %project_home.1 = bf16[384,1024]{1,0:T(8,128)(2,1)} custom-call(bf16[128,2048]{1,0:T(8,128)(2,1)} %shard_map.81.refs_0_, bf16[128,2048]{1,0:T(8,128)(2,1)} %shard_map.86.refs_1_, bf16[128,2048]{1,0:T(8,128)(2,1)} %shard_map.91.refs_2_, bf16[2048,512]{1,0:T(8,128)(2,1)} %refs_3_.3, bf16[1024,512]{1,0:T(8,128)(2,1)} %collective-permute-done.20.refs_4_, ...), custom_call_target="tpu_custom_call" | custom-call | flops 3221225472 | bytes 8388608 | tf_op jit(solution)/shard_map/project_home/pallas_call | solution.py:916
  (55 shorter events, 60.2 us)
Async XLA Ops:
  0.0 37.8 %collective-permute-start.2 = (bf16[384,2048]{1,0:T(8,128)(2,1)}, bf16[384,2048]{1,0:T(8,128)(2,1)}, u32[]{:S(2)}, u32[]{:S(2)}) collective-permute-start(bf16[384,2048]{1,0:T(8,128)(2,1)} %refs_4_.1), channel_id=1, source_target_pairs={{0,8},{4,12},{8,0},{12,4},{16,24},{20,28},{24,16},{28,20},{1,9},{5... | collective-permute-start | bytes 4718600 | tf_op jit(solution)/shard_map/ppermute | solution.py:728
  3.1 36.5 %collective-permute-start.1 = (bf16[384,2048]{1,0:T(8,128)(2,1)}, bf16[384,2048]{1,0:T(8,128)(2,1)}, u32[]{:S(2)}, u32[]{:S(2)}) collective-permute-start(bf16[384,2048]{1,0:T(8,128)(2,1)} %refs_4_.1), channel_id=1, source_target_pairs={{8,16},{12,20},{16,8},{20,12},{9,17},{13,21},{17,9},{21,13},{10,18... | collective-permute-start | bytes 4718600 | tf_op jit(solution)/shard_map/ppermute | solution.py:728
  23.7 37.6 %collective-permute-start.7 = (bf16[3,2,512,256]{3,2,1,0:T(8,128)(2,1)}, bf16[3,2,512,256]{3,2,1,0:T(8,128)(2,1)}, u32[]{:S(2)}, u32[]{:S(2)}) collective-permute-start(bf16[3,2,512,256]{3,2,1,0:T(8,128)(2,1)} %get-tuple-element.17), channel_id=1, source_target_pairs={{0,4},{4,0},{8,12},{12,8},{16,20},{20,16},{24,28},{28,24},{1,5},{5... | collective-permute-start | bytes 4718600 | tf_op jit(solution)/shard_map/ppermute | solution.py:728
  37.8 25.2 %collective-permute-start.3 = (bf16[384,2048]{1,0:T(8,128)(2,1)}, bf16[384,2048]{1,0:T(8,128)(2,1)}, u32[]{:S(2)}, u32[]{:S(2)}) collective-permute-start(bf16[384,2048]{1,0:T(8,128)(2,1)} %collective-permute-done.2.refs_3_), channel_id=1, source_target_pairs={{8,16},{12,20},{16,8},{20,12},{9,17},{13,21},{17,9},{21,13},{10,18... | collective-permute-start | bytes 4718600 | tf_op jit(solution)/shard_map/ppermute | solution.py:728
  39.6 38.6 %collective-permute-start.6 = (bf16[384,2048]{1,0:T(8,128)(2,1)}, bf16[384,2048]{1,0:T(8,128)(2,1)}, u32[]{:S(2)}, u32[]{:S(2)}) collective-permute-start(bf16[384,2048]{1,0:T(8,128)(2,1)} %collective-permute-done.1.refs_3_), channel_id=1, source_target_pairs={{8,0},{12,4},{16,24},{20,28},{9,1},{13,5},{17,25},{21,29},{10,2},{... | collective-permute-start | bytes 4718600 | tf_op jit(solution)/shard_map/ppermute | solution.py:728
  40.9 99.0 %collective-permute-start.5 = (bf16[3,2,512,256]{3,2,1,0:T(8,128)(2,1)}, bf16[3,2,512,256]{3,2,1,0:T(8,128)(2,1)}, u32[]{:S(2)}, u32[]{:S(2)}) collective-permute-start(bf16[3,2,512,256]{3,2,1,0:T(8,128)(2,1)} %get-tuple-element.16), channel_id=1, source_target_pairs={{0,4},{4,0},{8,12},{12,8},{16,20},{20,16},{24,28},{28,24},{1,5},{5... | collective-permute-start | bytes 4718600 | tf_op jit(solution)/shard_map/ppermute | solution.py:728
  45.6 72.0 %collective-permute-start.20 = (bf16[1024,512]{1,0:T(8,128)(2,1)}, bf16[1024,512]{1,0:T(8,128)(2,1)}, u32[]{:S(2)}, u32[]{:S(2)}) collective-permute-start(bf16[1024,512]{1,0:T(8,128)(2,1)} %get-tuple-element.20), channel_id=1, source_target_pairs={{0,4},{4,0},{8,12},{12,8},{16,20},{20,16},{24,28},{28,24},{1,5},{5... | collective-permute-start | bytes 3145736 | tf_op jit(solution)/shard_map/ppermute | solution.py:728
  61.3 77.2 %collective-permute-start.21 = (bf16[1024,512]{1,0:T(8,128)(2,1)}, bf16[1024,512]{1,0:T(8,128)(2,1)}, u32[]{:S(2)}, u32[]{:S(2)}) collective-permute-start(bf16[1024,512]{1,0:T(8,128)(2,1)} %get-tuple-element.19), channel_id=1, source_target_pairs={{0,4},{4,0},{8,12},{12,8},{16,20},{20,16},{24,28},{28,24},{1,5},{5... | collective-permute-start | bytes 3145736 | tf_op jit(solution)/shard_map/ppermute | solution.py:728
  63.0 78.6 %collective-permute-start.4 = (bf16[384,2048]{1,0:T(8,128)(2,1)}, bf16[384,2048]{1,0:T(8,128)(2,1)}, u32[]{:S(2)}, u32[]{:S(2)}) collective-permute-start(bf16[384,2048]{1,0:T(8,128)(2,1)} %collective-permute-done.3.refs_3_), channel_id=1, source_target_pairs={{8,0},{12,4},{16,24},{20,28},{9,1},{13,5},{17,25},{21,29},{10,2},{... | collective-permute-start | bytes 4718600 | tf_op jit(solution)/shard_map/ppermute | solution.py:728
  93.7 63.8 %collective-permute-start.8 = (bf16[3,136,2048]{2,1,0:T(8,128)(2,1)}, bf16[3,136,2048]{2,1,0:T(8,128)(2,1)}, u32[]{:S(2)}, u32[]{:S(2)}) collective-permute-start(bf16[3,136,2048]{2,1,0:T(8,128)(2,1)} %shard_map.75.a_ref), channel_id=1, source_target_pairs={{0,8},{4,12},{24,16},{28,20},{1,9},{5,13},{25,17},{29,21},{2,10},{... | collective-permute-start | bytes 5013512 | tf_op jit(solution)/shard_map/ppermute | solution.py:728
  117.5 61.5 %collective-permute-start.22 = (bf16[2048,512]{1,0:T(8,128)(2,1)}, bf16[2048,512]{1,0:T(8,128)(2,1)}, u32[]{:S(2)}, u32[]{:S(2)}) collective-permute-start(bf16[2048,512]{1,0:T(8,128)(2,1)} %refs_3_.3), channel_id=1, source_target_pairs={{0,16},{4,20},{24,8},{28,12},{1,17},{5,21},{25,9},{29,13},{2,18},{... | collective-permute-start | bytes 6291464 | tf_op jit(solution)/shard_map/ppermute | solution.py:728
  138.6 85.5 %collective-permute-start.24 = (bf16[2048,512]{1,0:T(8,128)(2,1)}, bf16[2048,512]{1,0:T(8,128)(2,1)}, u32[]{:S(2)}, u32[]{:S(2)}) collective-permute-start(bf16[2048,512]{1,0:T(8,128)(2,1)} %refs_3_.3), channel_id=1, source_target_pairs={{8,24},{12,28},{16,0},{20,4},{9,25},{13,29},{17,1},{21,5},{10,26},... | collective-permute-start | bytes 6291464 | tf_op jit(solution)/shard_map/ppermute | solution.py:728
  139.9 37.6 %collective-permute-start = (bf16[3,2,512,256]{3,2,1,0:T(8,128)(2,1)}, bf16[3,2,512,256]{3,2,1,0:T(8,128)(2,1)}, u32[]{:S(2)}, u32[]{:S(2)}) collective-permute-start(bf16[3,2,512,256]{3,2,1,0:T(8,128)(2,1)} %get-tuple-element.15), channel_id=1, source_target_pairs={{0,4},{4,0},{8,12},{12,8},{16,20},{20,16},{24,28},{28,24},{1,5},{5... | collective-permute-start | bytes 4718600 | tf_op jit(solution)/shard_map/ppermute | solution.py:728
  141.6 88.1 %collective-permute-start.10 = (bf16[3,2,512,256]{3,2,1,0:T(8,128)(2,1)}, bf16[3,2,512,256]{3,2,1,0:T(8,128)(2,1)}, u32[]{:S(2)}, u32[]{:S(2)}) collective-permute-start(bf16[3,2,512,256]{3,2,1,0:T(8,128)(2,1)} %get-tuple-element.18), channel_id=1, source_target_pairs={{0,4},{4,0},{8,12},{12,8},{16,20},{20,16},{24,28},{28,24},{1,5},{5... | collective-permute-start | bytes 4718600 | tf_op jit(solution)/shard_map/ppermute | solution.py:728
  157.5 108.3 %collective-permute-start.11 = (bf16[3,136,2048]{2,1,0:T(8,128)(2,1)}, bf16[3,136,2048]{2,1,0:T(8,128)(2,1)}, u32[]{:S(2)}, u32[]{:S(2)}) collective-permute-start(bf16[3,136,2048]{2,1,0:T(8,128)(2,1)} %shard_map.74.a_ref), channel_id=1, source_target_pairs={{0,8},{4,12},{24,16},{28,20},{1,9},{5,13},{25,17},{29,21},{2,10},{... | collective-permute-start | bytes 5013512 | tf_op jit(solution)/shard_map/ppermute | solution.py:728
  177.5 55.6 %collective-permute-start.9 = (bf16[1,136,2048]{2,1,0:T(8,128)(2,1)}, bf16[1,136,2048]{2,1,0:T(8,128)(2,1)}, u32[]{:S(2)}, u32[]{:S(2)}) collective-permute-start(bf16[1,136,2048]{2,1,0:T(8,128)(2,1)} %shard_map.76), channel_id=1, source_target_pairs={{8,16},{12,20},{16,8},{20,12},{9,17},{13,21},{17,9},{21,13},{10,18... | collective-permute-start | bytes 1671176 | tf_op jit(solution)/shard_map/ppermute | solution.py:728
  179.0 149.3 %collective-permute-start.23 = (bf16[2048,512]{1,0:T(8,128)(2,1)}, bf16[2048,512]{1,0:T(8,128)(2,1)}, u32[]{:S(2)}, u32[]{:S(2)}) collective-permute-start(bf16[2048,512]{1,0:T(8,128)(2,1)} %collective-permute-done.22.refs_6_), channel_id=1, source_target_pairs={{8,12},{12,8},{16,20},{20,16},{9,13},{13,9},{17,21},{21,17},{10,14... | collective-permute-start | bytes 6291464 | tf_op jit(solution)/shard_map/ppermute | solution.py:728
  224.1 104.2 %collective-permute-start.25 = (bf16[2048,512]{1,0:T(8,128)(2,1)}, bf16[2048,512]{1,0:T(8,128)(2,1)}, u32[]{:S(2)}, u32[]{:S(2)}) collective-permute-start(bf16[2048,512]{1,0:T(8,128)(2,1)} %collective-permute-done.24.refs_8_), channel_id=1, source_target_pairs={{0,4},{4,0},{24,28},{28,24},{1,5},{5,1},{25,29},{29,25},{2,6},{6,2... | collective-permute-start | bytes 6291464 | tf_op jit(solution)/shard_map/ppermute | solution.py:728
  229.6 29.2 %collective-permute-start.14 = (bf16[1,136,2048]{2,1,0:T(8,128)(2,1)}, bf16[1,136,2048]{2,1,0:T(8,128)(2,1)}, u32[]{:S(2)}, u32[]{:S(2)}) collective-permute-start(bf16[1,136,2048]{2,1,0:T(8,128)(2,1)} %shard_map.82), channel_id=1, source_target_pairs={{8,16},{12,20},{16,8},{20,12},{9,17},{13,21},{17,9},{21,13},{10,18... | collective-permute-start | bytes 1671176 | tf_op jit(solution)/shard_map/ppermute | solution.py:728
  233.2 35.1 %collective-permute-start.17 = (bf16[1,136,2048]{2,1,0:T(8,128)(2,1)}, bf16[1,136,2048]{2,1,0:T(8,128)(2,1)}, u32[]{:S(2)}, u32[]{:S(2)}) collective-permute-start(bf16[1,136,2048]{2,1,0:T(8,128)(2,1)} %shard_map.87), channel_id=1, source_target_pairs={{8,16},{12,20},{16,8},{20,12},{9,17},{13,21},{17,9},{21,13},{10,18... | collective-permute-start | bytes 1671176 | tf_op jit(solution)/shard_map/ppermute | solution.py:728
  258.8 18.7 %collective-permute-start.26 = (bf16[1,136,2048]{2,1,0:T(8,128)(2,1)}, bf16[1,136,2048]{2,1,0:T(8,128)(2,1)}, u32[]{:S(2)}, u32[]{:S(2)}) collective-permute-start(bf16[1,136,2048]{2,1,0:T(8,128)(2,1)} %shard_map.77.a_ref), channel_id=1, source_target_pairs={{0,8},{4,12},{8,0},{12,4},{16,24},{20,28},{24,16},{28,20},{1,9},{5... | collective-permute-start | bytes 1671176 | tf_op jit(solution)/shard_map/ppermute | solution.py:728
  265.8 22.6 %collective-permute-start.27 = (bf16[1,136,2048]{2,1,0:T(8,128)(2,1)}, bf16[1,136,2048]{2,1,0:T(8,128)(2,1)}, u32[]{:S(2)}, u32[]{:S(2)}) collective-permute-start(bf16[1,136,2048]{2,1,0:T(8,128)(2,1)} %shard_map.83.a_ref), channel_id=1, source_target_pairs={{0,8},{4,12},{8,0},{12,4},{16,24},{20,28},{24,16},{28,20},{1,9},{5... | collective-permute-start | bytes 1671176 | tf_op jit(solution)/shard_map/ppermute | solution.py:728
  268.3 23.6 %collective-permute-start.12 = (bf16[1,136,2048]{2,1,0:T(8,128)(2,1)}, bf16[1,136,2048]{2,1,0:T(8,128)(2,1)}, u32[]{:S(2)}, u32[]{:S(2)}) collective-permute-start(bf16[1,136,2048]{2,1,0:T(8,128)(2,1)} %shard_map.79), channel_id=1, source_target_pairs={{8,16},{12,20},{16,8},{20,12},{9,17},{13,21},{17,9},{21,13},{10,18... | collective-permute-start | bytes 1671176 | tf_op jit(solution)/shard_map/ppermute | solution.py:728
  277.5 36.1 %collective-permute-start.15 = (bf16[1,136,2048]{2,1,0:T(8,128)(2,1)}, bf16[1,136,2048]{2,1,0:T(8,128)(2,1)}, u32[]{:S(2)}, u32[]{:S(2)}) collective-permute-start(bf16[1,136,2048]{2,1,0:T(8,128)(2,1)} %shard_map.84), channel_id=1, source_target_pairs={{8,16},{12,20},{16,8},{20,12},{9,17},{13,21},{17,9},{21,13},{10,18... | collective-permute-start | bytes 1671176 | tf_op jit(solution)/shard_map/ppermute | solution.py:728
  288.4 27.8 %collective-permute-start.18 = (bf16[1,136,2048]{2,1,0:T(8,128)(2,1)}, bf16[1,136,2048]{2,1,0:T(8,128)(2,1)}, u32[]{:S(2)}, u32[]{:S(2)}) collective-permute-start(bf16[1,136,2048]{2,1,0:T(8,128)(2,1)} %shard_map.89), channel_id=1, source_target_pairs={{8,16},{12,20},{16,8},{20,12},{9,17},{13,21},{17,9},{21,13},{10,18... | collective-permute-start | bytes 1671176 | tf_op jit(solution)/shard_map/ppermute | solution.py:728
  291.9 28.5 %collective-permute-start.28 = (bf16[1,136,2048]{2,1,0:T(8,128)(2,1)}, bf16[1,136,2048]{2,1,0:T(8,128)(2,1)}, u32[]{:S(2)}, u32[]{:S(2)}) collective-permute-start(bf16[1,136,2048]{2,1,0:T(8,128)(2,1)} %shard_map.88.a_ref), channel_id=1, source_target_pairs={{0,8},{4,12},{8,0},{12,4},{16,24},{20,28},{24,16},{28,20},{1,9},{5... | collective-permute-start | bytes 1671176 | tf_op jit(solution)/shard_map/ppermute | solution.py:728
  313.7 23.1 %collective-permute-start.13 = (bf16[1,136,2048]{2,1,0:T(8,128)(2,1)}, bf16[1,136,2048]{2,1,0:T(8,128)(2,1)}, u32[]{:S(2)}, u32[]{:S(2)}) collective-permute-start(bf16[1,136,2048]{2,1,0:T(8,128)(2,1)} %shard_map.80.a_ref), channel_id=1, source_target_pairs={{0,8},{4,12},{8,0},{12,4},{16,24},{20,28},{24,16},{28,20},{1,9},{5... | collective-permute-start | bytes 1671176 | tf_op jit(solution)/shard_map/ppermute | solution.py:728
  316.2 25.2 %collective-permute-start.16 = (bf16[1,136,2048]{2,1,0:T(8,128)(2,1)}, bf16[1,136,2048]{2,1,0:T(8,128)(2,1)}, u32[]{:S(2)}, u32[]{:S(2)}) collective-permute-start(bf16[1,136,2048]{2,1,0:T(8,128)(2,1)} %shard_map.85.a_ref), channel_id=1, source_target_pairs={{0,8},{4,12},{8,0},{12,4},{16,24},{20,28},{24,16},{28,20},{1,9},{5... | collective-permute-start | bytes 1671176 | tf_op jit(solution)/shard_map/ppermute | solution.py:728
  320.5 30.8 %collective-permute-start.19 = (bf16[1,136,2048]{2,1,0:T(8,128)(2,1)}, bf16[1,136,2048]{2,1,0:T(8,128)(2,1)}, u32[]{:S(2)}, u32[]{:S(2)}) collective-permute-start(bf16[1,136,2048]{2,1,0:T(8,128)(2,1)} %shard_map.90.a_ref), channel_id=1, source_target_pairs={{0,8},{4,12},{8,0},{12,4},{16,24},{20,28},{24,16},{28,20},{1,9},{5... | collective-permute-start | bytes 1671176 | tf_op jit(solution)/shard_map/ppermute | solution.py:728

commit v4 on v3

--- a/solution.py
+++ b/solution.py
@@ -348,6 +348,7 @@
 
 LINE = 4
 EXTRA = 8
+ITEM_ORDER = (2, 0, 3, 1)
 VMEM_BYTES = 67043328
 
 
@@ -376,48 +377,55 @@
         send_cnt[k] = 0
         far_cnt[k] = 0
 
+    def take(i):
+        return pltpu.make_async_copy(cache_ref.at[send_row[i]], buf.at[i], in_sem.at[i])
+
     def question(q, carry):
         slot = qslot_ref[q]
         dest = slot // per_device
         local = slot - dest * per_device
         k = (dest // 2) ^ z
-        same = dest % 2 == x
-        for t in range(topp):
-            row = pslot_ref[lists_ref[t, q]]
-            owner = row // pass_dev
-            mine = owner == me
-
-            @pl.when(jnp.logical_and(mine, same))
-            def _():
-                at = k * most + near_cnt[k]
-                row_ref[at] = row - owner * pass_dev
-                tag_ref[at] = local
-                near_cnt[k] = near_cnt[k] + 1
-
-            @pl.when(jnp.logical_and(mine, jnp.logical_not(same)))
-            def _():
-                send_row[k * most + send_cnt[k]] = row - owner * pass_dev
-                send_cnt[k] = send_cnt[k] + 1
-
-            @pl.when(jnp.logical_and(owner == (me ^ 1), same))
-            def _():
-                far_tag_ref[k * most + far_cnt[k]] = local
-                far_cnt[k] = far_cnt[k] + 1
+
+        @pl.when(dest % 2 == x)
+        def _():
+            for t in range(topp):
+                row = pslot_ref[lists_ref[t, q]]
+                owner = row // pass_dev
+
+                @pl.when(owner == me)
+                def _():
+                    at = k * most + near_cnt[k]
+                    row_ref[at] = row - owner * pass_dev
+                    tag_ref[at] = local
+                    near_cnt[k] = near_cnt[k] + 1
+
+                @pl.when(owner == (me ^ 1))
+                def _():
+                    far_tag_ref[k * most + far_cnt[k]] = local
+                    far_cnt[k] = far_cnt[k] + 1
+
+        @pl.when(dest % 2 != x)
+        def _():
+            for t in range(topp):
+                row = pslot_ref[lists_ref[t, q]]
+                owner = row // pass_dev
+
+                @pl.when(owner == me)
+                def _():
+                    at = k * most + send_cnt[k]
+                    send_row[at] = row - owner * pass_dev
+                    send_cnt[k] = send_cnt[k] + 1
+                    take(at).start()
 
         return carry
 
     lax.fori_loop(0, nq, question, 0)
-    copies = []
-    for k in (1, 2, 3, 0):
-        for r in range(most):
-            i = k * most + r
-            get = pltpu.make_async_copy(cache_ref.at[send_row[i]], buf.at[i], in_sem.at[i])
-            get.start()
-            copies.append((get, pltpu.make_async_copy(buf.at[i], outs[k].at[r], out_sem.at[i])))
-    for get, put in copies:
-        get.wait()
+    slots = [k * most + r for k in ITEM_ORDER for r in range(most)]
+    puts = [pltpu.make_async_copy(buf.at[i], outs[i // most].at[i % most], out_sem.at[i]) for i in slots]
+    for i, put in zip(slots, puts):
+        take(i).wait()
         put.start()
-    for get, put in copies:
+    for put in puts:
         put.wait()
 
 
@@ -722,7 +730,6 @@
     per_device = queries.shape[0] // LQ
     heads = own_kv.shape[1]
     most = per_device * lists.shape[1] // (2 * LINE)
-    half = out_weight.shape[0] // 2
 
     def send(value, pairs):
         return lax.ppermute(value, "pass", pairs)
@@ -740,8 +747,7 @@
     inward, outward = mirror(1, "outer"), mirror(1, "inner")
     q_near = send(queries, near)
     q_mid = send(queries, middle)
-    w_across0 = send(out_weight[:half], across)
-    w_across1 = send(out_weight[half:], across)
+    w_across = send(out_weight, across)
     cache = jnp.transpose(passage_cache, (0, 2, 1, 3))
     row, tag, far_tag, *items = sort_items(
         lists, passage_slot, question_slot, cache, most, per_device
@@ -772,12 +778,22 @@
         back1 = send(near1, near)
         near_rows.append(join(near1, beside, q, False))
         own_rows.append(join(near0, back1, q, False))
-    weights = (out_weight, w_across0, w_across1, w_in, w_in_both, w_out, w_out_both)
-    far_out = project_call(near_rows, weights, True)
+    weights = (out_weight, w_across, w_in, w_in_both, w_out, w_out_both)
+    sums = project_call(near_rows, weights, True)
+    far_out = send_far(sums)
     home_out = project_call(own_rows, weights, False)
     return jnp.where(at_home(), home_out, far_out)
 
 
+def send_far(sums):
+    pairs = []
+    for p in range(2 * LINE):
+        for h in range(LINE):
+            if h % 2 != (p // 2) % 2:
+                pairs.append((p * LINE + h, (p ^ 2) * LINE + (h ^ 1)))
+    return lax.ppermute(sums, ("pass", "head"), pairs)
+
+
 MESH = pl.DeviceIdType.MESH
 
 
@@ -785,21 +801,19 @@
     return lax.axis_index("head") % 2 == lax.axis_index("pass") // 2 % 2
 
 
-def project_kernel(pieces, hops, *refs):
+def project_kernel(pieces, far, *refs):
     rows_refs = refs[:pieces]
-    own_ref, a0_ref, a1_ref, in_ref, in2_ref, out1_ref, out2_ref = refs[pieces : pieces + 7]
-    refs = refs[pieces + 7 :]
-    out_ref, context_ref, w_ref, part_ref, core_ref, y_ref, ysend_ref, zsend_ref = refs[:8]
-    row_sem, w_sem, send_sem, recv_sem = refs[8:]
+    own_ref, across_ref, in_ref, in2_ref, out1_ref, out2_ref = refs[pieces : pieces + 6]
+    refs = refs[pieces + 6 :]
+    out_ref, context_ref, w_ref, part_ref, core_ref, y_ref, ysend_ref = refs[:7]
+    row_sem, w_sem, send_sem, recv_sem = refs[7:]
     me, head = lax.axis_index("pass"), lax.axis_index("head")
     z, x, y = me // 2, me % 2, head // 2
     wide = w_ref.shape[3]
-    half = a0_ref.shape[0]
     inner = is_inner()
     core_peer = (me, head ^ 1)
     y_peer = (me, head ^ 2)
-    z_peer = (me ^ 2, head ^ 1)
-    sums = jnp.logical_not(at_home()) if hops else at_home()
+    sums = jnp.logical_not(at_home()) if far else at_home()
 
     row_loads = [
         pltpu.make_async_copy(ref, context_ref.at[pl.ds(i * LQ, LQ)], row_sem.at[i])
@@ -810,9 +824,7 @@
 
     def load_here():
         pltpu.make_async_copy(own_ref, w_ref.at[0, x], w_sem.at[0, x]).start()
-        low, high = w_ref.at[0, 1 - x, pl.ds(0, half)], w_ref.at[0, 1 - x, pl.ds(half, half)]
-        pltpu.make_async_copy(a0_ref, low, w_sem.at[0, 1 - x]).start()
-        pltpu.make_async_copy(a1_ref, high, w_sem.at[0, 1 - x]).start()
+        pltpu.make_async_copy(across_ref, w_ref.at[0, 1 - x], w_sem.at[0, 1 - x]).start()
 
     def load_there():
         for which, (one, two) in (
@@ -838,9 +850,9 @@
         load_here()
 
     barrier = pltpu.get_barrier_semaphore()
-    for peer in (core_peer, y_peer, z_peer):
+    for peer in (core_peer, y_peer):
         pl.semaphore_signal(barrier, inc=1, device_id=peer, device_id_type=MESH)
-    pl.semaphore_wait(barrier, 3)
+    pl.semaphore_wait(barrier, 2)
 
     def remote(src, dst, i, peer):
         return pltpu.make_async_remote_copy(
@@ -860,7 +872,6 @@
         for s in range(2)
     ]
     y_copies = [remote(ysend_ref.at[j], y_ref.at[j], 4 + j, y_peer) for j in range(2)]
-    z_copies = [remote(zsend_ref.at[j], out_ref.at[:, columns(j)], 6 + j, z_peer) for j in range(2)]
 
     for load in row_loads:
         load.wait()
@@ -888,19 +899,12 @@
                 else:
                     y_copies[j].wait_recv()
                     total = (value + y_ref[j].astype(jnp.float32)).astype(out_ref.dtype)
-                    if hops:
-                        zsend_ref[j] = total
-                        z_copies[j].start()
-                    else:
-                        out_ref[:, columns(j)] = total
+                    out_ref[:, columns(j)] = total
 
     @pl.when(sums)
     def _():
         for copy in y_copies:
             copy.wait_send()
-        if hops:
-            for copy in z_copies:
-                copy.wait()
 
     @pl.when(jnp.logical_not(sums))
     def _():
@@ -909,12 +913,12 @@
                 copy.wait_send()
 
 
-def project_call(pieces, weights, hops):
+def project_call(pieces, weights, far):
     own = weights[0]
     rows, (depth, wide) = len(pieces) * LQ, own.shape
     dtype = own.dtype
     return pl.pallas_call(
-        functools.partial(project_kernel, len(pieces), hops),
+        functools.partial(project_kernel, len(pieces), far),
         out_shape=jax.ShapeDtypeStruct((rows, 2 * wide), dtype),
         in_specs=[pl.BlockSpec(memory_space=pl.ANY)] * (len(pieces) + len(weights)),
         out_specs=pl.BlockSpec(memory_space=pltpu.VMEM),
@@ -925,16 +929,15 @@
             pltpu.VMEM((2, 2, rows, wide), dtype),
             pltpu.VMEM((2, rows, wide), dtype),
             pltpu.VMEM((2, rows, wide), dtype),
-            pltpu.VMEM((2, rows, wide), dtype),
             pltpu.SemaphoreType.DMA((len(pieces),)),
             pltpu.SemaphoreType.DMA((2, 2)),
-            pltpu.SemaphoreType.DMA((8,)),
-            pltpu.SemaphoreType.DMA((8,)),
+            pltpu.SemaphoreType.DMA((6,)),
+            pltpu.SemaphoreType.DMA((6,)),
         ],
         compiler_params=pltpu.CompilerParams(
-            collective_id=int(hops), has_side_effects=True, vmem_limit_bytes=VMEM_BYTES
+            collective_id=int(far), has_side_effects=True, vmem_limit_bytes=VMEM_BYTES
         ),
-        name="project_far" if hops else "project_home",
+        name="project_far" if far else "project_home",
         cost_estimate=pl.CostEstimate(
             flops=2 * 4 * rows * depth * wide,
             bytes_accessed=4 * depth * wide * 2,

time: 389 us -> 396 us (1.018)
  starting transfers between devices: 62.9 us -> 87.7 us
  Pallas kernels: 158 us -> 142 us
    ppermute x29 -> x28, starting transfers between devices: 62.9 us -> 86.1 us  [send(): return lax.ppermute(value, 'pass', pairs)]
    pallas_call x2, Pallas kernels: 40.8 us -> 27.9 us  [project_call(): pl.pallas_call(functools.partial(project_kernel, len(pieces), far), out_s...]
    ppermute x29 -> x28, waiting for transfers between devices: 152 us -> 151 us  [send(): return lax.ppermute(value, 'pass', pairs)]
  transfers between devices with their start and end apart: 29 -> 29, of which waited for: 12 -> 11; matrix products, arithmetic and copies ran while one was open for 3% -> 3% of each run, Pallas kernels for 32% -> 36%
where the time goes in v4:
time: 396 us; the launch traced here: 394 us
  waiting for transfers between devices  151 us (38%)
  Pallas kernels  142 us (36%)
  starting transfers between devices  87.7 us (22%)
  local copies, waits for them, and re-layouts  9.98 us (3%)
    ppermute x28, waiting for transfers between devices, send(): return lax.ppermute(value, 'pass', pairs)  151 us
    ppermute x28, starting transfers between devices, send(): return lax.ppermute(value, 'pass', pairs)  86.1 us
    pallas_call x4, Pallas kernels, part_call(): pl.pallas_call(functools.partial(part_kernel, k, most, heads), out_shape=...  66.8 us
    pallas_call x18, Pallas kernels, join_call(): pl.pallas_call(merge_kernel if leveled else finish_kernel, out_shape=jax....  39.9 us
    pallas_call x2, Pallas kernels, project_call(): pl.pallas_call(functools.partial(project_kernel, len(pieces), far), out_s...  27.9 us
    unnamed x1, local copies, waits for them, and re-layouts  8.19 us
  transfers between devices with their start and end apart: 29, of which 11 were waited for; matrix products, arithmetic and copies ran while one was open for 3% of the time, Pallas kernels for 36%

profile of v4, /device:TPU:0, one launch (start us, length us, event | category | flops | bytes accessed | tf_op | source)
XLA Modules:
  0.0 393.7 jit_solution(8907958366088301725)
XLA Ops:
  0.0 3.1 collective-permute-start.2
  4.9 32.9 %collective-permute-done.2.refs_3_ = bf16[384,2048]{1,0:T(8,128)(2,1)} collective-permute-done((bf16[384,2048]{1,0:T(8,128)(2,1)}, bf16[384,2048]{1,0:T(8,128)(2,1)}, u32[]{:S(2)}, u32[]{:S(2)}) %collective-permute-start.2) | collective-permute-done | bytes 1572896 | tf_op jit(solution)/shard_map/ppermute | solution.py:735
  39.7 8.2 %copy.16 = bf16[16,512,2,256]{3,1,2,0:T(8,128)(2,1)} copy(bf16[16,512,2,256]{3,2,1,0:T(2,128)(2,1)} %param.9) | data formatting | bytes 16777216 | tf_op args[2]
  47.9 7.8 %sort_items.1 = (s32[12]{0:T(128)}, s32[12]{0:T(128)}, s32[12]{0:T(128)}, bf16[3,2,512,256]{3,2,1,0:T(8,128)(2,1)}, bf16[3,2,512,256]{3,2,1,0:T(8,128)(2,1)}, /*...) custom-call(s32[8,24]{1,0:T(8,128)} %bitcast.15, s32[128]{0:T(128)} %pslot_ref.1, s32[24]{0:T(128)} %qslot_ref.1, ...), custom_call_target="tpu_custom_call" | custom-call | bytes 12582912 | tf_op jit(solution)/shard_map/sort_items/pallas_call | solution.py:437
  55.7 2.8 collective-permute-start.7
  61.2 32.9 %collective-permute-done.7.refs_6_ = bf16[3,2,512,256]{3,2,1,0:T(8,128)(2,1)} collective-permute-done((bf16[3,2,512,256]{3,2,1,0:T(8,128)(2,1)}, bf16[3,2,512,256]{3,2,1,0:T(8,128)(2,1)}, u32[]{:S(2)}, u32[]{:S(2)}) %collective-permute-start.7) | collective-permute-done | bytes 1572896 | tf_op jit(solution)/shard_map/ppermute | solution.py:735
  94.0 3.9 collective-permute-done.6.refs_4_
  97.9 15.5 %shard_map.75.a_ref = bf16[3,136,2048]{2,1,0:T(8,128)(2,1)} custom-call(s32[12]{0:T(128)} %get-tuple-element.12.refs_0_, s32[12]{0:T(128)} %get-tuple-element.13.refs_1_, s32[12]{0:T(128)} %get-tuple-element.14.refs_2_, bf16[384,2048]{1,0:T(8,128)(2,1)} %collective-permute-done.3.refs_3_, bf16[384,2048]{1,0:T(8,128)(2,1)} %collective-permute-done.6.refs_4_, ...), custom_call_target="tpu_custom_call" | custom-call | flops 3221225472 | bytes 3145728 | tf_op jit(solution)/shard_map/pallas_call | solution.py:624
  113.5 2.7 collective-permute-start.8
  116.1 2.7 collective-permute-start.21
  119.8 8.0 %collective-permute-done.5.refs_6_ = bf16[3,2,512,256]{3,2,1,0:T(8,128)(2,1)} collective-permute-done((bf16[3,2,512,256]{3,2,1,0:T(8,128)(2,1)}, bf16[3,2,512,256]{3,2,1,0:T(8,128)(2,1)}, u32[]{:S(2)}, u32[]{:S(2)}) %collective-permute-start.5) | collective-permute-done | bytes 1572896 | tf_op jit(solution)/shard_map/ppermute | solution.py:735
  131.1 15.6 %shard_map.74.a_ref = bf16[3,136,2048]{2,1,0:T(8,128)(2,1)} custom-call(s32[12]{0:T(128)} %get-tuple-element.12.refs_0_, s32[12]{0:T(128)} %get-tuple-element.13.refs_1_, s32[12]{0:T(128)} %get-tuple-element.14.refs_2_, bf16[384,2048]{1,0:T(8,128)(2,1)} %collective-permute-done.1.refs_3_, bf16[384,2048]{1,0:T(8,128)(2,1)} %collective-permute-done.4.refs_4_, ...), custom_call_target="tpu_custom_call" | custom-call | flops 3221225472 | bytes 3145728 | tf_op jit(solution)/shard_map/pallas_call | solution.py:624
  146.7 5.4 %collective-permute-done.8.b_ref = bf16[3,136,2048]{2,1,0:T(8,128)(2,1)} collective-permute-done((bf16[3,136,2048]{2,1,0:T(8,128)(2,1)}, bf16[3,136,2048]{2,1,0:T(8,128)(2,1)}, u32[]{:S(2)}, u32[]{:S(2)}) %collective-permute-start.8) | collective-permute-done | bytes 1671200 | tf_op jit(solution)/shard_map/ppermute | solution.py:735
  152.1 5.6 %collective-permute-start.11 = (bf16[3,136,2048]{2,1,0:T(8,128)(2,1)}, bf16[3,136,2048]{2,1,0:T(8,128)(2,1)}, u32[]{:S(2)}, u32[]{:S(2)}) collective-permute-start(bf16[3,136,2048]{2,1,0:T(8,128)(2,1)} %shard_map.74.a_ref), channel_id=1, source_target_pairs={{0,8},{4,12},{24,16},{28,20},{1,9},{5,13},{25,17},{29,21},{2,10},{... | collective-permute-start | bytes 5013512 | tf_op jit(solution)/shard_map/ppermute | solution.py:735
  163.3 30.1 %collective-permute-done.10.refs_5_ = bf16[3,2,512,256]{3,2,1,0:T(8,128)(2,1)} collective-permute-done((bf16[3,2,512,256]{3,2,1,0:T(8,128)(2,1)}, bf16[3,2,512,256]{3,2,1,0:T(8,128)(2,1)}, u32[]{:S(2)}, u32[]{:S(2)}) %collective-permute-start.10) | collective-permute-done | bytes 1572896 | tf_op jit(solution)/shard_map/ppermute | solution.py:735
  198.6 27.7 %collective-permute-done.23.refs_7_ = bf16[2048,512]{1,0:T(8,128)(2,1)} collective-permute-done((bf16[2048,512]{1,0:T(8,128)(2,1)}, bf16[2048,512]{1,0:T(8,128)(2,1)}, u32[]{:S(2)}, u32[]{:S(2)}) %collective-permute-start.23) | collective-permute-done | bytes 2097184 | tf_op jit(solution)/shard_map/ppermute | solution.py:735
  228.3 4.1 %collective-permute-start.24 = (bf16[2048,512]{1,0:T(8,128)(2,1)}, bf16[2048,512]{1,0:T(8,128)(2,1)}, u32[]{:S(2)}, u32[]{:S(2)}) collective-permute-start(bf16[2048,512]{1,0:T(8,128)(2,1)} %collective-permute-done.23.refs_7_), channel_id=1, source_target_pairs={{0,4},{4,0},{24,28},{28,24},{1,5},{5,1},{25,29},{29,25},{2,6},{6,2... | collective-permute-start | bytes 6291464 | tf_op jit(solution)/shard_map/ppermute | solution.py:735
  234.2 20.3 %shard_map.73.a_ref = bf16[3,136,2048]{2,1,0:T(8,128)(2,1)} custom-call(s32[12]{0:T(128)} %get-tuple-element.12.refs_0_, s32[12]{0:T(128)} %get-tuple-element.13.refs_1_, s32[12]{0:T(128)} %get-tuple-element.14.refs_2_, bf16[3,2,128,256]{3,2,1,0:T(8,128)(2,1)} %bitcast.13, bf16[384,2048]{1,0:T(8,128)(2,1)} %refs_4_.1, bf16[16,2,512,256]{3,2,1,0:T(8,128)(2,1)} %bitcast.11, ...), custom_call_target="tpu_custom_call" | custom-call | flops 3221225472 | bytes 3145728 | tf_op jit(solution)/shard_map/pallas_call | solution.py:624
  256.5 20.8 %collective-permute-start.25 = (bf16[1,136,2048]{2,1,0:T(8,128)(2,1)}, bf16[1,136,2048]{2,1,0:T(8,128)(2,1)}, u32[]{:S(2)}, u32[]{:S(2)}) collective-permute-start(bf16[1,136,2048]{2,1,0:T(8,128)(2,1)} %shard_map.77.a_ref), channel_id=1, source_target_pairs={{0,8},{4,12},{8,0},{12,4},{16,24},{20,28},{24,16},{28,20},{1,9},{5... | collective-permute-start | bytes 1671176 | tf_op jit(solution)/shard_map/ppermute | solution.py:735
  292.3 15.7 %collective-permute-start.26 = (bf16[1,136,2048]{2,1,0:T(8,128)(2,1)}, bf16[1,136,2048]{2,1,0:T(8,128)(2,1)}, u32[]{:S(2)}, u32[]{:S(2)}) collective-permute-start(bf16[1,136,2048]{2,1,0:T(8,128)(2,1)} %shard_map.83.a_ref), channel_id=1, source_target_pairs={{0,8},{4,12},{8,0},{12,4},{16,24},{20,28},{24,16},{28,20},{1,9},{5... | collective-permute-start | bytes 1671176 | tf_op jit(solution)/shard_map/ppermute | solution.py:735
  310.1 3.9 collective-permute-start.27
  314.0 15.4 %shard_map.78.a_ref = bf16[3,136,2048]{2,1,0:T(8,128)(2,1)} custom-call(s32[12]{0:T(128)} %get-tuple-element.12.refs_0_, s32[12]{0:T(128)} %get-tuple-element.13.refs_1_, s32[12]{0:T(128)} %get-tuple-element.14.refs_2_, bf16[384,2048]{1,0:T(8,128)(2,1)} %collective-permute-done.2.refs_3_, bf16[16,2,512,256]{3,2,1,0:T(8,128)(2,1)} %bitcast.12, ...), custom_call_target="tpu_custom_call" | custom-call | flops 3221225472 | bytes 3145728 | tf_op jit(solution)/shard_map/pallas_call | solution.py:624
  335.9 2.4 shard_map.92.refs_0_
  339.6 2.5 shard_map.93.refs_1_
  342.9 2.5 shard_map.94.refs_2_
  346.6 8.4 %project_far.1 = bf16[384,1024]{1,0:T(8,128)(2,1)} custom-call(bf16[128,2048]{1,0:T(8,128)(2,1)} %shard_map.92.refs_0_, bf16[128,2048]{1,0:T(8,128)(2,1)} %shard_map.93.refs_1_, bf16[128,2048]{1,0:T(8,128)(2,1)} %shard_map.94.refs_2_, bf16[2048,512]{1,0:T(8,128)(2,1)} %refs_3_.3, bf16[2048,512]{1,0:T(8,128)(2,1)} %collective-permute-done.20.refs_4_, ...), custom_call_target="tpu_custom_call" | custom-call | flops 3221225472 | bytes 8388608 | tf_op jit(solution)/shard_map/project_far/pallas_call | solution.py:920
  356.7 2.5 shard_map.81.refs_0_
  359.1 4.5 %collective-permute-done.16.b_ref = bf16[1,136,2048]{2,1,0:T(8,128)(2,1)} collective-permute-done((bf16[1,136,2048]{2,1,0:T(8,128)(2,1)}, bf16[1,136,2048]{2,1,0:T(8,128)(2,1)}, u32[]{:S(2)}, u32[]{:S(2)}) %collective-permute-start.16) | collective-permute-done | bytes 557088 | tf_op jit(solution)/shard_map/ppermute | solution.py:735
  363.6 2.5 shard_map.86.refs_1_
  366.1 3.5 collective-permute-done.19.b_ref
  369.6 2.5 shard_map.91.refs_2_
  372.0 19.5 %project_home.1 = bf16[384,1024]{1,0:T(8,128)(2,1)} custom-call(bf16[128,2048]{1,0:T(8,128)(2,1)} %shard_map.81.refs_0_, bf16[128,2048]{1,0:T(8,128)(2,1)} %shard_map.86.refs_1_, bf16[128,2048]{1,0:T(8,128)(2,1)} %shard_map.91.refs_2_, bf16[2048,512]{1,0:T(8,128)(2,1)} %refs_3_.3, bf16[2048,512]{1,0:T(8,128)(2,1)} %collective-permute-done.20.refs_4_, ...), custom_call_target="tpu_custom_call" | custom-call | flops 3221225472 | bytes 8388608 | tf_op jit(solution)/shard_map/project_home/pallas_call | solution.py:920
  (54 shorter events, 57.9 us)
Async XLA Ops:
  0.0 37.8 %collective-permute-start.2 = (bf16[384,2048]{1,0:T(8,128)(2,1)}, bf16[384,2048]{1,0:T(8,128)(2,1)}, u32[]{:S(2)}, u32[]{:S(2)}) collective-permute-start(bf16[384,2048]{1,0:T(8,128)(2,1)} %refs_4_.1), channel_id=1, source_target_pairs={{0,8},{4,12},{8,0},{12,4},{16,24},{20,28},{24,16},{28,20},{1,9},{5... | collective-permute-start | bytes 4718600 | tf_op jit(solution)/shard_map/ppermute | solution.py:735
  3.1 55.4 %collective-permute-start.1 = (bf16[384,2048]{1,0:T(8,128)(2,1)}, bf16[384,2048]{1,0:T(8,128)(2,1)}, u32[]{:S(2)}, u32[]{:S(2)}) collective-permute-start(bf16[384,2048]{1,0:T(8,128)(2,1)} %refs_4_.1), channel_id=1, source_target_pairs={{8,16},{12,20},{16,8},{20,12},{9,17},{13,21},{17,9},{21,13},{10,18... | collective-permute-start | bytes 4718600 | tf_op jit(solution)/shard_map/ppermute | solution.py:735
  37.8 22.1 %collective-permute-start.3 = (bf16[384,2048]{1,0:T(8,128)(2,1)}, bf16[384,2048]{1,0:T(8,128)(2,1)}, u32[]{:S(2)}, u32[]{:S(2)}) collective-permute-start(bf16[384,2048]{1,0:T(8,128)(2,1)} %collective-permute-done.2.refs_3_), channel_id=1, source_target_pairs={{8,16},{12,20},{16,8},{20,12},{9,17},{13,21},{17,9},{21,13},{10,18... | collective-permute-start | bytes 4718600 | tf_op jit(solution)/shard_map/ppermute | solution.py:735
  55.7 38.4 %collective-permute-start.7 = (bf16[3,2,512,256]{3,2,1,0:T(8,128)(2,1)}, bf16[3,2,512,256]{3,2,1,0:T(8,128)(2,1)}, u32[]{:S(2)}, u32[]{:S(2)}) collective-permute-start(bf16[3,2,512,256]{3,2,1,0:T(8,128)(2,1)} %get-tuple-element.17), channel_id=1, source_target_pairs={{0,4},{4,0},{8,12},{12,8},{16,20},{20,16},{24,28},{28,24},{1,5},{5... | collective-permute-start | bytes 4718600 | tf_op jit(solution)/shard_map/ppermute | solution.py:735
  58.5 39.5 %collective-permute-start.6 = (bf16[384,2048]{1,0:T(8,128)(2,1)}, bf16[384,2048]{1,0:T(8,128)(2,1)}, u32[]{:S(2)}, u32[]{:S(2)}) collective-permute-start(bf16[384,2048]{1,0:T(8,128)(2,1)} %collective-permute-done.1.refs_3_), channel_id=1, source_target_pairs={{8,0},{12,4},{16,24},{20,28},{9,1},{13,5},{17,25},{21,29},{10,2},{... | collective-permute-start | bytes 4718600 | tf_op jit(solution)/shard_map/ppermute | solution.py:735
  59.8 68.0 %collective-permute-start.5 = (bf16[3,2,512,256]{3,2,1,0:T(8,128)(2,1)}, bf16[3,2,512,256]{3,2,1,0:T(8,128)(2,1)}, u32[]{:S(2)}, u32[]{:S(2)}) collective-permute-start(bf16[3,2,512,256]{3,2,1,0:T(8,128)(2,1)} %get-tuple-element.16), channel_id=1, source_target_pairs={{0,4},{4,0},{8,12},{12,8},{16,20},{20,16},{24,28},{28,24},{1,5},{5... | collective-permute-start | bytes 4718600 | tf_op jit(solution)/shard_map/ppermute | solution.py:735
  59.9 69.9 %collective-permute-start.4 = (bf16[384,2048]{1,0:T(8,128)(2,1)}, bf16[384,2048]{1,0:T(8,128)(2,1)}, u32[]{:S(2)}, u32[]{:S(2)}) collective-permute-start(bf16[384,2048]{1,0:T(8,128)(2,1)} %collective-permute-done.3.refs_3_), channel_id=1, source_target_pairs={{8,0},{12,4},{16,24},{20,28},{9,1},{13,5},{17,25},{21,29},{10,2},{... | collective-permute-start | bytes 4718600 | tf_op jit(solution)/shard_map/ppermute | solution.py:735
  113.5 38.6 %collective-permute-start.8 = (bf16[3,136,2048]{2,1,0:T(8,128)(2,1)}, bf16[3,136,2048]{2,1,0:T(8,128)(2,1)}, u32[]{:S(2)}, u32[]{:S(2)}) collective-permute-start(bf16[3,136,2048]{2,1,0:T(8,128)(2,1)} %shard_map.75.a_ref), channel_id=1, source_target_pairs={{0,8},{4,12},{24,16},{28,20},{1,9},{5,13},{25,17},{29,21},{2,10},{... | collective-permute-start | bytes 5013512 | tf_op jit(solution)/shard_map/ppermute | solution.py:735
  116.1 81.0 %collective-permute-start.21 = (bf16[2048,512]{1,0:T(8,128)(2,1)}, bf16[2048,512]{1,0:T(8,128)(2,1)}, u32[]{:S(2)}, u32[]{:S(2)}) collective-permute-start(bf16[2048,512]{1,0:T(8,128)(2,1)} %refs_3_.3), channel_id=1, source_target_pairs={{0,16},{4,20},{24,8},{28,12},{1,17},{5,21},{25,9},{29,13},{2,18},{... | collective-permute-start | bytes 6291464 | tf_op jit(solution)/shard_map/ppermute | solution.py:735
  118.8 43.1 %collective-permute-start = (bf16[3,2,512,256]{3,2,1,0:T(8,128)(2,1)}, bf16[3,2,512,256]{3,2,1,0:T(8,128)(2,1)}, u32[]{:S(2)}, u32[]{:S(2)}) collective-permute-start(bf16[3,2,512,256]{3,2,1,0:T(8,128)(2,1)} %get-tuple-element.15), channel_id=1, source_target_pairs={{0,4},{4,0},{8,12},{12,8},{16,20},{20,16},{24,28},{28,24},{1,5},{5... | collective-permute-start | bytes 4718600 | tf_op jit(solution)/shard_map/ppermute | solution.py:735
  127.7 65.7 %collective-permute-start.10 = (bf16[3,2,512,256]{3,2,1,0:T(8,128)(2,1)}, bf16[3,2,512,256]{3,2,1,0:T(8,128)(2,1)}, u32[]{:S(2)}, u32[]{:S(2)}) collective-permute-start(bf16[3,2,512,256]{3,2,1,0:T(8,128)(2,1)} %get-tuple-element.18), channel_id=1, source_target_pairs={{0,4},{4,0},{8,12},{12,8},{16,20},{20,16},{24,28},{28,24},{1,5},{5... | collective-permute-start | bytes 4718600 | tf_op jit(solution)/shard_map/ppermute | solution.py:735
  129.8 96.5 %collective-permute-start.23 = (bf16[2048,512]{1,0:T(8,128)(2,1)}, bf16[2048,512]{1,0:T(8,128)(2,1)}, u32[]{:S(2)}, u32[]{:S(2)}) collective-permute-start(bf16[2048,512]{1,0:T(8,128)(2,1)} %refs_3_.3), channel_id=1, source_target_pairs={{8,24},{12,28},{16,0},{20,4},{9,25},{13,29},{17,1},{21,5},{10,26},... | collective-permute-start | bytes 6291464 | tf_op jit(solution)/shard_map/ppermute | solution.py:735
  152.1 104.4 %collective-permute-start.11 = (bf16[3,136,2048]{2,1,0:T(8,128)(2,1)}, bf16[3,136,2048]{2,1,0:T(8,128)(2,1)}, u32[]{:S(2)}, u32[]{:S(2)}) collective-permute-start(bf16[3,136,2048]{2,1,0:T(8,128)(2,1)} %shard_map.74.a_ref), channel_id=1, source_target_pairs={{0,8},{4,12},{24,16},{28,20},{1,9},{5,13},{25,17},{29,21},{2,10},{... | collective-permute-start | bytes 5013512 | tf_op jit(solution)/shard_map/ppermute | solution.py:735
  161.9 64.5 %collective-permute-start.9 = (bf16[1,136,2048]{2,1,0:T(8,128)(2,1)}, bf16[1,136,2048]{2,1,0:T(8,128)(2,1)}, u32[]{:S(2)}, u32[]{:S(2)}) collective-permute-start(bf16[1,136,2048]{2,1,0:T(8,128)(2,1)} %shard_map.76), channel_id=1, source_target_pairs={{8,16},{12,20},{16,8},{20,12},{9,17},{13,21},{17,9},{21,13},{10,18... | collective-permute-start | bytes 1671176 | tf_op jit(solution)/shard_map/ppermute | solution.py:735
  193.4 34.9 %collective-permute-start.14 = (bf16[1,136,2048]{2,1,0:T(8,128)(2,1)}, bf16[1,136,2048]{2,1,0:T(8,128)(2,1)}, u32[]{:S(2)}, u32[]{:S(2)}) collective-permute-start(bf16[1,136,2048]{2,1,0:T(8,128)(2,1)} %shard_map.82), channel_id=1, source_target_pairs={{8,16},{12,20},{16,8},{20,12},{9,17},{13,21},{17,9},{21,13},{10,18... | collective-permute-start | bytes 1671176 | tf_op jit(solution)/shard_map/ppermute | solution.py:735
  197.1 82.3 %collective-permute-start.17 = (bf16[1,136,2048]{2,1,0:T(8,128)(2,1)}, bf16[1,136,2048]{2,1,0:T(8,128)(2,1)}, u32[]{:S(2)}, u32[]{:S(2)}) collective-permute-start(bf16[1,136,2048]{2,1,0:T(8,128)(2,1)} %shard_map.87), channel_id=1, source_target_pairs={{8,16},{12,20},{16,8},{20,12},{9,17},{13,21},{17,9},{21,13},{10,18... | collective-permute-start | bytes 1671176 | tf_op jit(solution)/shard_map/ppermute | solution.py:735
  226.3 119.1 %collective-permute-start.20 = (bf16[2048,512]{1,0:T(8,128)(2,1)}, bf16[2048,512]{1,0:T(8,128)(2,1)}, u32[]{:S(2)}, u32[]{:S(2)}) collective-permute-start(bf16[2048,512]{1,0:T(8,128)(2,1)} %refs_3_.3), channel_id=1, source_target_pairs={{0,4},{4,0},{8,12},{12,8},{16,20},{20,16},{24,28},{28,24},{1,5},{5... | collective-permute-start | bytes 6291464 | tf_op jit(solution)/shard_map/ppermute | solution.py:735
  226.3 120.3 %collective-permute-start.22 = (bf16[2048,512]{1,0:T(8,128)(2,1)}, bf16[2048,512]{1,0:T(8,128)(2,1)}, u32[]{:S(2)}, u32[]{:S(2)}) collective-permute-start(bf16[2048,512]{1,0:T(8,128)(2,1)} %collective-permute-done.21.refs_5_), channel_id=1, source_target_pairs={{8,12},{12,8},{16,20},{20,16},{9,13},{13,9},{17,21},{21,17},{10,14... | collective-permute-start | bytes 6291464 | tf_op jit(solution)/shard_map/ppermute | solution.py:735
  228.3 118.3 %collective-permute-start.24 = (bf16[2048,512]{1,0:T(8,128)(2,1)}, bf16[2048,512]{1,0:T(8,128)(2,1)}, u32[]{:S(2)}, u32[]{:S(2)}) collective-permute-start(bf16[2048,512]{1,0:T(8,128)(2,1)} %collective-permute-done.23.refs_7_), channel_id=1, source_target_pairs={{0,4},{4,0},{24,28},{28,24},{1,5},{5,1},{25,29},{29,25},{2,6},{6,2... | collective-permute-start | bytes 6291464 | tf_op jit(solution)/shard_map/ppermute | solution.py:735
  256.5 28.6 %collective-permute-start.25 = (bf16[1,136,2048]{2,1,0:T(8,128)(2,1)}, bf16[1,136,2048]{2,1,0:T(8,128)(2,1)}, u32[]{:S(2)}, u32[]{:S(2)}) collective-permute-start(bf16[1,136,2048]{2,1,0:T(8,128)(2,1)} %shard_map.77.a_ref), channel_id=1, source_target_pairs={{0,8},{4,12},{8,0},{12,4},{16,24},{20,28},{24,16},{28,20},{1,9},{5... | collective-permute-start | bytes 1671176 | tf_op jit(solution)/shard_map/ppermute | solution.py:735
  279.4 9.4 %collective-permute-start.12 = (bf16[1,136,2048]{2,1,0:T(8,128)(2,1)}, bf16[1,136,2048]{2,1,0:T(8,128)(2,1)}, u32[]{:S(2)}, u32[]{:S(2)}) collective-permute-start(bf16[1,136,2048]{2,1,0:T(8,128)(2,1)} %shard_map.79), channel_id=1, source_target_pairs={{8,16},{12,20},{16,8},{20,12},{9,17},{13,21},{17,9},{21,13},{10,18... | collective-permute-start | bytes 1671176 | tf_op jit(solution)/shard_map/ppermute | solution.py:735
  285.1 7.2 %collective-permute-start.15 = (bf16[1,136,2048]{2,1,0:T(8,128)(2,1)}, bf16[1,136,2048]{2,1,0:T(8,128)(2,1)}, u32[]{:S(2)}, u32[]{:S(2)}) collective-permute-start(bf16[1,136,2048]{2,1,0:T(8,128)(2,1)} %shard_map.84), channel_id=1, source_target_pairs={{8,16},{12,20},{16,8},{20,12},{9,17},{13,21},{17,9},{21,13},{10,18... | collective-permute-start | bytes 1671176 | tf_op jit(solution)/shard_map/ppermute | solution.py:735
  288.8 21.4 %collective-permute-start.18 = (bf16[1,136,2048]{2,1,0:T(8,128)(2,1)}, bf16[1,136,2048]{2,1,0:T(8,128)(2,1)}, u32[]{:S(2)}, u32[]{:S(2)}) collective-permute-start(bf16[1,136,2048]{2,1,0:T(8,128)(2,1)} %shard_map.89), channel_id=1, source_target_pairs={{8,16},{12,20},{16,8},{20,12},{9,17},{13,21},{17,9},{21,13},{10,18... | collective-permute-start | bytes 1671176 | tf_op jit(solution)/shard_map/ppermute | solution.py:735
  292.3 46.0 %collective-permute-start.26 = (bf16[1,136,2048]{2,1,0:T(8,128)(2,1)}, bf16[1,136,2048]{2,1,0:T(8,128)(2,1)}, u32[]{:S(2)}, u32[]{:S(2)}) collective-permute-start(bf16[1,136,2048]{2,1,0:T(8,128)(2,1)} %shard_map.83.a_ref), channel_id=1, source_target_pairs={{0,8},{4,12},{8,0},{12,4},{16,24},{20,28},{24,16},{28,20},{1,9},{5... | collective-permute-start | bytes 1671176 | tf_op jit(solution)/shard_map/ppermute | solution.py:735
  310.1 32.0 %collective-permute-start.27 = (bf16[1,136,2048]{2,1,0:T(8,128)(2,1)}, bf16[1,136,2048]{2,1,0:T(8,128)(2,1)}, u32[]{:S(2)}, u32[]{:S(2)}) collective-permute-start(bf16[1,136,2048]{2,1,0:T(8,128)(2,1)} %shard_map.88.a_ref), channel_id=1, source_target_pairs={{0,8},{4,12},{8,0},{12,4},{16,24},{20,28},{24,16},{28,20},{1,9},{5... | collective-permute-start | bytes 1671176 | tf_op jit(solution)/shard_map/ppermute | solution.py:735
  338.4 18.3 %collective-permute-start.13 = (bf16[1,136,2048]{2,1,0:T(8,128)(2,1)}, bf16[1,136,2048]{2,1,0:T(8,128)(2,1)}, u32[]{:S(2)}, u32[]{:S(2)}) collective-permute-start(bf16[1,136,2048]{2,1,0:T(8,128)(2,1)} %shard_map.80.a_ref), channel_id=1, source_target_pairs={{0,8},{4,12},{8,0},{12,4},{16,24},{20,28},{24,16},{28,20},{1,9},{5... | collective-permute-start | bytes 1671176 | tf_op jit(solution)/shard_map/ppermute | solution.py:735
  342.1 21.5 %collective-permute-start.16 = (bf16[1,136,2048]{2,1,0:T(8,128)(2,1)}, bf16[1,136,2048]{2,1,0:T(8,128)(2,1)}, u32[]{:S(2)}, u32[]{:S(2)}) collective-permute-start(bf16[1,136,2048]{2,1,0:T(8,128)(2,1)} %shard_map.85.a_ref), channel_id=1, source_target_pairs={{0,8},{4,12},{8,0},{12,4},{16,24},{20,28},{24,16},{28,20},{1,9},{5... | collective-permute-start | bytes 1671176 | tf_op jit(solution)/shard_map/ppermute | solution.py:735
  345.4 24.2 %collective-permute-start.19 = (bf16[1,136,2048]{2,1,0:T(8,128)(2,1)}, bf16[1,136,2048]{2,1,0:T(8,128)(2,1)}, u32[]{:S(2)}, u32[]{:S(2)}) collective-permute-start(bf16[1,136,2048]{2,1,0:T(8,128)(2,1)} %shard_map.90.a_ref), channel_id=1, source_target_pairs={{0,8},{4,12},{8,0},{12,4},{16,24},{20,28},{24,16},{28,20},{1,9},{5... | collective-permute-start | bytes 1671176 | tf_op jit(solution)/shard_map/ppermute | solution.py:735
  355.0 36.5 %collective-permute-start.28 = (bf16[384,1024]{1,0:T(8,128)(2,1)}, bf16[384,1024]{1,0:T(8,128)(2,1)}, u32[]{:S(2)}, u32[]{:S(2)}) collective-permute-start(bf16[384,1024]{1,0:T(8,128)(2,1)} %project_far.1), channel_id=1, source_target_pairs={{1,8},{3,10},{5,12},{7,14},{8,1},{10,3},{12,5},{14,7},{17,24},{19,... | collective-permute-start | bytes 2359304 | tf_op jit(solution)/shard_map/ppermute | solution.py:794

commit v5 on v4

--- a/solution.py
+++ b/solution.py
@@ -779,10 +779,9 @@
         near_rows.append(join(near1, beside, q, False))
         own_rows.append(join(near0, back1, q, False))
     weights = (out_weight, w_across, w_in, w_in_both, w_out, w_out_both)
-    sums = project_call(near_rows, weights, True)
-    far_out = send_far(sums)
-    home_out = project_call(own_rows, weights, False)
-    return jnp.where(at_home(), home_out, far_out)
+    far_send, far_keep = project_call(near_rows, weights, None)
+    far_sent = send_far(far_send)
+    return project_call(own_rows, weights, (far_keep, far_sent))
 
 
 def send_far(sums):
@@ -790,7 +789,7 @@
     for p in range(2 * LINE):
         for h in range(LINE):
             if h % 2 != (p // 2) % 2:
-                pairs.append((p * LINE + h, (p ^ 2) * LINE + (h ^ 1)))
+                pairs.append((p * LINE + h, p * LINE + (h ^ 2)))
     return lax.ppermute(sums, ("pass", "head"), pairs)
 
 
@@ -805,15 +804,19 @@
     rows_refs = refs[:pieces]
     own_ref, across_ref, in_ref, in2_ref, out1_ref, out2_ref = refs[pieces : pieces + 6]
     refs = refs[pieces + 6 :]
-    out_ref, context_ref, w_ref, part_ref, core_ref, y_ref, ysend_ref = refs[:7]
-    row_sem, w_sem, send_sem, recv_sem = refs[7:]
+    if far:
+        send_ref, keep_ref = refs[:2]
+    else:
+        far_keep_ref, far_sent_ref, out_ref = refs[:3]
+        refs = refs[1:]
+    context_ref, w_ref, part_ref, core_ref, row_sem, w_sem, send_sem, recv_sem = refs[2:10]
     me, head = lax.axis_index("pass"), lax.axis_index("head")
     z, x, y = me // 2, me % 2, head // 2
     wide = w_ref.shape[3]
     inner = is_inner()
-    core_peer = (me, head ^ 1)
-    y_peer = (me, head ^ 2)
-    sums = jnp.logical_not(at_home()) if far else at_home()
+    core_peer, y_peer, z_peer = (me, head ^ 1), (me, head ^ 2), (me ^ 2, head ^ 1)
+    home = at_home()
+    sums = jnp.logical_not(home) if far else home
 
     row_loads = [
         pltpu.make_async_copy(ref, context_ref.at[pl.ds(i * LQ, LQ)], row_sem.at[i])
@@ -850,9 +853,10 @@
         load_here()
 
     barrier = pltpu.get_barrier_semaphore()
-    for peer in (core_peer, y_peer):
+    peers = (core_peer,) if far else (core_peer, y_peer, z_peer)
+    for peer in peers:
         pl.semaphore_signal(barrier, inc=1, device_id=peer, device_id_type=MESH)
-    pl.semaphore_wait(barrier, 2)
+    pl.semaphore_wait(barrier, len(peers))
 
     def remote(src, dst, i, peer):
         return pltpu.make_async_remote_copy(
@@ -871,40 +875,61 @@
         [remote(part_ref.at[s, j], core_ref.at[s, j], s * 2 + j, core_peer) for j in range(2)]
         for s in range(2)
     ]
-    y_copies = [remote(ysend_ref.at[j], y_ref.at[j], 4 + j, y_peer) for j in range(2)]
+    if not far:
+        y_ref, ysend_ref, zsend_ref = refs[10:]
+        y_copies = [remote(ysend_ref.at[j], y_ref.at[j], 4 + j, y_peer) for j in range(2)]
+        z_copies = [
+            remote(zsend_ref.at[j], out_ref.at[:, columns(j)], 6 + j, z_peer) for j in range(2)
+        ]
+
+        @pl.when(jnp.logical_not(home))
+        def _():
+            for j in range(2):
+                zsend_ref[j] = (
+                    far_keep_ref[j].astype(jnp.float32) + far_sent_ref[j].astype(jnp.float32)
+                ).astype(zsend_ref.dtype)
+                z_copies[j].start()
 
     for load in row_loads:
         load.wait()
 
+    def multiply(s, to_y, j):
+        here = jnp.where(to_y == z // 2, 0, 1)
+        block = w_ref.at[here, j]
+        pltpu.make_async_copy(block, block, w_sem.at[here, j]).wait()
+        part_ref[s, j] = jnp.dot(
+            context_ref[...], w_ref[here, j], preferred_element_type=jnp.float32
+        ).astype(part_ref.dtype)
+
+        @pl.when(jnp.logical_not(sums))
+        def _():
+            core_copies[s][j].start()
+
+    def add_up(s, j):
+        @pl.when(sums)
+        def _():
+            core_copies[s][j].wait_recv()
+            value = part_ref[s, j].astype(jnp.float32) + core_ref[s, j].astype(jnp.float32)
+            if far:
+                target = keep_ref if s else send_ref
+                target[j] = value.astype(target.dtype)
+            elif s == 0:
+                ysend_ref[j] = value.astype(ysend_ref.dtype)
+                y_copies[j].start()
+            else:
+                y_copies[j].wait_recv()
+                out_ref[:, columns(j)] = (value + y_ref[j].astype(jnp.float32)).astype(
+                    out_ref.dtype
+                )
+
+    late = None
     for s, to_y in enumerate((1 - y, y)):
-        here = jnp.where(to_y == z // 2, 0, 1)
         for j in range(2):
-            block = w_ref.at[here, j]
-            pltpu.make_async_copy(block, block, w_sem.at[here, j]).wait()
-            part_ref[s, j] = jnp.dot(
-                context_ref[...], w_ref[here, j], preferred_element_type=jnp.float32
-            ).astype(part_ref.dtype)
-
-            @pl.when(jnp.logical_not(sums))
-            def _():
-                core_copies[s][j].start()
-
-            @pl.when(sums)
-            def _():
-                core_copies[s][j].wait_recv()
-                value = part_ref[s, j].astype(jnp.float32) + core_ref[s, j].astype(jnp.float32)
-                if s == 0:
-                    ysend_ref[j] = value.astype(ysend_ref.dtype)
-                    y_copies[j].start()
-                else:
-                    y_copies[j].wait_recv()
-                    total = (value + y_ref[j].astype(jnp.float32)).astype(out_ref.dtype)
-                    out_ref[:, columns(j)] = total
-
-    @pl.when(sums)
-    def _():
-        for copy in y_copies:
-            copy.wait_send()
+            multiply(s, to_y, j)
+            if late is not None:
+                add_up(*late)
+            late = (s, j)
+    add_up(*late)
 
     @pl.when(jnp.logical_not(sums))
     def _():
@@ -912,28 +937,50 @@
             for copy in copies:
                 copy.wait_send()
 
-
-def project_call(pieces, weights, far):
+    if not far:
+
+        @pl.when(home)
+        def _():
+            for copy in y_copies:
+                copy.wait_send()
+
+        @pl.when(jnp.logical_not(home))
+        def _():
+            for copy in z_copies:
+                copy.wait()
+
+
+def project_call(pieces, weights, far_sums):
     own = weights[0]
     rows, (depth, wide) = len(pieces) * LQ, own.shape
     dtype = own.dtype
+    far = far_sums is None
+    vmem = pl.BlockSpec(memory_space=pltpu.VMEM)
+    blocks = (2, rows, wide)
+    scratch = [
+        pltpu.VMEM((rows, depth), dtype),
+        pltpu.VMEM((2, 2, depth, wide), dtype),
+        pltpu.VMEM((2,) + blocks, dtype),
+        pltpu.VMEM((2,) + blocks, dtype),
+        pltpu.SemaphoreType.DMA((len(pieces),)),
+        pltpu.SemaphoreType.DMA((2, 2)),
+        pltpu.SemaphoreType.DMA((8,)),
+        pltpu.SemaphoreType.DMA((8,)),
+    ]
+    if far:
+        out_shape = [jax.ShapeDtypeStruct(blocks, dtype)] * 2
+        out_specs = [vmem] * 2
+    else:
+        out_shape = jax.ShapeDtypeStruct((rows, 2 * wide), dtype)
+        out_specs = vmem
+        scratch += [pltpu.VMEM(blocks, dtype)] * 3
     return pl.pallas_call(
         functools.partial(project_kernel, len(pieces), far),
-        out_shape=jax.ShapeDtypeStruct((rows, 2 * wide), dtype),
-        in_specs=[pl.BlockSpec(memory_space=pl.ANY)] * (len(pieces) + len(weights)),
-        out_specs=pl.BlockSpec(memory_space=pltpu.VMEM),
-        scratch_shapes=[
-            pltpu.VMEM((rows, depth), dtype),
-            pltpu.VMEM((2, 2, depth, wide), dtype),
-            pltpu.VMEM((2, 2, rows, wide), dtype),
-            pltpu.VMEM((2, 2, rows, wide), dtype),
-            pltpu.VMEM((2, rows, wide), dtype),
-            pltpu.VMEM((2, rows, wide), dtype),
-            pltpu.SemaphoreType.DMA((len(pieces),)),
-            pltpu.SemaphoreType.DMA((2, 2)),
-            pltpu.SemaphoreType.DMA((6,)),
-            pltpu.SemaphoreType.DMA((6,)),
-        ],
+        out_shape=out_shape,
+        in_specs=[pl.BlockSpec(memory_space=pl.ANY)] * (len(pieces) + len(weights))
+        + [vmem] * (0 if far else 2),
+        out_specs=out_specs,
+        scratch_shapes=scratch,
         compiler_params=pltpu.CompilerParams(
             collective_id=int(far), has_side_effects=True, vmem_limit_bytes=VMEM_BYTES
         ),
@@ -943,7 +990,7 @@
             bytes_accessed=4 * depth * wide * 2,
             transcendentals=0,
         ),
-    )(*pieces, *weights)
+    )(*pieces, *weights, *(far_sums or ()))
 
 
 def suits_line(mesh, queries, lists):

time: 396 us -> 421 us (1.063)
  waiting for transfers between devices: 151 us -> 173 us
    ppermute x28, waiting for transfers between devices: 151 us -> 173 us  [send(): return lax.ppermute(value, 'pass', pairs)]
    unnamed x1 -> x2, local copies, waits for them, and re-layouts: 8.19 us -> 10.3 us
  transfers between devices with their start and end apart: 29 -> 29, of which waited for: 11 -> 12; matrix products, arithmetic and copies ran while one was open for 3% -> 2% of each run, Pallas kernels for 36% -> 27%
where the time goes in v5:
time: 421 us; the launch traced here: 420 us
  waiting for transfers between devices  173 us (41%)
  Pallas kernels  146 us (35%)
  starting transfers between devices  89.3 us (21%)
  local copies, waits for them, and re-layouts  12 us (3%)
    ppermute x28, waiting for transfers between devices, send(): return lax.ppermute(value, 'pass', pairs)  173 us
    ppermute x28, starting transfers between devices, send(): return lax.ppermute(value, 'pass', pairs)  87.7 us
    pallas_call x4, Pallas kernels, part_call(): pl.pallas_call(functools.partial(part_kernel, k, most, heads), out_shape=...  66.8 us
    pallas_call x18, Pallas kernels, join_call(): pl.pallas_call(merge_kernel if leveled else finish_kernel, out_shape=jax....  40 us
    pallas_call x2, Pallas kernels, project_call(): pl.pallas_call(functools.partial(project_kernel, len(pieces), far), out_s...  31.1 us
    unnamed x2, local copies, waits for them, and re-layouts  10.3 us
  transfers between devices with their start and end apart: 29, of which 12 were waited for; matrix products, arithmetic and copies ran while one was open for 2% of the time, Pallas kernels for 27%

profile of v5, /device:TPU:0, one launch (start us, length us, event | category | flops | bytes accessed | tf_op | source)
XLA Modules:
  0.0 420.0 jit_solution(10123206528731802964)
XLA Ops:
  0.0 3.1 collective-permute-start.2
  4.9 32.9 %collective-permute-done.2.refs_3_ = bf16[384,2048]{1,0:T(8,128)(2,1)} collective-permute-done((bf16[384,2048]{1,0:T(8,128)(2,1)}, bf16[384,2048]{1,0:T(8,128)(2,1)}, u32[]{:S(2)}, u32[]{:S(2)}) %collective-permute-start.2) | collective-permute-done | bytes 1572896 | tf_op jit(solution)/shard_map/ppermute | solution.py:735
  39.7 8.2 %copy.16 = bf16[16,512,2,256]{3,1,2,0:T(8,128)(2,1)} copy(bf16[16,512,2,256]{3,2,1,0:T(2,128)(2,1)} %param.9) | data formatting | bytes 16777216 | tf_op args[2]
  47.8 7.8 %sort_items.1 = (s32[12]{0:T(128)}, s32[12]{0:T(128)}, s32[12]{0:T(128)}, bf16[3,2,512,256]{3,2,1,0:T(8,128)(2,1)}, bf16[3,2,512,256]{3,2,1,0:T(8,128)(2,1)}, /*...) custom-call(s32[8,24]{1,0:T(8,128)} %bitcast.15, s32[128]{0:T(128)} %pslot_ref.1, s32[24]{0:T(128)} %qslot_ref.1, ...), custom_call_target="tpu_custom_call" | custom-call | bytes 12582912 | tf_op jit(solution)/shard_map/sort_items/pallas_call | solution.py:437
  55.7 2.8 collective-permute-start.7
  61.2 32.9 %collective-permute-done.7.refs_6_ = bf16[3,2,512,256]{3,2,1,0:T(8,128)(2,1)} collective-permute-done((bf16[3,2,512,256]{3,2,1,0:T(8,128)(2,1)}, bf16[3,2,512,256]{3,2,1,0:T(8,128)(2,1)}, u32[]{:S(2)}, u32[]{:S(2)}) %collective-permute-start.7) | collective-permute-done | bytes 1572896 | tf_op jit(solution)/shard_map/ppermute | solution.py:735
  94.0 3.9 collective-permute-done.6.refs_4_
  97.9 15.5 %shard_map.75.a_ref = bf16[3,136,2048]{2,1,0:T(8,128)(2,1)} custom-call(s32[12]{0:T(128)} %get-tuple-element.14.refs_0_, s32[12]{0:T(128)} %get-tuple-element.15.refs_1_, s32[12]{0:T(128)} %get-tuple-element.16.refs_2_, bf16[384,2048]{1,0:T(8,128)(2,1)} %collective-permute-done.3.refs_3_, bf16[384,2048]{1,0:T(8,128)(2,1)} %collective-permute-done.6.refs_4_, ...), custom_call_target="tpu_custom_call" | custom-call | flops 3221225472 | bytes 3145728 | tf_op jit(solution)/shard_map/pallas_call | solution.py:624
  113.5 2.6 collective-permute-start.8
  116.1 2.7 collective-permute-start.21
  119.8 8.0 %collective-permute-done.5.refs_6_ = bf16[3,2,512,256]{3,2,1,0:T(8,128)(2,1)} collective-permute-done((bf16[3,2,512,256]{3,2,1,0:T(8,128)(2,1)}, bf16[3,2,512,256]{3,2,1,0:T(8,128)(2,1)}, u32[]{:S(2)}, u32[]{:S(2)}) %collective-permute-start.5) | collective-permute-done | bytes 1572896 | tf_op jit(solution)/shard_map/ppermute | solution.py:735
  131.1 15.6 %shard_map.74.a_ref = bf16[3,136,2048]{2,1,0:T(8,128)(2,1)} custom-call(s32[12]{0:T(128)} %get-tuple-element.14.refs_0_, s32[12]{0:T(128)} %get-tuple-element.15.refs_1_, s32[12]{0:T(128)} %get-tuple-element.16.refs_2_, bf16[384,2048]{1,0:T(8,128)(2,1)} %collective-permute-done.1.refs_3_, bf16[384,2048]{1,0:T(8,128)(2,1)} %collective-permute-done.4.refs_4_, ...), custom_call_target="tpu_custom_call" | custom-call | flops 3221225472 | bytes 3145728 | tf_op jit(solution)/shard_map/pallas_call | solution.py:624
  146.7 5.4 %collective-permute-done.8.b_ref = bf16[3,136,2048]{2,1,0:T(8,128)(2,1)} collective-permute-done((bf16[3,136,2048]{2,1,0:T(8,128)(2,1)}, bf16[3,136,2048]{2,1,0:T(8,128)(2,1)}, u32[]{:S(2)}, u32[]{:S(2)}) %collective-permute-start.8) | collective-permute-done | bytes 1671200 | tf_op jit(solution)/shard_map/ppermute | solution.py:735
  152.1 5.6 %collective-permute-start.11 = (bf16[3,136,2048]{2,1,0:T(8,128)(2,1)}, bf16[3,136,2048]{2,1,0:T(8,128)(2,1)}, u32[]{:S(2)}, u32[]{:S(2)}) collective-permute-start(bf16[3,136,2048]{2,1,0:T(8,128)(2,1)} %shard_map.74.a_ref), channel_id=1, source_target_pairs={{0,8},{4,12},{24,16},{28,20},{1,9},{5,13},{25,17},{29,21},{2,10},{... | collective-permute-start | bytes 5013512 | tf_op jit(solution)/shard_map/ppermute | solution.py:735
  163.3 30.1 %collective-permute-done.10.refs_5_ = bf16[3,2,512,256]{3,2,1,0:T(8,128)(2,1)} collective-permute-done((bf16[3,2,512,256]{3,2,1,0:T(8,128)(2,1)}, bf16[3,2,512,256]{3,2,1,0:T(8,128)(2,1)}, u32[]{:S(2)}, u32[]{:S(2)}) %collective-permute-start.10) | collective-permute-done | bytes 1572896 | tf_op jit(solution)/shard_map/ppermute | solution.py:735
  198.6 27.7 %collective-permute-done.23.refs_7_ = bf16[2048,512]{1,0:T(8,128)(2,1)} collective-permute-done((bf16[2048,512]{1,0:T(8,128)(2,1)}, bf16[2048,512]{1,0:T(8,128)(2,1)}, u32[]{:S(2)}, u32[]{:S(2)}) %collective-permute-start.23) | collective-permute-done | bytes 2097184 | tf_op jit(solution)/shard_map/ppermute | solution.py:735
  228.3 4.1 collective-permute-start.24
  234.2 20.3 %shard_map.73.a_ref = bf16[3,136,2048]{2,1,0:T(8,128)(2,1)} custom-call(s32[12]{0:T(128)} %get-tuple-element.14.refs_0_, s32[12]{0:T(128)} %get-tuple-element.15.refs_1_, s32[12]{0:T(128)} %get-tuple-element.16.refs_2_, bf16[3,2,128,256]{3,2,1,0:T(8,128)(2,1)} %bitcast.13, bf16[384,2048]{1,0:T(8,128)(2,1)} %refs_4_.1, bf16[16,2,512,256]{3,2,1,0:T(8,128)(2,1)} %bitcast.11, ...), custom_call_target="tpu_custom_call" | custom-call | flops 3221225472 | bytes 3145728 | tf_op jit(solution)/shard_map/pallas_call | solution.py:624
  256.6 20.8 %collective-permute-start.25 = (bf16[1,136,2048]{2,1,0:T(8,128)(2,1)}, bf16[1,136,2048]{2,1,0:T(8,128)(2,1)}, u32[]{:S(2)}, u32[]{:S(2)}) collective-permute-start(bf16[1,136,2048]{2,1,0:T(8,128)(2,1)} %shard_map.77.a_ref), channel_id=1, source_target_pairs={{0,8},{4,12},{8,0},{12,4},{16,24},{20,28},{24,16},{28,20},{1,9},{5... | collective-permute-start | bytes 1671176 | tf_op jit(solution)/shard_map/ppermute | solution.py:735
  292.3 15.7 %collective-permute-start.26 = (bf16[1,136,2048]{2,1,0:T(8,128)(2,1)}, bf16[1,136,2048]{2,1,0:T(8,128)(2,1)}, u32[]{:S(2)}, u32[]{:S(2)}) collective-permute-start(bf16[1,136,2048]{2,1,0:T(8,128)(2,1)} %shard_map.83.a_ref), channel_id=1, source_target_pairs={{0,8},{4,12},{8,0},{12,4},{16,24},{20,28},{24,16},{28,20},{1,9},{5... | collective-permute-start | bytes 1671176 | tf_op jit(solution)/shard_map/ppermute | solution.py:735
  310.1 3.9 collective-permute-start.27
  314.0 15.4 %shard_map.78.a_ref = bf16[3,136,2048]{2,1,0:T(8,128)(2,1)} custom-call(s32[12]{0:T(128)} %get-tuple-element.14.refs_0_, s32[12]{0:T(128)} %get-tuple-element.15.refs_1_, s32[12]{0:T(128)} %get-tuple-element.16.refs_2_, bf16[384,2048]{1,0:T(8,128)(2,1)} %collective-permute-done.2.refs_3_, bf16[16,2,512,256]{3,2,1,0:T(8,128)(2,1)} %bitcast.12, ...), custom_call_target="tpu_custom_call" | custom-call | flops 3221225472 | bytes 3145728 | tf_op jit(solution)/shard_map/pallas_call | solution.py:624
  336.0 2.5 shard_map.92.refs_0_
  338.4 2.5 shard_map.93.refs_1_
  340.9 2.5 shard_map.94.refs_2_
  343.4 10.0 %project_far.1 = (bf16[2,384,512]{2,1,0:T(8,128)(2,1)}, bf16[2,384,512]{2,1,0:T(8,128)(2,1)}) custom-call(bf16[128,2048]{1,0:T(8,128)(2,1)} %shard_map.92.refs_0_, bf16[128,2048]{1,0:T(8,128)(2,1)} %shard_map.93.refs_1_, bf16[128,2048]{1,0:T(8,128)(2,1)} %shard_map.94.refs_2_, bf16[2048,512]{1,0:T(8,128)(2,1)} %refs_3_.3, ...), custom_call_target="tpu_custom_call" | custom-call | flops 3221225472 | bytes 8388608 | tf_op jit(solution)/shard_map/project_far/pallas_call | solution.py:977
  355.0 2.7 collective-permute-start.13
  359.7 11.3 %collective-permute-done.13.b_ref = bf16[1,136,2048]{2,1,0:T(8,128)(2,1)} collective-permute-done((bf16[1,136,2048]{2,1,0:T(8,128)(2,1)}, bf16[1,136,2048]{2,1,0:T(8,128)(2,1)}, u32[]{:S(2)}, u32[]{:S(2)}) %collective-permute-start.13) | collective-permute-done | bytes 557088 | tf_op jit(solution)/shard_map/ppermute | solution.py:735
  373.4 9.5 %collective-permute-done.16.b_ref = bf16[1,136,2048]{2,1,0:T(8,128)(2,1)} collective-permute-done((bf16[1,136,2048]{2,1,0:T(8,128)(2,1)}, bf16[1,136,2048]{2,1,0:T(8,128)(2,1)}, u32[]{:S(2)}, u32[]{:S(2)}) %collective-permute-start.16) | collective-permute-done | bytes 557088 | tf_op jit(solution)/shard_map/ppermute | solution.py:735
  385.4 8.9 %collective-permute-done.19.b_ref = bf16[1,136,2048]{2,1,0:T(8,128)(2,1)} collective-permute-done((bf16[1,136,2048]{2,1,0:T(8,128)(2,1)}, bf16[1,136,2048]{2,1,0:T(8,128)(2,1)}, u32[]{:S(2)}, u32[]{:S(2)}) %collective-permute-start.19) | collective-permute-done | bytes 557088 | tf_op jit(solution)/shard_map/ppermute | solution.py:735
  394.3 2.5 shard_map.91.refs_2_
  396.8 21.1 %project_home.1 = bf16[384,1024]{1,0:T(8,128)(2,1)} custom-call(bf16[128,2048]{1,0:T(8,128)(2,1)} %shard_map.81.refs_0_, bf16[128,2048]{1,0:T(8,128)(2,1)} %shard_map.86.refs_1_, bf16[128,2048]{1,0:T(8,128)(2,1)} %shard_map.91.refs_2_, bf16[2048,512]{1,0:T(8,128)(2,1)} %refs_3_.3, bf16[2048,512]{1,0:T(8,128)(2,1)} %collective-permute-done.20.refs_4_, ...), custom_call_target="tpu_custom_call" | custom-call | flops 3221225472 | bytes 8388608 | tf_op jit(solution)/shard_map/project_home/pallas_call | solution.py:977
  (54 shorter events, 61.5 us)
Async XLA Ops:
  0.0 37.8 %collective-permute-start.2 = (bf16[384,2048]{1,0:T(8,128)(2,1)}, bf16[384,2048]{1,0:T(8,128)(2,1)}, u32[]{:S(2)}, u32[]{:S(2)}) collective-permute-start(bf16[384,2048]{1,0:T(8,128)(2,1)} %refs_4_.1), channel_id=1, source_target_pairs={{0,8},{4,12},{8,0},{12,4},{16,24},{20,28},{24,16},{28,20},{1,9},{5... | collective-permute-start | bytes 4718600 | tf_op jit(solution)/shard_map/ppermute | solution.py:735
  3.1 55.4 %collective-permute-start.1 = (bf16[384,2048]{1,0:T(8,128)(2,1)}, bf16[384,2048]{1,0:T(8,128)(2,1)}, u32[]{:S(2)}, u32[]{:S(2)}) collective-permute-start(bf16[384,2048]{1,0:T(8,128)(2,1)} %refs_4_.1), channel_id=1, source_target_pairs={{8,16},{12,20},{16,8},{20,12},{9,17},{13,21},{17,9},{21,13},{10,18... | collective-permute-start | bytes 4718600 | tf_op jit(solution)/shard_map/ppermute | solution.py:735
  37.8 22.1 %collective-permute-start.3 = (bf16[384,2048]{1,0:T(8,128)(2,1)}, bf16[384,2048]{1,0:T(8,128)(2,1)}, u32[]{:S(2)}, u32[]{:S(2)}) collective-permute-start(bf16[384,2048]{1,0:T(8,128)(2,1)} %collective-permute-done.2.refs_3_), channel_id=1, source_target_pairs={{8,16},{12,20},{16,8},{20,12},{9,17},{13,21},{17,9},{21,13},{10,18... | collective-permute-start | bytes 4718600 | tf_op jit(solution)/shard_map/ppermute | solution.py:735
  55.7 38.4 %collective-permute-start.7 = (bf16[3,2,512,256]{3,2,1,0:T(8,128)(2,1)}, bf16[3,2,512,256]{3,2,1,0:T(8,128)(2,1)}, u32[]{:S(2)}, u32[]{:S(2)}) collective-permute-start(bf16[3,2,512,256]{3,2,1,0:T(8,128)(2,1)} %get-tuple-element.19), channel_id=1, source_target_pairs={{0,4},{4,0},{8,12},{12,8},{16,20},{20,16},{24,28},{28,24},{1,5},{5... | collective-permute-start | bytes 4718600 | tf_op jit(solution)/shard_map/ppermute | solution.py:735
  58.5 39.5 %collective-permute-start.6 = (bf16[384,2048]{1,0:T(8,128)(2,1)}, bf16[384,2048]{1,0:T(8,128)(2,1)}, u32[]{:S(2)}, u32[]{:S(2)}) collective-permute-start(bf16[384,2048]{1,0:T(8,128)(2,1)} %collective-permute-done.1.refs_3_), channel_id=1, source_target_pairs={{8,0},{12,4},{16,24},{20,28},{9,1},{13,5},{17,25},{21,29},{10,2},{... | collective-permute-start | bytes 4718600 | tf_op jit(solution)/shard_map/ppermute | solution.py:735
  59.8 68.0 %collective-permute-start.5 = (bf16[3,2,512,256]{3,2,1,0:T(8,128)(2,1)}, bf16[3,2,512,256]{3,2,1,0:T(8,128)(2,1)}, u32[]{:S(2)}, u32[]{:S(2)}) collective-permute-start(bf16[3,2,512,256]{3,2,1,0:T(8,128)(2,1)} %get-tuple-element.18), channel_id=1, source_target_pairs={{0,4},{4,0},{8,12},{12,8},{16,20},{20,16},{24,28},{28,24},{1,5},{5... | collective-permute-start | bytes 4718600 | tf_op jit(solution)/shard_map/ppermute | solution.py:735
  59.9 69.9 %collective-permute-start.4 = (bf16[384,2048]{1,0:T(8,128)(2,1)}, bf16[384,2048]{1,0:T(8,128)(2,1)}, u32[]{:S(2)}, u32[]{:S(2)}) collective-permute-start(bf16[384,2048]{1,0:T(8,128)(2,1)} %collective-permute-done.3.refs_3_), channel_id=1, source_target_pairs={{8,0},{12,4},{16,24},{20,28},{9,1},{13,5},{17,25},{21,29},{10,2},{... | collective-permute-start | bytes 4718600 | tf_op jit(solution)/shard_map/ppermute | solution.py:735
  113.5 38.6 %collective-permute-start.8 = (bf16[3,136,2048]{2,1,0:T(8,128)(2,1)}, bf16[3,136,2048]{2,1,0:T(8,128)(2,1)}, u32[]{:S(2)}, u32[]{:S(2)}) collective-permute-start(bf16[3,136,2048]{2,1,0:T(8,128)(2,1)} %shard_map.75.a_ref), channel_id=1, source_target_pairs={{0,8},{4,12},{24,16},{28,20},{1,9},{5,13},{25,17},{29,21},{2,10},{... | collective-permute-start | bytes 5013512 | tf_op jit(solution)/shard_map/ppermute | solution.py:735
  116.1 81.0 %collective-permute-start.21 = (bf16[2048,512]{1,0:T(8,128)(2,1)}, bf16[2048,512]{1,0:T(8,128)(2,1)}, u32[]{:S(2)}, u32[]{:S(2)}) collective-permute-start(bf16[2048,512]{1,0:T(8,128)(2,1)} %refs_3_.3), channel_id=1, source_target_pairs={{0,16},{4,20},{24,8},{28,12},{1,17},{5,21},{25,9},{29,13},{2,18},{... | collective-permute-start | bytes 6291464 | tf_op jit(solution)/shard_map/ppermute | solution.py:735
  118.8 43.1 %collective-permute-start = (bf16[3,2,512,256]{3,2,1,0:T(8,128)(2,1)}, bf16[3,2,512,256]{3,2,1,0:T(8,128)(2,1)}, u32[]{:S(2)}, u32[]{:S(2)}) collective-permute-start(bf16[3,2,512,256]{3,2,1,0:T(8,128)(2,1)} %get-tuple-element.17), channel_id=1, source_target_pairs={{0,4},{4,0},{8,12},{12,8},{16,20},{20,16},{24,28},{28,24},{1,5},{5... | collective-permute-start | bytes 4718600 | tf_op jit(solution)/shard_map/ppermute | solution.py:735
  127.7 65.7 %collective-permute-start.10 = (bf16[3,2,512,256]{3,2,1,0:T(8,128)(2,1)}, bf16[3,2,512,256]{3,2,1,0:T(8,128)(2,1)}, u32[]{:S(2)}, u32[]{:S(2)}) collective-permute-start(bf16[3,2,512,256]{3,2,1,0:T(8,128)(2,1)} %get-tuple-element.20), channel_id=1, source_target_pairs={{0,4},{4,0},{8,12},{12,8},{16,20},{20,16},{24,28},{28,24},{1,5},{5... | collective-permute-start | bytes 4718600 | tf_op jit(solution)/shard_map/ppermute | solution.py:735
  129.8 96.5 %collective-permute-start.23 = (bf16[2048,512]{1,0:T(8,128)(2,1)}, bf16[2048,512]{1,0:T(8,128)(2,1)}, u32[]{:S(2)}, u32[]{:S(2)}) collective-permute-start(bf16[2048,512]{1,0:T(8,128)(2,1)} %refs_3_.3), channel_id=1, source_target_pairs={{8,24},{12,28},{16,0},{20,4},{9,25},{13,29},{17,1},{21,5},{10,26},... | collective-permute-start | bytes 6291464 | tf_op jit(solution)/shard_map/ppermute | solution.py:735
  152.1 104.5 %collective-permute-start.11 = (bf16[3,136,2048]{2,1,0:T(8,128)(2,1)}, bf16[3,136,2048]{2,1,0:T(8,128)(2,1)}, u32[]{:S(2)}, u32[]{:S(2)}) collective-permute-start(bf16[3,136,2048]{2,1,0:T(8,128)(2,1)} %shard_map.74.a_ref), channel_id=1, source_target_pairs={{0,8},{4,12},{24,16},{28,20},{1,9},{5,13},{25,17},{29,21},{2,10},{... | collective-permute-start | bytes 5013512 | tf_op jit(solution)/shard_map/ppermute | solution.py:735
  161.8 64.5 %collective-permute-start.9 = (bf16[1,136,2048]{2,1,0:T(8,128)(2,1)}, bf16[1,136,2048]{2,1,0:T(8,128)(2,1)}, u32[]{:S(2)}, u32[]{:S(2)}) collective-permute-start(bf16[1,136,2048]{2,1,0:T(8,128)(2,1)} %shard_map.76), channel_id=1, source_target_pairs={{8,16},{12,20},{16,8},{20,12},{9,17},{13,21},{17,9},{21,13},{10,18... | collective-permute-start | bytes 1671176 | tf_op jit(solution)/shard_map/ppermute | solution.py:735
  193.4 34.9 %collective-permute-start.14 = (bf16[1,136,2048]{2,1,0:T(8,128)(2,1)}, bf16[1,136,2048]{2,1,0:T(8,128)(2,1)}, u32[]{:S(2)}, u32[]{:S(2)}) collective-permute-start(bf16[1,136,2048]{2,1,0:T(8,128)(2,1)} %shard_map.82), channel_id=1, source_target_pairs={{8,16},{12,20},{16,8},{20,12},{9,17},{13,21},{17,9},{21,13},{10,18... | collective-permute-start | bytes 1671176 | tf_op jit(solution)/shard_map/ppermute | solution.py:735
  197.1 82.3 %collective-permute-start.17 = (bf16[1,136,2048]{2,1,0:T(8,128)(2,1)}, bf16[1,136,2048]{2,1,0:T(8,128)(2,1)}, u32[]{:S(2)}, u32[]{:S(2)}) collective-permute-start(bf16[1,136,2048]{2,1,0:T(8,128)(2,1)} %shard_map.87), channel_id=1, source_target_pairs={{8,16},{12,20},{16,8},{20,12},{9,17},{13,21},{17,9},{21,13},{10,18... | collective-permute-start | bytes 1671176 | tf_op jit(solution)/shard_map/ppermute | solution.py:735
  226.3 117.1 %collective-permute-start.20 = (bf16[2048,512]{1,0:T(8,128)(2,1)}, bf16[2048,512]{1,0:T(8,128)(2,1)}, u32[]{:S(2)}, u32[]{:S(2)}) collective-permute-start(bf16[2048,512]{1,0:T(8,128)(2,1)} %refs_3_.3), channel_id=1, source_target_pairs={{0,4},{4,0},{8,12},{12,8},{16,20},{20,16},{24,28},{28,24},{1,5},{5... | collective-permute-start | bytes 6291464 | tf_op jit(solution)/shard_map/ppermute | solution.py:735
  226.4 117.0 %collective-permute-start.22 = (bf16[2048,512]{1,0:T(8,128)(2,1)}, bf16[2048,512]{1,0:T(8,128)(2,1)}, u32[]{:S(2)}, u32[]{:S(2)}) collective-permute-start(bf16[2048,512]{1,0:T(8,128)(2,1)} %collective-permute-done.21.refs_5_), channel_id=1, source_target_pairs={{8,12},{12,8},{16,20},{20,16},{9,13},{13,9},{17,21},{21,17},{10,14... | collective-permute-start | bytes 6291464 | tf_op jit(solution)/shard_map/ppermute | solution.py:735
  228.3 115.1 %collective-permute-start.24 = (bf16[2048,512]{1,0:T(8,128)(2,1)}, bf16[2048,512]{1,0:T(8,128)(2,1)}, u32[]{:S(2)}, u32[]{:S(2)}) collective-permute-start(bf16[2048,512]{1,0:T(8,128)(2,1)} %collective-permute-done.23.refs_7_), channel_id=1, source_target_pairs={{0,4},{4,0},{24,28},{28,24},{1,5},{5,1},{25,29},{29,25},{2,6},{6,2... | collective-permute-start | bytes 6291464 | tf_op jit(solution)/shard_map/ppermute | solution.py:735
  256.6 28.6 %collective-permute-start.25 = (bf16[1,136,2048]{2,1,0:T(8,128)(2,1)}, bf16[1,136,2048]{2,1,0:T(8,128)(2,1)}, u32[]{:S(2)}, u32[]{:S(2)}) collective-permute-start(bf16[1,136,2048]{2,1,0:T(8,128)(2,1)} %shard_map.77.a_ref), channel_id=1, source_target_pairs={{0,8},{4,12},{8,0},{12,4},{16,24},{20,28},{24,16},{28,20},{1,9},{5... | collective-permute-start | bytes 1671176 | tf_op jit(solution)/shard_map/ppermute | solution.py:735
  279.4 9.3 %collective-permute-start.12 = (bf16[1,136,2048]{2,1,0:T(8,128)(2,1)}, bf16[1,136,2048]{2,1,0:T(8,128)(2,1)}, u32[]{:S(2)}, u32[]{:S(2)}) collective-permute-start(bf16[1,136,2048]{2,1,0:T(8,128)(2,1)} %shard_map.79), channel_id=1, source_target_pairs={{8,16},{12,20},{16,8},{20,12},{9,17},{13,21},{17,9},{21,13},{10,18... | collective-permute-start | bytes 1671176 | tf_op jit(solution)/shard_map/ppermute | solution.py:735
  285.1 7.2 %collective-permute-start.15 = (bf16[1,136,2048]{2,1,0:T(8,128)(2,1)}, bf16[1,136,2048]{2,1,0:T(8,128)(2,1)}, u32[]{:S(2)}, u32[]{:S(2)}) collective-permute-start(bf16[1,136,2048]{2,1,0:T(8,128)(2,1)} %shard_map.84), channel_id=1, source_target_pairs={{8,16},{12,20},{16,8},{20,12},{9,17},{13,21},{17,9},{21,13},{10,18... | collective-permute-start | bytes 1671176 | tf_op jit(solution)/shard_map/ppermute | solution.py:735
  288.8 21.4 %collective-permute-start.18 = (bf16[1,136,2048]{2,1,0:T(8,128)(2,1)}, bf16[1,136,2048]{2,1,0:T(8,128)(2,1)}, u32[]{:S(2)}, u32[]{:S(2)}) collective-permute-start(bf16[1,136,2048]{2,1,0:T(8,128)(2,1)} %shard_map.89), channel_id=1, source_target_pairs={{8,16},{12,20},{16,8},{20,12},{9,17},{13,21},{17,9},{21,13},{10,18... | collective-permute-start | bytes 1671176 | tf_op jit(solution)/shard_map/ppermute | solution.py:735
  292.3 46.1 %collective-permute-start.26 = (bf16[1,136,2048]{2,1,0:T(8,128)(2,1)}, bf16[1,136,2048]{2,1,0:T(8,128)(2,1)}, u32[]{:S(2)}, u32[]{:S(2)}) collective-permute-start(bf16[1,136,2048]{2,1,0:T(8,128)(2,1)} %shard_map.83.a_ref), channel_id=1, source_target_pairs={{0,8},{4,12},{8,0},{12,4},{16,24},{20,28},{24,16},{28,20},{1,9},{5... | collective-permute-start | bytes 1671176 | tf_op jit(solution)/shard_map/ppermute | solution.py:735
  310.1 30.7 %collective-permute-start.27 = (bf16[1,136,2048]{2,1,0:T(8,128)(2,1)}, bf16[1,136,2048]{2,1,0:T(8,128)(2,1)}, u32[]{:S(2)}, u32[]{:S(2)}) collective-permute-start(bf16[1,136,2048]{2,1,0:T(8,128)(2,1)} %shard_map.88.a_ref), channel_id=1, source_target_pairs={{0,8},{4,12},{8,0},{12,4},{16,24},{20,28},{24,16},{28,20},{1,9},{5... | collective-permute-start | bytes 1671176 | tf_op jit(solution)/shard_map/ppermute | solution.py:735
  353.4 43.4 %collective-permute-start.28 = (bf16[2,384,512]{2,1,0:T(8,128)(2,1)}, bf16[2,384,512]{2,1,0:T(8,128)(2,1)}, u32[]{:S(2)}, u32[]{:S(2)}) collective-permute-start(bf16[2,384,512]{2,1,0:T(8,128)(2,1)} %get-tuple-element.22), channel_id=1, source_target_pairs={{1,3},{3,1},{5,7},{7,5},{8,10},{10,8},{12,14},{14,12},{17,19},{19,... | collective-permute-start | bytes 2359304 | tf_op jit(solution)/shard_map/ppermute | solution.py:793
  355.0 16.0 %collective-permute-start.13 = (bf16[1,136,2048]{2,1,0:T(8,128)(2,1)}, bf16[1,136,2048]{2,1,0:T(8,128)(2,1)}, u32[]{:S(2)}, u32[]{:S(2)}) collective-permute-start(bf16[1,136,2048]{2,1,0:T(8,128)(2,1)} %shard_map.80.a_ref), channel_id=1, source_target_pairs={{0,8},{4,12},{8,0},{12,4},{16,24},{20,28},{24,16},{28,20},{1,9},{5... | collective-permute-start | bytes 1671176 | tf_op jit(solution)/shard_map/ppermute | solution.py:735
  357.7 25.3 %collective-permute-start.16 = (bf16[1,136,2048]{2,1,0:T(8,128)(2,1)}, bf16[1,136,2048]{2,1,0:T(8,128)(2,1)}, u32[]{:S(2)}, u32[]{:S(2)}) collective-permute-start(bf16[1,136,2048]{2,1,0:T(8,128)(2,1)} %shard_map.85.a_ref), channel_id=1, source_target_pairs={{0,8},{4,12},{8,0},{12,4},{16,24},{20,28},{24,16},{28,20},{1,9},{5... | collective-permute-start | bytes 1671176 | tf_op jit(solution)/shard_map/ppermute | solution.py:735
  357.7 36.5 %collective-permute-start.19 = (bf16[1,136,2048]{2,1,0:T(8,128)(2,1)}, bf16[1,136,2048]{2,1,0:T(8,128)(2,1)}, u32[]{:S(2)}, u32[]{:S(2)}) collective-permute-start(bf16[1,136,2048]{2,1,0:T(8,128)(2,1)} %shard_map.90.a_ref), channel_id=1, source_target_pairs={{0,8},{4,12},{8,0},{12,4},{16,24},{20,28},{24,16},{28,20},{1,9},{5... | collective-permute-start | bytes 1671176 | tf_op jit(solution)/shard_map/ppermute | solution.py:735

commit v6 on v5

--- a/solution.py
+++ b/solution.py
@@ -350,6 +350,7 @@
 EXTRA = 8
 ITEM_ORDER = (2, 0, 3, 1)
 VMEM_BYTES = 67043328
+WIDE = 2
 
 
 def mirror(k, ends=None):
@@ -457,47 +458,36 @@
     )(lists.T, passage_slot, question_slot, cache)
 
 
-def unit():
-    r = lax.broadcasted_iota(jnp.int32, (LQ, LQ), 0)
-    c = lax.broadcasted_iota(jnp.int32, (LQ, LQ), 1)
-    return r == c
-
-
 def part_step(q_ref, m_ref, l_ref, acc_ref, question, head, keys, values, causal):
-    rows = GROUP * LQ
-    width = keys.shape[0]
-    ones = jnp.ones(values.shape, values.dtype)
-    extended = jnp.concatenate([values, ones], axis=1)
+    turned = values.T
     tokens = pl.ds(pl.multiple_of(question * LQ, LQ), LQ)
-    for start in range(0, rows, ROWS):
-        part = pl.ds(start, ROWS)
+    for start in range(0, GROUP, WIDE):
         q = jnp.concatenate(
             [
                 q_ref[tokens, pl.ds(pl.multiple_of((head * GROUP + g) * HD, HD), HD)]
-                for g in range(start // LQ, (start + ROWS) // LQ)
+                for g in range(start, start + WIDE)
             ],
             axis=0,
         )
-        scores = (
-            lax.dot_general(q, keys, (((1,), (1,)), ((), ())), preferred_element_type=jnp.float32)
-            * COEF
+        columns = pl.ds(start * LQ, WIDE * LQ)
+        scores = lax.dot_general(
+            keys, q, (((1,), (1,)), ((), ())), preferred_element_type=jnp.float32
         )
         if causal:
-            token = lax.broadcasted_iota(jnp.int32, scores.shape, 0) % LQ
-            column = lax.broadcasted_iota(jnp.int32, scores.shape, 1)
-            scores = jnp.where(column <= token, scores, NEG)
-        old = m_ref[question, head, part, :]
-        new = jnp.maximum(old, jnp.max(scores, axis=1, keepdims=True))
-        weights = jnp.exp2(scores - jnp.concatenate([new] * (width // HD), axis=1))
-        mixed = jnp.dot(
-            weights.astype(jnp.bfloat16), extended, preferred_element_type=jnp.float32
+            key = lax.broadcasted_iota(jnp.int32, scores.shape, 0)
+            token = lax.broadcasted_iota(jnp.int32, scores.shape, 1) % LQ
+            scores = jnp.where(key <= token, scores, NEG)
+        old = m_ref[question, head, :, columns]
+        new = jnp.maximum(old, jnp.max(scores, axis=0, keepdims=True))
+        weights = jnp.exp2((scores - new) * COEF)
+        alpha = jnp.exp2((old - new) * COEF)
+        m_ref[question, head, :, columns] = new
+        l_ref[question, head, :, columns] = l_ref[question, head, :, columns] * alpha + jnp.sum(
+            weights, axis=0, keepdims=True
         )
-        alpha = jnp.exp2(old - new)
-        m_ref[question, head, part, :] = new
-        l_ref[question, head, part, :] = l_ref[question, head, part, :] * alpha + mixed[:, HD:]
-        acc_ref[question, head, part, :] = (
-            acc_ref[question, head, part, :] * alpha + mixed[:, :HD]
-        )
+        acc_ref[question, head, :, columns] = acc_ref[
+            question, head, :, columns
+        ] * alpha + jnp.dot(turned, weights.astype(turned.dtype), preferred_element_type=jnp.float32)
 
 
 def part_kernel(k, most, heads, *refs):
@@ -584,38 +574,33 @@
         return carry
 
     lax.fori_loop(0, entries, item, 0)
-    eye = unit()
-
-    def close(c, carry):
-        head, g = c // GROUP, lax.rem(c, GROUP)
-        columns = pl.ds(pl.multiple_of(c * HD, HD), HD)
-        part = pl.ds(pl.multiple_of(g * LQ, LQ), LQ)
-        for question in range(per_device):
-            total = l_ref[question, head, part, :]
-            some = total > 0.0
-            safe = jnp.where(some, total, 1.0)
-            out_ref[question, :LQ, columns] = (
-                acc_ref[question, head, part, :] / safe
-            ).astype(out_ref.dtype)
-            level = jnp.where(some, m_ref[question, head, part, :] + jnp.log2(safe), NEG)
-            line = jnp.sum(jnp.where(eye, level, 0.0), axis=0, keepdims=True)
-            store_level(out_ref, question, columns, line)
+
+    def close(i, carry):
+        question, head = i // heads, lax.rem(i, heads)
+        columns = pl.ds(pl.multiple_of(head * GROUP * LQ, GROUP * LQ), GROUP * LQ)
+        total = l_ref[question, head]
+        some = total > 0.0
+        safe = jnp.where(some, total, 1.0)
+        out_ref[question, :HD, columns] = (acc_ref[question, head] / safe).astype(out_ref.dtype)
+        level = jnp.where(some, m_ref[question, head] * COEF + jnp.log2(safe), NEG)
+        store_level(out_ref, question, columns, level)
         return carry
 
-    lax.fori_loop(0, heads * GROUP, close, 0)
+    lax.fori_loop(0, per_device * heads, close, 0)
 
 
 def store_level(out_ref, question, columns, line):
     row_of = lax.broadcasted_iota(jnp.int32, (EXTRA, line.shape[1]), 0)
     high = line.astype(jnp.bfloat16).astype(jnp.float32)
     both = jnp.where(row_of == 0, high, jnp.where(row_of == 1, line - high, 0.0))
-    out_ref[question, LQ:, columns] = both.astype(out_ref.dtype)
+    out_ref[question, HD:, columns] = both.astype(out_ref.dtype)
 
 
 def part_call(k, most, tables, own, questions, cache, items):
     tokens, columns = questions[0].shape
     heads, item = cache.shape[1], cache.shape[1:]
-    state = (tokens // LQ, heads, GROUP * LQ, HD)
+    state = (tokens // LQ, heads, HD, GROUP * LQ)
+    row_state = (tokens // LQ, heads, 1, GROUP * LQ)
     smem = pl.BlockSpec(memory_space=pltpu.SMEM)
     vmem = pl.BlockSpec(memory_space=pltpu.VMEM)
     anyspace = pl.BlockSpec(memory_space=pl.ANY)
@@ -623,13 +608,13 @@
     weights = 2 * most * heads * GROUP * LQ * item[1]
     return pl.pallas_call(
         functools.partial(part_kernel, k, most, heads),
-        out_shape=jax.ShapeDtypeStruct((tokens // LQ, LQ + EXTRA, columns), cache.dtype),
+        out_shape=jax.ShapeDtypeStruct((tokens // LQ, HD + EXTRA, columns), cache.dtype),
         in_specs=[smem] * 3 + [vmem] * len(owned) + [anyspace] * (len(questions) + 2),
         out_specs=vmem,
         scratch_shapes=[
             pltpu.VMEM((tokens, columns), cache.dtype),
-            pltpu.VMEM(state, jnp.float32),
-            pltpu.VMEM(state, jnp.float32),
+            pltpu.VMEM(row_state, jnp.float32),
+            pltpu.VMEM(row_state, jnp.float32),
             pltpu.VMEM(state, jnp.float32),
             pltpu.VMEM((2,) + item, cache.dtype),
             pltpu.SemaphoreType.DMA((2,)),
@@ -645,11 +630,8 @@
 
 
 def blend(a_ref, b_ref, out_ref, leveled):
-    eye = unit()
-    ones = jnp.ones((2 * LQ, LQ), jnp.bfloat16)
-
     def level_of(ref):
-        both = ref[0, LQ:, :].astype(jnp.float32)
+        both = ref[0, HD:, :].astype(jnp.float32)
         return both[:1] + both[1:2]
 
     one, two = level_of(a_ref), level_of(b_ref)
@@ -657,25 +639,15 @@
     first, second = jnp.exp2(one - top), jnp.exp2(two - top)
     total = first + second
     share = first / total
-    high = share.astype(jnp.bfloat16).astype(jnp.float32)
-    low = share - high
-    for c in range(share.shape[1] // HD):
-        columns = slice(c * HD, (c + 1) * HD)
-        spread = jnp.concatenate(
-            [
-                jnp.where(eye, jnp.broadcast_to(v[:, columns], (LQ, LQ)), 0.0).astype(jnp.bfloat16)
-                for v in (high, low)
-            ],
-            axis=1,
-        )
-        column = jnp.dot(spread, ones, preferred_element_type=jnp.float32)
-        a = a_ref[0, :LQ, columns].astype(jnp.float32)
-        b = b_ref[0, :LQ, columns].astype(jnp.float32)
-        value = (b + (a - b) * column).astype(out_ref.dtype)
+    for c in range(share.shape[1] // LQ):
+        columns = slice(c * LQ, (c + 1) * LQ)
+        a = a_ref[0, :HD, columns].astype(jnp.float32)
+        b = b_ref[0, :HD, columns].astype(jnp.float32)
+        value = b + (a - b) * share[:, columns]
         if leveled:
-            out_ref[0, :LQ, columns] = value
+            out_ref[0, :HD, columns] = value.astype(out_ref.dtype)
         else:
-            out_ref[:, columns] = value
+            out_ref[:, columns] = value.T.astype(out_ref.dtype)
     if leveled:
         store_level(out_ref, 0, slice(None), top + jnp.log2(total))
 

time: 421 us -> 438 us (1.040)
  Pallas kernels: 146 us -> 179 us
  waiting for transfers between devices: 173 us -> 157 us
    pallas_call x4, Pallas kernels: 66.8 us -> 100 us  [part_call(): pl.pallas_call(functools.partial(part_kernel, k, most, heads), out_shape=...]
    ppermute x28, waiting for transfers between devices: 173 us -> 157 us  [send(): return lax.ppermute(value, 'pass', pairs)]
  transfers between devices with their start and end apart: 29 -> 29, of which waited for: 12 -> 12; matrix products, arithmetic and copies ran while one was open for 2% -> 2% of each run, Pallas kernels for 27% -> 34%
where the time goes in v6:
time: 438 us; the launch traced here: 436 us
  Pallas kernels  179 us (41%)
  waiting for transfers between devices  157 us (36%)
  starting transfers between devices  88.6 us (20%)
  local copies, waits for them, and re-layouts  12 us (3%)
    ppermute x28, waiting for transfers between devices, send(): return lax.ppermute(value, 'pass', pairs)  157 us
    pallas_call x4, Pallas kernels, part_call(): pl.pallas_call(functools.partial(part_kernel, k, most, heads), out_shape=...  100 us
    ppermute x28, starting transfers between devices, send(): return lax.ppermute(value, 'pass', pairs)  87 us
    pallas_call x18, Pallas kernels, join_call(): pl.pallas_call(merge_kernel if leveled else finish_kernel, out_shape=jax....  39.3 us
    pallas_call x2, Pallas kernels, project_call(): pl.pallas_call(functools.partial(project_kernel, len(pieces), far), out_s...  31.1 us
    unnamed x2, local copies, waits for them, and re-layouts  10.3 us
  transfers between devices with their start and end apart: 29, of which 12 were waited for; matrix products, arithmetic and copies ran while one was open for 2% of the time, Pallas kernels for 34%

profile of v6, /device:TPU:0, one launch (start us, length us, event | category | flops | bytes accessed | tf_op | source)
XLA Modules:
  0.0 436.4 jit_solution(15286431048640955612)
XLA Ops:
  0.0 3.1 collective-permute-start.2
  4.9 32.9 %collective-permute-done.2.refs_3_ = bf16[384,2048]{1,0:T(8,128)(2,1)} collective-permute-done((bf16[384,2048]{1,0:T(8,128)(2,1)}, bf16[384,2048]{1,0:T(8,128)(2,1)}, u32[]{:S(2)}, u32[]{:S(2)}) %collective-permute-start.2) | collective-permute-done | bytes 1572896 | tf_op jit(solution)/shard_map/ppermute | solution.py:707
  39.7 8.2 %copy.16 = bf16[16,512,2,256]{3,1,2,0:T(8,128)(2,1)} copy(bf16[16,512,2,256]{3,2,1,0:T(2,128)(2,1)} %param.9) | data formatting | bytes 16777216 | tf_op args[2]
  47.8 7.8 %sort_items.1 = (s32[12]{0:T(128)}, s32[12]{0:T(128)}, s32[12]{0:T(128)}, bf16[3,2,512,256]{3,2,1,0:T(8,128)(2,1)}, bf16[3,2,512,256]{3,2,1,0:T(8,128)(2,1)}, /*...) custom-call(s32[8,24]{1,0:T(8,128)} %bitcast.15, s32[128]{0:T(128)} %pslot_ref.1, s32[24]{0:T(128)} %qslot_ref.1, ...), custom_call_target="tpu_custom_call" | custom-call | bytes 12582912 | tf_op jit(solution)/shard_map/sort_items/pallas_call | solution.py:438
  55.7 2.8 collective-permute-start.7
  61.2 32.9 %collective-permute-done.7.refs_6_ = bf16[3,2,512,256]{3,2,1,0:T(8,128)(2,1)} collective-permute-done((bf16[3,2,512,256]{3,2,1,0:T(8,128)(2,1)}, bf16[3,2,512,256]{3,2,1,0:T(8,128)(2,1)}, u32[]{:S(2)}, u32[]{:S(2)}) %collective-permute-start.7) | collective-permute-done | bytes 1572896 | tf_op jit(solution)/shard_map/ppermute | solution.py:707
  94.0 3.9 collective-permute-done.6.refs_4_
  97.9 24.0 %shard_map.75.a_ref = bf16[3,136,2048]{2,1,0:T(8,128)(2,1)} custom-call(s32[12]{0:T(128)} %get-tuple-element.14.refs_0_, s32[12]{0:T(128)} %get-tuple-element.15.refs_1_, s32[12]{0:T(128)} %get-tuple-element.16.refs_2_, bf16[384,2048]{1,0:T(8,128)(2,1)} %collective-permute-done.3.refs_3_, bf16[384,2048]{1,0:T(8,128)(2,1)} %collective-permute-done.6.refs_4_, ...), custom_call_target="tpu_custom_call" | custom-call | flops 3221225472 | bytes 3145728 | tf_op jit(solution)/shard_map/pallas_call | solution.py:609
  122.0 2.6 collective-permute-start.8
  124.6 2.7 collective-permute-start.21
  130.7 24.1 %shard_map.74.a_ref = bf16[3,136,2048]{2,1,0:T(8,128)(2,1)} custom-call(s32[12]{0:T(128)} %get-tuple-element.14.refs_0_, s32[12]{0:T(128)} %get-tuple-element.15.refs_1_, s32[12]{0:T(128)} %get-tuple-element.16.refs_2_, bf16[384,2048]{1,0:T(8,128)(2,1)} %collective-permute-done.1.refs_3_, bf16[384,2048]{1,0:T(8,128)(2,1)} %collective-permute-done.4.refs_4_, ...), custom_call_target="tpu_custom_call" | custom-call | flops 3221225472 | bytes 3145728 | tf_op jit(solution)/shard_map/pallas_call | solution.py:609
  154.8 5.8 %collective-permute-done.8.b_ref = bf16[3,136,2048]{2,1,0:T(8,128)(2,1)} collective-permute-done((bf16[3,136,2048]{2,1,0:T(8,128)(2,1)}, bf16[3,136,2048]{2,1,0:T(8,128)(2,1)}, u32[]{:S(2)}, u32[]{:S(2)}) %collective-permute-start.8) | collective-permute-done | bytes 1671200 | tf_op jit(solution)/shard_map/ppermute | solution.py:707
  160.6 5.6 %collective-permute-start.11 = (bf16[3,136,2048]{2,1,0:T(8,128)(2,1)}, bf16[3,136,2048]{2,1,0:T(8,128)(2,1)}, u32[]{:S(2)}, u32[]{:S(2)}) collective-permute-start(bf16[3,136,2048]{2,1,0:T(8,128)(2,1)} %shard_map.74.a_ref), channel_id=1, source_target_pairs={{0,8},{4,12},{24,16},{28,20},{1,9},{5,13},{25,17},{29,21},{2,10},{... | collective-permute-start | bytes 5013512 | tf_op jit(solution)/shard_map/ppermute | solution.py:707
  171.8 21.6 %collective-permute-done.10.refs_5_ = bf16[3,2,512,256]{3,2,1,0:T(8,128)(2,1)} collective-permute-done((bf16[3,2,512,256]{3,2,1,0:T(8,128)(2,1)}, bf16[3,2,512,256]{3,2,1,0:T(8,128)(2,1)}, u32[]{:S(2)}, u32[]{:S(2)}) %collective-permute-start.10) | collective-permute-done | bytes 1572896 | tf_op jit(solution)/shard_map/ppermute | solution.py:707
  197.0 8.6 %collective-permute-done.21.refs_5_ = bf16[2048,512]{1,0:T(8,128)(2,1)} collective-permute-done((bf16[2048,512]{1,0:T(8,128)(2,1)}, bf16[2048,512]{1,0:T(8,128)(2,1)}, u32[]{:S(2)}, u32[]{:S(2)}) %collective-permute-start.21) | collective-permute-done | bytes 2097184 | tf_op jit(solution)/shard_map/ppermute | solution.py:707
  207.1 18.8 %collective-permute-done.23.refs_7_ = bf16[2048,512]{1,0:T(8,128)(2,1)} collective-permute-done((bf16[2048,512]{1,0:T(8,128)(2,1)}, bf16[2048,512]{1,0:T(8,128)(2,1)}, u32[]{:S(2)}, u32[]{:S(2)}) %collective-permute-start.23) | collective-permute-done | bytes 2097184 | tf_op jit(solution)/shard_map/ppermute | solution.py:707
  228.9 3.1 collective-permute-start.24
  233.8 28.3 %shard_map.73.a_ref = bf16[3,136,2048]{2,1,0:T(8,128)(2,1)} custom-call(s32[12]{0:T(128)} %get-tuple-element.14.refs_0_, s32[12]{0:T(128)} %get-tuple-element.15.refs_1_, s32[12]{0:T(128)} %get-tuple-element.16.refs_2_, bf16[3,2,128,256]{3,2,1,0:T(8,128)(2,1)} %bitcast.13, bf16[384,2048]{1,0:T(8,128)(2,1)} %refs_4_.1, bf16[16,2,512,256]{3,2,1,0:T(8,128)(2,1)} %bitcast.11, ...), custom_call_target="tpu_custom_call" | custom-call | flops 3221225472 | bytes 3145728 | tf_op jit(solution)/shard_map/pallas_call | solution.py:609
  264.2 20.7 %collective-permute-start.25 = (bf16[1,136,2048]{2,1,0:T(8,128)(2,1)}, bf16[1,136,2048]{2,1,0:T(8,128)(2,1)}, u32[]{:S(2)}, u32[]{:S(2)}) collective-permute-start(bf16[1,136,2048]{2,1,0:T(8,128)(2,1)} %shard_map.77.a_ref), channel_id=1, source_target_pairs={{0,8},{4,12},{8,0},{12,4},{16,24},{20,28},{24,16},{28,20},{1,9},{5... | collective-permute-start | bytes 1671176 | tf_op jit(solution)/shard_map/ppermute | solution.py:707
  299.9 16.5 %collective-permute-start.26 = (bf16[1,136,2048]{2,1,0:T(8,128)(2,1)}, bf16[1,136,2048]{2,1,0:T(8,128)(2,1)}, u32[]{:S(2)}, u32[]{:S(2)}) collective-permute-start(bf16[1,136,2048]{2,1,0:T(8,128)(2,1)} %shard_map.83.a_ref), channel_id=1, source_target_pairs={{0,8},{4,12},{8,0},{12,4},{16,24},{20,28},{24,16},{28,20},{1,9},{5... | collective-permute-start | bytes 1671176 | tf_op jit(solution)/shard_map/ppermute | solution.py:707
  318.5 3.9 collective-permute-start.27
  322.4 24.0 %shard_map.78.a_ref = bf16[3,136,2048]{2,1,0:T(8,128)(2,1)} custom-call(s32[12]{0:T(128)} %get-tuple-element.14.refs_0_, s32[12]{0:T(128)} %get-tuple-element.15.refs_1_, s32[12]{0:T(128)} %get-tuple-element.16.refs_2_, bf16[384,2048]{1,0:T(8,128)(2,1)} %collective-permute-done.2.refs_3_, bf16[16,2,512,256]{3,2,1,0:T(8,128)(2,1)} %bitcast.12, ...), custom_call_target="tpu_custom_call" | custom-call | flops 3221225472 | bytes 3145728 | tf_op jit(solution)/shard_map/pallas_call | solution.py:609
  352.8 2.4 shard_map.92.refs_0_
  355.2 2.4 shard_map.93.refs_1_
  357.5 2.4 shard_map.94.refs_2_
  359.9 10.0 %project_far.1 = (bf16[2,384,512]{2,1,0:T(8,128)(2,1)}, bf16[2,384,512]{2,1,0:T(8,128)(2,1)}) custom-call(bf16[128,2048]{1,0:T(8,128)(2,1)} %shard_map.92.refs_0_, bf16[128,2048]{1,0:T(8,128)(2,1)} %shard_map.93.refs_1_, bf16[128,2048]{1,0:T(8,128)(2,1)} %shard_map.94.refs_2_, bf16[2048,512]{1,0:T(8,128)(2,1)} %refs_3_.3, ...), custom_call_target="tpu_custom_call" | custom-call | flops 3221225472 | bytes 8388608 | tf_op jit(solution)/shard_map/project_far/pallas_call | solution.py:949
  371.5 2.4 collective-permute-start.13
  375.9 11.3 %collective-permute-done.13.b_ref = bf16[1,136,2048]{2,1,0:T(8,128)(2,1)} collective-permute-done((bf16[1,136,2048]{2,1,0:T(8,128)(2,1)}, bf16[1,136,2048]{2,1,0:T(8,128)(2,1)}, u32[]{:S(2)}, u32[]{:S(2)}) %collective-permute-start.13) | collective-permute-done | bytes 557088 | tf_op jit(solution)/shard_map/ppermute | solution.py:707
  389.6 9.6 %collective-permute-done.16.b_ref = bf16[1,136,2048]{2,1,0:T(8,128)(2,1)} collective-permute-done((bf16[1,136,2048]{2,1,0:T(8,128)(2,1)}, bf16[1,136,2048]{2,1,0:T(8,128)(2,1)}, u32[]{:S(2)}, u32[]{:S(2)}) %collective-permute-start.16) | collective-permute-done | bytes 557088 | tf_op jit(solution)/shard_map/ppermute | solution.py:707
  401.5 9.3 %collective-permute-done.19.b_ref = bf16[1,136,2048]{2,1,0:T(8,128)(2,1)} collective-permute-done((bf16[1,136,2048]{2,1,0:T(8,128)(2,1)}, bf16[1,136,2048]{2,1,0:T(8,128)(2,1)}, u32[]{:S(2)}, u32[]{:S(2)}) %collective-permute-start.19) | collective-permute-done | bytes 557088 | tf_op jit(solution)/shard_map/ppermute | solution.py:707
  410.8 2.4 shard_map.91.refs_2_
  413.2 21.1 %project_home.1 = bf16[384,1024]{1,0:T(8,128)(2,1)} custom-call(bf16[128,2048]{1,0:T(8,128)(2,1)} %shard_map.81.refs_0_, bf16[128,2048]{1,0:T(8,128)(2,1)} %shard_map.86.refs_1_, bf16[128,2048]{1,0:T(8,128)(2,1)} %shard_map.91.refs_2_, bf16[2048,512]{1,0:T(8,128)(2,1)} %refs_3_.3, bf16[2048,512]{1,0:T(8,128)(2,1)} %collective-permute-done.20.refs_4_, ...), custom_call_target="tpu_custom_call" | custom-call | flops 3221225472 | bytes 8388608 | tf_op jit(solution)/shard_map/project_home/pallas_call | solution.py:949
  (54 shorter events, 61.2 us)
Async XLA Ops:
  0.0 37.8 %collective-permute-start.2 = (bf16[384,2048]{1,0:T(8,128)(2,1)}, bf16[384,2048]{1,0:T(8,128)(2,1)}, u32[]{:S(2)}, u32[]{:S(2)}) collective-permute-start(bf16[384,2048]{1,0:T(8,128)(2,1)} %refs_4_.1), channel_id=1, source_target_pairs={{0,8},{4,12},{8,0},{12,4},{16,24},{20,28},{24,16},{28,20},{1,9},{5... | collective-permute-start | bytes 4718600 | tf_op jit(solution)/shard_map/ppermute | solution.py:707
  3.1 55.4 %collective-permute-start.1 = (bf16[384,2048]{1,0:T(8,128)(2,1)}, bf16[384,2048]{1,0:T(8,128)(2,1)}, u32[]{:S(2)}, u32[]{:S(2)}) collective-permute-start(bf16[384,2048]{1,0:T(8,128)(2,1)} %refs_4_.1), channel_id=1, source_target_pairs={{8,16},{12,20},{16,8},{20,12},{9,17},{13,21},{17,9},{21,13},{10,18... | collective-permute-start | bytes 4718600 | tf_op jit(solution)/shard_map/ppermute | solution.py:707
  37.8 22.1 %collective-permute-start.3 = (bf16[384,2048]{1,0:T(8,128)(2,1)}, bf16[384,2048]{1,0:T(8,128)(2,1)}, u32[]{:S(2)}, u32[]{:S(2)}) collective-permute-start(bf16[384,2048]{1,0:T(8,128)(2,1)} %collective-permute-done.2.refs_3_), channel_id=1, source_target_pairs={{8,16},{12,20},{16,8},{20,12},{9,17},{13,21},{17,9},{21,13},{10,18... | collective-permute-start | bytes 4718600 | tf_op jit(solution)/shard_map/ppermute | solution.py:707
  55.7 38.4 %collective-permute-start.7 = (bf16[3,2,512,256]{3,2,1,0:T(8,128)(2,1)}, bf16[3,2,512,256]{3,2,1,0:T(8,128)(2,1)}, u32[]{:S(2)}, u32[]{:S(2)}) collective-permute-start(bf16[3,2,512,256]{3,2,1,0:T(8,128)(2,1)} %get-tuple-element.19), channel_id=1, source_target_pairs={{0,4},{4,0},{8,12},{12,8},{16,20},{20,16},{24,28},{28,24},{1,5},{5... | collective-permute-start | bytes 4718600 | tf_op jit(solution)/shard_map/ppermute | solution.py:707
  58.5 39.5 %collective-permute-start.6 = (bf16[384,2048]{1,0:T(8,128)(2,1)}, bf16[384,2048]{1,0:T(8,128)(2,1)}, u32[]{:S(2)}, u32[]{:S(2)}) collective-permute-start(bf16[384,2048]{1,0:T(8,128)(2,1)} %collective-permute-done.1.refs_3_), channel_id=1, source_target_pairs={{8,0},{12,4},{16,24},{20,28},{9,1},{13,5},{17,25},{21,29},{10,2},{... | collective-permute-start | bytes 4718600 | tf_op jit(solution)/shard_map/ppermute | solution.py:707
  59.8 68.5 %collective-permute-start.5 = (bf16[3,2,512,256]{3,2,1,0:T(8,128)(2,1)}, bf16[3,2,512,256]{3,2,1,0:T(8,128)(2,1)}, u32[]{:S(2)}, u32[]{:S(2)}) collective-permute-start(bf16[3,2,512,256]{3,2,1,0:T(8,128)(2,1)} %get-tuple-element.18), channel_id=1, source_target_pairs={{0,4},{4,0},{8,12},{12,8},{16,20},{20,16},{24,28},{28,24},{1,5},{5... | collective-permute-start | bytes 4718600 | tf_op jit(solution)/shard_map/ppermute | solution.py:707
  59.9 69.5 %collective-permute-start.4 = (bf16[384,2048]{1,0:T(8,128)(2,1)}, bf16[384,2048]{1,0:T(8,128)(2,1)}, u32[]{:S(2)}, u32[]{:S(2)}) collective-permute-start(bf16[384,2048]{1,0:T(8,128)(2,1)} %collective-permute-done.3.refs_3_), channel_id=1, source_target_pairs={{8,0},{12,4},{16,24},{20,28},{9,1},{13,5},{17,25},{21,29},{10,2},{... | collective-permute-start | bytes 4718600 | tf_op jit(solution)/shard_map/ppermute | solution.py:707
  122.0 38.6 %collective-permute-start.8 = (bf16[3,136,2048]{2,1,0:T(8,128)(2,1)}, bf16[3,136,2048]{2,1,0:T(8,128)(2,1)}, u32[]{:S(2)}, u32[]{:S(2)}) collective-permute-start(bf16[3,136,2048]{2,1,0:T(8,128)(2,1)} %shard_map.75.a_ref), channel_id=1, source_target_pairs={{0,8},{4,12},{24,16},{28,20},{1,9},{5,13},{25,17},{29,21},{2,10},{... | collective-permute-start | bytes 5013512 | tf_op jit(solution)/shard_map/ppermute | solution.py:707
  124.6 81.0 %collective-permute-start.21 = (bf16[2048,512]{1,0:T(8,128)(2,1)}, bf16[2048,512]{1,0:T(8,128)(2,1)}, u32[]{:S(2)}, u32[]{:S(2)}) collective-permute-start(bf16[2048,512]{1,0:T(8,128)(2,1)} %refs_3_.3), channel_id=1, source_target_pairs={{0,16},{4,20},{24,8},{28,12},{1,17},{5,21},{25,9},{29,13},{2,18},{... | collective-permute-start | bytes 6291464 | tf_op jit(solution)/shard_map/ppermute | solution.py:707
  127.3 43.1 %collective-permute-start = (bf16[3,2,512,256]{3,2,1,0:T(8,128)(2,1)}, bf16[3,2,512,256]{3,2,1,0:T(8,128)(2,1)}, u32[]{:S(2)}, u32[]{:S(2)}) collective-permute-start(bf16[3,2,512,256]{3,2,1,0:T(8,128)(2,1)} %get-tuple-element.17), channel_id=1, source_target_pairs={{0,4},{4,0},{8,12},{12,8},{16,20},{20,16},{24,28},{28,24},{1,5},{5... | collective-permute-start | bytes 4718600 | tf_op jit(solution)/shard_map/ppermute | solution.py:707
  128.3 65.1 %collective-permute-start.10 = (bf16[3,2,512,256]{3,2,1,0:T(8,128)(2,1)}, bf16[3,2,512,256]{3,2,1,0:T(8,128)(2,1)}, u32[]{:S(2)}, u32[]{:S(2)}) collective-permute-start(bf16[3,2,512,256]{3,2,1,0:T(8,128)(2,1)} %get-tuple-element.20), channel_id=1, source_target_pairs={{0,4},{4,0},{8,12},{12,8},{16,20},{20,16},{24,28},{28,24},{1,5},{5... | collective-permute-start | bytes 4718600 | tf_op jit(solution)/shard_map/ppermute | solution.py:707
  129.4 96.5 %collective-permute-start.23 = (bf16[2048,512]{1,0:T(8,128)(2,1)}, bf16[2048,512]{1,0:T(8,128)(2,1)}, u32[]{:S(2)}, u32[]{:S(2)}) collective-permute-start(bf16[2048,512]{1,0:T(8,128)(2,1)} %refs_3_.3), channel_id=1, source_target_pairs={{8,24},{12,28},{16,0},{20,4},{9,25},{13,29},{17,1},{21,5},{10,26},... | collective-permute-start | bytes 6291464 | tf_op jit(solution)/shard_map/ppermute | solution.py:707
  160.6 103.6 %collective-permute-start.11 = (bf16[3,136,2048]{2,1,0:T(8,128)(2,1)}, bf16[3,136,2048]{2,1,0:T(8,128)(2,1)}, u32[]{:S(2)}, u32[]{:S(2)}) collective-permute-start(bf16[3,136,2048]{2,1,0:T(8,128)(2,1)} %shard_map.74.a_ref), channel_id=1, source_target_pairs={{0,8},{4,12},{24,16},{28,20},{1,9},{5,13},{25,17},{29,21},{2,10},{... | collective-permute-start | bytes 5013512 | tf_op jit(solution)/shard_map/ppermute | solution.py:707
  170.4 56.5 %collective-permute-start.9 = (bf16[1,136,2048]{2,1,0:T(8,128)(2,1)}, bf16[1,136,2048]{2,1,0:T(8,128)(2,1)}, u32[]{:S(2)}, u32[]{:S(2)}) collective-permute-start(bf16[1,136,2048]{2,1,0:T(8,128)(2,1)} %shard_map.76), channel_id=1, source_target_pairs={{8,16},{12,20},{16,8},{20,12},{9,17},{13,21},{17,9},{21,13},{10,18... | collective-permute-start | bytes 1671176 | tf_op jit(solution)/shard_map/ppermute | solution.py:707
  193.4 35.4 %collective-permute-start.14 = (bf16[1,136,2048]{2,1,0:T(8,128)(2,1)}, bf16[1,136,2048]{2,1,0:T(8,128)(2,1)}, u32[]{:S(2)}, u32[]{:S(2)}) collective-permute-start(bf16[1,136,2048]{2,1,0:T(8,128)(2,1)} %shard_map.82), channel_id=1, source_target_pairs={{8,16},{12,20},{16,8},{20,12},{9,17},{13,21},{17,9},{21,13},{10,18... | collective-permute-start | bytes 1671176 | tf_op jit(solution)/shard_map/ppermute | solution.py:707
  205.6 81.4 %collective-permute-start.17 = (bf16[1,136,2048]{2,1,0:T(8,128)(2,1)}, bf16[1,136,2048]{2,1,0:T(8,128)(2,1)}, u32[]{:S(2)}, u32[]{:S(2)}) collective-permute-start(bf16[1,136,2048]{2,1,0:T(8,128)(2,1)} %shard_map.87), channel_id=1, source_target_pairs={{8,16},{12,20},{16,8},{20,12},{9,17},{13,21},{17,9},{21,13},{10,18... | collective-permute-start | bytes 1671176 | tf_op jit(solution)/shard_map/ppermute | solution.py:707
  225.9 134.0 %collective-permute-start.20 = (bf16[2048,512]{1,0:T(8,128)(2,1)}, bf16[2048,512]{1,0:T(8,128)(2,1)}, u32[]{:S(2)}, u32[]{:S(2)}) collective-permute-start(bf16[2048,512]{1,0:T(8,128)(2,1)} %refs_3_.3), channel_id=1, source_target_pairs={{0,4},{4,0},{8,12},{12,8},{16,20},{20,16},{24,28},{28,24},{1,5},{5... | collective-permute-start | bytes 6291464 | tf_op jit(solution)/shard_map/ppermute | solution.py:707
  226.9 133.0 %collective-permute-start.22 = (bf16[2048,512]{1,0:T(8,128)(2,1)}, bf16[2048,512]{1,0:T(8,128)(2,1)}, u32[]{:S(2)}, u32[]{:S(2)}) collective-permute-start(bf16[2048,512]{1,0:T(8,128)(2,1)} %collective-permute-done.21.refs_5_), channel_id=1, source_target_pairs={{8,12},{12,8},{16,20},{20,16},{9,13},{13,9},{17,21},{21,17},{10,14... | collective-permute-start | bytes 6291464 | tf_op jit(solution)/shard_map/ppermute | solution.py:707
  228.9 131.0 %collective-permute-start.24 = (bf16[2048,512]{1,0:T(8,128)(2,1)}, bf16[2048,512]{1,0:T(8,128)(2,1)}, u32[]{:S(2)}, u32[]{:S(2)}) collective-permute-start(bf16[2048,512]{1,0:T(8,128)(2,1)} %collective-permute-done.23.refs_7_), channel_id=1, source_target_pairs={{0,4},{4,0},{24,28},{28,24},{1,5},{5,1},{25,29},{29,25},{2,6},{6,2... | collective-permute-start | bytes 6291464 | tf_op jit(solution)/shard_map/ppermute | solution.py:707
  264.2 28.5 %collective-permute-start.25 = (bf16[1,136,2048]{2,1,0:T(8,128)(2,1)}, bf16[1,136,2048]{2,1,0:T(8,128)(2,1)}, u32[]{:S(2)}, u32[]{:S(2)}) collective-permute-start(bf16[1,136,2048]{2,1,0:T(8,128)(2,1)} %shard_map.77.a_ref), channel_id=1, source_target_pairs={{0,8},{4,12},{8,0},{12,4},{16,24},{20,28},{24,16},{28,20},{1,9},{5... | collective-permute-start | bytes 1671176 | tf_op jit(solution)/shard_map/ppermute | solution.py:707
  287.0 9.3 %collective-permute-start.12 = (bf16[1,136,2048]{2,1,0:T(8,128)(2,1)}, bf16[1,136,2048]{2,1,0:T(8,128)(2,1)}, u32[]{:S(2)}, u32[]{:S(2)}) collective-permute-start(bf16[1,136,2048]{2,1,0:T(8,128)(2,1)} %shard_map.79), channel_id=1, source_target_pairs={{8,16},{12,20},{16,8},{20,12},{9,17},{13,21},{17,9},{21,13},{10,18... | collective-permute-start | bytes 1671176 | tf_op jit(solution)/shard_map/ppermute | solution.py:707
  292.7 7.2 %collective-permute-start.15 = (bf16[1,136,2048]{2,1,0:T(8,128)(2,1)}, bf16[1,136,2048]{2,1,0:T(8,128)(2,1)}, u32[]{:S(2)}, u32[]{:S(2)}) collective-permute-start(bf16[1,136,2048]{2,1,0:T(8,128)(2,1)} %shard_map.84), channel_id=1, source_target_pairs={{8,16},{12,20},{16,8},{20,12},{9,17},{13,21},{17,9},{21,13},{10,18... | collective-permute-start | bytes 1671176 | tf_op jit(solution)/shard_map/ppermute | solution.py:707
  296.3 22.2 %collective-permute-start.18 = (bf16[1,136,2048]{2,1,0:T(8,128)(2,1)}, bf16[1,136,2048]{2,1,0:T(8,128)(2,1)}, u32[]{:S(2)}, u32[]{:S(2)}) collective-permute-start(bf16[1,136,2048]{2,1,0:T(8,128)(2,1)} %shard_map.89), channel_id=1, source_target_pairs={{8,16},{12,20},{16,8},{20,12},{9,17},{13,21},{17,9},{21,13},{10,18... | collective-permute-start | bytes 1671176 | tf_op jit(solution)/shard_map/ppermute | solution.py:707
  299.9 55.3 %collective-permute-start.26 = (bf16[1,136,2048]{2,1,0:T(8,128)(2,1)}, bf16[1,136,2048]{2,1,0:T(8,128)(2,1)}, u32[]{:S(2)}, u32[]{:S(2)}) collective-permute-start(bf16[1,136,2048]{2,1,0:T(8,128)(2,1)} %shard_map.83.a_ref), channel_id=1, source_target_pairs={{0,8},{4,12},{8,0},{12,4},{16,24},{20,28},{24,16},{28,20},{1,9},{5... | collective-permute-start | bytes 1671176 | tf_op jit(solution)/shard_map/ppermute | solution.py:707
  318.5 39.1 %collective-permute-start.27 = (bf16[1,136,2048]{2,1,0:T(8,128)(2,1)}, bf16[1,136,2048]{2,1,0:T(8,128)(2,1)}, u32[]{:S(2)}, u32[]{:S(2)}) collective-permute-start(bf16[1,136,2048]{2,1,0:T(8,128)(2,1)} %shard_map.88.a_ref), channel_id=1, source_target_pairs={{0,8},{4,12},{8,0},{12,4},{16,24},{20,28},{24,16},{28,20},{1,9},{5... | collective-permute-start | bytes 1671176 | tf_op jit(solution)/shard_map/ppermute | solution.py:707
  369.9 43.3 %collective-permute-start.28 = (bf16[2,384,512]{2,1,0:T(8,128)(2,1)}, bf16[2,384,512]{2,1,0:T(8,128)(2,1)}, u32[]{:S(2)}, u32[]{:S(2)}) collective-permute-start(bf16[2,384,512]{2,1,0:T(8,128)(2,1)} %get-tuple-element.22), channel_id=1, source_target_pairs={{1,3},{3,1},{5,7},{7,5},{8,10},{10,8},{12,14},{14,12},{17,19},{19,... | collective-permute-start | bytes 2359304 | tf_op jit(solution)/shard_map/ppermute | solution.py:765
  371.5 15.7 %collective-permute-start.13 = (bf16[1,136,2048]{2,1,0:T(8,128)(2,1)}, bf16[1,136,2048]{2,1,0:T(8,128)(2,1)}, u32[]{:S(2)}, u32[]{:S(2)}) collective-permute-start(bf16[1,136,2048]{2,1,0:T(8,128)(2,1)} %shard_map.80.a_ref), channel_id=1, source_target_pairs={{0,8},{4,12},{8,0},{12,4},{16,24},{20,28},{24,16},{28,20},{1,9},{5... | collective-permute-start | bytes 1671176 | tf_op jit(solution)/shard_map/ppermute | solution.py:707
  373.9 25.3 %collective-permute-start.16 = (bf16[1,136,2048]{2,1,0:T(8,128)(2,1)}, bf16[1,136,2048]{2,1,0:T(8,128)(2,1)}, u32[]{:S(2)}, u32[]{:S(2)}) collective-permute-start(bf16[1,136,2048]{2,1,0:T(8,128)(2,1)} %shard_map.85.a_ref), channel_id=1, source_target_pairs={{0,8},{4,12},{8,0},{12,4},{16,24},{20,28},{24,16},{28,20},{1,9},{5... | collective-permute-start | bytes 1671176 | tf_op jit(solution)/shard_map/ppermute | solution.py:707
  374.0 36.8 %collective-permute-start.19 = (bf16[1,136,2048]{2,1,0:T(8,128)(2,1)}, bf16[1,136,2048]{2,1,0:T(8,128)(2,1)}, u32[]{:S(2)}, u32[]{:S(2)}) collective-permute-start(bf16[1,136,2048]{2,1,0:T(8,128)(2,1)} %shard_map.90.a_ref), channel_id=1, source_target_pairs={{0,8},{4,12},{8,0},{12,4},{16,24},{20,28},{24,16},{28,20},{1,9},{5... | collective-permute-start | bytes 1671176 | tf_op jit(solution)/shard_map/ppermute | solution.py:707

commit v7 on v5

--- a/solution.py
+++ b/solution.py
@@ -500,26 +500,31 @@
         )
 
 
-def part_kernel(k, most, heads, *refs):
+def part_kernel(k, most, first, last, heads, *refs):
     refs = list(refs)
     row_ref, tag_ref, far_tag_ref = refs.pop(0), refs.pop(0), refs.pop(0)
     own_ref = refs.pop(0) if k == 0 else None
     questions = [refs.pop(0) for _ in range(2 if k > 1 else 1)]
-    cache_ref, items_ref, out_ref, q_ref, m_ref, l_ref, acc_ref, buf, sem, q_sem = refs
+    cache_ref = refs.pop(0)
+    items_ref = refs.pop(0) if last > most else None
+    out_ref, q_ref, m_ref, l_ref, acc_ref, buf, sem, q_sem = refs
     per_device = q_ref.shape[0] // LQ
-    entries = 2 * most
 
     def fetch(i, slot):
-        @pl.when(i < most)
-        def _():
-            row = row_ref[k * most + jnp.minimum(i, most - 1)]
-            pltpu.make_async_copy(cache_ref.at[row], buf.at[slot], sem.at[slot]).start()
-
-        @pl.when(i >= most)
-        def _():
-            pltpu.make_async_copy(
-                items_ref.at[jnp.maximum(i - most, 0)], buf.at[slot], sem.at[slot]
-            ).start()
+        if first < most:
+
+            @pl.when(i < most)
+            def _():
+                row = row_ref[k * most + jnp.minimum(i, most - 1)]
+                pltpu.make_async_copy(cache_ref.at[row], buf.at[slot], sem.at[slot]).start()
+
+        if last > most:
+
+            @pl.when(i >= most)
+            def _():
+                pltpu.make_async_copy(
+                    items_ref.at[jnp.maximum(i - most, 0)], buf.at[slot], sem.at[slot]
+                ).start()
 
     if len(questions) == 1:
         pltpu.make_async_copy(questions[0], q_ref, q_sem).start()
@@ -534,7 +539,7 @@
         def _():
             pltpu.make_async_copy(questions[1], q_ref, q_sem).start()
 
-    fetch(jnp.int32(0), 0)
+    fetch(jnp.int32(first), first % 2)
     m_ref[...] = jnp.full(m_ref.shape, NEG, jnp.float32)
     l_ref[...] = jnp.zeros(l_ref.shape, jnp.float32)
     acc_ref[...] = jnp.zeros(acc_ref.shape, jnp.float32)
@@ -562,7 +567,7 @@
         slot = lax.rem(i, 2)
         pltpu.make_async_copy(buf.at[slot], buf.at[slot], sem.at[slot]).wait()
 
-        @pl.when(i + 1 < entries)
+        @pl.when(i + 1 < last)
         def _():
             fetch(i + 1, lax.rem(i + 1, 2))
 
@@ -583,7 +588,7 @@
             )
         return carry
 
-    lax.fori_loop(0, entries, item, 0)
+    lax.fori_loop(first, last, item, 0)
     eye = unit()
 
     def close(c, carry):
@@ -612,7 +617,7 @@
     out_ref[question, LQ:, columns] = both.astype(out_ref.dtype)
 
 
-def part_call(k, most, tables, own, questions, cache, items):
+def part_call(k, most, tables, own, questions, cache, items, local=True):
     tokens, columns = questions[0].shape
     heads, item = cache.shape[1], cache.shape[1:]
     state = (tokens // LQ, heads, GROUP * LQ, HD)
@@ -620,11 +625,15 @@
     vmem = pl.BlockSpec(memory_space=pltpu.VMEM)
     anyspace = pl.BlockSpec(memory_space=pl.ANY)
     owned = [own] if k == 0 else []
-    weights = 2 * most * heads * GROUP * LQ * item[1]
+    received = [items] if items is not None else []
+    first, last = 0 if local else most, 2 * most if received else most
+    weights = (last - first) * heads * GROUP * LQ * item[1]
     return pl.pallas_call(
-        functools.partial(part_kernel, k, most, heads),
+        functools.partial(part_kernel, k, most, first, last, heads),
         out_shape=jax.ShapeDtypeStruct((tokens // LQ, LQ + EXTRA, columns), cache.dtype),
-        in_specs=[smem] * 3 + [vmem] * len(owned) + [anyspace] * (len(questions) + 2),
+        in_specs=[smem] * 3
+        + [vmem] * len(owned)
+        + [anyspace] * (len(questions) + 1 + len(received)),
         out_specs=vmem,
         scratch_shapes=[
             pltpu.VMEM((tokens, columns), cache.dtype),
@@ -638,13 +647,13 @@
         compiler_params=pltpu.CompilerParams(vmem_limit_bytes=VMEM_BYTES),
         cost_estimate=pl.CostEstimate(
             flops=weights * HD * 4,
-            bytes_accessed=2 * most * math.prod(item) * 2,
+            bytes_accessed=(last - first) * math.prod(item) * 2,
             transcendentals=weights,
         ),
-    )(*tables, *owned, *questions, cache, items)
-
-
-def blend(a_ref, b_ref, out_ref, leveled):
+    )(*tables, *owned, *questions, cache, *received)
+
+
+def blend(refs, out_ref, leveled):
     eye = unit()
     ones = jnp.ones((2 * LQ, LQ), jnp.bfloat16)
 
@@ -652,26 +661,32 @@
         both = ref[0, LQ:, :].astype(jnp.float32)
         return both[:1] + both[1:2]
 
-    one, two = level_of(a_ref), level_of(b_ref)
-    top = jnp.maximum(one, two)
-    first, second = jnp.exp2(one - top), jnp.exp2(two - top)
-    total = first + second
-    share = first / total
-    high = share.astype(jnp.bfloat16).astype(jnp.float32)
-    low = share - high
-    for c in range(share.shape[1] // HD):
+    levels = [level_of(ref) for ref in refs]
+    top = functools.reduce(jnp.maximum, levels)
+    weights = [jnp.exp2(level - top) for level in levels]
+    total = functools.reduce(jnp.add, weights)
+    shares = []
+    for weight in weights[1:]:
+        share = weight / total
+        high = share.astype(jnp.bfloat16).astype(jnp.float32)
+        shares.append((high, share - high))
+    for c in range(total.shape[1] // HD):
         columns = slice(c * HD, (c + 1) * HD)
-        spread = jnp.concatenate(
-            [
-                jnp.where(eye, jnp.broadcast_to(v[:, columns], (LQ, LQ)), 0.0).astype(jnp.bfloat16)
-                for v in (high, low)
-            ],
-            axis=1,
-        )
-        column = jnp.dot(spread, ones, preferred_element_type=jnp.float32)
-        a = a_ref[0, :LQ, columns].astype(jnp.float32)
-        b = b_ref[0, :LQ, columns].astype(jnp.float32)
-        value = (b + (a - b) * column).astype(out_ref.dtype)
+        base = refs[0][0, :LQ, columns].astype(jnp.float32)
+        value = base
+        for ref, pair in zip(refs[1:], shares):
+            spread = jnp.concatenate(
+                [
+                    jnp.where(eye, jnp.broadcast_to(v[:, columns], (LQ, LQ)), 0.0).astype(
+                        jnp.bfloat16
+                    )
+                    for v in pair
+                ],
+                axis=1,
+            )
+            column = jnp.dot(spread, ones, preferred_element_type=jnp.float32)
+            value = value + (ref[0, :LQ, columns].astype(jnp.float32) - base) * column
+        value = value.astype(out_ref.dtype)
         if leveled:
             out_ref[0, :LQ, columns] = value
         else:
@@ -680,50 +695,51 @@
         store_level(out_ref, 0, slice(None), top + jnp.log2(total))
 
 
-def merge_kernel(a_ref, b_ref, out_ref):
+def merge_kernel(*refs):
+    *parts, out_ref = refs
     inner = is_inner()
 
     @pl.when(inner)
     def _():
-        blend(a_ref, b_ref, out_ref, True)
+        blend(parts, out_ref, True)
 
     @pl.when(jnp.logical_not(inner))
     def _():
-        out_ref[...] = a_ref[...]
+        if len(parts) > 2:
+            blend(parts[:-1], out_ref, True)
+        else:
+            out_ref[...] = parts[0][...]
 
 
 def finish_kernel(a_ref, b_ref, out_ref):
-    blend(a_ref, b_ref, out_ref, False)
+    blend((a_ref, b_ref), out_ref, False)
 
 
 def question_spec(value, at):
     shape = (1,) + value.shape[1:]
     if value.shape[0] == 1:
         return pl.BlockSpec(shape, lambda q: (0, 0, 0))
-    if at is None:
-        return pl.BlockSpec(shape, lambda q: (q, 0, 0))
     return pl.BlockSpec(shape, lambda q: (at, 0, 0))
 
 
-def join_call(a, b, at, leveled):
-    questions = a.shape[0] if at is None else 1
-    columns = a.shape[2]
+def join_call(parts, at, leveled):
+    columns = parts[0].shape[2]
     if leveled:
-        shape, block = (questions,) + a.shape[1:], (1,) + a.shape[1:]
-        out_spec = pl.BlockSpec(block, lambda q: (q, 0, 0))
+        shape = (1,) + parts[0].shape[1:]
+        out_spec = pl.BlockSpec(shape, lambda q: (0, 0, 0))
     else:
-        shape = (questions * LQ, columns)
-        out_spec = pl.BlockSpec((LQ, columns), lambda q: (q, 0))
-    size = questions * LQ * columns
+        shape = (LQ, columns)
+        out_spec = pl.BlockSpec(shape, lambda q: (0, 0))
+    size = LQ * columns
     return pl.pallas_call(
         merge_kernel if leveled else finish_kernel,
-        out_shape=jax.ShapeDtypeStruct(shape, a.dtype),
-        grid=(questions,),
-        in_specs=[question_spec(a, at), question_spec(b, at)],
+        out_shape=jax.ShapeDtypeStruct(shape, parts[0].dtype),
+        grid=(1,),
+        in_specs=[question_spec(part, at) for part in parts],
         out_specs=out_spec,
         compiler_params=pltpu.CompilerParams(vmem_limit_bytes=VMEM_BYTES),
         cost_estimate=pl.CostEstimate(flops=size * 8, bytes_accessed=size * 6, transcendentals=0),
-    )(a, b)
+    )(*parts)
 
 
 def line_steps(queries, own_kv, passage_cache, out_weight, lists, passage_slot, question_slot):
@@ -734,11 +750,11 @@
     def send(value, pairs):
         return lax.ppermute(value, "pass", pairs)
 
-    def part(k, *args):
-        return part_call(k, most, tables, own if k == 0 else None, *args)
-
-    def join(a, b, at=None, leveled=True):
-        return join_call(a, b, at, leveled)
+    def part(k, *args, local=True):
+        return part_call(k, most, tables, own if k == 0 else None, *args, local=local)
+
+    def join(at, *parts, leveled=True):
+        return join_call(parts, at, leveled)
 
     across = [(p, p ^ 1) for p in range(2 * LINE)]
     inner_across = [(p, d) for p, d in across if p // 2 in (1, 2)]
@@ -747,7 +763,9 @@
     inward, outward = mirror(1, "outer"), mirror(1, "inner")
     q_near = send(queries, near)
     q_mid = send(queries, middle)
-    w_across = send(out_weight, across)
+    half = out_weight.shape[0] // 2
+    w_across0 = send(out_weight[:half], across)
+    w_across1 = send(out_weight[half:], across)
     cache = jnp.transpose(passage_cache, (0, 2, 1, 3))
     row, tag, far_tag, *items = sort_items(
         lists, passage_slot, question_slot, cache, most, per_device
@@ -761,7 +779,8 @@
     part2 = part(2, [q_cross, q_out], cache, far[2])
     part3 = part(3, [q_mid, q_end], cache, far[3])
     part0 = part(0, [queries], cache, far[0])
-    part1 = part(1, [q_near], cache, far[1])
+    part1 = part(1, [q_near], cache, None)
+    part1_far = part(1, [q_near], cache, far[1], local=False)
     back2 = send(part2, inward)
     w_in = send(out_weight, mirror(2, "outer"))
     w_out = send(out_weight, mirror(2, "inner"))
@@ -770,15 +789,15 @@
     w_out_both = send(w_out, outer_across)
     own_rows, near_rows = [], []
     for q in range(per_device):
-        cross3 = send(join(part3, back2, q), middle)
-        near0 = join(part0, cross3, q)
+        cross3 = send(join(q, part3, back2), middle)
+        near0 = join(q, part0, cross3)
         beside = send(near0, near)
-        cross2 = send(join(part2, back3, q), middle)
-        near1 = join(part1, cross2, q)
+        cross2 = send(join(q, part2, back3), middle)
+        near1 = join(q, part1, part1_far, cross2)
         back1 = send(near1, near)
-        near_rows.append(join(near1, beside, q, False))
-        own_rows.append(join(near0, back1, q, False))
-    weights = (out_weight, w_across, w_in, w_in_both, w_out, w_out_both)
+        near_rows.append(join(q, near1, beside, leveled=False))
+        own_rows.append(join(q, near0, back1, leveled=False))
+    weights = (out_weight, w_across0, w_across1, w_in, w_in_both, w_out, w_out_both)
     far_send, far_keep = project_call(near_rows, weights, None)
     far_sent = send_far(far_send)
     return project_call(own_rows, weights, (far_keep, far_sent))
@@ -802,8 +821,8 @@
 
 def project_kernel(pieces, far, *refs):
     rows_refs = refs[:pieces]
-    own_ref, across_ref, in_ref, in2_ref, out1_ref, out2_ref = refs[pieces : pieces + 6]
-    refs = refs[pieces + 6 :]
+    own_ref, a0_ref, a1_ref, in_ref, in2_ref, out1_ref, out2_ref = refs[pieces : pieces + 7]
+    refs = refs[pieces + 7 :]
     if far:
         send_ref, keep_ref = refs[:2]
     else:
@@ -827,7 +846,10 @@
 
     def load_here():
         pltpu.make_async_copy(own_ref, w_ref.at[0, x], w_sem.at[0, x]).start()
-        pltpu.make_async_copy(across_ref, w_ref.at[0, 1 - x], w_sem.at[0, 1 - x]).start()
+        half = a0_ref.shape[0]
+        low, high = w_ref.at[0, 1 - x, pl.ds(0, half)], w_ref.at[0, 1 - x, pl.ds(half, half)]
+        pltpu.make_async_copy(a0_ref, low, w_sem.at[0, 1 - x]).start()
+        pltpu.make_async_copy(a1_ref, high, w_sem.at[0, 1 - x]).start()
 
     def load_there():
         for which, (one, two) in (

time: 421 us -> 412 us (0.979)
  waiting for transfers between devices: 173 us -> 144 us
  Pallas kernels: 146 us -> 154 us
  starting transfers between devices: 89.3 us -> 97.1 us
    ppermute x28 -> x29, waiting for transfers between devices: 173 us -> 144 us  [send(): return lax.ppermute(value, 'pass', pairs)]
    ppermute x28 -> x29, starting transfers between devices: 87.7 us -> 95.5 us  [send(): return lax.ppermute(value, 'pass', pairs)]
    pallas_call x4 -> x5, Pallas kernels: 66.8 us -> 71.8 us  [part_call(): pl.pallas_call(functools.partial(part_kernel, k, most, first, last, heads...]
  transfers between devices with their start and end apart: 29 -> 30, of which waited for: 12 -> 12; matrix products, arithmetic and copies ran while one was open for 2% -> 3% of each run, Pallas kernels for 27% -> 30%
where the time goes in v7:
time: 412 us; the launch traced here: 410 us
  Pallas kernels  154 us (37%)
  waiting for transfers between devices  144 us (35%)
  starting transfers between devices  97.1 us (24%)
  local copies, waits for them, and re-layouts  15.1 us (4%)
    ppermute x29, waiting for transfers between devices, send(): return lax.ppermute(value, 'pass', pairs)  144 us
    ppermute x29, starting transfers between devices, send(): return lax.ppermute(value, 'pass', pairs)  95.5 us
    pallas_call x5, Pallas kernels, part_call(): pl.pallas_call(functools.partial(part_kernel, k, most, first, last, heads...  71.8 us
    pallas_call x18, Pallas kernels, join_call(): pl.pallas_call(merge_kernel if leveled else finish_kernel, out_shape=jax....  41.5 us
    pallas_call x2, Pallas kernels, project_call(): pl.pallas_call(functools.partial(project_kernel, len(pieces), far), out_s...  32.8 us
    unnamed x2, local copies, waits for them, and re-layouts  10.2 us
  transfers between devices with their start and end apart: 30, of which 12 were waited for; matrix products, arithmetic and copies ran while one was open for 3% of the time, Pallas kernels for 30%

profile of v7, /device:TPU:0, one launch (start us, length us, event | category | flops | bytes accessed | tf_op | source)
XLA Modules:
  0.0 410.4 jit_solution(16056095950809668702)
XLA Ops:
  0.0 3.1 collective-permute-start.2
  4.9 32.9 %collective-permute-done.2.refs_3_ = bf16[384,2048]{1,0:T(8,128)(2,1)} collective-permute-done((bf16[384,2048]{1,0:T(8,128)(2,1)}, bf16[384,2048]{1,0:T(8,128)(2,1)}, u32[]{:S(2)}, u32[]{:S(2)}) %collective-permute-start.2) | collective-permute-done | bytes 1572896 | tf_op jit(solution)/shard_map/ppermute | solution.py:751
  39.6 8.2 %copy.16 = bf16[16,512,2,256]{3,1,2,0:T(8,128)(2,1)} copy(bf16[16,512,2,256]{3,2,1,0:T(2,128)(2,1)} %param.9) | data formatting | bytes 16777216 | tf_op args[2]
  47.8 7.9 %sort_items.1 = (s32[12]{0:T(128)}, s32[12]{0:T(128)}, s32[12]{0:T(128)}, bf16[3,2,512,256]{3,2,1,0:T(8,128)(2,1)}, bf16[3,2,512,256]{3,2,1,0:T(8,128)(2,1)}, /*...) custom-call(s32[8,24]{1,0:T(8,128)} %bitcast.16, s32[128]{0:T(128)} %pslot_ref.1, s32[24]{0:T(128)} %qslot_ref.1, ...), custom_call_target="tpu_custom_call" | custom-call | bytes 12582912 | tf_op jit(solution)/shard_map/sort_items/pallas_call | solution.py:437
  55.7 2.8 collective-permute-start.7
  61.2 32.9 %collective-permute-done.7.refs_6_ = bf16[3,2,512,256]{3,2,1,0:T(8,128)(2,1)} collective-permute-done((bf16[3,2,512,256]{3,2,1,0:T(8,128)(2,1)}, bf16[3,2,512,256]{3,2,1,0:T(8,128)(2,1)}, u32[]{:S(2)}, u32[]{:S(2)}) %collective-permute-start.7) | collective-permute-done | bytes 1572896 | tf_op jit(solution)/shard_map/ppermute | solution.py:751
  94.1 3.9 collective-permute-done.6.refs_4_
  98.0 15.6 %shard_map.75.refs_0_ = bf16[3,136,2048]{2,1,0:T(8,128)(2,1)} custom-call(s32[12]{0:T(128)} %get-tuple-element.14.refs_0_, s32[12]{0:T(128)} %get-tuple-element.15.refs_1_, s32[12]{0:T(128)} %get-tuple-element.16.refs_2_, bf16[384,2048]{1,0:T(8,128)(2,1)} %collective-permute-done.3.refs_3_, bf16[384,2048]{1,0:T(8,128)(2,1)} %collective-permute-done.6.refs_4_, ...), custom_call_target="tpu_custom_call" | custom-call | flops 3221225472 | bytes 3145728 | tf_op jit(solution)/shard_map/pallas_call | solution.py:631
  113.5 2.6 collective-permute-start.8
  117.2 2.7 collective-permute-start.22
  119.9 7.9 %collective-permute-done.5.refs_6_ = bf16[3,2,512,256]{3,2,1,0:T(8,128)(2,1)} collective-permute-done((bf16[3,2,512,256]{3,2,1,0:T(8,128)(2,1)}, bf16[3,2,512,256]{3,2,1,0:T(8,128)(2,1)}, u32[]{:S(2)}, u32[]{:S(2)}) %collective-permute-start.5) | collective-permute-done | bytes 1572896 | tf_op jit(solution)/shard_map/ppermute | solution.py:751
  131.1 15.5 %shard_map.74.refs_0_ = bf16[3,136,2048]{2,1,0:T(8,128)(2,1)} custom-call(s32[12]{0:T(128)} %get-tuple-element.14.refs_0_, s32[12]{0:T(128)} %get-tuple-element.15.refs_1_, s32[12]{0:T(128)} %get-tuple-element.16.refs_2_, bf16[384,2048]{1,0:T(8,128)(2,1)} %collective-permute-done.1.refs_3_, bf16[384,2048]{1,0:T(8,128)(2,1)} %collective-permute-done.4.refs_4_, ...), custom_call_target="tpu_custom_call" | custom-call | flops 3221225472 | bytes 3145728 | tf_op jit(solution)/shard_map/pallas_call | solution.py:631
  146.6 5.6 %collective-permute-done.8.refs_1_ = bf16[3,136,2048]{2,1,0:T(8,128)(2,1)} collective-permute-done((bf16[3,136,2048]{2,1,0:T(8,128)(2,1)}, bf16[3,136,2048]{2,1,0:T(8,128)(2,1)}, u32[]{:S(2)}, u32[]{:S(2)}) %collective-permute-start.8) | collective-permute-done | bytes 1671200 | tf_op jit(solution)/shard_map/ppermute | solution.py:751
  152.2 5.6 %collective-permute-start.11 = (bf16[3,136,2048]{2,1,0:T(8,128)(2,1)}, bf16[3,136,2048]{2,1,0:T(8,128)(2,1)}, u32[]{:S(2)}, u32[]{:S(2)}) collective-permute-start(bf16[3,136,2048]{2,1,0:T(8,128)(2,1)} %shard_map.74.refs_0_), channel_id=1, source_target_pairs={{0,8},{4,12},{24,16},{28,20},{1,9},{5,13},{25,17},{29,21},{2,10},{... | collective-permute-start | bytes 5013512 | tf_op jit(solution)/shard_map/ppermute | solution.py:751
  165.1 28.4 %collective-permute-done.10.refs_5_ = bf16[3,2,512,256]{3,2,1,0:T(8,128)(2,1)} collective-permute-done((bf16[3,2,512,256]{3,2,1,0:T(8,128)(2,1)}, bf16[3,2,512,256]{3,2,1,0:T(8,128)(2,1)}, u32[]{:S(2)}, u32[]{:S(2)}) %collective-permute-start.10) | collective-permute-done | bytes 1572896 | tf_op jit(solution)/shard_map/ppermute | solution.py:751
  196.8 20.3 %shard_map.73.refs_0_ = bf16[3,136,2048]{2,1,0:T(8,128)(2,1)} custom-call(s32[12]{0:T(128)} %get-tuple-element.14.refs_0_, s32[12]{0:T(128)} %get-tuple-element.15.refs_1_, s32[12]{0:T(128)} %get-tuple-element.16.refs_2_, bf16[3,2,128,256]{3,2,1,0:T(8,128)(2,1)} %bitcast.14, bf16[384,2048]{1,0:T(8,128)(2,1)} %refs_4_.1, bf16[16,2,512,256]{3,2,1,0:T(8,128)(2,1)} %bitcast.11, ...), custom_call_target="tpu_custom_call" | custom-call | flops 3221225472 | bytes 3145728 | tf_op jit(solution)/shard_map/pallas_call | solution.py:631
  222.7 22.2 %collective-permute-start.26 = (bf16[1,136,2048]{2,1,0:T(8,128)(2,1)}, bf16[1,136,2048]{2,1,0:T(8,128)(2,1)}, u32[]{:S(2)}, u32[]{:S(2)}) collective-permute-start(bf16[1,136,2048]{2,1,0:T(8,128)(2,1)} %shard_map.77.a_ref), channel_id=1, source_target_pairs={{0,8},{4,12},{8,0},{12,4},{16,24},{20,28},{24,16},{28,20},{1,9},{5... | collective-permute-start | bytes 1671176 | tf_op jit(solution)/shard_map/ppermute | solution.py:751
  251.3 3.9 collective-permute-start.27
  266.1 3.1 fusion
  273.3 23.2 %collective-permute-start.28 = (bf16[1,136,2048]{2,1,0:T(8,128)(2,1)}, bf16[1,136,2048]{2,1,0:T(8,128)(2,1)}, u32[]{:S(2)}, u32[]{:S(2)}) collective-permute-start(bf16[1,136,2048]{2,1,0:T(8,128)(2,1)} %shard_map.89.a_ref), channel_id=1, source_target_pairs={{0,8},{4,12},{8,0},{12,4},{16,24},{20,28},{24,16},{28,20},{1,9},{5... | collective-permute-start | bytes 1671176 | tf_op jit(solution)/shard_map/ppermute | solution.py:751
  296.4 10.2 %shard_map.78.refs_0_ = bf16[3,136,2048]{2,1,0:T(8,128)(2,1)} custom-call(s32[12]{0:T(128)} %get-tuple-element.14.refs_0_, s32[12]{0:T(128)} %get-tuple-element.15.refs_1_, s32[12]{0:T(128)} %get-tuple-element.16.refs_2_, bf16[384,2048]{1,0:T(8,128)(2,1)} %collective-permute-done.2.refs_3_, bf16[16,2,512,256]{3,2,1,0:T(8,128)(2,1)} %bitcast.12), custom_call_target="tpu_custom_call" | custom-call | flops 1610612736 | bytes 1572864 | tf_op jit(solution)/shard_map/pallas_call | solution.py:631
  306.6 10.2 %shard_map.79.refs_1_ = bf16[3,136,2048]{2,1,0:T(8,128)(2,1)} custom-call(s32[12]{0:T(128)} %get-tuple-element.14.refs_0_, s32[12]{0:T(128)} %get-tuple-element.15.refs_1_, s32[12]{0:T(128)} %get-tuple-element.16.refs_2_, bf16[384,2048]{1,0:T(8,128)(2,1)} %collective-permute-done.2.refs_3_, bf16[16,2,512,256]{3,2,1,0:T(8,128)(2,1)} %bitcast.13, ...), custom_call_target="tpu_custom_call" | custom-call | flops 1610612736 | bytes 1572864 | tf_op jit(solution)/shard_map/pallas_call | solution.py:631
  316.8 2.7 shard_map.81.a_ref
  319.5 2.6 shard_map.86.a_ref
  322.1 2.6 shard_map.91.a_ref
  329.7 2.5 shard_map.95.refs_2_
  334.0 8.8 %project_far.1 = (bf16[2,384,512]{2,1,0:T(8,128)(2,1)}, bf16[2,384,512]{2,1,0:T(8,128)(2,1)}) custom-call(bf16[128,2048]{1,0:T(8,128)(2,1)} %shard_map.93.refs_0_, bf16[128,2048]{1,0:T(8,128)(2,1)} %shard_map.94.refs_1_, bf16[128,2048]{1,0:T(8,128)(2,1)} %shard_map.95.refs_2_, bf16[2048,512]{1,0:T(8,128)(2,1)} %refs_3_.3, ...), custom_call_target="tpu_custom_call" | custom-call | flops 3221225472 | bytes 8388608 | tf_op jit(solution)/shard_map/project_far/pallas_call | solution.py:999
  348.1 9.8 %collective-permute-done.13.b_ref = bf16[1,136,2048]{2,1,0:T(8,128)(2,1)} collective-permute-done((bf16[1,136,2048]{2,1,0:T(8,128)(2,1)}, bf16[1,136,2048]{2,1,0:T(8,128)(2,1)}, u32[]{:S(2)}, u32[]{:S(2)}) %collective-permute-start.13) | collective-permute-done | bytes 557088 | tf_op jit(solution)/shard_map/ppermute | solution.py:751
  357.9 2.5 shard_map.82.refs_0_
  360.4 9.4 %collective-permute-done.16.b_ref = bf16[1,136,2048]{2,1,0:T(8,128)(2,1)} collective-permute-done((bf16[1,136,2048]{2,1,0:T(8,128)(2,1)}, bf16[1,136,2048]{2,1,0:T(8,128)(2,1)}, u32[]{:S(2)}, u32[]{:S(2)}) %collective-permute-start.16) | collective-permute-done | bytes 557088 | tf_op jit(solution)/shard_map/ppermute | solution.py:751
  372.3 9.5 %collective-permute-done.19.b_ref = bf16[1,136,2048]{2,1,0:T(8,128)(2,1)} collective-permute-done((bf16[1,136,2048]{2,1,0:T(8,128)(2,1)}, bf16[1,136,2048]{2,1,0:T(8,128)(2,1)}, u32[]{:S(2)}, u32[]{:S(2)}) %collective-permute-start.19) | collective-permute-done | bytes 557088 | tf_op jit(solution)/shard_map/ppermute | solution.py:751
  384.3 24.1 %project_home.1 = bf16[384,1024]{1,0:T(8,128)(2,1)} custom-call(bf16[128,2048]{1,0:T(8,128)(2,1)} %shard_map.82.refs_0_, bf16[128,2048]{1,0:T(8,128)(2,1)} %shard_map.87.refs_1_, bf16[128,2048]{1,0:T(8,128)(2,1)} %shard_map.92.refs_2_, bf16[2048,512]{1,0:T(8,128)(2,1)} %refs_3_.3, bf16[1024,512]{1,0:T(8,128)(2,1)} %collective-permute-done.20.refs_4_, ...), custom_call_target="tpu_custom_call" | custom-call | flops 3221225472 | bytes 8388608 | tf_op jit(solution)/shard_map/project_home/pallas_call | solution.py:999
  (58 shorter events, 67.4 us)
Async XLA Ops:
  0.0 37.8 %collective-permute-start.2 = (bf16[384,2048]{1,0:T(8,128)(2,1)}, bf16[384,2048]{1,0:T(8,128)(2,1)}, u32[]{:S(2)}, u32[]{:S(2)}) collective-permute-start(bf16[384,2048]{1,0:T(8,128)(2,1)} %refs_4_.1), channel_id=1, source_target_pairs={{0,8},{4,12},{8,0},{12,4},{16,24},{20,28},{24,16},{28,20},{1,9},{5... | collective-permute-start | bytes 4718600 | tf_op jit(solution)/shard_map/ppermute | solution.py:751
  3.1 55.5 %collective-permute-start.1 = (bf16[384,2048]{1,0:T(8,128)(2,1)}, bf16[384,2048]{1,0:T(8,128)(2,1)}, u32[]{:S(2)}, u32[]{:S(2)}) collective-permute-start(bf16[384,2048]{1,0:T(8,128)(2,1)} %refs_4_.1), channel_id=1, source_target_pairs={{8,16},{12,20},{16,8},{20,12},{9,17},{13,21},{17,9},{21,13},{10,18... | collective-permute-start | bytes 4718600 | tf_op jit(solution)/shard_map/ppermute | solution.py:751
  37.8 22.1 %collective-permute-start.3 = (bf16[384,2048]{1,0:T(8,128)(2,1)}, bf16[384,2048]{1,0:T(8,128)(2,1)}, u32[]{:S(2)}, u32[]{:S(2)}) collective-permute-start(bf16[384,2048]{1,0:T(8,128)(2,1)} %collective-permute-done.2.refs_3_), channel_id=1, source_target_pairs={{8,16},{12,20},{16,8},{20,12},{9,17},{13,21},{17,9},{21,13},{10,18... | collective-permute-start | bytes 4718600 | tf_op jit(solution)/shard_map/ppermute | solution.py:751
  55.7 38.4 %collective-permute-start.7 = (bf16[3,2,512,256]{3,2,1,0:T(8,128)(2,1)}, bf16[3,2,512,256]{3,2,1,0:T(8,128)(2,1)}, u32[]{:S(2)}, u32[]{:S(2)}) collective-permute-start(bf16[3,2,512,256]{3,2,1,0:T(8,128)(2,1)} %get-tuple-element.19), channel_id=1, source_target_pairs={{0,4},{4,0},{8,12},{12,8},{16,20},{20,16},{24,28},{28,24},{1,5},{5... | collective-permute-start | bytes 4718600 | tf_op jit(solution)/shard_map/ppermute | solution.py:751
  58.5 39.5 %collective-permute-start.6 = (bf16[384,2048]{1,0:T(8,128)(2,1)}, bf16[384,2048]{1,0:T(8,128)(2,1)}, u32[]{:S(2)}, u32[]{:S(2)}) collective-permute-start(bf16[384,2048]{1,0:T(8,128)(2,1)} %collective-permute-done.1.refs_3_), channel_id=1, source_target_pairs={{8,0},{12,4},{16,24},{20,28},{9,1},{13,5},{17,25},{21,29},{10,2},{... | collective-permute-start | bytes 4718600 | tf_op jit(solution)/shard_map/ppermute | solution.py:751
  59.8 68.0 %collective-permute-start.5 = (bf16[3,2,512,256]{3,2,1,0:T(8,128)(2,1)}, bf16[3,2,512,256]{3,2,1,0:T(8,128)(2,1)}, u32[]{:S(2)}, u32[]{:S(2)}) collective-permute-start(bf16[3,2,512,256]{3,2,1,0:T(8,128)(2,1)} %get-tuple-element.18), channel_id=1, source_target_pairs={{0,4},{4,0},{8,12},{12,8},{16,20},{20,16},{24,28},{28,24},{1,5},{5... | collective-permute-start | bytes 4718600 | tf_op jit(solution)/shard_map/ppermute | solution.py:751
  59.9 69.9 %collective-permute-start.4 = (bf16[384,2048]{1,0:T(8,128)(2,1)}, bf16[384,2048]{1,0:T(8,128)(2,1)}, u32[]{:S(2)}, u32[]{:S(2)}) collective-permute-start(bf16[384,2048]{1,0:T(8,128)(2,1)} %collective-permute-done.3.refs_3_), channel_id=1, source_target_pairs={{8,0},{12,4},{16,24},{20,28},{9,1},{13,5},{17,25},{21,29},{10,2},{... | collective-permute-start | bytes 4718600 | tf_op jit(solution)/shard_map/ppermute | solution.py:751
  113.5 38.6 %collective-permute-start.8 = (bf16[3,136,2048]{2,1,0:T(8,128)(2,1)}, bf16[3,136,2048]{2,1,0:T(8,128)(2,1)}, u32[]{:S(2)}, u32[]{:S(2)}) collective-permute-start(bf16[3,136,2048]{2,1,0:T(8,128)(2,1)} %shard_map.75.refs_0_), channel_id=1, source_target_pairs={{0,8},{4,12},{24,16},{28,20},{1,9},{5,13},{25,17},{29,21},{2,10},{... | collective-permute-start | bytes 5013512 | tf_op jit(solution)/shard_map/ppermute | solution.py:751
  116.2 45.3 %collective-permute-start = (bf16[3,2,512,256]{3,2,1,0:T(8,128)(2,1)}, bf16[3,2,512,256]{3,2,1,0:T(8,128)(2,1)}, u32[]{:S(2)}, u32[]{:S(2)}) collective-permute-start(bf16[3,2,512,256]{3,2,1,0:T(8,128)(2,1)} %get-tuple-element.17), channel_id=1, source_target_pairs={{0,4},{4,0},{8,12},{12,8},{16,20},{20,16},{24,28},{28,24},{1,5},{5... | collective-permute-start | bytes 4718600 | tf_op jit(solution)/shard_map/ppermute | solution.py:751
  117.2 105.5 %collective-permute-start.22 = (bf16[2048,512]{1,0:T(8,128)(2,1)}, bf16[2048,512]{1,0:T(8,128)(2,1)}, u32[]{:S(2)}, u32[]{:S(2)}) collective-permute-start(bf16[2048,512]{1,0:T(8,128)(2,1)} %refs_3_.3), channel_id=1, source_target_pairs={{0,16},{4,20},{24,8},{28,12},{1,17},{5,21},{25,9},{29,13},{2,18},{... | collective-permute-start | bytes 6291464 | tf_op jit(solution)/shard_map/ppermute | solution.py:751
  127.8 65.7 %collective-permute-start.10 = (bf16[3,2,512,256]{3,2,1,0:T(8,128)(2,1)}, bf16[3,2,512,256]{3,2,1,0:T(8,128)(2,1)}, u32[]{:S(2)}, u32[]{:S(2)}) collective-permute-start(bf16[3,2,512,256]{3,2,1,0:T(8,128)(2,1)} %get-tuple-element.20), channel_id=1, source_target_pairs={{0,4},{4,0},{8,12},{12,8},{16,20},{20,16},{24,28},{28,24},{1,5},{5... | collective-permute-start | bytes 4718600 | tf_op jit(solution)/shard_map/ppermute | solution.py:751
  129.8 115.1 %collective-permute-start.24 = (bf16[2048,512]{1,0:T(8,128)(2,1)}, bf16[2048,512]{1,0:T(8,128)(2,1)}, u32[]{:S(2)}, u32[]{:S(2)}) collective-permute-start(bf16[2048,512]{1,0:T(8,128)(2,1)} %refs_3_.3), channel_id=1, source_target_pairs={{8,24},{12,28},{16,0},{20,4},{9,25},{13,29},{17,1},{21,5},{10,26},... | collective-permute-start | bytes 6291464 | tf_op jit(solution)/shard_map/ppermute | solution.py:751
  152.2 99.2 %collective-permute-start.11 = (bf16[3,136,2048]{2,1,0:T(8,128)(2,1)}, bf16[3,136,2048]{2,1,0:T(8,128)(2,1)}, u32[]{:S(2)}, u32[]{:S(2)}) collective-permute-start(bf16[3,136,2048]{2,1,0:T(8,128)(2,1)} %shard_map.74.refs_0_), channel_id=1, source_target_pairs={{0,8},{4,12},{24,16},{28,20},{1,9},{5,13},{25,17},{29,21},{2,10},{... | collective-permute-start | bytes 5013512 | tf_op jit(solution)/shard_map/ppermute | solution.py:751
  161.5 57.7 %collective-permute-start.9 = (bf16[1,136,2048]{2,1,0:T(8,128)(2,1)}, bf16[1,136,2048]{2,1,0:T(8,128)(2,1)}, u32[]{:S(2)}, u32[]{:S(2)}) collective-permute-start(bf16[1,136,2048]{2,1,0:T(8,128)(2,1)} %shard_map.76), channel_id=1, source_target_pairs={{8,16},{12,20},{16,8},{20,12},{9,17},{13,21},{17,9},{21,13},{10,18... | collective-permute-start | bytes 1671176 | tf_op jit(solution)/shard_map/ppermute | solution.py:751
  193.5 53.3 %collective-permute-start.14 = (bf16[1,136,2048]{2,1,0:T(8,128)(2,1)}, bf16[1,136,2048]{2,1,0:T(8,128)(2,1)}, u32[]{:S(2)}, u32[]{:S(2)}) collective-permute-start(bf16[1,136,2048]{2,1,0:T(8,128)(2,1)} %shard_map.83), channel_id=1, source_target_pairs={{8,16},{12,20},{16,8},{20,12},{9,17},{13,21},{17,9},{21,13},{10,18... | collective-permute-start | bytes 1671176 | tf_op jit(solution)/shard_map/ppermute | solution.py:751
  219.2 38.1 %collective-permute-start.17 = (bf16[1,136,2048]{2,1,0:T(8,128)(2,1)}, bf16[1,136,2048]{2,1,0:T(8,128)(2,1)}, u32[]{:S(2)}, u32[]{:S(2)}) collective-permute-start(bf16[1,136,2048]{2,1,0:T(8,128)(2,1)} %shard_map.88), channel_id=1, source_target_pairs={{8,16},{12,20},{16,8},{20,12},{9,17},{13,21},{17,9},{21,13},{10,18... | collective-permute-start | bytes 1671176 | tf_op jit(solution)/shard_map/ppermute | solution.py:751
  222.7 38.1 %collective-permute-start.26 = (bf16[1,136,2048]{2,1,0:T(8,128)(2,1)}, bf16[1,136,2048]{2,1,0:T(8,128)(2,1)}, u32[]{:S(2)}, u32[]{:S(2)}) collective-permute-start(bf16[1,136,2048]{2,1,0:T(8,128)(2,1)} %shard_map.77.a_ref), channel_id=1, source_target_pairs={{0,8},{4,12},{8,0},{12,4},{16,24},{20,28},{24,16},{28,20},{1,9},{5... | collective-permute-start | bytes 1671176 | tf_op jit(solution)/shard_map/ppermute | solution.py:751
  244.9 89.2 %collective-permute-start.23 = (bf16[2048,512]{1,0:T(8,128)(2,1)}, bf16[2048,512]{1,0:T(8,128)(2,1)}, u32[]{:S(2)}, u32[]{:S(2)}) collective-permute-start(bf16[2048,512]{1,0:T(8,128)(2,1)} %collective-permute-done.22.refs_6_), channel_id=1, source_target_pairs={{8,12},{12,8},{16,20},{20,16},{9,13},{13,9},{17,21},{21,17},{10,14... | collective-permute-start | bytes 6291464 | tf_op jit(solution)/shard_map/ppermute | solution.py:751
  246.8 87.2 %collective-permute-start.25 = (bf16[2048,512]{1,0:T(8,128)(2,1)}, bf16[2048,512]{1,0:T(8,128)(2,1)}, u32[]{:S(2)}, u32[]{:S(2)}) collective-permute-start(bf16[2048,512]{1,0:T(8,128)(2,1)} %collective-permute-done.24.refs_8_), channel_id=1, source_target_pairs={{0,4},{4,0},{24,28},{28,24},{1,5},{5,1},{25,29},{29,25},{2,6},{6,2... | collective-permute-start | bytes 6291464 | tf_op jit(solution)/shard_map/ppermute | solution.py:751
  251.3 13.3 %collective-permute-start.27 = (bf16[1,136,2048]{2,1,0:T(8,128)(2,1)}, bf16[1,136,2048]{2,1,0:T(8,128)(2,1)}, u32[]{:S(2)}, u32[]{:S(2)}) collective-permute-start(bf16[1,136,2048]{2,1,0:T(8,128)(2,1)} %shard_map.84.a_ref), channel_id=1, source_target_pairs={{0,8},{4,12},{8,0},{12,4},{16,24},{20,28},{24,16},{28,20},{1,9},{5... | collective-permute-start | bytes 1671176 | tf_op jit(solution)/shard_map/ppermute | solution.py:751
  257.3 11.9 %collective-permute-start.12 = (bf16[1,136,2048]{2,1,0:T(8,128)(2,1)}, bf16[1,136,2048]{2,1,0:T(8,128)(2,1)}, u32[]{:S(2)}, u32[]{:S(2)}) collective-permute-start(bf16[1,136,2048]{2,1,0:T(8,128)(2,1)} %shard_map.80), channel_id=1, source_target_pairs={{8,16},{12,20},{16,8},{20,12},{9,17},{13,21},{17,9},{21,13},{10,18... | collective-permute-start | bytes 1671176 | tf_op jit(solution)/shard_map/ppermute | solution.py:751
  260.8 8.9 %collective-permute-start.15 = (bf16[1,136,2048]{2,1,0:T(8,128)(2,1)}, bf16[1,136,2048]{2,1,0:T(8,128)(2,1)}, u32[]{:S(2)}, u32[]{:S(2)}) collective-permute-start(bf16[1,136,2048]{2,1,0:T(8,128)(2,1)} %shard_map.85), channel_id=1, source_target_pairs={{8,16},{12,20},{16,8},{20,12},{9,17},{13,21},{17,9},{21,13},{10,18... | collective-permute-start | bytes 1671176 | tf_op jit(solution)/shard_map/ppermute | solution.py:751
  264.6 8.6 %collective-permute-start.18 = (bf16[1,136,2048]{2,1,0:T(8,128)(2,1)}, bf16[1,136,2048]{2,1,0:T(8,128)(2,1)}, u32[]{:S(2)}, u32[]{:S(2)}) collective-permute-start(bf16[1,136,2048]{2,1,0:T(8,128)(2,1)} %shard_map.90), channel_id=1, source_target_pairs={{8,16},{12,20},{16,8},{20,12},{9,17},{13,21},{17,9},{21,13},{10,18... | collective-permute-start | bytes 1671176 | tf_op jit(solution)/shard_map/ppermute | solution.py:751
  269.2 63.0 %collective-permute-start.20 = (bf16[1024,512]{1,0:T(8,128)(2,1)}, bf16[1024,512]{1,0:T(8,128)(2,1)}, u32[]{:S(2)}, u32[]{:S(2)}) collective-permute-start(bf16[1024,512]{1,0:T(8,128)(2,1)} %get-tuple-element.24), channel_id=1, source_target_pairs={{0,4},{4,0},{8,12},{12,8},{16,20},{20,16},{24,28},{28,24},{1,5},{5... | collective-permute-start | bytes 3145736 | tf_op jit(solution)/shard_map/ppermute | solution.py:751
  269.7 64.3 %collective-permute-start.21 = (bf16[1024,512]{1,0:T(8,128)(2,1)}, bf16[1024,512]{1,0:T(8,128)(2,1)}, u32[]{:S(2)}, u32[]{:S(2)}) collective-permute-start(bf16[1024,512]{1,0:T(8,128)(2,1)} %get-tuple-element.23), channel_id=1, source_target_pairs={{0,4},{4,0},{8,12},{12,8},{16,20},{20,16},{24,28},{28,24},{1,5},{5... | collective-permute-start | bytes 3145736 | tf_op jit(solution)/shard_map/ppermute | solution.py:751
  273.3 56.4 %collective-permute-start.28 = (bf16[1,136,2048]{2,1,0:T(8,128)(2,1)}, bf16[1,136,2048]{2,1,0:T(8,128)(2,1)}, u32[]{:S(2)}, u32[]{:S(2)}) collective-permute-start(bf16[1,136,2048]{2,1,0:T(8,128)(2,1)} %shard_map.89.a_ref), channel_id=1, source_target_pairs={{0,8},{4,12},{8,0},{12,4},{16,24},{20,28},{24,16},{28,20},{1,9},{5... | collective-permute-start | bytes 1671176 | tf_op jit(solution)/shard_map/ppermute | solution.py:751
  342.8 41.5 %collective-permute-start.29 = (bf16[2,384,512]{2,1,0:T(8,128)(2,1)}, bf16[2,384,512]{2,1,0:T(8,128)(2,1)}, u32[]{:S(2)}, u32[]{:S(2)}) collective-permute-start(bf16[2,384,512]{2,1,0:T(8,128)(2,1)} %get-tuple-element.22), channel_id=1, source_target_pairs={{1,3},{3,1},{5,7},{7,5},{8,10},{10,8},{12,14},{14,12},{17,19},{19,... | collective-permute-start | bytes 2359304 | tf_op jit(solution)/shard_map/ppermute | solution.py:812
  344.4 13.5 %collective-permute-start.13 = (bf16[1,136,2048]{2,1,0:T(8,128)(2,1)}, bf16[1,136,2048]{2,1,0:T(8,128)(2,1)}, u32[]{:S(2)}, u32[]{:S(2)}) collective-permute-start(bf16[1,136,2048]{2,1,0:T(8,128)(2,1)} %shard_map.81.a_ref), channel_id=1, source_target_pairs={{0,8},{4,12},{8,0},{12,4},{16,24},{20,28},{24,16},{28,20},{1,9},{5... | collective-permute-start | bytes 1671176 | tf_op jit(solution)/shard_map/ppermute | solution.py:751
  346.1 23.8 %collective-permute-start.16 = (bf16[1,136,2048]{2,1,0:T(8,128)(2,1)}, bf16[1,136,2048]{2,1,0:T(8,128)(2,1)}, u32[]{:S(2)}, u32[]{:S(2)}) collective-permute-start(bf16[1,136,2048]{2,1,0:T(8,128)(2,1)} %shard_map.86.a_ref), channel_id=1, source_target_pairs={{0,8},{4,12},{8,0},{12,4},{16,24},{20,28},{24,16},{28,20},{1,9},{5... | collective-permute-start | bytes 1671176 | tf_op jit(solution)/shard_map/ppermute | solution.py:751
  346.4 35.3 %collective-permute-start.19 = (bf16[1,136,2048]{2,1,0:T(8,128)(2,1)}, bf16[1,136,2048]{2,1,0:T(8,128)(2,1)}, u32[]{:S(2)}, u32[]{:S(2)}) collective-permute-start(bf16[1,136,2048]{2,1,0:T(8,128)(2,1)} %shard_map.91.a_ref), channel_id=1, source_target_pairs={{0,8},{4,12},{8,0},{12,4},{16,24},{20,28},{24,16},{28,20},{1,9},{5... | collective-permute-start | bytes 1671176 | tf_op jit(solution)/shard_map/ppermute | solution.py:751

commit v8 on v7

--- a/solution.py
+++ b/solution.py
@@ -653,7 +653,7 @@
     )(*tables, *owned, *questions, cache, *received)
 
 
-def blend(refs, out_ref, leveled):
+def blend(refs, share_ref, out_ref, leveled):
     eye = unit()
     ones = jnp.ones((2 * LQ, LQ), jnp.bfloat16)
 
@@ -665,22 +665,23 @@
     top = functools.reduce(jnp.maximum, levels)
     weights = [jnp.exp2(level - top) for level in levels]
     total = functools.reduce(jnp.add, weights)
-    shares = []
-    for weight in weights[1:]:
+    for n, weight in enumerate(weights[1:]):
         share = weight / total
         high = share.astype(jnp.bfloat16).astype(jnp.float32)
-        shares.append((high, share - high))
-    for c in range(total.shape[1] // HD):
-        columns = slice(c * HD, (c + 1) * HD)
+        share_ref[2 * n : 2 * n + 1, :] = high
+        share_ref[2 * n + 1 : 2 * n + 2, :] = share - high
+
+    def tile(c, carry):
+        columns = pl.ds(pl.multiple_of(c * HD, HD), HD)
         base = refs[0][0, :LQ, columns].astype(jnp.float32)
         value = base
-        for ref, pair in zip(refs[1:], shares):
+        for n, ref in enumerate(refs[1:]):
             spread = jnp.concatenate(
                 [
-                    jnp.where(eye, jnp.broadcast_to(v[:, columns], (LQ, LQ)), 0.0).astype(
-                        jnp.bfloat16
-                    )
-                    for v in pair
+                    jnp.where(
+                        eye, jnp.broadcast_to(share_ref[r : r + 1, columns], (LQ, LQ)), 0.0
+                    ).astype(jnp.bfloat16)
+                    for r in (2 * n, 2 * n + 1)
                 ],
                 axis=1,
             )
@@ -691,28 +692,31 @@
             out_ref[0, :LQ, columns] = value
         else:
             out_ref[:, columns] = value
+        return carry
+
+    lax.fori_loop(0, total.shape[1] // HD, tile, 0, unroll=4)
     if leveled:
         store_level(out_ref, 0, slice(None), top + jnp.log2(total))
 
 
 def merge_kernel(*refs):
-    *parts, out_ref = refs
+    *parts, out_ref, share_ref = refs
     inner = is_inner()
 
     @pl.when(inner)
     def _():
-        blend(parts, out_ref, True)
+        blend(parts, share_ref, out_ref, True)
 
     @pl.when(jnp.logical_not(inner))
     def _():
         if len(parts) > 2:
-            blend(parts[:-1], out_ref, True)
+            blend(parts[:-1], share_ref, out_ref, True)
         else:
             out_ref[...] = parts[0][...]
 
 
-def finish_kernel(a_ref, b_ref, out_ref):
-    blend((a_ref, b_ref), out_ref, False)
+def finish_kernel(a_ref, b_ref, out_ref, share_ref):
+    blend((a_ref, b_ref), share_ref, out_ref, False)
 
 
 def question_spec(value, at):
@@ -737,6 +741,7 @@
         grid=(1,),
         in_specs=[question_spec(part, at) for part in parts],
         out_specs=out_spec,
+        scratch_shapes=[pltpu.VMEM((8, columns), jnp.float32)],
         compiler_params=pltpu.CompilerParams(vmem_limit_bytes=VMEM_BYTES),
         cost_estimate=pl.CostEstimate(flops=size * 8, bytes_accessed=size * 6, transcendentals=0),
     )(*parts)
@@ -764,8 +769,7 @@
     q_near = send(queries, near)
     q_mid = send(queries, middle)
     half = out_weight.shape[0] // 2
-    w_across0 = send(out_weight[:half], across)
-    w_across1 = send(out_weight[half:], across)
+    w_across = send(out_weight, across)
     cache = jnp.transpose(passage_cache, (0, 2, 1, 3))
     row, tag, far_tag, *items = sort_items(
         lists, passage_slot, question_slot, cache, most, per_device
@@ -782,10 +786,12 @@
     part1 = part(1, [q_near], cache, None)
     part1_far = part(1, [q_near], cache, far[1], local=False)
     back2 = send(part2, inward)
-    w_in = send(out_weight, mirror(2, "outer"))
+    w_in0 = send(out_weight[:half], mirror(2, "outer"))
+    w_in1 = send(out_weight[half:], mirror(2, "outer"))
     w_out = send(out_weight, mirror(2, "inner"))
     back3 = send(part3, inward)
-    w_in_both = send(w_in, inner_across)
+    w_in0_both = send(w_in0, inner_across)
+    w_in1_both = send(w_in1, inner_across)
     w_out_both = send(w_out, outer_across)
     own_rows, near_rows = [], []
     for q in range(per_device):
@@ -797,7 +803,7 @@
         back1 = send(near1, near)
         near_rows.append(join(q, near1, beside, leveled=False))
         own_rows.append(join(q, near0, back1, leveled=False))
-    weights = (out_weight, w_across0, w_across1, w_in, w_in_both, w_out, w_out_both)
+    weights = (out_weight, w_across, w_in0, w_in1, w_in0_both, w_in1_both, w_out, w_out_both)
     far_send, far_keep = project_call(near_rows, weights, None)
     far_sent = send_far(far_send)
     return project_call(own_rows, weights, (far_keep, far_sent))
@@ -821,8 +827,8 @@
 
 def project_kernel(pieces, far, *refs):
     rows_refs = refs[:pieces]
-    own_ref, a0_ref, a1_ref, in_ref, in2_ref, out1_ref, out2_ref = refs[pieces : pieces + 7]
-    refs = refs[pieces + 7 :]
+    own_ref, across_ref, *line_refs = refs[pieces : pieces + 8]
+    refs = refs[pieces + 8 :]
     if far:
         send_ref, keep_ref = refs[:2]
     else:
@@ -846,21 +852,21 @@
 
     def load_here():
         pltpu.make_async_copy(own_ref, w_ref.at[0, x], w_sem.at[0, x]).start()
-        half = a0_ref.shape[0]
-        low, high = w_ref.at[0, 1 - x, pl.ds(0, half)], w_ref.at[0, 1 - x, pl.ds(half, half)]
-        pltpu.make_async_copy(a0_ref, low, w_sem.at[0, 1 - x]).start()
-        pltpu.make_async_copy(a1_ref, high, w_sem.at[0, 1 - x]).start()
+        pltpu.make_async_copy(across_ref, w_ref.at[0, 1 - x], w_sem.at[0, 1 - x]).start()
 
     def load_there():
-        for which, (one, two) in (
-            (inner, (in_ref, in2_ref)),
-            (jnp.logical_not(inner), (out1_ref, out2_ref)),
-        ):
-
-            @pl.when(which)
-            def _():
-                pltpu.make_async_copy(one, w_ref.at[1, x], w_sem.at[1, x]).start()
-                pltpu.make_async_copy(two, w_ref.at[1, 1 - x], w_sem.at[1, 1 - x]).start()
+        @pl.when(inner)
+        def _():
+            for side, low, high in ((x, 0, 1), (1 - x, 2, 3)):
+                half = line_refs[low].shape[0]
+                for at, ref in ((0, line_refs[low]), (half, line_refs[high])):
+                    block = w_ref.at[1, side, pl.ds(at, half)]
+                    pltpu.make_async_copy(ref, block, w_sem.at[1, side]).start()
+
+        @pl.when(jnp.logical_not(inner))
+        def _():
+            for side, ref in ((x, line_refs[4]), (1 - x, line_refs[5])):
+                pltpu.make_async_copy(ref, w_ref.at[1, side], w_sem.at[1, side]).start()
 
     here_first = y != z // 2
 
@@ -890,23 +896,29 @@
             device_id_type=MESH,
         )
 
+    chunks = part_ref.shape[1]
+    step = part_ref.shape[3]
+
     def columns(j):
-        return pl.ds(j * wide, wide)
+        return pl.ds(j * step, step)
 
     core_copies = [
-        [remote(part_ref.at[s, j], core_ref.at[s, j], s * 2 + j, core_peer) for j in range(2)]
+        [remote(part_ref.at[s, j], core_ref.at[s, j], s * chunks + j, core_peer) for j in range(chunks)]
         for s in range(2)
     ]
     if not far:
         y_ref, ysend_ref, zsend_ref = refs[10:]
-        y_copies = [remote(ysend_ref.at[j], y_ref.at[j], 4 + j, y_peer) for j in range(2)]
+        y_copies = [
+            remote(ysend_ref.at[j], y_ref.at[j], 2 * chunks + j, y_peer) for j in range(chunks)
+        ]
         z_copies = [
-            remote(zsend_ref.at[j], out_ref.at[:, columns(j)], 6 + j, z_peer) for j in range(2)
+            remote(zsend_ref.at[j], out_ref.at[:, columns(j)], 3 * chunks + j, z_peer)
+            for j in range(chunks)
         ]
 
         @pl.when(jnp.logical_not(home))
         def _():
-            for j in range(2):
+            for j in range(chunks):
                 zsend_ref[j] = (
                     far_keep_ref[j].astype(jnp.float32) + far_sent_ref[j].astype(jnp.float32)
                 ).astype(zsend_ref.dtype)
@@ -917,10 +929,14 @@
 
     def multiply(s, to_y, j):
         here = jnp.where(to_y == z // 2, 0, 1)
-        block = w_ref.at[here, j]
-        pltpu.make_async_copy(block, block, w_sem.at[here, j]).wait()
+        side, at = j * step // wide, j * step % wide
+        if at == 0:
+            block = w_ref.at[here, side]
+            pltpu.make_async_copy(block, block, w_sem.at[here, side]).wait()
         part_ref[s, j] = jnp.dot(
-            context_ref[...], w_ref[here, j], preferred_element_type=jnp.float32
+            context_ref[...],
+            w_ref[here, side, :, pl.ds(at, step)],
+            preferred_element_type=jnp.float32,
         ).astype(part_ref.dtype)
 
         @pl.when(jnp.logical_not(sums))
@@ -946,7 +962,7 @@
 
     late = None
     for s, to_y in enumerate((1 - y, y)):
-        for j in range(2):
+        for j in range(chunks):
             multiply(s, to_y, j)
             if late is not None:
                 add_up(*late)
@@ -978,7 +994,9 @@
     dtype = own.dtype
     far = far_sums is None
     vmem = pl.BlockSpec(memory_space=pltpu.VMEM)
-    blocks = (2, rows, wide)
+    step = math.gcd(wide, 256)
+    chunks = 2 * wide // step
+    blocks = (chunks, rows, step)
     scratch = [
         pltpu.VMEM((rows, depth), dtype),
         pltpu.VMEM((2, 2, depth, wide), dtype),
@@ -986,8 +1004,8 @@
         pltpu.VMEM((2,) + blocks, dtype),
         pltpu.SemaphoreType.DMA((len(pieces),)),
         pltpu.SemaphoreType.DMA((2, 2)),
-        pltpu.SemaphoreType.DMA((8,)),
-        pltpu.SemaphoreType.DMA((8,)),
+        pltpu.SemaphoreType.DMA((4 * chunks,)),
+        pltpu.SemaphoreType.DMA((4 * chunks,)),
     ]
     if far:
         out_shape = [jax.ShapeDtypeStruct(blocks, dtype)] * 2

time: 412 us -> 430 us (1.044)
  starting transfers between devices: 97.1 us -> 111 us
  Pallas kernels: 154 us -> 159 us
    ppermute x29 -> x30, starting transfers between devices: 95.5 us -> 109 us  [send(): return lax.ppermute(value, 'pass', pairs)]
    pallas_call x18, Pallas kernels: 41.5 us -> 46.2 us  [join_call(): pl.pallas_call(merge_kernel if leveled else finish_kernel, out_shape=jax....]
    ppermute x29 -> x30, waiting for transfers between devices: 144 us -> 143 us  [send(): return lax.ppermute(value, 'pass', pairs)]
  transfers between devices with their start and end apart: 30 -> 31, of which waited for: 12 -> 10; matrix products, arithmetic and copies ran while one was open for 3% -> 3% of each run, Pallas kernels for 30% -> 29%
where the time goes in v8:
time: 430 us; the launch traced here: 428 us
  Pallas kernels  159 us (37%)
  waiting for transfers between devices  143 us (33%)
  starting transfers between devices  111 us (26%)
  local copies, waits for them, and re-layouts  15.1 us (4%)
    ppermute x30, waiting for transfers between devices, send(): return lax.ppermute(value, 'pass', pairs)  143 us
    ppermute x30, starting transfers between devices, send(): return lax.ppermute(value, 'pass', pairs)  109 us
    pallas_call x5, Pallas kernels, part_call(): pl.pallas_call(functools.partial(part_kernel, k, most, first, last, heads...  71.8 us
    pallas_call x18, Pallas kernels, join_call(): pl.pallas_call(merge_kernel if leveled else finish_kernel, out_shape=jax....  46.2 us
    pallas_call x2, Pallas kernels, project_call(): pl.pallas_call(functools.partial(project_kernel, len(pieces), far), out_s...  33.4 us
    unnamed x2, local copies, waits for them, and re-layouts  10.3 us
  transfers between devices with their start and end apart: 31, of which 10 were waited for; matrix products, arithmetic and copies ran while one was open for 3% of the time, Pallas kernels for 29%

profile of v8, /device:TPU:0, one launch (start us, length us, event | category | flops | bytes accessed | tf_op | source)
XLA Modules:
  0.0 428.3 jit_solution(15321752793875549319)
XLA Ops:
  0.0 3.1 collective-permute-start.2
  4.9 32.9 %collective-permute-done.2.refs_3_ = bf16[384,2048]{1,0:T(8,128)(2,1)} collective-permute-done((bf16[384,2048]{1,0:T(8,128)(2,1)}, bf16[384,2048]{1,0:T(8,128)(2,1)}, u32[]{:S(2)}, u32[]{:S(2)}) %collective-permute-start.2) | collective-permute-done | bytes 1572896 | tf_op jit(solution)/shard_map/ppermute | solution.py:756
  39.6 8.2 %copy.16 = bf16[16,512,2,256]{3,1,2,0:T(8,128)(2,1)} copy(bf16[16,512,2,256]{3,2,1,0:T(2,128)(2,1)} %param.9) | data formatting | bytes 16777216 | tf_op args[2]
  47.8 7.8 %sort_items.1 = (s32[12]{0:T(128)}, s32[12]{0:T(128)}, s32[12]{0:T(128)}, bf16[3,2,512,256]{3,2,1,0:T(8,128)(2,1)}, bf16[3,2,512,256]{3,2,1,0:T(8,128)(2,1)}, /*...) custom-call(s32[8,24]{1,0:T(8,128)} %bitcast.16, s32[128]{0:T(128)} %pslot_ref.1, s32[24]{0:T(128)} %qslot_ref.1, ...), custom_call_target="tpu_custom_call" | custom-call | bytes 12582912 | tf_op jit(solution)/shard_map/sort_items/pallas_call | solution.py:437
  61.1 32.9 %collective-permute-done.7.refs_6_ = bf16[3,2,512,256]{3,2,1,0:T(8,128)(2,1)} collective-permute-done((bf16[3,2,512,256]{3,2,1,0:T(8,128)(2,1)}, bf16[3,2,512,256]{3,2,1,0:T(8,128)(2,1)}, u32[]{:S(2)}, u32[]{:S(2)}) %collective-permute-start.7) | collective-permute-done | bytes 1572896 | tf_op jit(solution)/shard_map/ppermute | solution.py:756
  94.0 3.9 collective-permute-done.6.refs_4_
  97.9 15.5 %shard_map.75.refs_0_ = bf16[3,136,2048]{2,1,0:T(8,128)(2,1)} custom-call(s32[12]{0:T(128)} %get-tuple-element.14.refs_0_, s32[12]{0:T(128)} %get-tuple-element.15.refs_1_, s32[12]{0:T(128)} %get-tuple-element.16.refs_2_, bf16[384,2048]{1,0:T(8,128)(2,1)} %collective-permute-done.3.refs_3_, bf16[384,2048]{1,0:T(8,128)(2,1)} %collective-permute-done.6.refs_4_, ...), custom_call_target="tpu_custom_call" | custom-call | flops 3221225472 | bytes 3145728 | tf_op jit(solution)/shard_map/pallas_call | solution.py:631
  117.2 3.0 fusion
  122.5 5.2 %collective-permute-done.5.refs_6_ = bf16[3,2,512,256]{3,2,1,0:T(8,128)(2,1)} collective-permute-done((bf16[3,2,512,256]{3,2,1,0:T(8,128)(2,1)}, bf16[3,2,512,256]{3,2,1,0:T(8,128)(2,1)}, u32[]{:S(2)}, u32[]{:S(2)}) %collective-permute-start.5) | collective-permute-done | bytes 1572896 | tf_op jit(solution)/shard_map/ppermute | solution.py:756
  131.1 15.6 %shard_map.74.refs_0_ = bf16[3,136,2048]{2,1,0:T(8,128)(2,1)} custom-call(s32[12]{0:T(128)} %get-tuple-element.14.refs_0_, s32[12]{0:T(128)} %get-tuple-element.15.refs_1_, s32[12]{0:T(128)} %get-tuple-element.16.refs_2_, bf16[384,2048]{1,0:T(8,128)(2,1)} %collective-permute-done.1.refs_3_, bf16[384,2048]{1,0:T(8,128)(2,1)} %collective-permute-done.4.refs_4_, ...), custom_call_target="tpu_custom_call" | custom-call | flops 3221225472 | bytes 3145728 | tf_op jit(solution)/shard_map/pallas_call | solution.py:631
  146.7 22.7 %collective-permute-done.21.refs_5_ = bf16[1024,512]{1,0:T(8,128)(2,1)} collective-permute-done((bf16[1024,512]{1,0:T(8,128)(2,1)}, bf16[1024,512]{1,0:T(8,128)(2,1)}, u32[]{:S(2)}, u32[]{:S(2)}) %collective-permute-start.21) | collective-permute-done | bytes 1048608 | tf_op jit(solution)/shard_map/ppermute | solution.py:756
  169.3 7.2 %collective-permute-start.11 = (bf16[3,136,2048]{2,1,0:T(8,128)(2,1)}, bf16[3,136,2048]{2,1,0:T(8,128)(2,1)}, u32[]{:S(2)}, u32[]{:S(2)}) collective-permute-start(bf16[3,136,2048]{2,1,0:T(8,128)(2,1)} %shard_map.74.refs_0_), channel_id=1, source_target_pairs={{0,8},{4,12},{24,16},{28,20},{1,9},{5,13},{25,17},{29,21},{2,10},{... | collective-permute-start | bytes 5013512 | tf_op jit(solution)/shard_map/ppermute | solution.py:756
  187.6 20.3 %shard_map.73.refs_0_ = bf16[3,136,2048]{2,1,0:T(8,128)(2,1)} custom-call(s32[12]{0:T(128)} %get-tuple-element.14.refs_0_, s32[12]{0:T(128)} %get-tuple-element.15.refs_1_, s32[12]{0:T(128)} %get-tuple-element.16.refs_2_, bf16[3,2,128,256]{3,2,1,0:T(8,128)(2,1)} %bitcast.14, bf16[384,2048]{1,0:T(8,128)(2,1)} %refs_4_.1, bf16[16,2,512,256]{3,2,1,0:T(8,128)(2,1)} %bitcast.11, ...), custom_call_target="tpu_custom_call" | custom-call | flops 3221225472 | bytes 3145728 | tf_op jit(solution)/shard_map/pallas_call | solution.py:631
  212.1 16.3 %collective-permute-done.22.refs_6_ = bf16[1024,512]{1,0:T(8,128)(2,1)} collective-permute-done((bf16[1024,512]{1,0:T(8,128)(2,1)}, bf16[1024,512]{1,0:T(8,128)(2,1)}, u32[]{:S(2)}, u32[]{:S(2)}) %collective-permute-start.22) | collective-permute-done | bytes 1048608 | tf_op jit(solution)/shard_map/ppermute | solution.py:756
  229.9 38.8 %collective-permute-start.27 = (bf16[1,136,2048]{2,1,0:T(8,128)(2,1)}, bf16[1,136,2048]{2,1,0:T(8,128)(2,1)}, u32[]{:S(2)}, u32[]{:S(2)}) collective-permute-start(bf16[1,136,2048]{2,1,0:T(8,128)(2,1)} %shard_map.77.a_ref), channel_id=1, source_target_pairs={{0,8},{4,12},{8,0},{12,4},{16,24},{20,28},{24,16},{28,20},{1,9},{5... | collective-permute-start | bytes 1671176 | tf_op jit(solution)/shard_map/ppermute | solution.py:756
  291.6 17.2 %collective-permute-start.29 = (bf16[1,136,2048]{2,1,0:T(8,128)(2,1)}, bf16[1,136,2048]{2,1,0:T(8,128)(2,1)}, u32[]{:S(2)}, u32[]{:S(2)}) collective-permute-start(bf16[1,136,2048]{2,1,0:T(8,128)(2,1)} %shard_map.89.a_ref), channel_id=1, source_target_pairs={{0,8},{4,12},{8,0},{12,4},{16,24},{20,28},{24,16},{28,20},{1,9},{5... | collective-permute-start | bytes 1671176 | tf_op jit(solution)/shard_map/ppermute | solution.py:756
  308.8 10.2 %shard_map.78.refs_0_ = bf16[3,136,2048]{2,1,0:T(8,128)(2,1)} custom-call(s32[12]{0:T(128)} %get-tuple-element.14.refs_0_, s32[12]{0:T(128)} %get-tuple-element.15.refs_1_, s32[12]{0:T(128)} %get-tuple-element.16.refs_2_, bf16[384,2048]{1,0:T(8,128)(2,1)} %collective-permute-done.2.refs_3_, bf16[16,2,512,256]{3,2,1,0:T(8,128)(2,1)} %bitcast.12), custom_call_target="tpu_custom_call" | custom-call | flops 1610612736 | bytes 1572864 | tf_op jit(solution)/shard_map/pallas_call | solution.py:631
  319.0 10.2 %shard_map.79.refs_1_ = bf16[3,136,2048]{2,1,0:T(8,128)(2,1)} custom-call(s32[12]{0:T(128)} %get-tuple-element.14.refs_0_, s32[12]{0:T(128)} %get-tuple-element.15.refs_1_, s32[12]{0:T(128)} %get-tuple-element.16.refs_2_, bf16[384,2048]{1,0:T(8,128)(2,1)} %collective-permute-done.2.refs_3_, bf16[16,2,512,256]{3,2,1,0:T(8,128)(2,1)} %bitcast.13, ...), custom_call_target="tpu_custom_call" | custom-call | flops 1610612736 | bytes 1572864 | tf_op jit(solution)/shard_map/pallas_call | solution.py:631
  329.2 3.2 shard_map.81.a_ref
  332.4 3.2 shard_map.86.a_ref
  335.7 3.2 shard_map.91.a_ref
  338.8 3.0 shard_map.93.refs_0_
  341.8 3.0 shard_map.94.refs_1_
  347.8 12.6 %project_far.1 = (bf16[4,384,256]{2,1,0:T(8,128)(2,1)}, bf16[4,384,256]{2,1,0:T(8,128)(2,1)}) custom-call(bf16[128,2048]{1,0:T(8,128)(2,1)} %shard_map.93.refs_0_, bf16[128,2048]{1,0:T(8,128)(2,1)} %shard_map.94.refs_1_, bf16[128,2048]{1,0:T(8,128)(2,1)} %shard_map.95.refs_2_, bf16[2048,512]{1,0:T(8,128)(2,1)} %refs_3_.3, ...), custom_call_target="tpu_custom_call" | custom-call | flops 3221225472 | bytes 8388608 | tf_op jit(solution)/shard_map/project_far/pallas_call | solution.py:1017
  362.0 3.8 collective-permute-start.13
  367.8 11.3 %collective-permute-done.13.b_ref = bf16[1,136,2048]{2,1,0:T(8,128)(2,1)} collective-permute-done((bf16[1,136,2048]{2,1,0:T(8,128)(2,1)}, bf16[1,136,2048]{2,1,0:T(8,128)(2,1)}, u32[]{:S(2)}, u32[]{:S(2)}) %collective-permute-start.13) | collective-permute-done | bytes 557088 | tf_op jit(solution)/shard_map/ppermute | solution.py:756
  379.1 3.0 shard_map.82.refs_0_
  382.1 8.9 %collective-permute-done.16.b_ref = bf16[1,136,2048]{2,1,0:T(8,128)(2,1)} collective-permute-done((bf16[1,136,2048]{2,1,0:T(8,128)(2,1)}, bf16[1,136,2048]{2,1,0:T(8,128)(2,1)}, u32[]{:S(2)}, u32[]{:S(2)}) %collective-permute-start.16) | collective-permute-done | bytes 557088 | tf_op jit(solution)/shard_map/ppermute | solution.py:756
  391.1 3.0 shard_map.87.refs_1_
  394.1 8.4 %collective-permute-done.19.b_ref = bf16[1,136,2048]{2,1,0:T(8,128)(2,1)} collective-permute-done((bf16[1,136,2048]{2,1,0:T(8,128)(2,1)}, bf16[1,136,2048]{2,1,0:T(8,128)(2,1)}, u32[]{:S(2)}, u32[]{:S(2)}) %collective-permute-start.19) | collective-permute-done | bytes 557088 | tf_op jit(solution)/shard_map/ppermute | solution.py:756
  402.4 3.0 shard_map.92.refs_2_
  405.4 20.8 %project_home.1 = bf16[384,1024]{1,0:T(8,128)(2,1)} custom-call(bf16[128,2048]{1,0:T(8,128)(2,1)} %shard_map.82.refs_0_, bf16[128,2048]{1,0:T(8,128)(2,1)} %shard_map.87.refs_1_, bf16[128,2048]{1,0:T(8,128)(2,1)} %shard_map.92.refs_2_, bf16[2048,512]{1,0:T(8,128)(2,1)} %refs_3_.3, bf16[2048,512]{1,0:T(8,128)(2,1)} %collective-permute-done.20.refs_4_, ...), custom_call_target="tpu_custom_call" | custom-call | flops 3221225472 | bytes 8388608 | tf_op jit(solution)/shard_map/project_home/pallas_call | solution.py:1017
  (60 shorter events, 66.8 us)
Async XLA Ops:
  0.0 37.8 %collective-permute-start.2 = (bf16[384,2048]{1,0:T(8,128)(2,1)}, bf16[384,2048]{1,0:T(8,128)(2,1)}, u32[]{:S(2)}, u32[]{:S(2)}) collective-permute-start(bf16[384,2048]{1,0:T(8,128)(2,1)} %refs_4_.1), channel_id=1, source_target_pairs={{0,8},{4,12},{8,0},{12,4},{16,24},{20,28},{24,16},{28,20},{1,9},{5... | collective-permute-start | bytes 4718600 | tf_op jit(solution)/shard_map/ppermute | solution.py:756
  3.1 55.4 %collective-permute-start.1 = (bf16[384,2048]{1,0:T(8,128)(2,1)}, bf16[384,2048]{1,0:T(8,128)(2,1)}, u32[]{:S(2)}, u32[]{:S(2)}) collective-permute-start(bf16[384,2048]{1,0:T(8,128)(2,1)} %refs_4_.1), channel_id=1, source_target_pairs={{8,16},{12,20},{16,8},{20,12},{9,17},{13,21},{17,9},{21,13},{10,18... | collective-permute-start | bytes 4718600 | tf_op jit(solution)/shard_map/ppermute | solution.py:756
  37.8 22.1 %collective-permute-start.3 = (bf16[384,2048]{1,0:T(8,128)(2,1)}, bf16[384,2048]{1,0:T(8,128)(2,1)}, u32[]{:S(2)}, u32[]{:S(2)}) collective-permute-start(bf16[384,2048]{1,0:T(8,128)(2,1)} %collective-permute-done.2.refs_3_), channel_id=1, source_target_pairs={{8,16},{12,20},{16,8},{20,12},{9,17},{13,21},{17,9},{21,13},{10,18... | collective-permute-start | bytes 4718600 | tf_op jit(solution)/shard_map/ppermute | solution.py:756
  55.6 38.4 %collective-permute-start.7 = (bf16[3,2,512,256]{3,2,1,0:T(8,128)(2,1)}, bf16[3,2,512,256]{3,2,1,0:T(8,128)(2,1)}, u32[]{:S(2)}, u32[]{:S(2)}) collective-permute-start(bf16[3,2,512,256]{3,2,1,0:T(8,128)(2,1)} %get-tuple-element.19), channel_id=1, source_target_pairs={{0,4},{4,0},{8,12},{12,8},{16,20},{20,16},{24,28},{28,24},{1,5},{5... | collective-permute-start | bytes 4718600 | tf_op jit(solution)/shard_map/ppermute | solution.py:756
  58.4 39.5 %collective-permute-start.6 = (bf16[384,2048]{1,0:T(8,128)(2,1)}, bf16[384,2048]{1,0:T(8,128)(2,1)}, u32[]{:S(2)}, u32[]{:S(2)}) collective-permute-start(bf16[384,2048]{1,0:T(8,128)(2,1)} %collective-permute-done.1.refs_3_), channel_id=1, source_target_pairs={{8,0},{12,4},{16,24},{20,28},{9,1},{13,5},{17,25},{21,29},{10,2},{... | collective-permute-start | bytes 4718600 | tf_op jit(solution)/shard_map/ppermute | solution.py:756
  59.7 68.0 %collective-permute-start.5 = (bf16[3,2,512,256]{3,2,1,0:T(8,128)(2,1)}, bf16[3,2,512,256]{3,2,1,0:T(8,128)(2,1)}, u32[]{:S(2)}, u32[]{:S(2)}) collective-permute-start(bf16[3,2,512,256]{3,2,1,0:T(8,128)(2,1)} %get-tuple-element.18), channel_id=1, source_target_pairs={{0,4},{4,0},{8,12},{12,8},{16,20},{20,16},{24,28},{28,24},{1,5},{5... | collective-permute-start | bytes 4718600 | tf_op jit(solution)/shard_map/ppermute | solution.py:756
  59.8 69.5 %collective-permute-start.4 = (bf16[384,2048]{1,0:T(8,128)(2,1)}, bf16[384,2048]{1,0:T(8,128)(2,1)}, u32[]{:S(2)}, u32[]{:S(2)}) collective-permute-start(bf16[384,2048]{1,0:T(8,128)(2,1)} %collective-permute-done.3.refs_3_), channel_id=1, source_target_pairs={{8,0},{12,4},{16,24},{20,28},{9,1},{13,5},{17,25},{21,29},{10,2},{... | collective-permute-start | bytes 4718600 | tf_op jit(solution)/shard_map/ppermute | solution.py:756
  113.4 63.1 %collective-permute-start.8 = (bf16[3,136,2048]{2,1,0:T(8,128)(2,1)}, bf16[3,136,2048]{2,1,0:T(8,128)(2,1)}, u32[]{:S(2)}, u32[]{:S(2)}) collective-permute-start(bf16[3,136,2048]{2,1,0:T(8,128)(2,1)} %shard_map.75.refs_0_), channel_id=1, source_target_pairs={{0,8},{4,12},{24,16},{28,20},{1,9},{5,13},{25,17},{29,21},{2,10},{... | collective-permute-start | bytes 5013512 | tf_op jit(solution)/shard_map/ppermute | solution.py:756
  116.1 64.7 %collective-permute-start = (bf16[3,2,512,256]{3,2,1,0:T(8,128)(2,1)}, bf16[3,2,512,256]{3,2,1,0:T(8,128)(2,1)}, u32[]{:S(2)}, u32[]{:S(2)}) collective-permute-start(bf16[3,2,512,256]{3,2,1,0:T(8,128)(2,1)} %get-tuple-element.17), channel_id=1, source_target_pairs={{0,4},{4,0},{8,12},{12,8},{16,20},{20,16},{24,28},{28,24},{1,5},{5... | collective-permute-start | bytes 4718600 | tf_op jit(solution)/shard_map/ppermute | solution.py:756
  120.2 49.1 %collective-permute-start.21 = (bf16[1024,512]{1,0:T(8,128)(2,1)}, bf16[1024,512]{1,0:T(8,128)(2,1)}, u32[]{:S(2)}, u32[]{:S(2)}) collective-permute-start(bf16[1024,512]{1,0:T(8,128)(2,1)} %get-tuple-element.24), channel_id=1, source_target_pairs={{0,16},{4,20},{24,8},{28,12},{1,17},{5,21},{25,9},{29,13},{2,18},{... | collective-permute-start | bytes 3145736 | tf_op jit(solution)/shard_map/ppermute | solution.py:756
  127.7 141.0 %collective-permute-start.25 = (bf16[2048,512]{1,0:T(8,128)(2,1)}, bf16[2048,512]{1,0:T(8,128)(2,1)}, u32[]{:S(2)}, u32[]{:S(2)}) collective-permute-start(bf16[2048,512]{1,0:T(8,128)(2,1)} %refs_3_.3), channel_id=1, source_target_pairs={{8,24},{12,28},{16,0},{20,4},{9,25},{13,29},{17,1},{21,5},{10,26},... | collective-permute-start | bytes 6291464 | tf_op jit(solution)/shard_map/ppermute | solution.py:756
  129.3 100.5 %collective-permute-start.10 = (bf16[3,2,512,256]{3,2,1,0:T(8,128)(2,1)}, bf16[3,2,512,256]{3,2,1,0:T(8,128)(2,1)}, u32[]{:S(2)}, u32[]{:S(2)}) collective-permute-start(bf16[3,2,512,256]{3,2,1,0:T(8,128)(2,1)} %get-tuple-element.20), channel_id=1, source_target_pairs={{0,4},{4,0},{8,12},{12,8},{16,20},{20,16},{24,28},{28,24},{1,5},{5... | collective-permute-start | bytes 4718600 | tf_op jit(solution)/shard_map/ppermute | solution.py:756
  169.3 105.4 %collective-permute-start.11 = (bf16[3,136,2048]{2,1,0:T(8,128)(2,1)}, bf16[3,136,2048]{2,1,0:T(8,128)(2,1)}, u32[]{:S(2)}, u32[]{:S(2)}) collective-permute-start(bf16[3,136,2048]{2,1,0:T(8,128)(2,1)} %shard_map.74.refs_0_), channel_id=1, source_target_pairs={{0,8},{4,12},{24,16},{28,20},{1,9},{5,13},{25,17},{29,21},{2,10},{... | collective-permute-start | bytes 5013512 | tf_op jit(solution)/shard_map/ppermute | solution.py:756
  176.5 51.9 %collective-permute-start.22 = (bf16[1024,512]{1,0:T(8,128)(2,1)}, bf16[1024,512]{1,0:T(8,128)(2,1)}, u32[]{:S(2)}, u32[]{:S(2)}) collective-permute-start(bf16[1024,512]{1,0:T(8,128)(2,1)} %get-tuple-element.23), channel_id=1, source_target_pairs={{0,16},{4,20},{24,8},{28,12},{1,17},{5,21},{25,9},{29,13},{2,18},{... | collective-permute-start | bytes 3145736 | tf_op jit(solution)/shard_map/ppermute | solution.py:756
  180.8 3.5 collective-permute-start.9
  184.4 86.1 %collective-permute-start.14 = (bf16[1,136,2048]{2,1,0:T(8,128)(2,1)}, bf16[1,136,2048]{2,1,0:T(8,128)(2,1)}, u32[]{:S(2)}, u32[]{:S(2)}) collective-permute-start(bf16[1,136,2048]{2,1,0:T(8,128)(2,1)} %shard_map.83), channel_id=1, source_target_pairs={{8,16},{12,20},{16,8},{20,12},{9,17},{13,21},{17,9},{21,13},{10,18... | collective-permute-start | bytes 1671176 | tf_op jit(solution)/shard_map/ppermute | solution.py:756
  228.4 51.4 %collective-permute-start.17 = (bf16[1,136,2048]{2,1,0:T(8,128)(2,1)}, bf16[1,136,2048]{2,1,0:T(8,128)(2,1)}, u32[]{:S(2)}, u32[]{:S(2)}) collective-permute-start(bf16[1,136,2048]{2,1,0:T(8,128)(2,1)} %shard_map.88), channel_id=1, source_target_pairs={{8,16},{12,20},{16,8},{20,12},{9,17},{13,21},{17,9},{21,13},{10,18... | collective-permute-start | bytes 1671176 | tf_op jit(solution)/shard_map/ppermute | solution.py:756
  229.9 51.3 %collective-permute-start.27 = (bf16[1,136,2048]{2,1,0:T(8,128)(2,1)}, bf16[1,136,2048]{2,1,0:T(8,128)(2,1)}, u32[]{:S(2)}, u32[]{:S(2)}) collective-permute-start(bf16[1,136,2048]{2,1,0:T(8,128)(2,1)} %shard_map.77.a_ref), channel_id=1, source_target_pairs={{0,8},{4,12},{8,0},{12,4},{16,24},{20,28},{24,16},{28,20},{1,9},{5... | collective-permute-start | bytes 1671176 | tf_op jit(solution)/shard_map/ppermute | solution.py:756
  268.7 79.1 %collective-permute-start.20 = (bf16[2048,512]{1,0:T(8,128)(2,1)}, bf16[2048,512]{1,0:T(8,128)(2,1)}, u32[]{:S(2)}, u32[]{:S(2)}) collective-permute-start(bf16[2048,512]{1,0:T(8,128)(2,1)} %refs_3_.3), channel_id=1, source_target_pairs={{0,4},{4,0},{8,12},{12,8},{16,20},{20,16},{24,28},{28,24},{1,5},{5... | collective-permute-start | bytes 6291464 | tf_op jit(solution)/shard_map/ppermute | solution.py:756
  270.5 77.3 %collective-permute-start.26 = (bf16[2048,512]{1,0:T(8,128)(2,1)}, bf16[2048,512]{1,0:T(8,128)(2,1)}, u32[]{:S(2)}, u32[]{:S(2)}) collective-permute-start(bf16[2048,512]{1,0:T(8,128)(2,1)} %collective-permute-done.25.refs_9_), channel_id=1, source_target_pairs={{0,4},{4,0},{24,28},{28,24},{1,5},{5,1},{25,29},{29,25},{2,6},{6,2... | collective-permute-start | bytes 6291464 | tf_op jit(solution)/shard_map/ppermute | solution.py:756
  274.7 10.0 %collective-permute-start.28 = (bf16[1,136,2048]{2,1,0:T(8,128)(2,1)}, bf16[1,136,2048]{2,1,0:T(8,128)(2,1)}, u32[]{:S(2)}, u32[]{:S(2)}) collective-permute-start(bf16[1,136,2048]{2,1,0:T(8,128)(2,1)} %shard_map.84.a_ref), channel_id=1, source_target_pairs={{0,8},{4,12},{8,0},{12,4},{16,24},{20,28},{24,16},{28,20},{1,9},{5... | collective-permute-start | bytes 1671176 | tf_op jit(solution)/shard_map/ppermute | solution.py:756
  279.8 6.5 %collective-permute-start.12 = (bf16[1,136,2048]{2,1,0:T(8,128)(2,1)}, bf16[1,136,2048]{2,1,0:T(8,128)(2,1)}, u32[]{:S(2)}, u32[]{:S(2)}) collective-permute-start(bf16[1,136,2048]{2,1,0:T(8,128)(2,1)} %shard_map.80), channel_id=1, source_target_pairs={{8,16},{12,20},{16,8},{20,12},{9,17},{13,21},{17,9},{21,13},{10,18... | collective-permute-start | bytes 1671176 | tf_op jit(solution)/shard_map/ppermute | solution.py:756
  281.2 6.7 %collective-permute-start.15 = (bf16[1,136,2048]{2,1,0:T(8,128)(2,1)}, bf16[1,136,2048]{2,1,0:T(8,128)(2,1)}, u32[]{:S(2)}, u32[]{:S(2)}) collective-permute-start(bf16[1,136,2048]{2,1,0:T(8,128)(2,1)} %shard_map.85), channel_id=1, source_target_pairs={{8,16},{12,20},{16,8},{20,12},{9,17},{13,21},{17,9},{21,13},{10,18... | collective-permute-start | bytes 1671176 | tf_op jit(solution)/shard_map/ppermute | solution.py:756
  284.8 6.9 %collective-permute-start.18 = (bf16[1,136,2048]{2,1,0:T(8,128)(2,1)}, bf16[1,136,2048]{2,1,0:T(8,128)(2,1)}, u32[]{:S(2)}, u32[]{:S(2)}) collective-permute-start(bf16[1,136,2048]{2,1,0:T(8,128)(2,1)} %shard_map.90), channel_id=1, source_target_pairs={{8,16},{12,20},{16,8},{20,12},{9,17},{13,21},{17,9},{21,13},{10,18... | collective-permute-start | bytes 1671176 | tf_op jit(solution)/shard_map/ppermute | solution.py:756
  286.3 61.6 %collective-permute-start.23 = (bf16[1024,512]{1,0:T(8,128)(2,1)}, bf16[1024,512]{1,0:T(8,128)(2,1)}, u32[]{:S(2)}, u32[]{:S(2)}) collective-permute-start(bf16[1024,512]{1,0:T(8,128)(2,1)} %collective-permute-done.21.refs_5_), channel_id=1, source_target_pairs={{8,12},{12,8},{16,20},{20,16},{9,13},{13,9},{17,21},{21,17},{10,14... | collective-permute-start | bytes 3145736 | tf_op jit(solution)/shard_map/ppermute | solution.py:756
  287.9 59.9 %collective-permute-start.24 = (bf16[1024,512]{1,0:T(8,128)(2,1)}, bf16[1024,512]{1,0:T(8,128)(2,1)}, u32[]{:S(2)}, u32[]{:S(2)}) collective-permute-start(bf16[1024,512]{1,0:T(8,128)(2,1)} %collective-permute-done.22.refs_6_), channel_id=1, source_target_pairs={{8,12},{12,8},{16,20},{20,16},{9,13},{13,9},{17,21},{21,17},{10,14... | collective-permute-start | bytes 3145736 | tf_op jit(solution)/shard_map/ppermute | solution.py:756
  291.6 53.2 %collective-permute-start.29 = (bf16[1,136,2048]{2,1,0:T(8,128)(2,1)}, bf16[1,136,2048]{2,1,0:T(8,128)(2,1)}, u32[]{:S(2)}, u32[]{:S(2)}) collective-permute-start(bf16[1,136,2048]{2,1,0:T(8,128)(2,1)} %shard_map.89.a_ref), channel_id=1, source_target_pairs={{0,8},{4,12},{8,0},{12,4},{16,24},{20,28},{24,16},{28,20},{1,9},{5... | collective-permute-start | bytes 1671176 | tf_op jit(solution)/shard_map/ppermute | solution.py:756
  360.4 44.9 %collective-permute-start.30 = (bf16[4,384,256]{2,1,0:T(8,128)(2,1)}, bf16[4,384,256]{2,1,0:T(8,128)(2,1)}, u32[]{:S(2)}, u32[]{:S(2)}) collective-permute-start(bf16[4,384,256]{2,1,0:T(8,128)(2,1)} %get-tuple-element.22), channel_id=1, source_target_pairs={{1,3},{3,1},{5,7},{7,5},{8,10},{10,8},{12,14},{14,12},{17,19},{19,... | collective-permute-start | bytes 2359304 | tf_op jit(solution)/shard_map/ppermute | solution.py:818
  362.0 17.1 %collective-permute-start.13 = (bf16[1,136,2048]{2,1,0:T(8,128)(2,1)}, bf16[1,136,2048]{2,1,0:T(8,128)(2,1)}, u32[]{:S(2)}, u32[]{:S(2)}) collective-permute-start(bf16[1,136,2048]{2,1,0:T(8,128)(2,1)} %shard_map.81.a_ref), channel_id=1, source_target_pairs={{0,8},{4,12},{8,0},{12,4},{16,24},{20,28},{24,16},{28,20},{1,9},{5... | collective-permute-start | bytes 1671176 | tf_op jit(solution)/shard_map/ppermute | solution.py:756
  365.8 25.3 %collective-permute-start.16 = (bf16[1,136,2048]{2,1,0:T(8,128)(2,1)}, bf16[1,136,2048]{2,1,0:T(8,128)(2,1)}, u32[]{:S(2)}, u32[]{:S(2)}) collective-permute-start(bf16[1,136,2048]{2,1,0:T(8,128)(2,1)} %shard_map.86.a_ref), channel_id=1, source_target_pairs={{0,8},{4,12},{8,0},{12,4},{16,24},{20,28},{24,16},{28,20},{1,9},{5... | collective-permute-start | bytes 1671176 | tf_op jit(solution)/shard_map/ppermute | solution.py:756
  365.9 36.5 %collective-permute-start.19 = (bf16[1,136,2048]{2,1,0:T(8,128)(2,1)}, bf16[1,136,2048]{2,1,0:T(8,128)(2,1)}, u32[]{:S(2)}, u32[]{:S(2)}) collective-permute-start(bf16[1,136,2048]{2,1,0:T(8,128)(2,1)} %shard_map.91.a_ref), channel_id=1, source_target_pairs={{0,8},{4,12},{8,0},{12,4},{16,24},{20,28},{24,16},{28,20},{1,9},{5... | collective-permute-start | bytes 1671176 | tf_op jit(solution)/shard_map/ppermute | solution.py:756

commit v9 on v7

--- a/solution.py
+++ b/solution.py
@@ -765,12 +765,13 @@
     q_mid = send(queries, middle)
     half = out_weight.shape[0] // 2
     w_across0 = send(out_weight[:half], across)
-    w_across1 = send(out_weight[half:], across)
     cache = jnp.transpose(passage_cache, (0, 2, 1, 3))
     row, tag, far_tag, *items = sort_items(
         lists, passage_slot, question_slot, cache, most, per_device
     )
     tables = (row, tag, far_tag)
+    later, _ = lax.optimization_barrier((out_weight, row))
+    w_across1 = send(later[half:], across)
     q_out = send(q_mid, outward)
     q_cross = send(q_near, middle)
     q_end = send(q_cross, outward)
@@ -795,8 +796,12 @@
         cross2 = send(join(q, part2, back3), middle)
         near1 = join(q, part1, part1_far, cross2)
         back1 = send(near1, near)
-        near_rows.append(join(q, near1, beside, leveled=False))
-        own_rows.append(join(q, near0, back1, leveled=False))
+        if q + 1 < per_device:
+            near_rows.append(join(q, near1, beside, leveled=False))
+            own_rows.append(join(q, near0, back1, leveled=False))
+        else:
+            near_rows += [near1, beside]
+            own_rows += [near0, back1]
     weights = (out_weight, w_across0, w_across1, w_in, w_in_both, w_out, w_out_both)
     far_send, far_keep = project_call(near_rows, weights, None)
     far_sent = send_far(far_send)
@@ -828,7 +833,7 @@
     else:
         far_keep_ref, far_sent_ref, out_ref = refs[:3]
         refs = refs[1:]
-    context_ref, w_ref, part_ref, core_ref, row_sem, w_sem, send_sem, recv_sem = refs[2:10]
+    context_ref, w_ref, part_ref, core_ref, pair_ref, row_sem, w_sem, send_sem, recv_sem = refs[2:11]
     me, head = lax.axis_index("pass"), lax.axis_index("head")
     z, x, y = me // 2, me % 2, head // 2
     wide = w_ref.shape[3]
@@ -837,9 +842,14 @@
     home = at_home()
     sums = jnp.logical_not(home) if far else home
 
+    done = pieces - 2
     row_loads = [
+        pltpu.make_async_copy(ref, pair_ref.at[i], row_sem.at[done + i])
+        for i, ref in enumerate(rows_refs[done:])
+    ]
+    row_loads += [
         pltpu.make_async_copy(ref, context_ref.at[pl.ds(i * LQ, LQ)], row_sem.at[i])
-        for i, ref in enumerate(rows_refs)
+        for i, ref in enumerate(rows_refs[:done])
     ]
     for load in row_loads:
         load.start()
@@ -898,7 +908,7 @@
         for s in range(2)
     ]
     if not far:
-        y_ref, ysend_ref, zsend_ref = refs[10:]
+        y_ref, ysend_ref, zsend_ref = refs[11:]
         y_copies = [remote(ysend_ref.at[j], y_ref.at[j], 4 + j, y_peer) for j in range(2)]
         z_copies = [
             remote(zsend_ref.at[j], out_ref.at[:, columns(j)], 6 + j, z_peer) for j in range(2)
@@ -914,6 +924,7 @@
 
     for load in row_loads:
         load.wait()
+    blend((pair_ref.at[0], pair_ref.at[1]), context_ref.at[pl.ds(done * LQ, LQ)], False)
 
     def multiply(s, to_y, j):
         here = jnp.where(to_y == z // 2, 0, 1)
@@ -974,7 +985,7 @@
 
 def project_call(pieces, weights, far_sums):
     own = weights[0]
-    rows, (depth, wide) = len(pieces) * LQ, own.shape
+    rows, (depth, wide) = (len(pieces) - 1) * LQ, own.shape
     dtype = own.dtype
     far = far_sums is None
     vmem = pl.BlockSpec(memory_space=pltpu.VMEM)
@@ -984,6 +995,7 @@
         pltpu.VMEM((2, 2, depth, wide), dtype),
         pltpu.VMEM((2,) + blocks, dtype),
         pltpu.VMEM((2,) + blocks, dtype),
+        pltpu.VMEM((2,) + pieces[-1].shape, dtype),
         pltpu.SemaphoreType.DMA((len(pieces),)),
         pltpu.SemaphoreType.DMA((2, 2)),
         pltpu.SemaphoreType.DMA((8,)),
@@ -1018,7 +1030,8 @@
 def suits_line(mesh, queries, lists):
     passes, heads = mesh.shape["pass"], mesh.shape["head"]
     entries = queries.shape[0] // LQ // passes * lists.shape[1]
-    return passes == 2 * LINE and heads == LINE and entries % passes == 0
+    several = queries.shape[0] // LQ >= 2 * passes
+    return passes == 2 * LINE and heads == LINE and several and entries % passes == 0
 
 
 def solution(mesh):

time: 412 us -> 417 us (1.012)
  starting transfers between devices: 97.1 us -> 136 us
  waiting for transfers between devices: 144 us -> 115 us
  Pallas kernels: 154 us -> 149 us
    ppermute x29, starting transfers between devices: 95.5 us -> 134 us  [send(): return lax.ppermute(value, 'pass', pairs)]
    ppermute x29, waiting for transfers between devices: 144 us -> 115 us  [send(): return lax.ppermute(value, 'pass', pairs)]
    pallas_call x18 -> x16, Pallas kernels: 41.5 us -> 36.5 us  [join_call(): pl.pallas_call(merge_kernel if leveled else finish_kernel, out_shape=jax....]
    unnamed x2 -> x4, local copies, waits for them, and re-layouts: 10.2 us -> 10.3 us
  transfers between devices with their start and end apart: 30 -> 30, of which waited for: 12 -> 14; matrix products, arithmetic and copies ran while one was open for 3% -> 3% of each run, Pallas kernels for 30% -> 28%
where the time goes in v9:
time: 417 us; the launch traced here: 416 us
  Pallas kernels  149 us (36%)
  starting transfers between devices  136 us (33%)
  waiting for transfers between devices  115 us (28%)
  local copies, waits for them, and re-layouts  15.4 us (4%)
    ppermute x29, starting transfers between devices, send(): return lax.ppermute(value, 'pass', pairs)  134 us
    ppermute x29, waiting for transfers between devices, send(): return lax.ppermute(value, 'pass', pairs)  115 us
    pallas_call x5, Pallas kernels, part_call(): pl.pallas_call(functools.partial(part_kernel, k, most, first, last, heads...  71.7 us
    pallas_call x16, Pallas kernels, join_call(): pl.pallas_call(merge_kernel if leveled else finish_kernel, out_shape=jax....  36.5 us
    pallas_call x2, Pallas kernels, project_call(): pl.pallas_call(functools.partial(project_kernel, len(pieces), far), out_s...  33.3 us
    unnamed x4, local copies, waits for them, and re-layouts  10.3 us
  transfers between devices with their start and end apart: 30, of which 14 were waited for; matrix products, arithmetic and copies ran while one was open for 3% of the time, Pallas kernels for 28%

profile of v9, /device:TPU:0, one launch (start us, length us, event | category | flops | bytes accessed | tf_op | source)
XLA Modules:
  0.0 415.5 jit_solution(2990744419123411323)
XLA Ops:
  0.0 3.1 collective-permute-start.2
  4.9 8.2 %copy.16 = bf16[16,512,2,256]{3,1,2,0:T(8,128)(2,1)} copy(bf16[16,512,2,256]{3,2,1,0:T(2,128)(2,1)} %param.9) | data formatting | bytes 16777216 | tf_op args[2]
  13.1 7.8 %sort_items.1 = (s32[12]{0:T(128)}, s32[12]{0:T(128)}, s32[12]{0:T(128)}, bf16[3,2,512,256]{3,2,1,0:T(8,128)(2,1)}, bf16[3,2,512,256]{3,2,1,0:T(8,128)(2,1)}, /*...) custom-call(s32[8,24]{1,0:T(8,128)} %bitcast.16, s32[128]{0:T(128)} %pslot_ref.1, s32[24]{0:T(128)} %qslot_ref.1, ...), custom_call_target="tpu_custom_call" | custom-call | bytes 12582912 | tf_op jit(solution)/shard_map/sort_items/pallas_call | solution.py:437
  21.0 16.8 %collective-permute-done.2.refs_3_ = bf16[384,2048]{1,0:T(8,128)(2,1)} collective-permute-done((bf16[384,2048]{1,0:T(8,128)(2,1)}, bf16[384,2048]{1,0:T(8,128)(2,1)}, u32[]{:S(2)}, u32[]{:S(2)}) %collective-permute-start.2) | collective-permute-done | bytes 1572896 | tf_op jit(solution)/shard_map/ppermute | solution.py:751
  44.3 32.9 %collective-permute-done.7.refs_6_ = bf16[3,2,512,256]{3,2,1,0:T(8,128)(2,1)} collective-permute-done((bf16[3,2,512,256]{3,2,1,0:T(8,128)(2,1)}, bf16[3,2,512,256]{3,2,1,0:T(8,128)(2,1)}, u32[]{:S(2)}, u32[]{:S(2)}) %collective-permute-start.7) | collective-permute-done | bytes 1572896 | tf_op jit(solution)/shard_map/ppermute | solution.py:751
  77.2 3.5 collective-permute-done.6.refs_4_
  80.7 15.5 %shard_map.75.refs_0_ = bf16[3,136,2048]{2,1,0:T(8,128)(2,1)} custom-call(s32[12]{0:T(128)} %get-tuple-element.15.refs_0_, s32[12]{0:T(128)} %get-tuple-element.16.refs_1_, s32[12]{0:T(128)} %get-tuple-element.17.refs_2_, bf16[384,2048]{1,0:T(8,128)(2,1)} %collective-permute-done.3.refs_3_, bf16[384,2048]{1,0:T(8,128)(2,1)} %collective-permute-done.6.refs_4_, ...), custom_call_target="tpu_custom_call" | custom-call | flops 3221225472 | bytes 3145728 | tf_op jit(solution)/shard_map/pallas_call | solution.py:631
  96.2 3.1 collective-permute-start.8
  100.8 2.6 collective-permute-start.22
  103.4 7.4 %collective-permute-done.5.refs_6_ = bf16[3,2,512,256]{3,2,1,0:T(8,128)(2,1)} collective-permute-done((bf16[3,2,512,256]{3,2,1,0:T(8,128)(2,1)}, bf16[3,2,512,256]{3,2,1,0:T(8,128)(2,1)}, u32[]{:S(2)}, u32[]{:S(2)}) %collective-permute-start.5) | collective-permute-done | bytes 1572896 | tf_op jit(solution)/shard_map/ppermute | solution.py:751
  113.9 15.5 %shard_map.74.refs_0_ = bf16[3,136,2048]{2,1,0:T(8,128)(2,1)} custom-call(s32[12]{0:T(128)} %get-tuple-element.15.refs_0_, s32[12]{0:T(128)} %get-tuple-element.16.refs_1_, s32[12]{0:T(128)} %get-tuple-element.17.refs_2_, bf16[384,2048]{1,0:T(8,128)(2,1)} %collective-permute-done.1.refs_3_, bf16[384,2048]{1,0:T(8,128)(2,1)} %collective-permute-done.4.refs_4_, ...), custom_call_target="tpu_custom_call" | custom-call | flops 3221225472 | bytes 3145728 | tf_op jit(solution)/shard_map/pallas_call | solution.py:631
  129.4 5.9 %collective-permute-done.8.refs_1_ = bf16[3,136,2048]{2,1,0:T(8,128)(2,1)} collective-permute-done((bf16[3,136,2048]{2,1,0:T(8,128)(2,1)}, bf16[3,136,2048]{2,1,0:T(8,128)(2,1)}, u32[]{:S(2)}, u32[]{:S(2)}) %collective-permute-start.8) | collective-permute-done | bytes 1671200 | tf_op jit(solution)/shard_map/ppermute | solution.py:751
  135.3 5.5 %collective-permute-start.11 = (bf16[3,136,2048]{2,1,0:T(8,128)(2,1)}, bf16[3,136,2048]{2,1,0:T(8,128)(2,1)}, u32[]{:S(2)}, u32[]{:S(2)}) collective-permute-start(bf16[3,136,2048]{2,1,0:T(8,128)(2,1)} %shard_map.74.refs_0_), channel_id=1, source_target_pairs={{0,8},{4,12},{24,16},{28,20},{1,9},{5,13},{25,17},{29,21},{2,10},{... | collective-permute-start | bytes 5013512 | tf_op jit(solution)/shard_map/ppermute | solution.py:751
  151.4 20.3 %shard_map.73.refs_0_ = bf16[3,136,2048]{2,1,0:T(8,128)(2,1)} custom-call(s32[12]{0:T(128)} %get-tuple-element.15.refs_0_, s32[12]{0:T(128)} %get-tuple-element.16.refs_1_, s32[12]{0:T(128)} %get-tuple-element.17.refs_2_, bf16[3,2,128,256]{3,2,1,0:T(8,128)(2,1)} %bitcast.14, bf16[384,2048]{1,0:T(8,128)(2,1)} %refs_4_.3, bf16[16,2,512,256]{3,2,1,0:T(8,128)(2,1)} %bitcast.11, ...), custom_call_target="tpu_custom_call" | custom-call | flops 3221225472 | bytes 3145728 | tf_op jit(solution)/shard_map/pallas_call | solution.py:631
  180.3 68.7 %collective-permute-start.26 = (bf16[1,136,2048]{2,1,0:T(8,128)(2,1)}, bf16[1,136,2048]{2,1,0:T(8,128)(2,1)}, u32[]{:S(2)}, u32[]{:S(2)}) collective-permute-start(bf16[1,136,2048]{2,1,0:T(8,128)(2,1)} %shard_map.77.a_ref), channel_id=1, source_target_pairs={{0,8},{4,12},{8,0},{12,4},{16,24},{20,28},{24,16},{28,20},{1,9},{5... | collective-permute-start | bytes 1671176 | tf_op jit(solution)/shard_map/ppermute | solution.py:751
  250.9 3.4 collective-permute-start.25
  266.1 2.9 collective-permute-done.27.b_ref
  277.9 20.3 %collective-permute-start.28 = (bf16[1,136,2048]{2,1,0:T(8,128)(2,1)}, bf16[1,136,2048]{2,1,0:T(8,128)(2,1)}, u32[]{:S(2)}, u32[]{:S(2)}) collective-permute-start(bf16[1,136,2048]{2,1,0:T(8,128)(2,1)} %shard_map.89.refs_2_), channel_id=1, source_target_pairs={{0,8},{4,12},{8,0},{12,4},{16,24},{20,28},{24,16},{28,20},{1,9},{5... | collective-permute-start | bytes 1671176 | tf_op jit(solution)/shard_map/ppermute | solution.py:751
  298.2 10.1 %shard_map.78.refs_0_ = bf16[3,136,2048]{2,1,0:T(8,128)(2,1)} custom-call(s32[12]{0:T(128)} %get-tuple-element.15.refs_0_, s32[12]{0:T(128)} %get-tuple-element.16.refs_1_, s32[12]{0:T(128)} %get-tuple-element.17.refs_2_, bf16[384,2048]{1,0:T(8,128)(2,1)} %collective-permute-done.2.refs_3_, bf16[16,2,512,256]{3,2,1,0:T(8,128)(2,1)} %bitcast.12), custom_call_target="tpu_custom_call" | custom-call | flops 1610612736 | bytes 1572864 | tf_op jit(solution)/shard_map/pallas_call | solution.py:631
  308.3 10.2 %shard_map.79.refs_1_ = bf16[3,136,2048]{2,1,0:T(8,128)(2,1)} custom-call(s32[12]{0:T(128)} %get-tuple-element.15.refs_0_, s32[12]{0:T(128)} %get-tuple-element.16.refs_1_, s32[12]{0:T(128)} %get-tuple-element.17.refs_2_, bf16[384,2048]{1,0:T(8,128)(2,1)} %collective-permute-done.2.refs_3_, bf16[16,2,512,256]{3,2,1,0:T(8,128)(2,1)} %bitcast.13, ...), custom_call_target="tpu_custom_call" | custom-call | flops 1610612736 | bytes 1572864 | tf_op jit(solution)/shard_map/pallas_call | solution.py:631
  318.5 2.7 shard_map.81.a_ref
  321.2 2.7 shard_map.86.a_ref
  323.9 2.7 shard_map.91.refs_2_
  326.5 2.5 shard_map.92.refs_0_
  329.0 2.5 shard_map.93.refs_1_
  331.5 8.9 %collective-permute-done.21.refs_6_ = bf16[1024,512]{1,0:T(8,128)(2,1)} collective-permute-done((bf16[1024,512]{1,0:T(8,128)(2,1)}, bf16[1024,512]{1,0:T(8,128)(2,1)}, u32[]{:S(2)}, u32[]{:S(2)}) %collective-permute-start.21) | collective-permute-done | bytes 1048608 | tf_op jit(solution)/shard_map/ppermute | solution.py:751
  340.4 10.8 %project_far.1 = (bf16[2,384,512]{2,1,0:T(8,128)(2,1)}, bf16[2,384,512]{2,1,0:T(8,128)(2,1)}) custom-call(bf16[128,2048]{1,0:T(8,128)(2,1)} %shard_map.92.refs_0_, bf16[128,2048]{1,0:T(8,128)(2,1)} %shard_map.93.refs_1_, bf16[1,136,2048]{2,1,0:T(8,128)(2,1)} %shard_map.91.refs_2_, bf16[1,136,2048]{2,1,0:T(8,128)(2,1)} %collective-permute-done.28.refs_3_, ...), custom_call_target="tpu_custom_call" | custom-call | flops 3221225472 | bytes 8388608 | tf_op jit(solution)/shard_map/project_far/pallas_call | solution.py:1011
  354.7 12.3 %collective-permute-done.13.b_ref = bf16[1,136,2048]{2,1,0:T(8,128)(2,1)} collective-permute-done((bf16[1,136,2048]{2,1,0:T(8,128)(2,1)}, bf16[1,136,2048]{2,1,0:T(8,128)(2,1)}, u32[]{:S(2)}, u32[]{:S(2)}) %collective-permute-start.13) | collective-permute-done | bytes 557088 | tf_op jit(solution)/shard_map/ppermute | solution.py:751
  369.5 9.5 %collective-permute-done.16.b_ref = bf16[1,136,2048]{2,1,0:T(8,128)(2,1)} collective-permute-done((bf16[1,136,2048]{2,1,0:T(8,128)(2,1)}, bf16[1,136,2048]{2,1,0:T(8,128)(2,1)}, u32[]{:S(2)}, u32[]{:S(2)}) %collective-permute-start.16) | collective-permute-done | bytes 557088 | tf_op jit(solution)/shard_map/ppermute | solution.py:751
  379.0 2.5 shard_map.87.refs_1_
  381.4 9.5 %collective-permute-done.19.refs_3_ = bf16[1,136,2048]{2,1,0:T(8,128)(2,1)} collective-permute-done((bf16[1,136,2048]{2,1,0:T(8,128)(2,1)}, bf16[1,136,2048]{2,1,0:T(8,128)(2,1)}, u32[]{:S(2)}, u32[]{:S(2)}) %collective-permute-start.19) | collective-permute-done | bytes 557088 | tf_op jit(solution)/shard_map/ppermute | solution.py:751
  390.9 22.5 %project_home.1 = bf16[384,1024]{1,0:T(8,128)(2,1)} custom-call(bf16[128,2048]{1,0:T(8,128)(2,1)} %shard_map.82.refs_0_, bf16[128,2048]{1,0:T(8,128)(2,1)} %shard_map.87.refs_1_, bf16[1,136,2048]{2,1,0:T(8,128)(2,1)} %shard_map.89.refs_2_, bf16[1,136,2048]{2,1,0:T(8,128)(2,1)} %collective-permute-done.19.refs_3_, bf16[2048,512]{1,0:T(8,128)(2,1)} %refs_4_.5, ...), custom_call_target="tpu_custom_call" | custom-call | flops 3221225472 | bytes 8388608 | tf_op jit(solution)/shard_map/project_home/pallas_call | solution.py:1011
  (59 shorter events, 62.6 us)
Async XLA Ops:
  0.0 37.8 %collective-permute-start.2 = (bf16[384,2048]{1,0:T(8,128)(2,1)}, bf16[384,2048]{1,0:T(8,128)(2,1)}, u32[]{:S(2)}, u32[]{:S(2)}) collective-permute-start(bf16[384,2048]{1,0:T(8,128)(2,1)} %refs_4_.3), channel_id=1, source_target_pairs={{0,8},{4,12},{8,0},{12,4},{16,24},{20,28},{24,16},{28,20},{1,9},{5... | collective-permute-start | bytes 4718600 | tf_op jit(solution)/shard_map/ppermute | solution.py:751
  3.1 38.2 %collective-permute-start.1 = (bf16[384,2048]{1,0:T(8,128)(2,1)}, bf16[384,2048]{1,0:T(8,128)(2,1)}, u32[]{:S(2)}, u32[]{:S(2)}) collective-permute-start(bf16[384,2048]{1,0:T(8,128)(2,1)} %refs_4_.3), channel_id=1, source_target_pairs={{8,16},{12,20},{16,8},{20,12},{9,17},{13,21},{17,9},{21,13},{10,18... | collective-permute-start | bytes 4718600 | tf_op jit(solution)/shard_map/ppermute | solution.py:751
  37.8 5.2 %collective-permute-start.3 = (bf16[384,2048]{1,0:T(8,128)(2,1)}, bf16[384,2048]{1,0:T(8,128)(2,1)}, u32[]{:S(2)}, u32[]{:S(2)}) collective-permute-start(bf16[384,2048]{1,0:T(8,128)(2,1)} %collective-permute-done.2.refs_3_), channel_id=1, source_target_pairs={{8,16},{12,20},{16,8},{20,12},{9,17},{13,21},{17,9},{21,13},{10,18... | collective-permute-start | bytes 4718600 | tf_op jit(solution)/shard_map/ppermute | solution.py:751
  39.6 37.6 %collective-permute-start.7 = (bf16[3,2,512,256]{3,2,1,0:T(8,128)(2,1)}, bf16[3,2,512,256]{3,2,1,0:T(8,128)(2,1)}, u32[]{:S(2)}, u32[]{:S(2)}) collective-permute-start(bf16[3,2,512,256]{3,2,1,0:T(8,128)(2,1)} %get-tuple-element.20), channel_id=1, source_target_pairs={{0,4},{4,0},{8,12},{12,8},{16,20},{20,16},{24,28},{28,24},{1,5},{5... | collective-permute-start | bytes 4718600 | tf_op jit(solution)/shard_map/ppermute | solution.py:751
  41.2 39.4 %collective-permute-start.6 = (bf16[384,2048]{1,0:T(8,128)(2,1)}, bf16[384,2048]{1,0:T(8,128)(2,1)}, u32[]{:S(2)}, u32[]{:S(2)}) collective-permute-start(bf16[384,2048]{1,0:T(8,128)(2,1)} %collective-permute-done.1.refs_3_), channel_id=1, source_target_pairs={{8,0},{12,4},{16,24},{20,28},{9,1},{13,5},{17,25},{21,29},{10,2},{... | collective-permute-start | bytes 4718600 | tf_op jit(solution)/shard_map/ppermute | solution.py:751
  42.5 68.3 %collective-permute-start.5 = (bf16[3,2,512,256]{3,2,1,0:T(8,128)(2,1)}, bf16[3,2,512,256]{3,2,1,0:T(8,128)(2,1)}, u32[]{:S(2)}, u32[]{:S(2)}) collective-permute-start(bf16[3,2,512,256]{3,2,1,0:T(8,128)(2,1)} %get-tuple-element.19), channel_id=1, source_target_pairs={{0,4},{4,0},{8,12},{12,8},{16,20},{20,16},{24,28},{28,24},{1,5},{5... | collective-permute-start | bytes 4718600 | tf_op jit(solution)/shard_map/ppermute | solution.py:751
  43.0 69.8 %collective-permute-start.4 = (bf16[384,2048]{1,0:T(8,128)(2,1)}, bf16[384,2048]{1,0:T(8,128)(2,1)}, u32[]{:S(2)}, u32[]{:S(2)}) collective-permute-start(bf16[384,2048]{1,0:T(8,128)(2,1)} %collective-permute-done.3.refs_3_), channel_id=1, source_target_pairs={{8,0},{12,4},{16,24},{20,28},{9,1},{13,5},{17,25},{21,29},{10,2},{... | collective-permute-start | bytes 4718600 | tf_op jit(solution)/shard_map/ppermute | solution.py:751
  96.2 39.1 %collective-permute-start.8 = (bf16[3,136,2048]{2,1,0:T(8,128)(2,1)}, bf16[3,136,2048]{2,1,0:T(8,128)(2,1)}, u32[]{:S(2)}, u32[]{:S(2)}) collective-permute-start(bf16[3,136,2048]{2,1,0:T(8,128)(2,1)} %shard_map.75.refs_0_), channel_id=1, source_target_pairs={{0,8},{4,12},{24,16},{28,20},{1,9},{5,13},{25,17},{29,21},{2,10},{... | collective-permute-start | bytes 5013512 | tf_op jit(solution)/shard_map/ppermute | solution.py:751
  99.3 45.3 %collective-permute-start = (bf16[3,2,512,256]{3,2,1,0:T(8,128)(2,1)}, bf16[3,2,512,256]{3,2,1,0:T(8,128)(2,1)}, u32[]{:S(2)}, u32[]{:S(2)}) collective-permute-start(bf16[3,2,512,256]{3,2,1,0:T(8,128)(2,1)} %get-tuple-element.18), channel_id=1, source_target_pairs={{0,4},{4,0},{8,12},{12,8},{16,20},{20,16},{24,28},{28,24},{1,5},{5... | collective-permute-start | bytes 4718600 | tf_op jit(solution)/shard_map/ppermute | solution.py:751
  100.8 79.5 %collective-permute-start.22 = (bf16[2048,512]{1,0:T(8,128)(2,1)}, bf16[2048,512]{1,0:T(8,128)(2,1)}, u32[]{:S(2)}, u32[]{:S(2)}) collective-permute-start(bf16[2048,512]{1,0:T(8,128)(2,1)} %refs_4_.5), channel_id=1, source_target_pairs={{0,16},{4,20},{24,8},{28,12},{1,17},{5,21},{25,9},{29,13},{2,18},{... | collective-permute-start | bytes 6291464 | tf_op jit(solution)/shard_map/ppermute | solution.py:751
  110.9 138.1 %collective-permute-start.24 = (bf16[2048,512]{1,0:T(8,128)(2,1)}, bf16[2048,512]{1,0:T(8,128)(2,1)}, u32[]{:S(2)}, u32[]{:S(2)}) collective-permute-start(bf16[2048,512]{1,0:T(8,128)(2,1)} %refs_4_.5), channel_id=1, source_target_pairs={{8,24},{12,28},{16,0},{20,4},{9,25},{13,29},{17,1},{21,5},{10,26},... | collective-permute-start | bytes 6291464 | tf_op jit(solution)/shard_map/ppermute | solution.py:751
  112.8 63.8 %collective-permute-start.10 = (bf16[3,2,512,256]{3,2,1,0:T(8,128)(2,1)}, bf16[3,2,512,256]{3,2,1,0:T(8,128)(2,1)}, u32[]{:S(2)}, u32[]{:S(2)}) collective-permute-start(bf16[3,2,512,256]{3,2,1,0:T(8,128)(2,1)} %get-tuple-element.21), channel_id=1, source_target_pairs={{0,4},{4,0},{8,12},{12,8},{16,20},{20,16},{24,28},{28,24},{1,5},{5... | collective-permute-start | bytes 4718600 | tf_op jit(solution)/shard_map/ppermute | solution.py:751
  135.3 121.1 %collective-permute-start.11 = (bf16[3,136,2048]{2,1,0:T(8,128)(2,1)}, bf16[3,136,2048]{2,1,0:T(8,128)(2,1)}, u32[]{:S(2)}, u32[]{:S(2)}) collective-permute-start(bf16[3,136,2048]{2,1,0:T(8,128)(2,1)} %shard_map.74.refs_0_), channel_id=1, source_target_pairs={{0,8},{4,12},{24,16},{28,20},{1,9},{5,13},{25,17},{29,21},{2,10},{... | collective-permute-start | bytes 5013512 | tf_op jit(solution)/shard_map/ppermute | solution.py:751
  144.6 3.5 collective-permute-start.9
  148.1 102.8 %collective-permute-start.14 = (bf16[1,136,2048]{2,1,0:T(8,128)(2,1)}, bf16[1,136,2048]{2,1,0:T(8,128)(2,1)}, u32[]{:S(2)}, u32[]{:S(2)}) collective-permute-start(bf16[1,136,2048]{2,1,0:T(8,128)(2,1)} %shard_map.83), channel_id=1, source_target_pairs={{8,16},{12,20},{16,8},{20,12},{9,17},{13,21},{17,9},{21,13},{10,18... | collective-permute-start | bytes 1671176 | tf_op jit(solution)/shard_map/ppermute | solution.py:751
  176.6 84.5 %collective-permute-start.17 = (bf16[1,136,2048]{2,1,0:T(8,128)(2,1)}, bf16[1,136,2048]{2,1,0:T(8,128)(2,1)}, u32[]{:S(2)}, u32[]{:S(2)}) collective-permute-start(bf16[1,136,2048]{2,1,0:T(8,128)(2,1)} %shard_map.88), channel_id=1, source_target_pairs={{8,16},{12,20},{16,8},{20,12},{9,17},{13,21},{17,9},{21,13},{10,18... | collective-permute-start | bytes 1671176 | tf_op jit(solution)/shard_map/ppermute | solution.py:751
  180.3 82.3 %collective-permute-start.26 = (bf16[1,136,2048]{2,1,0:T(8,128)(2,1)}, bf16[1,136,2048]{2,1,0:T(8,128)(2,1)}, u32[]{:S(2)}, u32[]{:S(2)}) collective-permute-start(bf16[1,136,2048]{2,1,0:T(8,128)(2,1)} %shard_map.77.a_ref), channel_id=1, source_target_pairs={{0,8},{4,12},{8,0},{12,4},{16,24},{20,28},{24,16},{28,20},{1,9},{5... | collective-permute-start | bytes 1671176 | tf_op jit(solution)/shard_map/ppermute | solution.py:751
  249.0 91.4 %collective-permute-start.23 = (bf16[2048,512]{1,0:T(8,128)(2,1)}, bf16[2048,512]{1,0:T(8,128)(2,1)}, u32[]{:S(2)}, u32[]{:S(2)}) collective-permute-start(bf16[2048,512]{1,0:T(8,128)(2,1)} %collective-permute-done.22.refs_7_), channel_id=1, source_target_pairs={{8,12},{12,8},{16,20},{20,16},{9,13},{13,9},{17,21},{21,17},{10,14... | collective-permute-start | bytes 6291464 | tf_op jit(solution)/shard_map/ppermute | solution.py:751
  250.9 89.4 %collective-permute-start.25 = (bf16[2048,512]{1,0:T(8,128)(2,1)}, bf16[2048,512]{1,0:T(8,128)(2,1)}, u32[]{:S(2)}, u32[]{:S(2)}) collective-permute-start(bf16[2048,512]{1,0:T(8,128)(2,1)} %collective-permute-done.24.refs_9_), channel_id=1, source_target_pairs={{0,4},{4,0},{24,28},{28,24},{1,5},{5,1},{25,29},{29,25},{2,6},{6,2... | collective-permute-start | bytes 6291464 | tf_op jit(solution)/shard_map/ppermute | solution.py:751
  256.4 12.6 %collective-permute-start.27 = (bf16[1,136,2048]{2,1,0:T(8,128)(2,1)}, bf16[1,136,2048]{2,1,0:T(8,128)(2,1)}, u32[]{:S(2)}, u32[]{:S(2)}) collective-permute-start(bf16[1,136,2048]{2,1,0:T(8,128)(2,1)} %shard_map.84.a_ref), channel_id=1, source_target_pairs={{0,8},{4,12},{8,0},{12,4},{16,24},{20,28},{24,16},{28,20},{1,9},{5... | collective-permute-start | bytes 1671176 | tf_op jit(solution)/shard_map/ppermute | solution.py:751
  261.0 12.7 %collective-permute-start.12 = (bf16[1,136,2048]{2,1,0:T(8,128)(2,1)}, bf16[1,136,2048]{2,1,0:T(8,128)(2,1)}, u32[]{:S(2)}, u32[]{:S(2)}) collective-permute-start(bf16[1,136,2048]{2,1,0:T(8,128)(2,1)} %shard_map.80), channel_id=1, source_target_pairs={{8,16},{12,20},{16,8},{20,12},{9,17},{13,21},{17,9},{21,13},{10,18... | collective-permute-start | bytes 1671176 | tf_op jit(solution)/shard_map/ppermute | solution.py:751
  262.5 12.8 %collective-permute-start.15 = (bf16[1,136,2048]{2,1,0:T(8,128)(2,1)}, bf16[1,136,2048]{2,1,0:T(8,128)(2,1)}, u32[]{:S(2)}, u32[]{:S(2)}) collective-permute-start(bf16[1,136,2048]{2,1,0:T(8,128)(2,1)} %shard_map.85), channel_id=1, source_target_pairs={{8,16},{12,20},{16,8},{20,12},{9,17},{13,21},{17,9},{21,13},{10,18... | collective-permute-start | bytes 1671176 | tf_op jit(solution)/shard_map/ppermute | solution.py:751
  266.1 6.7 %copy-start = (bf16[2048,512]{1,0:T(8,128)(2,1)S(1)}, bf16[2048,512]{1,0:T(8,128)(2,1)}, u32[]{:S(2)}) copy-start(bf16[2048,512]{1,0:T(8,128)(2,1)} %refs_4_.5) | copy-start | bytes 6291460
  269.0 8.9 %collective-permute-start.18 = (bf16[1,136,2048]{2,1,0:T(8,128)(2,1)}, bf16[1,136,2048]{2,1,0:T(8,128)(2,1)}, u32[]{:S(2)}, u32[]{:S(2)}) collective-permute-start(bf16[1,136,2048]{2,1,0:T(8,128)(2,1)} %shard_map.90), channel_id=1, source_target_pairs={{8,16},{12,20},{16,8},{20,12},{9,17},{13,21},{17,9},{21,13},{10,18... | collective-permute-start | bytes 1671176 | tf_op jit(solution)/shard_map/ppermute | solution.py:751
  273.8 57.7 %collective-permute-start.20 = (bf16[1024,512]{1,0:T(8,128)(2,1)}, bf16[1024,512]{1,0:T(8,128)(2,1)}, u32[]{:S(2)}, u32[]{:S(2)}) collective-permute-start(bf16[1024,512]{1,0:T(8,128)(2,1)} %slice.6), channel_id=1, source_target_pairs={{0,4},{4,0},{8,12},{12,8},{16,20},{20,16},{24,28},{28,24},{1,5},{5... | collective-permute-start | bytes 3145736 | tf_op jit(solution)/shard_map/ppermute | solution.py:751
  275.3 65.1 %collective-permute-start.21 = (bf16[1024,512]{1,0:T(8,128)(2,1)}, bf16[1024,512]{1,0:T(8,128)(2,1)}, u32[]{:S(2)}, u32[]{:S(2)}) collective-permute-start(bf16[1024,512]{1,0:T(8,128)(2,1)} %slice.7), channel_id=1, source_target_pairs={{0,4},{4,0},{8,12},{12,8},{16,20},{20,16},{24,28},{28,24},{1,5},{5... | collective-permute-start | bytes 3145736 | tf_op jit(solution)/shard_map/ppermute | solution.py:751
  277.9 62.5 %collective-permute-start.28 = (bf16[1,136,2048]{2,1,0:T(8,128)(2,1)}, bf16[1,136,2048]{2,1,0:T(8,128)(2,1)}, u32[]{:S(2)}, u32[]{:S(2)}) collective-permute-start(bf16[1,136,2048]{2,1,0:T(8,128)(2,1)} %shard_map.89.refs_2_), channel_id=1, source_target_pairs={{0,8},{4,12},{8,0},{12,4},{16,24},{20,28},{24,16},{28,20},{1,9},{5... | collective-permute-start | bytes 1671176 | tf_op jit(solution)/shard_map/ppermute | solution.py:751
  351.2 39.8 %collective-permute-start.29 = (bf16[2,384,512]{2,1,0:T(8,128)(2,1)}, bf16[2,384,512]{2,1,0:T(8,128)(2,1)}, u32[]{:S(2)}, u32[]{:S(2)}) collective-permute-start(bf16[2,384,512]{2,1,0:T(8,128)(2,1)} %get-tuple-element.24), channel_id=1, source_target_pairs={{1,3},{3,1},{5,7},{7,5},{8,10},{10,8},{12,14},{14,12},{17,19},{19,... | collective-permute-start | bytes 2359304 | tf_op jit(solution)/shard_map/ppermute | solution.py:817
  352.7 14.3 %collective-permute-start.13 = (bf16[1,136,2048]{2,1,0:T(8,128)(2,1)}, bf16[1,136,2048]{2,1,0:T(8,128)(2,1)}, u32[]{:S(2)}, u32[]{:S(2)}) collective-permute-start(bf16[1,136,2048]{2,1,0:T(8,128)(2,1)} %shard_map.81.a_ref), channel_id=1, source_target_pairs={{0,8},{4,12},{8,0},{12,4},{16,24},{20,28},{24,16},{28,20},{1,9},{5... | collective-permute-start | bytes 1671176 | tf_op jit(solution)/shard_map/ppermute | solution.py:751
  352.7 26.3 %collective-permute-start.16 = (bf16[1,136,2048]{2,1,0:T(8,128)(2,1)}, bf16[1,136,2048]{2,1,0:T(8,128)(2,1)}, u32[]{:S(2)}, u32[]{:S(2)}) collective-permute-start(bf16[1,136,2048]{2,1,0:T(8,128)(2,1)} %shard_map.86.a_ref), channel_id=1, source_target_pairs={{0,8},{4,12},{8,0},{12,4},{16,24},{20,28},{24,16},{28,20},{1,9},{5... | collective-permute-start | bytes 1671176 | tf_op jit(solution)/shard_map/ppermute | solution.py:751
  354.7 36.2 %collective-permute-start.19 = (bf16[1,136,2048]{2,1,0:T(8,128)(2,1)}, bf16[1,136,2048]{2,1,0:T(8,128)(2,1)}, u32[]{:S(2)}, u32[]{:S(2)}) collective-permute-start(bf16[1,136,2048]{2,1,0:T(8,128)(2,1)} %shard_map.91.refs_2_), channel_id=1, source_target_pairs={{0,8},{4,12},{8,0},{12,4},{16,24},{20,28},{24,16},{28,20},{1,9},{5... | collective-permute-start | bytes 1671176 | tf_op jit(solution)/shard_map/ppermute | solution.py:751

commit v10 on v9

--- a/solution.py
+++ b/solution.py
@@ -803,18 +803,8 @@
             near_rows += [near1, beside]
             own_rows += [near0, back1]
     weights = (out_weight, w_across0, w_across1, w_in, w_in_both, w_out, w_out_both)
-    far_send, far_keep = project_call(near_rows, weights, None)
-    far_sent = send_far(far_send)
-    return project_call(own_rows, weights, (far_keep, far_sent))
-
-
-def send_far(sums):
-    pairs = []
-    for p in range(2 * LINE):
-        for h in range(LINE):
-            if h % 2 != (p // 2) % 2:
-                pairs.append((p * LINE + h, p * LINE + (h ^ 2)))
-    return lax.ppermute(sums, ("pass", "head"), pairs)
+    far_sums = project_call(near_rows, weights, None)
+    return project_call(own_rows, weights, far_sums)
 
 
 MESH = pl.DeviceIdType.MESH
@@ -828,12 +818,10 @@
     rows_refs = refs[:pieces]
     own_ref, a0_ref, a1_ref, in_ref, in2_ref, out1_ref, out2_ref = refs[pieces : pieces + 7]
     refs = refs[pieces + 7 :]
-    if far:
-        send_ref, keep_ref = refs[:2]
-    else:
-        far_keep_ref, far_sent_ref, out_ref = refs[:3]
-        refs = refs[1:]
-    context_ref, w_ref, part_ref, core_ref, pair_ref, row_sem, w_sem, send_sem, recv_sem = refs[2:11]
+    if not far:
+        far_ref, *refs = refs
+    out_ref, context_ref, w_ref, part_ref, core_ref, pair_ref, y_ref, ysend_ref = refs[:8]
+    row_sem, w_sem, send_sem, recv_sem = refs[8:]
     me, head = lax.axis_index("pass"), lax.axis_index("head")
     z, x, y = me // 2, me % 2, head // 2
     wide = w_ref.shape[3]
@@ -885,7 +873,7 @@
         load_here()
 
     barrier = pltpu.get_barrier_semaphore()
-    peers = (core_peer,) if far else (core_peer, y_peer, z_peer)
+    peers = (core_peer, y_peer) if far else (core_peer, y_peer, z_peer)
     for peer in peers:
         pl.semaphore_signal(barrier, inc=1, device_id=peer, device_id_type=MESH)
     pl.semaphore_wait(barrier, len(peers))
@@ -907,20 +895,16 @@
         [remote(part_ref.at[s, j], core_ref.at[s, j], s * 2 + j, core_peer) for j in range(2)]
         for s in range(2)
     ]
+    y_copies = [remote(ysend_ref.at[j], y_ref.at[j], 4 + j, y_peer) for j in range(2)]
     if not far:
-        y_ref, ysend_ref, zsend_ref = refs[11:]
-        y_copies = [remote(ysend_ref.at[j], y_ref.at[j], 4 + j, y_peer) for j in range(2)]
         z_copies = [
-            remote(zsend_ref.at[j], out_ref.at[:, columns(j)], 6 + j, z_peer) for j in range(2)
+            remote(far_ref.at[j], out_ref.at[:, columns(j)], 6 + j, z_peer) for j in range(2)
         ]
 
         @pl.when(jnp.logical_not(home))
         def _():
-            for j in range(2):
-                zsend_ref[j] = (
-                    far_keep_ref[j].astype(jnp.float32) + far_sent_ref[j].astype(jnp.float32)
-                ).astype(zsend_ref.dtype)
-                z_copies[j].start()
+            for copy in z_copies:
+                copy.start()
 
     for load in row_loads:
         load.wait()
@@ -943,17 +927,16 @@
         def _():
             core_copies[s][j].wait_recv()
             value = part_ref[s, j].astype(jnp.float32) + core_ref[s, j].astype(jnp.float32)
-            if far:
-                target = keep_ref if s else send_ref
-                target[j] = value.astype(target.dtype)
-            elif s == 0:
+            if s == 0:
                 ysend_ref[j] = value.astype(ysend_ref.dtype)
                 y_copies[j].start()
+                return
+            y_copies[j].wait_recv()
+            total = (value + y_ref[j].astype(jnp.float32)).astype(out_ref.dtype)
+            if far:
+                out_ref[j] = total
             else:
-                y_copies[j].wait_recv()
-                out_ref[:, columns(j)] = (value + y_ref[j].astype(jnp.float32)).astype(
-                    out_ref.dtype
-                )
+                out_ref[:, columns(j)] = total
 
     late = None
     for s, to_y in enumerate((1 - y, y)):
@@ -970,12 +953,12 @@
             for copy in copies:
                 copy.wait_send()
 
+    @pl.when(sums)
+    def _():
+        for copy in y_copies:
+            copy.wait_send()
+
     if not far:
-
-        @pl.when(home)
-        def _():
-            for copy in y_copies:
-                copy.wait_send()
 
         @pl.when(jnp.logical_not(home))
         def _():
@@ -996,24 +979,20 @@
         pltpu.VMEM((2,) + blocks, dtype),
         pltpu.VMEM((2,) + blocks, dtype),
         pltpu.VMEM((2,) + pieces[-1].shape, dtype),
+        pltpu.VMEM(blocks, dtype),
+        pltpu.VMEM(blocks, dtype),
         pltpu.SemaphoreType.DMA((len(pieces),)),
         pltpu.SemaphoreType.DMA((2, 2)),
         pltpu.SemaphoreType.DMA((8,)),
         pltpu.SemaphoreType.DMA((8,)),
     ]
-    if far:
-        out_shape = [jax.ShapeDtypeStruct(blocks, dtype)] * 2
-        out_specs = [vmem] * 2
-    else:
-        out_shape = jax.ShapeDtypeStruct((rows, 2 * wide), dtype)
-        out_specs = vmem
-        scratch += [pltpu.VMEM(blocks, dtype)] * 3
+    shape = blocks if far else (rows, 2 * wide)
     return pl.pallas_call(
         functools.partial(project_kernel, len(pieces), far),
-        out_shape=out_shape,
+        out_shape=jax.ShapeDtypeStruct(shape, dtype),
         in_specs=[pl.BlockSpec(memory_space=pl.ANY)] * (len(pieces) + len(weights))
-        + [vmem] * (0 if far else 2),
-        out_specs=out_specs,
+        + [vmem] * (0 if far else 1),
+        out_specs=vmem,
         scratch_shapes=scratch,
         compiler_params=pltpu.CompilerParams(
             collective_id=int(far), has_side_effects=True, vmem_limit_bytes=VMEM_BYTES
@@ -1024,7 +1003,7 @@
             bytes_accessed=4 * depth * wide * 2,
             transcendentals=0,
         ),
-    )(*pieces, *weights, *(far_sums or ()))
+    )(*pieces, *weights, *([] if far else [far_sums]))
 
 
 def suits_line(mesh, queries, lists):

time: 417 us -> 407 us (0.976)
  starting transfers between devices: 136 us -> 122 us
    ppermute x29, starting transfers between devices: 134 us -> 122 us  [send(): return lax.ppermute(value, 'pass', pairs)]
    unnamed x4 -> x2, local copies, waits for them, and re-layouts: 10.3 us -> 10.3 us
  transfers between devices with their start and end apart: 30 -> 29, of which waited for: 14 -> 7; matrix products, arithmetic and copies ran while one was open for 3% -> 3% of each run, Pallas kernels for 28% -> 31%
where the time goes in v10:
time: 407 us; the launch traced here: 405 us
  Pallas kernels  149 us (37%)
  starting transfers between devices  122 us (30%)
  waiting for transfers between devices  119 us (29%)
  local copies, waits for them, and re-layouts  15.6 us (4%)
    ppermute x29, starting transfers between devices, send(): return lax.ppermute(value, 'pass', pairs)  122 us
    ppermute x29, waiting for transfers between devices, send(): return lax.ppermute(value, 'pass', pairs)  119 us
    pallas_call x5, Pallas kernels, part_call(): pl.pallas_call(functools.partial(part_kernel, k, most, first, last, heads...  71.8 us
    pallas_call x16, Pallas kernels, join_call(): pl.pallas_call(merge_kernel if leveled else finish_kernel, out_shape=jax....  36.5 us
    pallas_call x2, Pallas kernels, project_call(): pl.pallas_call(functools.partial(project_kernel, len(pieces), far), out_s...  32.8 us
    unnamed x2, local copies, waits for them, and re-layouts  10.3 us
  transfers between devices with their start and end apart: 29, of which 7 were waited for; matrix products, arithmetic and copies ran while one was open for 3% of the time, Pallas kernels for 31%

profile of v10, /device:TPU:0, one launch (start us, length us, event | category | flops | bytes accessed | tf_op | source)
XLA Modules:
  0.0 405.3 jit_solution(2946744394309847526)
XLA Ops:
  0.0 3.1 collective-permute-start.2
  4.9 8.2 %copy.16 = bf16[16,512,2,256]{3,1,2,0:T(8,128)(2,1)} copy(bf16[16,512,2,256]{3,2,1,0:T(2,128)(2,1)} %param.9) | data formatting | bytes 16777216 | tf_op args[2]
  13.0 7.9 %sort_items.1 = (s32[12]{0:T(128)}, s32[12]{0:T(128)}, s32[12]{0:T(128)}, bf16[3,2,512,256]{3,2,1,0:T(8,128)(2,1)}, bf16[3,2,512,256]{3,2,1,0:T(8,128)(2,1)}, /*...) custom-call(s32[8,24]{1,0:T(8,128)} %bitcast.16, s32[128]{0:T(128)} %pslot_ref.1, s32[24]{0:T(128)} %qslot_ref.1, ...), custom_call_target="tpu_custom_call" | custom-call | bytes 12582912 | tf_op jit(solution)/shard_map/sort_items/pallas_call | solution.py:437
  21.0 2.6 collective-permute-start.7
  23.6 14.1 %collective-permute-done.2.refs_3_ = bf16[384,2048]{1,0:T(8,128)(2,1)} collective-permute-done((bf16[384,2048]{1,0:T(8,128)(2,1)}, bf16[384,2048]{1,0:T(8,128)(2,1)}, u32[]{:S(2)}, u32[]{:S(2)}) %collective-permute-start.2) | collective-permute-done | bytes 1572896 | tf_op jit(solution)/shard_map/ppermute | solution.py:751
  43.9 9.2 %collective-permute-start.22 = (bf16[2048,512]{1,0:T(8,128)(2,1)}, bf16[2048,512]{1,0:T(8,128)(2,1)}, u32[]{:S(2)}, u32[]{:S(2)}) collective-permute-start(bf16[2048,512]{1,0:T(8,128)(2,1)} %refs_4_.5), channel_id=1, source_target_pairs={{0,16},{4,20},{24,8},{28,12},{1,17},{5,21},{25,9},{29,13},{2,18},{... | collective-permute-start | bytes 6291464 | tf_op jit(solution)/shard_map/ppermute | solution.py:751
  53.2 27.4 %collective-permute-done.20.refs_5_ = bf16[1024,512]{1,0:T(8,128)(2,1)} collective-permute-done((bf16[1024,512]{1,0:T(8,128)(2,1)S(1)}, bf16[1024,512]{1,0:T(8,128)(2,1)}, u32[]{:S(2)}, u32[]{:S(2)}) %collective-permute-start.20) | collective-permute-done | bytes 1048608 | tf_op jit(solution)/shard_map/ppermute | solution.py:751
  84.9 2.3 slice.7
  87.4 15.5 %shard_map.75.refs_0_ = bf16[3,136,2048]{2,1,0:T(8,128)(2,1)} custom-call(s32[12]{0:T(128)} %get-tuple-element.13.refs_0_, s32[12]{0:T(128)} %get-tuple-element.14.refs_1_, s32[12]{0:T(128)} %get-tuple-element.15.refs_2_, bf16[384,2048]{1,0:T(8,128)(2,1)} %collective-permute-done.3.refs_3_, bf16[384,2048]{1,0:T(8,128)(2,1)} %collective-permute-done.6.refs_4_, ...), custom_call_target="tpu_custom_call" | custom-call | flops 3221225472 | bytes 3145728 | tf_op jit(solution)/shard_map/pallas_call | solution.py:631
  103.0 15.1 %collective-permute-done.5.refs_6_ = bf16[3,2,512,256]{3,2,1,0:T(8,128)(2,1)} collective-permute-done((bf16[3,2,512,256]{3,2,1,0:T(8,128)(2,1)}, bf16[3,2,512,256]{3,2,1,0:T(8,128)(2,1)}, u32[]{:S(2)}, u32[]{:S(2)}) %collective-permute-start.5) | collective-permute-done | bytes 1572896 | tf_op jit(solution)/shard_map/ppermute | solution.py:751
  118.1 30.7 %collective-permute-start.8 = (bf16[3,136,2048]{2,1,0:T(8,128)(2,1)}, bf16[3,136,2048]{2,1,0:T(8,128)(2,1)}, u32[]{:S(2)}, u32[]{:S(2)}) collective-permute-start(bf16[3,136,2048]{2,1,0:T(8,128)(2,1)} %shard_map.75.refs_0_), channel_id=1, source_target_pairs={{0,8},{4,12},{24,16},{28,20},{1,9},{5,13},{25,17},{29,21},{2,10},{... | collective-permute-start | bytes 5013512 | tf_op jit(solution)/shard_map/ppermute | solution.py:751
  149.3 50.2 %collective-permute-done.4.refs_4_ = bf16[384,2048]{1,0:T(8,128)(2,1)} collective-permute-done((bf16[384,2048]{1,0:T(8,128)(2,1)}, bf16[384,2048]{1,0:T(8,128)(2,1)}, u32[]{:S(2)}, u32[]{:S(2)}) %collective-permute-start.4) | collective-permute-done | bytes 1572896 | tf_op jit(solution)/shard_map/ppermute | solution.py:751
  201.5 15.6 %shard_map.74.refs_0_ = bf16[3,136,2048]{2,1,0:T(8,128)(2,1)} custom-call(s32[12]{0:T(128)} %get-tuple-element.13.refs_0_, s32[12]{0:T(128)} %get-tuple-element.14.refs_1_, s32[12]{0:T(128)} %get-tuple-element.15.refs_2_, bf16[384,2048]{1,0:T(8,128)(2,1)} %collective-permute-done.1.refs_3_, bf16[384,2048]{1,0:T(8,128)(2,1)} %collective-permute-done.4.refs_4_, ...), custom_call_target="tpu_custom_call" | custom-call | flops 3221225472 | bytes 3145728 | tf_op jit(solution)/shard_map/pallas_call | solution.py:631
  217.1 4.1 %collective-permute-start.11 = (bf16[3,136,2048]{2,1,0:T(8,128)(2,1)}, bf16[3,136,2048]{2,1,0:T(8,128)(2,1)}, u32[]{:S(2)}, u32[]{:S(2)}) collective-permute-start(bf16[3,136,2048]{2,1,0:T(8,128)(2,1)} %shard_map.74.refs_0_), channel_id=1, source_target_pairs={{0,8},{4,12},{24,16},{28,20},{1,9},{5,13},{25,17},{29,21},{2,10},{... | collective-permute-start | bytes 5013512 | tf_op jit(solution)/shard_map/ppermute | solution.py:751
  221.8 3.4 collective-permute-start.25
  230.5 20.3 %shard_map.73.refs_0_ = bf16[3,136,2048]{2,1,0:T(8,128)(2,1)} custom-call(s32[12]{0:T(128)} %get-tuple-element.13.refs_0_, s32[12]{0:T(128)} %get-tuple-element.14.refs_1_, s32[12]{0:T(128)} %get-tuple-element.15.refs_2_, bf16[3,2,128,256]{3,2,1,0:T(8,128)(2,1)} %bitcast.14, bf16[384,2048]{1,0:T(8,128)(2,1)} %refs_4_.3, bf16[16,2,512,256]{3,2,1,0:T(8,128)(2,1)} %bitcast.11, ...), custom_call_target="tpu_custom_call" | custom-call | flops 3221225472 | bytes 3145728 | tf_op jit(solution)/shard_map/pallas_call | solution.py:631
  252.9 6.0 %collective-permute-done.10.refs_5_ = bf16[3,2,512,256]{3,2,1,0:T(8,128)(2,1)} collective-permute-done((bf16[3,2,512,256]{3,2,1,0:T(8,128)(2,1)}, bf16[3,2,512,256]{3,2,1,0:T(8,128)(2,1)}, u32[]{:S(2)}, u32[]{:S(2)}) %collective-permute-start.10) | collective-permute-done | bytes 1572896 | tf_op jit(solution)/shard_map/ppermute | solution.py:751
  266.0 27.0 %collective-permute-start.26 = (bf16[1,136,2048]{2,1,0:T(8,128)(2,1)}, bf16[1,136,2048]{2,1,0:T(8,128)(2,1)}, u32[]{:S(2)}, u32[]{:S(2)}) collective-permute-start(bf16[1,136,2048]{2,1,0:T(8,128)(2,1)} %shard_map.77.a_ref), channel_id=1, source_target_pairs={{0,8},{4,12},{8,0},{12,4},{16,24},{20,28},{24,16},{28,20},{1,9},{5... | collective-permute-start | bytes 1671176 | tf_op jit(solution)/shard_map/ppermute | solution.py:751
  305.7 12.0 %collective-permute-start.27 = (bf16[1,136,2048]{2,1,0:T(8,128)(2,1)}, bf16[1,136,2048]{2,1,0:T(8,128)(2,1)}, u32[]{:S(2)}, u32[]{:S(2)}) collective-permute-start(bf16[1,136,2048]{2,1,0:T(8,128)(2,1)} %shard_map.84.a_ref), channel_id=1, source_target_pairs={{0,8},{4,12},{8,0},{12,4},{16,24},{20,28},{24,16},{28,20},{1,9},{5... | collective-permute-start | bytes 1671176 | tf_op jit(solution)/shard_map/ppermute | solution.py:751
  319.8 3.9 collective-permute-start.28
  323.7 10.2 %shard_map.78.refs_0_ = bf16[3,136,2048]{2,1,0:T(8,128)(2,1)} custom-call(s32[12]{0:T(128)} %get-tuple-element.13.refs_0_, s32[12]{0:T(128)} %get-tuple-element.14.refs_1_, s32[12]{0:T(128)} %get-tuple-element.15.refs_2_, bf16[384,2048]{1,0:T(8,128)(2,1)} %collective-permute-done.2.refs_3_, bf16[16,2,512,256]{3,2,1,0:T(8,128)(2,1)} %bitcast.12), custom_call_target="tpu_custom_call" | custom-call | flops 1610612736 | bytes 1572864 | tf_op jit(solution)/shard_map/pallas_call | solution.py:631
  333.9 10.2 %shard_map.79.refs_1_ = bf16[3,136,2048]{2,1,0:T(8,128)(2,1)} custom-call(s32[12]{0:T(128)} %get-tuple-element.13.refs_0_, s32[12]{0:T(128)} %get-tuple-element.14.refs_1_, s32[12]{0:T(128)} %get-tuple-element.15.refs_2_, bf16[384,2048]{1,0:T(8,128)(2,1)} %collective-permute-done.2.refs_3_, bf16[16,2,512,256]{3,2,1,0:T(8,128)(2,1)} %bitcast.13, ...), custom_call_target="tpu_custom_call" | custom-call | flops 1610612736 | bytes 1572864 | tf_op jit(solution)/shard_map/pallas_call | solution.py:631
  344.1 2.7 shard_map.81.a_ref
  347.1 2.6 shard_map.86.a_ref
  351.7 2.6 shard_map.91.refs_2_
  354.6 2.5 shard_map.92.refs_0_
  357.1 2.5 shard_map.93.refs_1_
  359.6 10.5 %project_far.1.refs_11_ = bf16[2,384,512]{2,1,0:T(8,128)(2,1)} custom-call(bf16[128,2048]{1,0:T(8,128)(2,1)} %shard_map.92.refs_0_, bf16[128,2048]{1,0:T(8,128)(2,1)} %shard_map.93.refs_1_, bf16[1,136,2048]{2,1,0:T(8,128)(2,1)} %shard_map.91.refs_2_, bf16[1,136,2048]{2,1,0:T(8,128)(2,1)} %collective-permute-done.28.refs_3_, bf16[2048,512]{1,0:T(8,128)(2,1)} %refs_4_.5, ...), custom_call_target="tpu_custom_call" | custom-call | flops 3221225472 | bytes 8388608 | tf_op jit(solution)/shard_map/project_far/pallas_call | solution.py:990
  370.1 2.5 shard_map.82.refs_0_
  374.5 2.5 shard_map.87.refs_1_
  377.0 3.9 collective-permute-done.19.refs_3_
  380.9 22.3 %project_home.1 = bf16[384,1024]{1,0:T(8,128)(2,1)} custom-call(bf16[128,2048]{1,0:T(8,128)(2,1)} %shard_map.82.refs_0_, bf16[128,2048]{1,0:T(8,128)(2,1)} %shard_map.87.refs_1_, bf16[1,136,2048]{2,1,0:T(8,128)(2,1)} %shard_map.89.refs_2_, bf16[1,136,2048]{2,1,0:T(8,128)(2,1)} %collective-permute-done.19.refs_3_, bf16[2048,512]{1,0:T(8,128)(2,1)} %refs_4_.5, ...), custom_call_target="tpu_custom_call" | custom-call | flops 3221225472 | bytes 8388608 | tf_op jit(solution)/shard_map/project_home/pallas_call | solution.py:990
  (55 shorter events, 51.5 us)
Async XLA Ops:
  0.0 37.8 %collective-permute-start.2 = (bf16[384,2048]{1,0:T(8,128)(2,1)}, bf16[384,2048]{1,0:T(8,128)(2,1)}, u32[]{:S(2)}, u32[]{:S(2)}) collective-permute-start(bf16[384,2048]{1,0:T(8,128)(2,1)} %refs_4_.3), channel_id=1, source_target_pairs={{0,8},{4,12},{8,0},{12,4},{16,24},{20,28},{24,16},{28,20},{1,9},{5... | collective-permute-start | bytes 4718600 | tf_op jit(solution)/shard_map/ppermute | solution.py:751
  3.1 39.6 %collective-permute-start.1 = (bf16[384,2048]{1,0:T(8,128)(2,1)}, bf16[384,2048]{1,0:T(8,128)(2,1)}, u32[]{:S(2)}, u32[]{:S(2)}) collective-permute-start(bf16[384,2048]{1,0:T(8,128)(2,1)} %refs_4_.3), channel_id=1, source_target_pairs={{8,16},{12,20},{16,8},{20,12},{9,17},{13,21},{17,9},{21,13},{10,18... | collective-permute-start | bytes 4718600 | tf_op jit(solution)/shard_map/ppermute | solution.py:751
  21.0 61.3 %collective-permute-start.7 = (bf16[3,2,512,256]{3,2,1,0:T(8,128)(2,1)}, bf16[3,2,512,256]{3,2,1,0:T(8,128)(2,1)}, u32[]{:S(2)}, u32[]{:S(2)}) collective-permute-start(bf16[3,2,512,256]{3,2,1,0:T(8,128)(2,1)} %get-tuple-element.18), channel_id=1, source_target_pairs={{0,4},{4,0},{8,12},{12,8},{16,20},{20,16},{24,28},{28,24},{1,5},{5... | collective-permute-start | bytes 4718600 | tf_op jit(solution)/shard_map/ppermute | solution.py:751
  37.8 45.8 %collective-permute-start.3 = (bf16[384,2048]{1,0:T(8,128)(2,1)}, bf16[384,2048]{1,0:T(8,128)(2,1)}, u32[]{:S(2)}, u32[]{:S(2)}) collective-permute-start(bf16[384,2048]{1,0:T(8,128)(2,1)} %collective-permute-done.2.refs_3_), channel_id=1, source_target_pairs={{8,16},{12,20},{16,8},{20,12},{9,17},{13,21},{17,9},{21,13},{10,18... | collective-permute-start | bytes 4718600 | tf_op jit(solution)/shard_map/ppermute | solution.py:751
  40.9 39.6 %collective-permute-start.20 = (bf16[1024,512]{1,0:T(8,128)(2,1)S(1)}, bf16[1024,512]{1,0:T(8,128)(2,1)}, u32[]{:S(2)}, u32[]{:S(2)}) collective-permute-start(bf16[1024,512]{1,0:T(8,128)(2,1)S(1)} %slice.6), channel_id=1, source_target_pairs={{0,4},{4,0},{8,12},{12,8},{16,20},{20,16},{24,28},{28,24},{1,5},{5... | collective-permute-start | bytes 3145736 | tf_op jit(solution)/shard_map/ppermute | solution.py:751
  42.7 44.5 %collective-permute-start.6 = (bf16[384,2048]{1,0:T(8,128)(2,1)}, bf16[384,2048]{1,0:T(8,128)(2,1)}, u32[]{:S(2)}, u32[]{:S(2)}) collective-permute-start(bf16[384,2048]{1,0:T(8,128)(2,1)} %collective-permute-done.1.refs_3_), channel_id=1, source_target_pairs={{8,0},{12,4},{16,24},{20,28},{9,1},{13,5},{17,25},{21,29},{10,2},{... | collective-permute-start | bytes 4718600 | tf_op jit(solution)/shard_map/ppermute | solution.py:751
  43.9 104.9 %collective-permute-start.22 = (bf16[2048,512]{1,0:T(8,128)(2,1)}, bf16[2048,512]{1,0:T(8,128)(2,1)}, u32[]{:S(2)}, u32[]{:S(2)}) collective-permute-start(bf16[2048,512]{1,0:T(8,128)(2,1)} %refs_4_.5), channel_id=1, source_target_pairs={{0,16},{4,20},{24,8},{28,12},{1,17},{5,21},{25,9},{29,13},{2,18},{... | collective-permute-start | bytes 6291464 | tf_op jit(solution)/shard_map/ppermute | solution.py:751
  80.5 37.6 %collective-permute-start.5 = (bf16[3,2,512,256]{3,2,1,0:T(8,128)(2,1)}, bf16[3,2,512,256]{3,2,1,0:T(8,128)(2,1)}, u32[]{:S(2)}, u32[]{:S(2)}) collective-permute-start(bf16[3,2,512,256]{3,2,1,0:T(8,128)(2,1)} %get-tuple-element.17), channel_id=1, source_target_pairs={{0,4},{4,0},{8,12},{12,8},{16,20},{20,16},{24,28},{28,24},{1,5},{5... | collective-permute-start | bytes 4718600 | tf_op jit(solution)/shard_map/ppermute | solution.py:751
  82.3 139.0 %collective-permute-start.24 = (bf16[2048,512]{1,0:T(8,128)(2,1)}, bf16[2048,512]{1,0:T(8,128)(2,1)}, u32[]{:S(2)}, u32[]{:S(2)}) collective-permute-start(bf16[2048,512]{1,0:T(8,128)(2,1)} %refs_4_.5), channel_id=1, source_target_pairs={{8,24},{12,28},{16,0},{20,4},{9,25},{13,29},{17,1},{21,5},{10,26},... | collective-permute-start | bytes 6291464 | tf_op jit(solution)/shard_map/ppermute | solution.py:751
  83.6 116.0 %collective-permute-start.4 = (bf16[384,2048]{1,0:T(8,128)(2,1)}, bf16[384,2048]{1,0:T(8,128)(2,1)}, u32[]{:S(2)}, u32[]{:S(2)}) collective-permute-start(bf16[384,2048]{1,0:T(8,128)(2,1)} %collective-permute-done.3.refs_3_), channel_id=1, source_target_pairs={{8,0},{12,4},{16,24},{20,28},{9,1},{13,5},{17,25},{21,29},{10,2},{... | collective-permute-start | bytes 4718600 | tf_op jit(solution)/shard_map/ppermute | solution.py:751
  87.1 130.0 %collective-permute-start.21 = (bf16[1024,512]{1,0:T(8,128)(2,1)}, bf16[1024,512]{1,0:T(8,128)(2,1)}, u32[]{:S(2)}, u32[]{:S(2)}) collective-permute-start(bf16[1024,512]{1,0:T(8,128)(2,1)} %slice.7), channel_id=1, source_target_pairs={{0,4},{4,0},{8,12},{12,8},{16,20},{20,16},{24,28},{28,24},{1,5},{5... | collective-permute-start | bytes 3145736 | tf_op jit(solution)/shard_map/ppermute | solution.py:751
  118.1 103.7 %collective-permute-start.8 = (bf16[3,136,2048]{2,1,0:T(8,128)(2,1)}, bf16[3,136,2048]{2,1,0:T(8,128)(2,1)}, u32[]{:S(2)}, u32[]{:S(2)}) collective-permute-start(bf16[3,136,2048]{2,1,0:T(8,128)(2,1)} %shard_map.75.refs_0_), channel_id=1, source_target_pairs={{0,8},{4,12},{24,16},{28,20},{1,9},{5,13},{25,17},{29,21},{2,10},{... | collective-permute-start | bytes 5013512 | tf_op jit(solution)/shard_map/ppermute | solution.py:751
  148.8 78.4 %collective-permute-start = (bf16[3,2,512,256]{3,2,1,0:T(8,128)(2,1)}, bf16[3,2,512,256]{3,2,1,0:T(8,128)(2,1)}, u32[]{:S(2)}, u32[]{:S(2)}) collective-permute-start(bf16[3,2,512,256]{3,2,1,0:T(8,128)(2,1)} %get-tuple-element.16), channel_id=1, source_target_pairs={{0,4},{4,0},{8,12},{12,8},{16,20},{20,16},{24,28},{28,24},{1,5},{5... | collective-permute-start | bytes 4718600 | tf_op jit(solution)/shard_map/ppermute | solution.py:751
  199.6 95.5 %collective-permute-start.23 = (bf16[2048,512]{1,0:T(8,128)(2,1)}, bf16[2048,512]{1,0:T(8,128)(2,1)}, u32[]{:S(2)}, u32[]{:S(2)}) collective-permute-start(bf16[2048,512]{1,0:T(8,128)(2,1)} %collective-permute-done.22.refs_7_), channel_id=1, source_target_pairs={{8,12},{12,8},{16,20},{20,16},{9,13},{13,9},{17,21},{21,17},{10,14... | collective-permute-start | bytes 6291464 | tf_op jit(solution)/shard_map/ppermute | solution.py:751
  217.1 48.8 %collective-permute-start.11 = (bf16[3,136,2048]{2,1,0:T(8,128)(2,1)}, bf16[3,136,2048]{2,1,0:T(8,128)(2,1)}, u32[]{:S(2)}, u32[]{:S(2)}) collective-permute-start(bf16[3,136,2048]{2,1,0:T(8,128)(2,1)} %shard_map.74.refs_0_), channel_id=1, source_target_pairs={{0,8},{4,12},{24,16},{28,20},{1,9},{5,13},{25,17},{29,21},{2,10},{... | collective-permute-start | bytes 5013512 | tf_op jit(solution)/shard_map/ppermute | solution.py:751
  221.2 37.6 %collective-permute-start.10 = (bf16[3,2,512,256]{3,2,1,0:T(8,128)(2,1)}, bf16[3,2,512,256]{3,2,1,0:T(8,128)(2,1)}, u32[]{:S(2)}, u32[]{:S(2)}) collective-permute-start(bf16[3,2,512,256]{3,2,1,0:T(8,128)(2,1)} %get-tuple-element.19), channel_id=1, source_target_pairs={{0,4},{4,0},{8,12},{12,8},{16,20},{20,16},{24,28},{28,24},{1,5},{5... | collective-permute-start | bytes 4718600 | tf_op jit(solution)/shard_map/ppermute | solution.py:751
  221.8 137.8 %collective-permute-start.25 = (bf16[2048,512]{1,0:T(8,128)(2,1)}, bf16[2048,512]{1,0:T(8,128)(2,1)}, u32[]{:S(2)}, u32[]{:S(2)}) collective-permute-start(bf16[2048,512]{1,0:T(8,128)(2,1)} %collective-permute-done.24.refs_9_), channel_id=1, source_target_pairs={{0,4},{4,0},{24,28},{28,24},{1,5},{5,1},{25,29},{29,25},{2,6},{6,2... | collective-permute-start | bytes 6291464 | tf_op jit(solution)/shard_map/ppermute | solution.py:751
  227.2 35.1 %collective-permute-start.9 = (bf16[1,136,2048]{2,1,0:T(8,128)(2,1)}, bf16[1,136,2048]{2,1,0:T(8,128)(2,1)}, u32[]{:S(2)}, u32[]{:S(2)}) collective-permute-start(bf16[1,136,2048]{2,1,0:T(8,128)(2,1)} %shard_map.76), channel_id=1, source_target_pairs={{8,16},{12,20},{16,8},{20,12},{9,17},{13,21},{17,9},{21,13},{10,18... | collective-permute-start | bytes 1671176 | tf_op jit(solution)/shard_map/ppermute | solution.py:751
  258.8 39.8 %collective-permute-start.14 = (bf16[1,136,2048]{2,1,0:T(8,128)(2,1)}, bf16[1,136,2048]{2,1,0:T(8,128)(2,1)}, u32[]{:S(2)}, u32[]{:S(2)}) collective-permute-start(bf16[1,136,2048]{2,1,0:T(8,128)(2,1)} %shard_map.83), channel_id=1, source_target_pairs={{8,16},{12,20},{16,8},{20,12},{9,17},{13,21},{17,9},{21,13},{10,18... | collective-permute-start | bytes 1671176 | tf_op jit(solution)/shard_map/ppermute | solution.py:751
  262.4 39.8 %collective-permute-start.17 = (bf16[1,136,2048]{2,1,0:T(8,128)(2,1)}, bf16[1,136,2048]{2,1,0:T(8,128)(2,1)}, u32[]{:S(2)}, u32[]{:S(2)}) collective-permute-start(bf16[1,136,2048]{2,1,0:T(8,128)(2,1)} %shard_map.88), channel_id=1, source_target_pairs={{8,16},{12,20},{16,8},{20,12},{9,17},{13,21},{17,9},{21,13},{10,18... | collective-permute-start | bytes 1671176 | tf_op jit(solution)/shard_map/ppermute | solution.py:751
  266.0 39.8 %collective-permute-start.26 = (bf16[1,136,2048]{2,1,0:T(8,128)(2,1)}, bf16[1,136,2048]{2,1,0:T(8,128)(2,1)}, u32[]{:S(2)}, u32[]{:S(2)}) collective-permute-start(bf16[1,136,2048]{2,1,0:T(8,128)(2,1)} %shard_map.77.a_ref), channel_id=1, source_target_pairs={{0,8},{4,12},{8,0},{12,4},{16,24},{20,28},{24,16},{28,20},{1,9},{5... | collective-permute-start | bytes 1671176 | tf_op jit(solution)/shard_map/ppermute | solution.py:751
  295.1 24.7 %collective-permute-start.12 = (bf16[1,136,2048]{2,1,0:T(8,128)(2,1)}, bf16[1,136,2048]{2,1,0:T(8,128)(2,1)}, u32[]{:S(2)}, u32[]{:S(2)}) collective-permute-start(bf16[1,136,2048]{2,1,0:T(8,128)(2,1)} %shard_map.80), channel_id=1, source_target_pairs={{8,16},{12,20},{16,8},{20,12},{9,17},{13,21},{17,9},{21,13},{10,18... | collective-permute-start | bytes 1671176 | tf_op jit(solution)/shard_map/ppermute | solution.py:751
  298.6 48.2 %collective-permute-start.15 = (bf16[1,136,2048]{2,1,0:T(8,128)(2,1)}, bf16[1,136,2048]{2,1,0:T(8,128)(2,1)}, u32[]{:S(2)}, u32[]{:S(2)}) collective-permute-start(bf16[1,136,2048]{2,1,0:T(8,128)(2,1)} %shard_map.85), channel_id=1, source_target_pairs={{8,16},{12,20},{16,8},{20,12},{9,17},{13,21},{17,9},{21,13},{10,18... | collective-permute-start | bytes 1671176 | tf_op jit(solution)/shard_map/ppermute | solution.py:751
  302.2 47.5 %collective-permute-start.18 = (bf16[1,136,2048]{2,1,0:T(8,128)(2,1)}, bf16[1,136,2048]{2,1,0:T(8,128)(2,1)}, u32[]{:S(2)}, u32[]{:S(2)}) collective-permute-start(bf16[1,136,2048]{2,1,0:T(8,128)(2,1)} %shard_map.90), channel_id=1, source_target_pairs={{8,16},{12,20},{16,8},{20,12},{9,17},{13,21},{17,9},{21,13},{10,18... | collective-permute-start | bytes 1671176 | tf_op jit(solution)/shard_map/ppermute | solution.py:751
  305.7 48.6 %collective-permute-start.27 = (bf16[1,136,2048]{2,1,0:T(8,128)(2,1)}, bf16[1,136,2048]{2,1,0:T(8,128)(2,1)}, u32[]{:S(2)}, u32[]{:S(2)}) collective-permute-start(bf16[1,136,2048]{2,1,0:T(8,128)(2,1)} %shard_map.84.a_ref), channel_id=1, source_target_pairs={{0,8},{4,12},{8,0},{12,4},{16,24},{20,28},{24,16},{28,20},{1,9},{5... | collective-permute-start | bytes 1671176 | tf_op jit(solution)/shard_map/ppermute | solution.py:751
  319.8 39.8 %collective-permute-start.28 = (bf16[1,136,2048]{2,1,0:T(8,128)(2,1)}, bf16[1,136,2048]{2,1,0:T(8,128)(2,1)}, u32[]{:S(2)}, u32[]{:S(2)}) collective-permute-start(bf16[1,136,2048]{2,1,0:T(8,128)(2,1)} %shard_map.89.refs_2_), channel_id=1, source_target_pairs={{0,8},{4,12},{8,0},{12,4},{16,24},{20,28},{24,16},{28,20},{1,9},{5... | collective-permute-start | bytes 1671176 | tf_op jit(solution)/shard_map/ppermute | solution.py:751
  346.8 23.3 %collective-permute-start.13 = (bf16[1,136,2048]{2,1,0:T(8,128)(2,1)}, bf16[1,136,2048]{2,1,0:T(8,128)(2,1)}, u32[]{:S(2)}, u32[]{:S(2)}) collective-permute-start(bf16[1,136,2048]{2,1,0:T(8,128)(2,1)} %shard_map.81.a_ref), channel_id=1, source_target_pairs={{0,8},{4,12},{8,0},{12,4},{16,24},{20,28},{24,16},{28,20},{1,9},{5... | collective-permute-start | bytes 1671176 | tf_op jit(solution)/shard_map/ppermute | solution.py:751
  349.7 24.8 %collective-permute-start.16 = (bf16[1,136,2048]{2,1,0:T(8,128)(2,1)}, bf16[1,136,2048]{2,1,0:T(8,128)(2,1)}, u32[]{:S(2)}, u32[]{:S(2)}) collective-permute-start(bf16[1,136,2048]{2,1,0:T(8,128)(2,1)} %shard_map.86.a_ref), channel_id=1, source_target_pairs={{0,8},{4,12},{8,0},{12,4},{16,24},{20,28},{24,16},{28,20},{1,9},{5... | collective-permute-start | bytes 1671176 | tf_op jit(solution)/shard_map/ppermute | solution.py:751
  354.4 26.5 %collective-permute-start.19 = (bf16[1,136,2048]{2,1,0:T(8,128)(2,1)}, bf16[1,136,2048]{2,1,0:T(8,128)(2,1)}, u32[]{:S(2)}, u32[]{:S(2)}) collective-permute-start(bf16[1,136,2048]{2,1,0:T(8,128)(2,1)} %shard_map.91.refs_2_), channel_id=1, source_target_pairs={{0,8},{4,12},{8,0},{12,4},{16,24},{20,28},{24,16},{28,20},{1,9},{5... | collective-permute-start | bytes 1671176 | tf_op jit(solution)/shard_map/ppermute | solution.py:751

commit v11 on v10

--- a/solution.py
+++ b/solution.py
@@ -788,7 +788,7 @@
     back3 = send(part3, inward)
     w_in_both = send(w_in, inner_across)
     w_out_both = send(w_out, outer_across)
-    own_rows, near_rows = [], []
+    own_pairs, near_rows, near_pairs = [], [], []
     for q in range(per_device):
         cross3 = send(join(q, part3, back2), middle)
         near0 = join(q, part0, cross3)
@@ -796,15 +796,14 @@
         cross2 = send(join(q, part2, back3), middle)
         near1 = join(q, part1, part1_far, cross2)
         back1 = send(near1, near)
+        own_pairs += [near0, back1]
         if q + 1 < per_device:
             near_rows.append(join(q, near1, beside, leveled=False))
-            own_rows.append(join(q, near0, back1, leveled=False))
         else:
-            near_rows += [near1, beside]
-            own_rows += [near0, back1]
+            near_pairs += [near1, beside]
     weights = (out_weight, w_across0, w_across1, w_in, w_in_both, w_out, w_out_both)
-    far_sums = project_call(near_rows, weights, None)
-    return project_call(own_rows, weights, far_sums)
+    far_sums = project_call(near_rows, near_pairs, weights, None)
+    return project_call([], own_pairs, weights, far_sums)
 
 
 MESH = pl.DeviceIdType.MESH
@@ -814,7 +813,7 @@
     return lax.axis_index("head") % 2 == lax.axis_index("pass") // 2 % 2
 
 
-def project_kernel(pieces, far, *refs):
+def project_kernel(done, pieces, far, *refs):
     rows_refs = refs[:pieces]
     own_ref, a0_ref, a1_ref, in_ref, in2_ref, out1_ref, out2_ref = refs[pieces : pieces + 7]
     refs = refs[pieces + 7 :]
@@ -830,9 +829,8 @@
     home = at_home()
     sums = jnp.logical_not(home) if far else home
 
-    done = pieces - 2
     row_loads = [
-        pltpu.make_async_copy(ref, pair_ref.at[i], row_sem.at[done + i])
+        pltpu.make_async_copy(ref, pair_ref.at[i // 2, i % 2], row_sem.at[done + i])
         for i, ref in enumerate(rows_refs[done:])
     ]
     row_loads += [
@@ -908,7 +906,9 @@
 
     for load in row_loads:
         load.wait()
-    blend((pair_ref.at[0], pair_ref.at[1]), context_ref.at[pl.ds(done * LQ, LQ)], False)
+    for i in range((pieces - done) // 2):
+        pair = (pair_ref.at[i, 0], pair_ref.at[i, 1])
+        blend(pair, context_ref.at[pl.ds((done + i) * LQ, LQ)], False)
 
     def multiply(s, to_y, j):
         here = jnp.where(to_y == z // 2, 0, 1)
@@ -966,9 +966,10 @@
                 copy.wait()
 
 
-def project_call(pieces, weights, far_sums):
+def project_call(finished, pairs, weights, far_sums):
     own = weights[0]
-    rows, (depth, wide) = (len(pieces) - 1) * LQ, own.shape
+    pieces = finished + pairs
+    rows, (depth, wide) = (len(finished) + len(pairs) // 2) * LQ, own.shape
     dtype = own.dtype
     far = far_sums is None
     vmem = pl.BlockSpec(memory_space=pltpu.VMEM)
@@ -978,7 +979,7 @@
         pltpu.VMEM((2, 2, depth, wide), dtype),
         pltpu.VMEM((2,) + blocks, dtype),
         pltpu.VMEM((2,) + blocks, dtype),
-        pltpu.VMEM((2,) + pieces[-1].shape, dtype),
+        pltpu.VMEM((len(pairs) // 2, 2) + pairs[0].shape, dtype),
         pltpu.VMEM(blocks, dtype),
         pltpu.VMEM(blocks, dtype),
         pltpu.SemaphoreType.DMA((len(pieces),)),
@@ -988,7 +989,7 @@
     ]
     shape = blocks if far else (rows, 2 * wide)
     return pl.pallas_call(
-        functools.partial(project_kernel, len(pieces), far),
+        functools.partial(project_kernel, len(finished), len(pieces), far),
         out_shape=jax.ShapeDtypeStruct(shape, dtype),
         in_specs=[pl.BlockSpec(memory_space=pl.ANY)] * (len(pieces) + len(weights))
         + [vmem] * (0 if far else 1),

time: 407 us -> 395 us (0.971)
  starting transfers between devices: 122 us -> 65.7 us
  waiting for transfers between devices: 119 us -> 169 us
  Pallas kernels: 149 us -> 143 us
    ppermute x29, starting transfers between devices: 122 us -> 65.7 us  [send(): return lax.ppermute(value, 'pass', pairs)]
    ppermute x29, waiting for transfers between devices: 119 us -> 169 us  [send(): return lax.ppermute(value, 'pass', pairs)]
    pallas_call x16 -> x14, Pallas kernels: 36.5 us -> 31.6 us  [join_call(): pl.pallas_call(merge_kernel if leveled else finish_kernel, out_shape=jax....]
  transfers between devices with their start and end apart: 29 -> 29, of which waited for: 7 -> 8; matrix products, arithmetic and copies ran while one was open for 3% -> 3% of each run, Pallas kernels for 31% -> 31%
where the time goes in v11:
time: 395 us; the launch traced here: 394 us
  waiting for transfers between devices  169 us (43%)
  Pallas kernels  143 us (36%)
  starting transfers between devices  65.7 us (17%)
  local copies, waits for them, and re-layouts  15.6 us (4%)
    ppermute x29, waiting for transfers between devices, send(): return lax.ppermute(value, 'pass', pairs)  169 us
    pallas_call x5, Pallas kernels, part_call(): pl.pallas_call(functools.partial(part_kernel, k, most, first, last, heads...  71.7 us
    ppermute x29, starting transfers between devices, send(): return lax.ppermute(value, 'pass', pairs)  65.7 us
    pallas_call x2, Pallas kernels, project_call(): pl.pallas_call(functools.partial(project_kernel, len(finished), len(piece...  31.8 us
    pallas_call x14, Pallas kernels, join_call(): pl.pallas_call(merge_kernel if leveled else finish_kernel, out_shape=jax....  31.6 us
    unnamed x2, local copies, waits for them, and re-layouts  10.3 us
  transfers between devices with their start and end apart: 29, of which 8 were waited for; matrix products, arithmetic and copies ran while one was open for 3% of the time, Pallas kernels for 31%

profile of v11, /device:TPU:0, one launch (start us, length us, event | category | flops | bytes accessed | tf_op | source)
XLA Modules:
  0.0 394.0 jit_solution(1812922608187124739)
XLA Ops:
  0.0 3.1 collective-permute-start.2
  4.9 32.9 %collective-permute-done.2.refs_3_ = bf16[384,2048]{1,0:T(8,128)(2,1)} collective-permute-done((bf16[384,2048]{1,0:T(8,128)(2,1)}, bf16[384,2048]{1,0:T(8,128)(2,1)}, u32[]{:S(2)}, u32[]{:S(2)}) %collective-permute-start.2) | collective-permute-done | bytes 1572896 | tf_op jit(solution)/shard_map/ppermute | solution.py:751
  39.6 8.2 %copy.16 = bf16[16,512,2,256]{3,1,2,0:T(8,128)(2,1)} copy(bf16[16,512,2,256]{3,2,1,0:T(2,128)(2,1)} %param.9) | data formatting | bytes 16777216 | tf_op args[2]
  47.8 7.9 %sort_items.1 = (s32[12]{0:T(128)}, s32[12]{0:T(128)}, s32[12]{0:T(128)}, bf16[3,2,512,256]{3,2,1,0:T(8,128)(2,1)}, bf16[3,2,512,256]{3,2,1,0:T(8,128)(2,1)}, /*...) custom-call(s32[8,24]{1,0:T(8,128)} %bitcast.16, s32[128]{0:T(128)} %pslot_ref.1, s32[24]{0:T(128)} %qslot_ref.1, ...), custom_call_target="tpu_custom_call" | custom-call | bytes 12582912 | tf_op jit(solution)/shard_map/sort_items/pallas_call | solution.py:437
  55.7 2.8 collective-permute-start.7
  61.2 8.6 %collective-permute-start.22 = (bf16[2048,512]{1,0:T(8,128)(2,1)}, bf16[2048,512]{1,0:T(8,128)(2,1)}, u32[]{:S(2)}, u32[]{:S(2)}) collective-permute-start(bf16[2048,512]{1,0:T(8,128)(2,1)} %refs_6_.1), channel_id=1, source_target_pairs={{0,16},{4,20},{24,8},{28,12},{1,17},{5,21},{25,9},{29,13},{2,18},{... | collective-permute-start | bytes 6291464 | tf_op jit(solution)/shard_map/ppermute | solution.py:751
  69.8 45.0 %collective-permute-done.20.refs_5_.refs_7_ = bf16[1024,512]{1,0:T(8,128)(2,1)} collective-permute-done((bf16[1024,512]{1,0:T(8,128)(2,1)S(1)}, bf16[1024,512]{1,0:T(8,128)(2,1)}, u32[]{:S(2)}, u32[]{:S(2)}) %collective-permute-start.20) | collective-permute-done | bytes 1048608 | tf_op jit(solution)/shard_map/ppermute | solution.py:751
  117.8 2.3 slice.7
  121.7 15.5 %shard_map.75.refs_0_ = bf16[3,136,2048]{2,1,0:T(8,128)(2,1)} custom-call(s32[12]{0:T(128)} %get-tuple-element.13.refs_0_, s32[12]{0:T(128)} %get-tuple-element.14.refs_1_, s32[12]{0:T(128)} %get-tuple-element.15.refs_2_, bf16[384,2048]{1,0:T(8,128)(2,1)} %collective-permute-done.3.refs_3_, bf16[384,2048]{1,0:T(8,128)(2,1)} %collective-permute-done.6.refs_4_, ...), custom_call_target="tpu_custom_call" | custom-call | flops 3221225472 | bytes 3145728 | tf_op jit(solution)/shard_map/pallas_call | solution.py:631
  137.3 35.0 %collective-permute-done.21.refs_6_.refs_8_ = bf16[1024,512]{1,0:T(8,128)(2,1)} collective-permute-done((bf16[1024,512]{1,0:T(8,128)(2,1)}, bf16[1024,512]{1,0:T(8,128)(2,1)}, u32[]{:S(2)}, u32[]{:S(2)}) %collective-permute-start.21) | collective-permute-done | bytes 1048608 | tf_op jit(solution)/shard_map/ppermute | solution.py:751
  172.3 5.1 %collective-permute-start.8 = (bf16[3,136,2048]{2,1,0:T(8,128)(2,1)}, bf16[3,136,2048]{2,1,0:T(8,128)(2,1)}, u32[]{:S(2)}, u32[]{:S(2)}) collective-permute-start(bf16[3,136,2048]{2,1,0:T(8,128)(2,1)} %shard_map.75.refs_0_), channel_id=1, source_target_pairs={{0,8},{4,12},{24,16},{28,20},{1,9},{5,13},{25,17},{29,21},{2,10},{... | collective-permute-start | bytes 5013512 | tf_op jit(solution)/shard_map/ppermute | solution.py:751
  178.8 22.3 %collective-permute-done.4.refs_4_ = bf16[384,2048]{1,0:T(8,128)(2,1)} collective-permute-done((bf16[384,2048]{1,0:T(8,128)(2,1)}, bf16[384,2048]{1,0:T(8,128)(2,1)}, u32[]{:S(2)}, u32[]{:S(2)}) %collective-permute-start.4) | collective-permute-done | bytes 1572896 | tf_op jit(solution)/shard_map/ppermute | solution.py:751
  202.6 15.5 %shard_map.74.refs_0_ = bf16[3,136,2048]{2,1,0:T(8,128)(2,1)} custom-call(s32[12]{0:T(128)} %get-tuple-element.13.refs_0_, s32[12]{0:T(128)} %get-tuple-element.14.refs_1_, s32[12]{0:T(128)} %get-tuple-element.15.refs_2_, bf16[384,2048]{1,0:T(8,128)(2,1)} %collective-permute-done.1.refs_3_, bf16[384,2048]{1,0:T(8,128)(2,1)} %collective-permute-done.4.refs_4_, ...), custom_call_target="tpu_custom_call" | custom-call | flops 3221225472 | bytes 3145728 | tf_op jit(solution)/shard_map/pallas_call | solution.py:631
  218.2 2.7 collective-permute-start.11
  222.8 2.4 collective-permute-start.25
  227.3 2.1 shard_map.82
  230.8 17.8 %collective-permute-done.10.refs_5_ = bf16[3,2,512,256]{3,2,1,0:T(8,128)(2,1)} collective-permute-done((bf16[3,2,512,256]{3,2,1,0:T(8,128)(2,1)}, bf16[3,2,512,256]{3,2,1,0:T(8,128)(2,1)}, u32[]{:S(2)}, u32[]{:S(2)}) %collective-permute-start.10) | collective-permute-done | bytes 1572896 | tf_op jit(solution)/shard_map/ppermute | solution.py:751
  261.8 2.1 shard_map.88
  267.1 20.3 %shard_map.73.refs_0_ = bf16[3,136,2048]{2,1,0:T(8,128)(2,1)} custom-call(s32[12]{0:T(128)} %get-tuple-element.13.refs_0_, s32[12]{0:T(128)} %get-tuple-element.14.refs_1_, s32[12]{0:T(128)} %get-tuple-element.15.refs_2_, bf16[3,2,128,256]{3,2,1,0:T(8,128)(2,1)} %bitcast.14, bf16[384,2048]{1,0:T(8,128)(2,1)} %refs_4_.2, bf16[16,2,512,256]{3,2,1,0:T(8,128)(2,1)} %bitcast.11, ...), custom_call_target="tpu_custom_call" | custom-call | flops 3221225472 | bytes 3145728 | tf_op jit(solution)/shard_map/pallas_call | solution.py:631
  291.6 12.6 %collective-permute-start.26 = (bf16[1,136,2048]{2,1,0:T(8,128)(2,1)}, bf16[1,136,2048]{2,1,0:T(8,128)(2,1)}, u32[]{:S(2)}, u32[]{:S(2)}) collective-permute-start(bf16[1,136,2048]{2,1,0:T(8,128)(2,1)} %shard_map.77.refs_0_), channel_id=1, source_target_pairs={{0,8},{4,12},{8,0},{12,4},{16,24},{20,28},{24,16},{28,20},{1,9},{5... | collective-permute-start | bytes 1671176 | tf_op jit(solution)/shard_map/ppermute | solution.py:751
  306.3 2.4 collective-permute-start.28
  308.6 10.2 %shard_map.78.refs_0_ = bf16[3,136,2048]{2,1,0:T(8,128)(2,1)} custom-call(s32[12]{0:T(128)} %get-tuple-element.13.refs_0_, s32[12]{0:T(128)} %get-tuple-element.14.refs_1_, s32[12]{0:T(128)} %get-tuple-element.15.refs_2_, bf16[384,2048]{1,0:T(8,128)(2,1)} %collective-permute-done.2.refs_3_, bf16[16,2,512,256]{3,2,1,0:T(8,128)(2,1)} %bitcast.12), custom_call_target="tpu_custom_call" | custom-call | flops 1610612736 | bytes 1572864 | tf_op jit(solution)/shard_map/pallas_call | solution.py:631
  318.8 10.2 %shard_map.79.refs_1_ = bf16[3,136,2048]{2,1,0:T(8,128)(2,1)} custom-call(s32[12]{0:T(128)} %get-tuple-element.13.refs_0_, s32[12]{0:T(128)} %get-tuple-element.14.refs_1_, s32[12]{0:T(128)} %get-tuple-element.15.refs_2_, bf16[384,2048]{1,0:T(8,128)(2,1)} %collective-permute-done.2.refs_3_, bf16[16,2,512,256]{3,2,1,0:T(8,128)(2,1)} %bitcast.13, ...), custom_call_target="tpu_custom_call" | custom-call | flops 1610612736 | bytes 1572864 | tf_op jit(solution)/shard_map/pallas_call | solution.py:631
  329.0 2.7 shard_map.81.a_ref
  331.7 2.7 shard_map.85.a_ref
  334.4 2.7 shard_map.89.refs_2_
  339.9 2.5 shard_map.90.refs_0_
  342.3 2.5 shard_map.91.refs_1_
  344.8 10.5 %project_far.1.refs_13_ = bf16[2,384,512]{2,1,0:T(8,128)(2,1)} custom-call(bf16[128,2048]{1,0:T(8,128)(2,1)} %shard_map.90.refs_0_, bf16[128,2048]{1,0:T(8,128)(2,1)} %shard_map.91.refs_1_, bf16[1,136,2048]{2,1,0:T(8,128)(2,1)} %shard_map.89.refs_2_, bf16[1,136,2048]{2,1,0:T(8,128)(2,1)} %collective-permute-done.28.refs_3_, bf16[2048,512]{1,0:T(8,128)(2,1)} %refs_6_.1, ...), custom_call_target="tpu_custom_call" | custom-call | flops 3221225472 | bytes 8388608 | tf_op jit(solution)/shard_map/project_far/pallas_call | solution.py:991
  355.3 9.2 %collective-permute-done.16.refs_3_ = bf16[1,136,2048]{2,1,0:T(8,128)(2,1)} collective-permute-done((bf16[1,136,2048]{2,1,0:T(8,128)(2,1)}, bf16[1,136,2048]{2,1,0:T(8,128)(2,1)}, u32[]{:S(2)}, u32[]{:S(2)}) %collective-permute-start.16) | collective-permute-done | bytes 557088 | tf_op jit(solution)/shard_map/ppermute | solution.py:751
  364.6 6.0 %collective-permute-done.19.refs_5_ = bf16[1,136,2048]{2,1,0:T(8,128)(2,1)} collective-permute-done((bf16[1,136,2048]{2,1,0:T(8,128)(2,1)}, bf16[1,136,2048]{2,1,0:T(8,128)(2,1)}, u32[]{:S(2)}, u32[]{:S(2)}) %collective-permute-start.19) | collective-permute-done | bytes 557088 | tf_op jit(solution)/shard_map/ppermute | solution.py:751
  370.5 21.3 %project_home.1 = bf16[384,1024]{1,0:T(8,128)(2,1)} custom-call(bf16[1,136,2048]{2,1,0:T(8,128)(2,1)} %shard_map.77.refs_0_, bf16[1,136,2048]{2,1,0:T(8,128)(2,1)} %collective-permute-done.13.refs_1_, bf16[1,136,2048]{2,1,0:T(8,128)(2,1)} %shard_map.83.refs_2_, bf16[1,136,2048]{2,1,0:T(8,128)(2,1)} %collective-permute-done.16.refs_3_, ...), custom_call_target="tpu_custom_call" | custom-call | flops 3221225472 | bytes 8388608 | tf_op jit(solution)/shard_map/project_home/pallas_call | solution.py:991
  (53 shorter events, 46.9 us)
Async XLA Ops:
  0.0 37.8 %collective-permute-start.2 = (bf16[384,2048]{1,0:T(8,128)(2,1)}, bf16[384,2048]{1,0:T(8,128)(2,1)}, u32[]{:S(2)}, u32[]{:S(2)}) collective-permute-start(bf16[384,2048]{1,0:T(8,128)(2,1)} %refs_4_.2), channel_id=1, source_target_pairs={{0,8},{4,12},{8,0},{12,4},{16,24},{20,28},{24,16},{28,20},{1,9},{5... | collective-permute-start | bytes 4718600 | tf_op jit(solution)/shard_map/ppermute | solution.py:751
  3.1 56.8 %collective-permute-start.1 = (bf16[384,2048]{1,0:T(8,128)(2,1)}, bf16[384,2048]{1,0:T(8,128)(2,1)}, u32[]{:S(2)}, u32[]{:S(2)}) collective-permute-start(bf16[384,2048]{1,0:T(8,128)(2,1)} %refs_4_.2), channel_id=1, source_target_pairs={{8,16},{12,20},{16,8},{20,12},{9,17},{13,21},{17,9},{21,13},{10,18... | collective-permute-start | bytes 4718600 | tf_op jit(solution)/shard_map/ppermute | solution.py:751
  37.8 78.8 %collective-permute-start.3 = (bf16[384,2048]{1,0:T(8,128)(2,1)}, bf16[384,2048]{1,0:T(8,128)(2,1)}, u32[]{:S(2)}, u32[]{:S(2)}) collective-permute-start(bf16[384,2048]{1,0:T(8,128)(2,1)} %collective-permute-done.2.refs_3_), channel_id=1, source_target_pairs={{8,16},{12,20},{16,8},{20,12},{9,17},{13,21},{17,9},{21,13},{10,18... | collective-permute-start | bytes 4718600 | tf_op jit(solution)/shard_map/ppermute | solution.py:751
  55.7 64.4 %collective-permute-start.7 = (bf16[3,2,512,256]{3,2,1,0:T(8,128)(2,1)}, bf16[3,2,512,256]{3,2,1,0:T(8,128)(2,1)}, u32[]{:S(2)}, u32[]{:S(2)}) collective-permute-start(bf16[3,2,512,256]{3,2,1,0:T(8,128)(2,1)} %get-tuple-element.18), channel_id=1, source_target_pairs={{0,4},{4,0},{8,12},{12,8},{16,20},{20,16},{24,28},{28,24},{1,5},{5... | collective-permute-start | bytes 4718600 | tf_op jit(solution)/shard_map/ppermute | solution.py:751
  59.8 55.0 %collective-permute-start.20 = (bf16[1024,512]{1,0:T(8,128)(2,1)S(1)}, bf16[1024,512]{1,0:T(8,128)(2,1)}, u32[]{:S(2)}, u32[]{:S(2)}) collective-permute-start(bf16[1024,512]{1,0:T(8,128)(2,1)S(1)} %slice.6), channel_id=1, source_target_pairs={{0,4},{4,0},{8,12},{12,8},{16,20},{20,16},{24,28},{28,24},{1,5},{5... | collective-permute-start | bytes 3145736 | tf_op jit(solution)/shard_map/ppermute | solution.py:751
  59.9 60.5 %collective-permute-start.6 = (bf16[384,2048]{1,0:T(8,128)(2,1)}, bf16[384,2048]{1,0:T(8,128)(2,1)}, u32[]{:S(2)}, u32[]{:S(2)}) collective-permute-start(bf16[384,2048]{1,0:T(8,128)(2,1)} %collective-permute-done.1.refs_3_), channel_id=1, source_target_pairs={{8,0},{12,4},{16,24},{20,28},{9,1},{13,5},{17,25},{21,29},{10,2},{... | collective-permute-start | bytes 4718600 | tf_op jit(solution)/shard_map/ppermute | solution.py:751
  61.2 157.0 %collective-permute-start.22 = (bf16[2048,512]{1,0:T(8,128)(2,1)}, bf16[2048,512]{1,0:T(8,128)(2,1)}, u32[]{:S(2)}, u32[]{:S(2)}) collective-permute-start(bf16[2048,512]{1,0:T(8,128)(2,1)} %refs_6_.1), channel_id=1, source_target_pairs={{0,16},{4,20},{24,8},{28,12},{1,17},{5,21},{25,9},{29,13},{2,18},{... | collective-permute-start | bytes 6291464 | tf_op jit(solution)/shard_map/ppermute | solution.py:751
  114.8 62.6 %collective-permute-start.5 = (bf16[3,2,512,256]{3,2,1,0:T(8,128)(2,1)}, bf16[3,2,512,256]{3,2,1,0:T(8,128)(2,1)}, u32[]{:S(2)}, u32[]{:S(2)}) collective-permute-start(bf16[3,2,512,256]{3,2,1,0:T(8,128)(2,1)} %get-tuple-element.17), channel_id=1, source_target_pairs={{0,4},{4,0},{8,12},{12,8},{16,20},{20,16},{24,28},{28,24},{1,5},{5... | collective-permute-start | bytes 4718600 | tf_op jit(solution)/shard_map/ppermute | solution.py:751
  116.6 84.6 %collective-permute-start.4 = (bf16[384,2048]{1,0:T(8,128)(2,1)}, bf16[384,2048]{1,0:T(8,128)(2,1)}, u32[]{:S(2)}, u32[]{:S(2)}) collective-permute-start(bf16[384,2048]{1,0:T(8,128)(2,1)} %collective-permute-done.3.refs_3_), channel_id=1, source_target_pairs={{8,0},{12,4},{16,24},{20,28},{9,1},{13,5},{17,25},{21,29},{10,2},{... | collective-permute-start | bytes 4718600 | tf_op jit(solution)/shard_map/ppermute | solution.py:751
  120.1 52.2 %collective-permute-start.21 = (bf16[1024,512]{1,0:T(8,128)(2,1)}, bf16[1024,512]{1,0:T(8,128)(2,1)}, u32[]{:S(2)}, u32[]{:S(2)}) collective-permute-start(bf16[1024,512]{1,0:T(8,128)(2,1)} %slice.7), channel_id=1, source_target_pairs={{0,4},{4,0},{8,12},{12,8},{16,20},{20,16},{24,28},{28,24},{1,5},{5... | collective-permute-start | bytes 3145736 | tf_op jit(solution)/shard_map/ppermute | solution.py:751
  120.4 100.4 %collective-permute-start.24 = (bf16[2048,512]{1,0:T(8,128)(2,1)}, bf16[2048,512]{1,0:T(8,128)(2,1)}, u32[]{:S(2)}, u32[]{:S(2)}) collective-permute-start(bf16[2048,512]{1,0:T(8,128)(2,1)} %refs_6_.1), channel_id=1, source_target_pairs={{8,24},{12,28},{16,0},{20,4},{9,25},{13,29},{17,1},{21,5},{10,26},... | collective-permute-start | bytes 6291464 | tf_op jit(solution)/shard_map/ppermute | solution.py:751
  172.3 50.5 %collective-permute-start.8 = (bf16[3,136,2048]{2,1,0:T(8,128)(2,1)}, bf16[3,136,2048]{2,1,0:T(8,128)(2,1)}, u32[]{:S(2)}, u32[]{:S(2)}) collective-permute-start(bf16[3,136,2048]{2,1,0:T(8,128)(2,1)} %shard_map.75.refs_0_), channel_id=1, source_target_pairs={{0,8},{4,12},{24,16},{28,20},{1,9},{5,13},{25,17},{29,21},{2,10},{... | collective-permute-start | bytes 5013512 | tf_op jit(solution)/shard_map/ppermute | solution.py:751
  177.4 52.0 %collective-permute-start = (bf16[3,2,512,256]{3,2,1,0:T(8,128)(2,1)}, bf16[3,2,512,256]{3,2,1,0:T(8,128)(2,1)}, u32[]{:S(2)}, u32[]{:S(2)}) collective-permute-start(bf16[3,2,512,256]{3,2,1,0:T(8,128)(2,1)} %get-tuple-element.16), channel_id=1, source_target_pairs={{0,4},{4,0},{8,12},{12,8},{16,20},{20,16},{24,28},{28,24},{1,5},{5... | collective-permute-start | bytes 4718600 | tf_op jit(solution)/shard_map/ppermute | solution.py:751
  201.1 47.5 %collective-permute-start.10 = (bf16[3,2,512,256]{3,2,1,0:T(8,128)(2,1)}, bf16[3,2,512,256]{3,2,1,0:T(8,128)(2,1)}, u32[]{:S(2)}, u32[]{:S(2)}) collective-permute-start(bf16[3,2,512,256]{3,2,1,0:T(8,128)(2,1)} %get-tuple-element.19), channel_id=1, source_target_pairs={{0,4},{4,0},{8,12},{12,8},{16,20},{20,16},{24,28},{28,24},{1,5},{5... | collective-permute-start | bytes 4718600 | tf_op jit(solution)/shard_map/ppermute | solution.py:751
  218.2 35.1 %collective-permute-start.11 = (bf16[3,136,2048]{2,1,0:T(8,128)(2,1)}, bf16[3,136,2048]{2,1,0:T(8,128)(2,1)}, u32[]{:S(2)}, u32[]{:S(2)}) collective-permute-start(bf16[3,136,2048]{2,1,0:T(8,128)(2,1)} %shard_map.74.refs_0_), channel_id=1, source_target_pairs={{0,8},{4,12},{24,16},{28,20},{1,9},{5,13},{25,17},{29,21},{2,10},{... | collective-permute-start | bytes 5013512 | tf_op jit(solution)/shard_map/ppermute | solution.py:751
  220.8 116.2 %collective-permute-start.23 = (bf16[2048,512]{1,0:T(8,128)(2,1)}, bf16[2048,512]{1,0:T(8,128)(2,1)}, u32[]{:S(2)}, u32[]{:S(2)}) collective-permute-start(bf16[2048,512]{1,0:T(8,128)(2,1)} %collective-permute-done.22.refs_7_.refs_9_), channel_id=1, source_target_pairs={{8,12},{12,8},{16,20},{20,16},{9,13},{13,9},{17,21},{21,17},{10,14... | collective-permute-start | bytes 6291464 | tf_op jit(solution)/shard_map/ppermute | solution.py:751
  222.8 122.1 %collective-permute-start.25 = (bf16[2048,512]{1,0:T(8,128)(2,1)}, bf16[2048,512]{1,0:T(8,128)(2,1)}, u32[]{:S(2)}, u32[]{:S(2)}) collective-permute-start(bf16[2048,512]{1,0:T(8,128)(2,1)} %collective-permute-done.24.refs_9_.refs_11_), channel_id=1, source_target_pairs={{0,4},{4,0},{24,28},{28,24},{1,5},{5,1},{25,29},{29,25},{2,6},{6,2... | collective-permute-start | bytes 6291464 | tf_op jit(solution)/shard_map/ppermute | solution.py:751
  229.4 29.5 %collective-permute-start.9 = (bf16[1,136,2048]{2,1,0:T(8,128)(2,1)}, bf16[1,136,2048]{2,1,0:T(8,128)(2,1)}, u32[]{:S(2)}, u32[]{:S(2)}) collective-permute-start(bf16[1,136,2048]{2,1,0:T(8,128)(2,1)} %shard_map.76), channel_id=1, source_target_pairs={{8,16},{12,20},{16,8},{20,12},{9,17},{13,21},{17,9},{21,13},{10,18... | collective-permute-start | bytes 1671176 | tf_op jit(solution)/shard_map/ppermute | solution.py:751
  248.7 11.6 %collective-permute-start.14 = (bf16[1,136,2048]{2,1,0:T(8,128)(2,1)}, bf16[1,136,2048]{2,1,0:T(8,128)(2,1)}, u32[]{:S(2)}, u32[]{:S(2)}) collective-permute-start(bf16[1,136,2048]{2,1,0:T(8,128)(2,1)} %shard_map.82), channel_id=1, source_target_pairs={{8,16},{12,20},{16,8},{20,12},{9,17},{13,21},{17,9},{21,13},{10,18... | collective-permute-start | bytes 1671176 | tf_op jit(solution)/shard_map/ppermute | solution.py:751
  253.2 10.6 %collective-permute-start.17 = (bf16[1,136,2048]{2,1,0:T(8,128)(2,1)}, bf16[1,136,2048]{2,1,0:T(8,128)(2,1)}, u32[]{:S(2)}, u32[]{:S(2)}) collective-permute-start(bf16[1,136,2048]{2,1,0:T(8,128)(2,1)} %shard_map.86), channel_id=1, source_target_pairs={{8,16},{12,20},{16,8},{20,12},{9,17},{13,21},{17,9},{21,13},{10,18... | collective-permute-start | bytes 1671176 | tf_op jit(solution)/shard_map/ppermute | solution.py:751
  258.8 32.7 %collective-permute-start.12 = (bf16[1,136,2048]{2,1,0:T(8,128)(2,1)}, bf16[1,136,2048]{2,1,0:T(8,128)(2,1)}, u32[]{:S(2)}, u32[]{:S(2)}) collective-permute-start(bf16[1,136,2048]{2,1,0:T(8,128)(2,1)} %shard_map.80), channel_id=1, source_target_pairs={{8,16},{12,20},{16,8},{20,12},{9,17},{13,21},{17,9},{21,13},{10,18... | collective-permute-start | bytes 1671176 | tf_op jit(solution)/shard_map/ppermute | solution.py:751
  260.3 43.8 %collective-permute-start.15 = (bf16[1,136,2048]{2,1,0:T(8,128)(2,1)}, bf16[1,136,2048]{2,1,0:T(8,128)(2,1)}, u32[]{:S(2)}, u32[]{:S(2)}) collective-permute-start(bf16[1,136,2048]{2,1,0:T(8,128)(2,1)} %shard_map.84), channel_id=1, source_target_pairs={{8,16},{12,20},{16,8},{20,12},{9,17},{13,21},{17,9},{21,13},{10,18... | collective-permute-start | bytes 1671176 | tf_op jit(solution)/shard_map/ppermute | solution.py:751
  263.9 42.4 %collective-permute-start.18 = (bf16[1,136,2048]{2,1,0:T(8,128)(2,1)}, bf16[1,136,2048]{2,1,0:T(8,128)(2,1)}, u32[]{:S(2)}, u32[]{:S(2)}) collective-permute-start(bf16[1,136,2048]{2,1,0:T(8,128)(2,1)} %shard_map.88), channel_id=1, source_target_pairs={{8,16},{12,20},{16,8},{20,12},{9,17},{13,21},{17,9},{21,13},{10,18... | collective-permute-start | bytes 1671176 | tf_op jit(solution)/shard_map/ppermute | solution.py:751
  291.6 46.3 %collective-permute-start.26 = (bf16[1,136,2048]{2,1,0:T(8,128)(2,1)}, bf16[1,136,2048]{2,1,0:T(8,128)(2,1)}, u32[]{:S(2)}, u32[]{:S(2)}) collective-permute-start(bf16[1,136,2048]{2,1,0:T(8,128)(2,1)} %shard_map.77.refs_0_), channel_id=1, source_target_pairs={{0,8},{4,12},{8,0},{12,4},{16,24},{20,28},{24,16},{28,20},{1,9},{5... | collective-permute-start | bytes 1671176 | tf_op jit(solution)/shard_map/ppermute | solution.py:751
  304.1 34.9 %collective-permute-start.27 = (bf16[1,136,2048]{2,1,0:T(8,128)(2,1)}, bf16[1,136,2048]{2,1,0:T(8,128)(2,1)}, u32[]{:S(2)}, u32[]{:S(2)}) collective-permute-start(bf16[1,136,2048]{2,1,0:T(8,128)(2,1)} %shard_map.83.refs_2_), channel_id=1, source_target_pairs={{0,8},{4,12},{8,0},{12,4},{16,24},{20,28},{24,16},{28,20},{1,9},{5... | collective-permute-start | bytes 1671176 | tf_op jit(solution)/shard_map/ppermute | solution.py:751
  306.3 38.6 %collective-permute-start.28 = (bf16[1,136,2048]{2,1,0:T(8,128)(2,1)}, bf16[1,136,2048]{2,1,0:T(8,128)(2,1)}, u32[]{:S(2)}, u32[]{:S(2)}) collective-permute-start(bf16[1,136,2048]{2,1,0:T(8,128)(2,1)} %shard_map.87.refs_4_), channel_id=1, source_target_pairs={{0,8},{4,12},{8,0},{12,4},{16,24},{20,28},{24,16},{28,20},{1,9},{5... | collective-permute-start | bytes 1671176 | tf_op jit(solution)/shard_map/ppermute | solution.py:751
  337.0 18.3 %collective-permute-start.13 = (bf16[1,136,2048]{2,1,0:T(8,128)(2,1)}, bf16[1,136,2048]{2,1,0:T(8,128)(2,1)}, u32[]{:S(2)}, u32[]{:S(2)}) collective-permute-start(bf16[1,136,2048]{2,1,0:T(8,128)(2,1)} %shard_map.81.a_ref), channel_id=1, source_target_pairs={{0,8},{4,12},{8,0},{12,4},{16,24},{20,28},{24,16},{28,20},{1,9},{5... | collective-permute-start | bytes 1671176 | tf_op jit(solution)/shard_map/ppermute | solution.py:751
  337.8 26.7 %collective-permute-start.16 = (bf16[1,136,2048]{2,1,0:T(8,128)(2,1)}, bf16[1,136,2048]{2,1,0:T(8,128)(2,1)}, u32[]{:S(2)}, u32[]{:S(2)}) collective-permute-start(bf16[1,136,2048]{2,1,0:T(8,128)(2,1)} %shard_map.85.a_ref), channel_id=1, source_target_pairs={{0,8},{4,12},{8,0},{12,4},{16,24},{20,28},{24,16},{28,20},{1,9},{5... | collective-permute-start | bytes 1671176 | tf_op jit(solution)/shard_map/ppermute | solution.py:751
  339.1 31.5 %collective-permute-start.19 = (bf16[1,136,2048]{2,1,0:T(8,128)(2,1)}, bf16[1,136,2048]{2,1,0:T(8,128)(2,1)}, u32[]{:S(2)}, u32[]{:S(2)}) collective-permute-start(bf16[1,136,2048]{2,1,0:T(8,128)(2,1)} %shard_map.89.refs_2_), channel_id=1, source_target_pairs={{0,8},{4,12},{8,0},{12,4},{16,24},{20,28},{24,16},{28,20},{1,9},{5... | collective-permute-start | bytes 1671176 | tf_op jit(solution)/shard_map/ppermute | solution.py:751

commit v12 on v11

--- a/solution.py
+++ b/solution.py
@@ -763,15 +763,15 @@
     inward, outward = mirror(1, "outer"), mirror(1, "inner")
     q_near = send(queries, near)
     q_mid = send(queries, middle)
-    half = out_weight.shape[0] // 2
-    w_across0 = send(out_weight[:half], across)
+    quarter = out_weight.shape[0] // 4
+    w_across0 = send(out_weight[:quarter], across)
     cache = jnp.transpose(passage_cache, (0, 2, 1, 3))
     row, tag, far_tag, *items = sort_items(
         lists, passage_slot, question_slot, cache, most, per_device
     )
     tables = (row, tag, far_tag)
     later, _ = lax.optimization_barrier((out_weight, row))
-    w_across1 = send(later[half:], across)
+    w_across1 = send(later[quarter:], across)
     q_out = send(q_mid, outward)
     q_cross = send(q_near, middle)
     q_end = send(q_cross, outward)
@@ -842,8 +842,8 @@
 
     def load_here():
         pltpu.make_async_copy(own_ref, w_ref.at[0, x], w_sem.at[0, x]).start()
-        half = a0_ref.shape[0]
-        low, high = w_ref.at[0, 1 - x, pl.ds(0, half)], w_ref.at[0, 1 - x, pl.ds(half, half)]
+        first, rest = a0_ref.shape[0], a1_ref.shape[0]
+        low, high = w_ref.at[0, 1 - x, pl.ds(0, first)], w_ref.at[0, 1 - x, pl.ds(first, rest)]
         pltpu.make_async_copy(a0_ref, low, w_sem.at[0, 1 - x]).start()
         pltpu.make_async_copy(a1_ref, high, w_sem.at[0, 1 - x]).start()
 

time: 395 us -> 395 us (level)
  starting transfers between devices: 65.7 us -> 102 us
  waiting for transfers between devices: 169 us -> 133 us
    ppermute x29, starting transfers between devices: 65.7 us -> 102 us  [send(): return lax.ppermute(value, 'pass', pairs)]
    ppermute x29, waiting for transfers between devices: 169 us -> 133 us  [send(): return lax.ppermute(value, 'pass', pairs)]
  transfers between devices with their start and end apart: 29 -> 29, of which waited for: 8 -> 9; matrix products, arithmetic and copies ran while one was open for 3% -> 3% of each run, Pallas kernels for 31% -> 31%
where the time goes in v12:
time: 395 us; the launch traced here: 394 us
  Pallas kernels  143 us (36%)
  waiting for transfers between devices  133 us (34%)
  starting transfers between devices  102 us (26%)
  local copies, waits for them, and re-layouts  15.8 us (4%)
    ppermute x29, waiting for transfers between devices, send(): return lax.ppermute(value, 'pass', pairs)  133 us
    ppermute x29, starting transfers between devices, send(): return lax.ppermute(value, 'pass', pairs)  102 us
    pallas_call x5, Pallas kernels, part_call(): pl.pallas_call(functools.partial(part_kernel, k, most, first, last, heads...  71.7 us
    pallas_call x2, Pallas kernels, project_call(): pl.pallas_call(functools.partial(project_kernel, len(finished), len(piece...  31.7 us
    pallas_call x14, Pallas kernels, join_call(): pl.pallas_call(merge_kernel if leveled else finish_kernel, out_shape=jax....  31.5 us
    unnamed x2, local copies, waits for them, and re-layouts  10.3 us
  transfers between devices with their start and end apart: 29, of which 9 were waited for; matrix products, arithmetic and copies ran while one was open for 3% of the time, Pallas kernels for 31%

profile of v12, /device:TPU:0, one launch (start us, length us, event | category | flops | bytes accessed | tf_op | source)
XLA Modules:
  0.0 393.8 jit_solution(4694293376443422986)
XLA Ops:
  0.0 3.1 collective-permute-start.2
  4.8 8.2 %copy.16 = bf16[16,512,2,256]{3,1,2,0:T(8,128)(2,1)} copy(bf16[16,512,2,256]{3,2,1,0:T(2,128)(2,1)} %param.9) | data formatting | bytes 16777216 | tf_op args[2]
  13.0 7.8 %sort_items.1 = (s32[12]{0:T(128)}, s32[12]{0:T(128)}, s32[12]{0:T(128)}, bf16[3,2,512,256]{3,2,1,0:T(8,128)(2,1)}, bf16[3,2,512,256]{3,2,1,0:T(8,128)(2,1)}, /*...) custom-call(s32[8,24]{1,0:T(8,128)} %bitcast.16, s32[128]{0:T(128)} %pslot_ref.1, s32[24]{0:T(128)} %qslot_ref.1, ...), custom_call_target="tpu_custom_call" | custom-call | bytes 12582912 | tf_op jit(solution)/shard_map/sort_items/pallas_call | solution.py:437
  20.8 2.6 collective-permute-start.7
  23.4 14.3 %collective-permute-done.2.refs_3_ = bf16[384,2048]{1,0:T(8,128)(2,1)} collective-permute-done((bf16[384,2048]{1,0:T(8,128)(2,1)}, bf16[384,2048]{1,0:T(8,128)(2,1)}, u32[]{:S(2)}, u32[]{:S(2)}) %collective-permute-start.2) | collective-permute-done | bytes 1572896 | tf_op jit(solution)/shard_map/ppermute | solution.py:751
  43.7 9.2 %collective-permute-start.22 = (bf16[2048,512]{1,0:T(8,128)(2,1)}, bf16[2048,512]{1,0:T(8,128)(2,1)}, u32[]{:S(2)}, u32[]{:S(2)}) collective-permute-start(bf16[2048,512]{1,0:T(8,128)(2,1)} %refs_6_.1), channel_id=1, source_target_pairs={{0,16},{4,20},{24,8},{28,12},{1,17},{5,21},{25,9},{29,13},{2,18},{... | collective-permute-start | bytes 6291464 | tf_op jit(solution)/shard_map/ppermute | solution.py:751
  52.9 16.2 %collective-permute-done.20.refs_5_.refs_7_ = bf16[512,512]{1,0:T(8,128)(2,1)} collective-permute-done((bf16[512,512]{1,0:T(8,128)(2,1)S(1)}, bf16[512,512]{1,0:T(8,128)(2,1)}, u32[]{:S(2)}, u32[]{:S(2)}) %collective-permute-start.20) | collective-permute-done | bytes 524320 | tf_op jit(solution)/shard_map/ppermute | solution.py:751
  72.4 5.4 %collective-permute-done.6.refs_4_ = bf16[384,2048]{1,0:T(8,128)(2,1)} collective-permute-done((bf16[384,2048]{1,0:T(8,128)(2,1)}, bf16[384,2048]{1,0:T(8,128)(2,1)}, u32[]{:S(2)}, u32[]{:S(2)}) %collective-permute-start.6) | collective-permute-done | bytes 1572896 | tf_op jit(solution)/shard_map/ppermute | solution.py:751
  79.1 15.5 %shard_map.75.refs_0_ = bf16[3,136,2048]{2,1,0:T(8,128)(2,1)} custom-call(s32[12]{0:T(128)} %get-tuple-element.13.refs_0_, s32[12]{0:T(128)} %get-tuple-element.14.refs_1_, s32[12]{0:T(128)} %get-tuple-element.15.refs_2_, bf16[384,2048]{1,0:T(8,128)(2,1)} %collective-permute-done.3.refs_3_, bf16[384,2048]{1,0:T(8,128)(2,1)} %collective-permute-done.6.refs_4_, ...), custom_call_target="tpu_custom_call" | custom-call | flops 3221225472 | bytes 3145728 | tf_op jit(solution)/shard_map/pallas_call | solution.py:631
  94.7 12.0 %collective-permute-done.refs_6_ = bf16[3,2,512,256]{3,2,1,0:T(8,128)(2,1)} collective-permute-done((bf16[3,2,512,256]{3,2,1,0:T(8,128)(2,1)}, bf16[3,2,512,256]{3,2,1,0:T(8,128)(2,1)}, u32[]{:S(2)}, u32[]{:S(2)}) %collective-permute-start) | collective-permute-done | bytes 1572896 | tf_op jit(solution)/shard_map/ppermute | solution.py:751
  106.7 39.0 %collective-permute-start.8 = (bf16[3,136,2048]{2,1,0:T(8,128)(2,1)}, bf16[3,136,2048]{2,1,0:T(8,128)(2,1)}, u32[]{:S(2)}, u32[]{:S(2)}) collective-permute-start(bf16[3,136,2048]{2,1,0:T(8,128)(2,1)} %shard_map.75.refs_0_), channel_id=1, source_target_pairs={{0,8},{4,12},{24,16},{28,20},{1,9},{5,13},{25,17},{29,21},{2,10},{... | collective-permute-start | bytes 5013512 | tf_op jit(solution)/shard_map/ppermute | solution.py:751
  145.7 2.6 slice.7
  149.8 51.3 %collective-permute-done.4.refs_4_ = bf16[384,2048]{1,0:T(8,128)(2,1)} collective-permute-done((bf16[384,2048]{1,0:T(8,128)(2,1)}, bf16[384,2048]{1,0:T(8,128)(2,1)}, u32[]{:S(2)}, u32[]{:S(2)}) %collective-permute-start.4) | collective-permute-done | bytes 1572896 | tf_op jit(solution)/shard_map/ppermute | solution.py:751
  202.6 15.5 %shard_map.74.refs_0_ = bf16[3,136,2048]{2,1,0:T(8,128)(2,1)} custom-call(s32[12]{0:T(128)} %get-tuple-element.13.refs_0_, s32[12]{0:T(128)} %get-tuple-element.14.refs_1_, s32[12]{0:T(128)} %get-tuple-element.15.refs_2_, bf16[384,2048]{1,0:T(8,128)(2,1)} %collective-permute-done.1.refs_3_, bf16[384,2048]{1,0:T(8,128)(2,1)} %collective-permute-done.4.refs_4_, ...), custom_call_target="tpu_custom_call" | custom-call | flops 3221225472 | bytes 3145728 | tf_op jit(solution)/shard_map/pallas_call | solution.py:631
  218.2 2.6 collective-permute-start.11
  222.8 2.4 collective-permute-start.25
  230.8 7.9 %collective-permute-done.21.refs_6_.refs_8_ = bf16[1536,512]{1,0:T(8,128)(2,1)} collective-permute-done((bf16[1536,512]{1,0:T(8,128)(2,1)}, bf16[1536,512]{1,0:T(8,128)(2,1)}, u32[]{:S(2)}, u32[]{:S(2)}) %collective-permute-start.21) | collective-permute-done | bytes 1572896 | tf_op jit(solution)/shard_map/ppermute | solution.py:751
  242.2 11.0 %collective-permute-done.11.refs_1_ = bf16[3,136,2048]{2,1,0:T(8,128)(2,1)} collective-permute-done((bf16[3,136,2048]{2,1,0:T(8,128)(2,1)}, bf16[3,136,2048]{2,1,0:T(8,128)(2,1)}, u32[]{:S(2)}, u32[]{:S(2)}) %collective-permute-start.11) | collective-permute-done | bytes 1671200 | tf_op jit(solution)/shard_map/ppermute | solution.py:751
  267.1 20.3 %shard_map.73.refs_0_ = bf16[3,136,2048]{2,1,0:T(8,128)(2,1)} custom-call(s32[12]{0:T(128)} %get-tuple-element.13.refs_0_, s32[12]{0:T(128)} %get-tuple-element.14.refs_1_, s32[12]{0:T(128)} %get-tuple-element.15.refs_2_, bf16[3,2,128,256]{3,2,1,0:T(8,128)(2,1)} %bitcast.14, bf16[384,2048]{1,0:T(8,128)(2,1)} %refs_4_.2, bf16[16,2,512,256]{3,2,1,0:T(8,128)(2,1)} %bitcast.11, ...), custom_call_target="tpu_custom_call" | custom-call | flops 3221225472 | bytes 3145728 | tf_op jit(solution)/shard_map/pallas_call | solution.py:631
  291.6 12.7 %collective-permute-start.26 = (bf16[1,136,2048]{2,1,0:T(8,128)(2,1)}, bf16[1,136,2048]{2,1,0:T(8,128)(2,1)}, u32[]{:S(2)}, u32[]{:S(2)}) collective-permute-start(bf16[1,136,2048]{2,1,0:T(8,128)(2,1)} %shard_map.77.refs_0_), channel_id=1, source_target_pairs={{0,8},{4,12},{8,0},{12,4},{16,24},{20,28},{24,16},{28,20},{1,9},{5... | collective-permute-start | bytes 1671176 | tf_op jit(solution)/shard_map/ppermute | solution.py:751
  306.4 2.4 collective-permute-start.28
  308.8 10.2 %shard_map.78.refs_0_ = bf16[3,136,2048]{2,1,0:T(8,128)(2,1)} custom-call(s32[12]{0:T(128)} %get-tuple-element.13.refs_0_, s32[12]{0:T(128)} %get-tuple-element.14.refs_1_, s32[12]{0:T(128)} %get-tuple-element.15.refs_2_, bf16[384,2048]{1,0:T(8,128)(2,1)} %collective-permute-done.2.refs_3_, bf16[16,2,512,256]{3,2,1,0:T(8,128)(2,1)} %bitcast.12), custom_call_target="tpu_custom_call" | custom-call | flops 1610612736 | bytes 1572864 | tf_op jit(solution)/shard_map/pallas_call | solution.py:631
  319.0 10.2 %shard_map.79.refs_1_ = bf16[3,136,2048]{2,1,0:T(8,128)(2,1)} custom-call(s32[12]{0:T(128)} %get-tuple-element.13.refs_0_, s32[12]{0:T(128)} %get-tuple-element.14.refs_1_, s32[12]{0:T(128)} %get-tuple-element.15.refs_2_, bf16[384,2048]{1,0:T(8,128)(2,1)} %collective-permute-done.2.refs_3_, bf16[16,2,512,256]{3,2,1,0:T(8,128)(2,1)} %bitcast.13, ...), custom_call_target="tpu_custom_call" | custom-call | flops 1610612736 | bytes 1572864 | tf_op jit(solution)/shard_map/pallas_call | solution.py:631
  329.2 2.7 shard_map.81.a_ref
  331.9 2.6 shard_map.85.a_ref
  334.5 2.6 shard_map.89.refs_2_
  340.0 2.5 shard_map.90.refs_0_
  342.5 2.5 shard_map.91.refs_1_
  344.9 10.3 %project_far.1.refs_13_ = bf16[2,384,512]{2,1,0:T(8,128)(2,1)} custom-call(bf16[128,2048]{1,0:T(8,128)(2,1)} %shard_map.90.refs_0_, bf16[128,2048]{1,0:T(8,128)(2,1)} %shard_map.91.refs_1_, bf16[1,136,2048]{2,1,0:T(8,128)(2,1)} %shard_map.89.refs_2_, bf16[1,136,2048]{2,1,0:T(8,128)(2,1)} %collective-permute-done.28.refs_3_, bf16[2048,512]{1,0:T(8,128)(2,1)} %refs_6_.1, ...), custom_call_target="tpu_custom_call" | custom-call | flops 3221225472 | bytes 8388608 | tf_op jit(solution)/shard_map/project_far/pallas_call | solution.py:991
  355.3 9.1 %collective-permute-done.16.refs_3_ = bf16[1,136,2048]{2,1,0:T(8,128)(2,1)} collective-permute-done((bf16[1,136,2048]{2,1,0:T(8,128)(2,1)}, bf16[1,136,2048]{2,1,0:T(8,128)(2,1)}, u32[]{:S(2)}, u32[]{:S(2)}) %collective-permute-start.16) | collective-permute-done | bytes 557088 | tf_op jit(solution)/shard_map/ppermute | solution.py:751
  364.4 6.0 %collective-permute-done.19.refs_5_ = bf16[1,136,2048]{2,1,0:T(8,128)(2,1)} collective-permute-done((bf16[1,136,2048]{2,1,0:T(8,128)(2,1)}, bf16[1,136,2048]{2,1,0:T(8,128)(2,1)}, u32[]{:S(2)}, u32[]{:S(2)}) %collective-permute-start.19) | collective-permute-done | bytes 557088 | tf_op jit(solution)/shard_map/ppermute | solution.py:751
  370.4 21.3 %project_home.1 = bf16[384,1024]{1,0:T(8,128)(2,1)} custom-call(bf16[1,136,2048]{2,1,0:T(8,128)(2,1)} %shard_map.77.refs_0_, bf16[1,136,2048]{2,1,0:T(8,128)(2,1)} %collective-permute-done.13.refs_1_, bf16[1,136,2048]{2,1,0:T(8,128)(2,1)} %shard_map.83.refs_2_, bf16[1,136,2048]{2,1,0:T(8,128)(2,1)} %collective-permute-done.16.refs_3_, ...), custom_call_target="tpu_custom_call" | custom-call | flops 3221225472 | bytes 8388608 | tf_op jit(solution)/shard_map/project_home/pallas_call | solution.py:991
  (53 shorter events, 51.5 us)
Async XLA Ops:
  0.0 37.8 %collective-permute-start.2 = (bf16[384,2048]{1,0:T(8,128)(2,1)}, bf16[384,2048]{1,0:T(8,128)(2,1)}, u32[]{:S(2)}, u32[]{:S(2)}) collective-permute-start(bf16[384,2048]{1,0:T(8,128)(2,1)} %refs_4_.2), channel_id=1, source_target_pairs={{0,8},{4,12},{8,0},{12,4},{16,24},{20,28},{24,16},{28,20},{1,9},{5... | collective-permute-start | bytes 4718600 | tf_op jit(solution)/shard_map/ppermute | solution.py:751
  3.1 36.6 %collective-permute-start.1 = (bf16[384,2048]{1,0:T(8,128)(2,1)}, bf16[384,2048]{1,0:T(8,128)(2,1)}, u32[]{:S(2)}, u32[]{:S(2)}) collective-permute-start(bf16[384,2048]{1,0:T(8,128)(2,1)} %refs_4_.2), channel_id=1, source_target_pairs={{8,16},{12,20},{16,8},{20,12},{9,17},{13,21},{17,9},{21,13},{10,18... | collective-permute-start | bytes 4718600 | tf_op jit(solution)/shard_map/ppermute | solution.py:751
  20.8 50.0 %collective-permute-start.7 = (bf16[3,2,512,256]{3,2,1,0:T(8,128)(2,1)}, bf16[3,2,512,256]{3,2,1,0:T(8,128)(2,1)}, u32[]{:S(2)}, u32[]{:S(2)}) collective-permute-start(bf16[3,2,512,256]{3,2,1,0:T(8,128)(2,1)} %get-tuple-element.18), channel_id=1, source_target_pairs={{0,4},{4,0},{8,12},{12,8},{16,20},{20,16},{24,28},{28,24},{1,5},{5... | collective-permute-start | bytes 4718600 | tf_op jit(solution)/shard_map/ppermute | solution.py:751
  37.8 33.4 %collective-permute-start.3 = (bf16[384,2048]{1,0:T(8,128)(2,1)}, bf16[384,2048]{1,0:T(8,128)(2,1)}, u32[]{:S(2)}, u32[]{:S(2)}) collective-permute-start(bf16[384,2048]{1,0:T(8,128)(2,1)} %collective-permute-done.2.refs_3_), channel_id=1, source_target_pairs={{8,16},{12,20},{16,8},{20,12},{9,17},{13,21},{17,9},{21,13},{10,18... | collective-permute-start | bytes 4718600 | tf_op jit(solution)/shard_map/ppermute | solution.py:751
  39.6 38.2 %collective-permute-start.6 = (bf16[384,2048]{1,0:T(8,128)(2,1)}, bf16[384,2048]{1,0:T(8,128)(2,1)}, u32[]{:S(2)}, u32[]{:S(2)}) collective-permute-start(bf16[384,2048]{1,0:T(8,128)(2,1)} %collective-permute-done.1.refs_3_), channel_id=1, source_target_pairs={{8,0},{12,4},{16,24},{20,28},{9,1},{13,5},{17,25},{21,29},{10,2},{... | collective-permute-start | bytes 4718600 | tf_op jit(solution)/shard_map/ppermute | solution.py:751
  42.0 27.1 %collective-permute-start.20 = (bf16[512,512]{1,0:T(8,128)(2,1)S(1)}, bf16[512,512]{1,0:T(8,128)(2,1)}, u32[]{:S(2)}, u32[]{:S(2)}) collective-permute-start(bf16[512,512]{1,0:T(8,128)(2,1)S(1)} %slice.6), channel_id=1, source_target_pairs={{0,4},{4,0},{8,12},{12,8},{16,20},{20,16},{24,28},{28,24},{1,5},{5... | collective-permute-start | bytes 1572872 | tf_op jit(solution)/shard_map/ppermute | solution.py:751
  43.7 174.4 %collective-permute-start.22 = (bf16[2048,512]{1,0:T(8,128)(2,1)}, bf16[2048,512]{1,0:T(8,128)(2,1)}, u32[]{:S(2)}, u32[]{:S(2)}) collective-permute-start(bf16[2048,512]{1,0:T(8,128)(2,1)} %refs_6_.1), channel_id=1, source_target_pairs={{0,16},{4,20},{24,8},{28,12},{1,17},{5,21},{25,9},{29,13},{2,18},{... | collective-permute-start | bytes 6291464 | tf_op jit(solution)/shard_map/ppermute | solution.py:751
  69.1 37.6 %collective-permute-start = (bf16[3,2,512,256]{3,2,1,0:T(8,128)(2,1)}, bf16[3,2,512,256]{3,2,1,0:T(8,128)(2,1)}, u32[]{:S(2)}, u32[]{:S(2)}) collective-permute-start(bf16[3,2,512,256]{3,2,1,0:T(8,128)(2,1)} %get-tuple-element.16), channel_id=1, source_target_pairs={{0,4},{4,0},{8,12},{12,8},{16,20},{20,16},{24,28},{28,24},{1,5},{5... | collective-permute-start | bytes 4718600 | tf_op jit(solution)/shard_map/ppermute | solution.py:751
  70.9 77.5 %collective-permute-start.5 = (bf16[3,2,512,256]{3,2,1,0:T(8,128)(2,1)}, bf16[3,2,512,256]{3,2,1,0:T(8,128)(2,1)}, u32[]{:S(2)}, u32[]{:S(2)}) collective-permute-start(bf16[3,2,512,256]{3,2,1,0:T(8,128)(2,1)} %get-tuple-element.17), channel_id=1, source_target_pairs={{0,4},{4,0},{8,12},{12,8},{16,20},{20,16},{24,28},{28,24},{1,5},{5... | collective-permute-start | bytes 4718600 | tf_op jit(solution)/shard_map/ppermute | solution.py:751
  71.1 130.0 %collective-permute-start.4 = (bf16[384,2048]{1,0:T(8,128)(2,1)}, bf16[384,2048]{1,0:T(8,128)(2,1)}, u32[]{:S(2)}, u32[]{:S(2)}) collective-permute-start(bf16[384,2048]{1,0:T(8,128)(2,1)} %collective-permute-done.3.refs_3_), channel_id=1, source_target_pairs={{8,0},{12,4},{16,24},{20,28},{9,1},{13,5},{17,25},{21,29},{10,2},{... | collective-permute-start | bytes 4718600 | tf_op jit(solution)/shard_map/ppermute | solution.py:751
  77.8 143.0 %collective-permute-start.24 = (bf16[2048,512]{1,0:T(8,128)(2,1)}, bf16[2048,512]{1,0:T(8,128)(2,1)}, u32[]{:S(2)}, u32[]{:S(2)}) collective-permute-start(bf16[2048,512]{1,0:T(8,128)(2,1)} %refs_6_.1), channel_id=1, source_target_pairs={{8,24},{12,28},{16,0},{20,4},{9,25},{13,29},{17,1},{21,5},{10,26},... | collective-permute-start | bytes 6291464 | tf_op jit(solution)/shard_map/ppermute | solution.py:751
  106.7 116.1 %collective-permute-start.8 = (bf16[3,136,2048]{2,1,0:T(8,128)(2,1)}, bf16[3,136,2048]{2,1,0:T(8,128)(2,1)}, u32[]{:S(2)}, u32[]{:S(2)}) collective-permute-start(bf16[3,136,2048]{2,1,0:T(8,128)(2,1)} %shard_map.75.refs_0_), channel_id=1, source_target_pairs={{0,8},{4,12},{24,16},{28,20},{1,9},{5,13},{25,17},{29,21},{2,10},{... | collective-permute-start | bytes 5013512 | tf_op jit(solution)/shard_map/ppermute | solution.py:751
  148.3 81.1 %collective-permute-start.10 = (bf16[3,2,512,256]{3,2,1,0:T(8,128)(2,1)}, bf16[3,2,512,256]{3,2,1,0:T(8,128)(2,1)}, u32[]{:S(2)}, u32[]{:S(2)}) collective-permute-start(bf16[3,2,512,256]{3,2,1,0:T(8,128)(2,1)} %get-tuple-element.19), channel_id=1, source_target_pairs={{0,4},{4,0},{8,12},{12,8},{16,20},{20,16},{24,28},{28,24},{1,5},{5... | collective-permute-start | bytes 4718600 | tf_op jit(solution)/shard_map/ppermute | solution.py:751
  201.1 37.6 %collective-permute-start.21 = (bf16[1536,512]{1,0:T(8,128)(2,1)}, bf16[1536,512]{1,0:T(8,128)(2,1)}, u32[]{:S(2)}, u32[]{:S(2)}) collective-permute-start(bf16[1536,512]{1,0:T(8,128)(2,1)} %slice.7), channel_id=1, source_target_pairs={{0,4},{4,0},{8,12},{12,8},{16,20},{20,16},{24,28},{28,24},{1,5},{5... | collective-permute-start | bytes 4718600 | tf_op jit(solution)/shard_map/ppermute | solution.py:751
  218.2 35.1 %collective-permute-start.11 = (bf16[3,136,2048]{2,1,0:T(8,128)(2,1)}, bf16[3,136,2048]{2,1,0:T(8,128)(2,1)}, u32[]{:S(2)}, u32[]{:S(2)}) collective-permute-start(bf16[3,136,2048]{2,1,0:T(8,128)(2,1)} %shard_map.74.refs_0_), channel_id=1, source_target_pairs={{0,8},{4,12},{24,16},{28,20},{1,9},{5,13},{25,17},{29,21},{2,10},{... | collective-permute-start | bytes 5013512 | tf_op jit(solution)/shard_map/ppermute | solution.py:751
  220.8 116.3 %collective-permute-start.23 = (bf16[2048,512]{1,0:T(8,128)(2,1)}, bf16[2048,512]{1,0:T(8,128)(2,1)}, u32[]{:S(2)}, u32[]{:S(2)}) collective-permute-start(bf16[2048,512]{1,0:T(8,128)(2,1)} %collective-permute-done.22.refs_7_.refs_9_), channel_id=1, source_target_pairs={{8,12},{12,8},{16,20},{20,16},{9,13},{13,9},{17,21},{21,17},{10,14... | collective-permute-start | bytes 6291464 | tf_op jit(solution)/shard_map/ppermute | solution.py:751
  222.8 122.1 %collective-permute-start.25 = (bf16[2048,512]{1,0:T(8,128)(2,1)}, bf16[2048,512]{1,0:T(8,128)(2,1)}, u32[]{:S(2)}, u32[]{:S(2)}) collective-permute-start(bf16[2048,512]{1,0:T(8,128)(2,1)} %collective-permute-done.24.refs_9_.refs_11_), channel_id=1, source_target_pairs={{0,4},{4,0},{24,28},{28,24},{1,5},{5,1},{25,29},{29,25},{2,6},{6,2... | collective-permute-start | bytes 6291464 | tf_op jit(solution)/shard_map/ppermute | solution.py:751
  229.4 29.5 %collective-permute-start.9 = (bf16[1,136,2048]{2,1,0:T(8,128)(2,1)}, bf16[1,136,2048]{2,1,0:T(8,128)(2,1)}, u32[]{:S(2)}, u32[]{:S(2)}) collective-permute-start(bf16[1,136,2048]{2,1,0:T(8,128)(2,1)} %shard_map.76), channel_id=1, source_target_pairs={{8,16},{12,20},{16,8},{20,12},{9,17},{13,21},{17,9},{21,13},{10,18... | collective-permute-start | bytes 1671176 | tf_op jit(solution)/shard_map/ppermute | solution.py:751
  238.7 21.6 %collective-permute-start.14 = (bf16[1,136,2048]{2,1,0:T(8,128)(2,1)}, bf16[1,136,2048]{2,1,0:T(8,128)(2,1)}, u32[]{:S(2)}, u32[]{:S(2)}) collective-permute-start(bf16[1,136,2048]{2,1,0:T(8,128)(2,1)} %shard_map.82), channel_id=1, source_target_pairs={{8,16},{12,20},{16,8},{20,12},{9,17},{13,21},{17,9},{21,13},{10,18... | collective-permute-start | bytes 1671176 | tf_op jit(solution)/shard_map/ppermute | solution.py:751
  253.2 10.6 %collective-permute-start.17 = (bf16[1,136,2048]{2,1,0:T(8,128)(2,1)}, bf16[1,136,2048]{2,1,0:T(8,128)(2,1)}, u32[]{:S(2)}, u32[]{:S(2)}) collective-permute-start(bf16[1,136,2048]{2,1,0:T(8,128)(2,1)} %shard_map.86), channel_id=1, source_target_pairs={{8,16},{12,20},{16,8},{20,12},{9,17},{13,21},{17,9},{21,13},{10,18... | collective-permute-start | bytes 1671176 | tf_op jit(solution)/shard_map/ppermute | solution.py:751
  258.8 32.8 %collective-permute-start.12 = (bf16[1,136,2048]{2,1,0:T(8,128)(2,1)}, bf16[1,136,2048]{2,1,0:T(8,128)(2,1)}, u32[]{:S(2)}, u32[]{:S(2)}) collective-permute-start(bf16[1,136,2048]{2,1,0:T(8,128)(2,1)} %shard_map.80), channel_id=1, source_target_pairs={{8,16},{12,20},{16,8},{20,12},{9,17},{13,21},{17,9},{21,13},{10,18... | collective-permute-start | bytes 1671176 | tf_op jit(solution)/shard_map/ppermute | solution.py:751
  260.3 43.9 %collective-permute-start.15 = (bf16[1,136,2048]{2,1,0:T(8,128)(2,1)}, bf16[1,136,2048]{2,1,0:T(8,128)(2,1)}, u32[]{:S(2)}, u32[]{:S(2)}) collective-permute-start(bf16[1,136,2048]{2,1,0:T(8,128)(2,1)} %shard_map.84), channel_id=1, source_target_pairs={{8,16},{12,20},{16,8},{20,12},{9,17},{13,21},{17,9},{21,13},{10,18... | collective-permute-start | bytes 1671176 | tf_op jit(solution)/shard_map/ppermute | solution.py:751
  263.9 42.5 %collective-permute-start.18 = (bf16[1,136,2048]{2,1,0:T(8,128)(2,1)}, bf16[1,136,2048]{2,1,0:T(8,128)(2,1)}, u32[]{:S(2)}, u32[]{:S(2)}) collective-permute-start(bf16[1,136,2048]{2,1,0:T(8,128)(2,1)} %shard_map.88), channel_id=1, source_target_pairs={{8,16},{12,20},{16,8},{20,12},{9,17},{13,21},{17,9},{21,13},{10,18... | collective-permute-start | bytes 1671176 | tf_op jit(solution)/shard_map/ppermute | solution.py:751
  291.6 46.4 %collective-permute-start.26 = (bf16[1,136,2048]{2,1,0:T(8,128)(2,1)}, bf16[1,136,2048]{2,1,0:T(8,128)(2,1)}, u32[]{:S(2)}, u32[]{:S(2)}) collective-permute-start(bf16[1,136,2048]{2,1,0:T(8,128)(2,1)} %shard_map.77.refs_0_), channel_id=1, source_target_pairs={{0,8},{4,12},{8,0},{12,4},{16,24},{20,28},{24,16},{28,20},{1,9},{5... | collective-permute-start | bytes 1671176 | tf_op jit(solution)/shard_map/ppermute | solution.py:751
  304.3 34.9 %collective-permute-start.27 = (bf16[1,136,2048]{2,1,0:T(8,128)(2,1)}, bf16[1,136,2048]{2,1,0:T(8,128)(2,1)}, u32[]{:S(2)}, u32[]{:S(2)}) collective-permute-start(bf16[1,136,2048]{2,1,0:T(8,128)(2,1)} %shard_map.83.refs_2_), channel_id=1, source_target_pairs={{0,8},{4,12},{8,0},{12,4},{16,24},{20,28},{24,16},{28,20},{1,9},{5... | collective-permute-start | bytes 1671176 | tf_op jit(solution)/shard_map/ppermute | solution.py:751
  306.4 38.5 %collective-permute-start.28 = (bf16[1,136,2048]{2,1,0:T(8,128)(2,1)}, bf16[1,136,2048]{2,1,0:T(8,128)(2,1)}, u32[]{:S(2)}, u32[]{:S(2)}) collective-permute-start(bf16[1,136,2048]{2,1,0:T(8,128)(2,1)} %shard_map.87.refs_4_), channel_id=1, source_target_pairs={{0,8},{4,12},{8,0},{12,4},{16,24},{20,28},{24,16},{28,20},{1,9},{5... | collective-permute-start | bytes 1671176 | tf_op jit(solution)/shard_map/ppermute | solution.py:751
  337.2 18.1 %collective-permute-start.13 = (bf16[1,136,2048]{2,1,0:T(8,128)(2,1)}, bf16[1,136,2048]{2,1,0:T(8,128)(2,1)}, u32[]{:S(2)}, u32[]{:S(2)}) collective-permute-start(bf16[1,136,2048]{2,1,0:T(8,128)(2,1)} %shard_map.81.a_ref), channel_id=1, source_target_pairs={{0,8},{4,12},{8,0},{12,4},{16,24},{20,28},{24,16},{28,20},{1,9},{5... | collective-permute-start | bytes 1671176 | tf_op jit(solution)/shard_map/ppermute | solution.py:751
  338.0 26.5 %collective-permute-start.16 = (bf16[1,136,2048]{2,1,0:T(8,128)(2,1)}, bf16[1,136,2048]{2,1,0:T(8,128)(2,1)}, u32[]{:S(2)}, u32[]{:S(2)}) collective-permute-start(bf16[1,136,2048]{2,1,0:T(8,128)(2,1)} %shard_map.85.a_ref), channel_id=1, source_target_pairs={{0,8},{4,12},{8,0},{12,4},{16,24},{20,28},{24,16},{28,20},{1,9},{5... | collective-permute-start | bytes 1671176 | tf_op jit(solution)/shard_map/ppermute | solution.py:751
  339.2 31.2 %collective-permute-start.19 = (bf16[1,136,2048]{2,1,0:T(8,128)(2,1)}, bf16[1,136,2048]{2,1,0:T(8,128)(2,1)}, u32[]{:S(2)}, u32[]{:S(2)}) collective-permute-start(bf16[1,136,2048]{2,1,0:T(8,128)(2,1)} %shard_map.89.refs_2_), channel_id=1, source_target_pairs={{0,8},{4,12},{8,0},{12,4},{16,24},{20,28},{24,16},{28,20},{1,9},{5... | collective-permute-start | bytes 1671176 | tf_op jit(solution)/shard_map/ppermute | solution.py:751

commit v13 on v12

--- a/solution.py
+++ b/solution.py
@@ -115,7 +115,7 @@
             pltpu.SemaphoreType.DMA((slots,)),
             pltpu.SemaphoreType.DMA((slots,)),
         ],
-        name="gather_items",
+        name="gather_it",
         cost_estimate=pl.CostEstimate(
             flops=0, bytes_accessed=2 * slots * math.prod(item) * 2, transcendentals=0
         ),
@@ -278,7 +278,7 @@
         in_specs=in_specs,
         out_specs=out_specs,
         scratch_shapes=scratch,
-        name="attend_first" if first else ("attend_last" if last else "attend_more"),
+        name="a1" if first else ("a3" if last else "a2"),
         cost_estimate=pl.CostEstimate(
             flops=weights * HD * 4,
             bytes_accessed=entries * math.prod(item) * 2,
@@ -450,7 +450,7 @@
             pltpu.SemaphoreType.DMA((slots,)),
         ],
         compiler_params=pltpu.CompilerParams(vmem_limit_bytes=VMEM_BYTES),
-        name="sort_items",
+        name="sort_it",
         cost_estimate=pl.CostEstimate(
             flops=0, bytes_accessed=2 * slots * math.prod(item) * 2, transcendentals=0
         ),
@@ -998,7 +998,7 @@
         compiler_params=pltpu.CompilerParams(
             collective_id=int(far), has_side_effects=True, vmem_limit_bytes=VMEM_BYTES
         ),
-        name="project_far" if far else "project_home",
+        name="pf" if far else "ph",
         cost_estimate=pl.CostEstimate(
             flops=2 * 4 * rows * depth * wide,
             bytes_accessed=4 * depth * wide * 2,

time: 395 us -> 395 us (level)
  no operation moved by 1% of the time
where the time goes in v13:
time: 395 us; the launch traced here: 394 us
  Pallas kernels  143 us (36%)
  waiting for transfers between devices  133 us (34%)
  starting transfers between devices  102 us (26%)
  local copies, waits for them, and re-layouts  15.8 us (4%)
    ppermute x29, waiting for transfers between devices, send(): return lax.ppermute(value, 'pass', pairs)  133 us
    ppermute x29, starting transfers between devices, send(): return lax.ppermute(value, 'pass', pairs)  102 us
    pallas_call x5, Pallas kernels, part_call(): pl.pallas_call(functools.partial(part_kernel, k, most, first, last, heads...  71.7 us
    pallas_call x2, Pallas kernels, project_call(): pl.pallas_call(functools.partial(project_kernel, len(finished), len(piece...  31.7 us
    pallas_call x14, Pallas kernels, join_call(): pl.pallas_call(merge_kernel if leveled else finish_kernel, out_shape=jax....  31.5 us
    unnamed x2, local copies, waits for them, and re-layouts  10.3 us
  transfers between devices with their start and end apart: 29, of which 9 were waited for; matrix products, arithmetic and copies ran while one was open for 3% of the time, Pallas kernels for 31%

profile of v13, /device:TPU:0, one launch (start us, length us, event | category | flops | bytes accessed | tf_op | source)
XLA Modules:
  0.0 393.8 jit_solution(4694293376443422986)
XLA Ops:
  0.0 3.1 collective-permute-start.2
  4.8 8.2 %copy.16 = bf16[16,512,2,256]{3,1,2,0:T(8,128)(2,1)} copy(bf16[16,512,2,256]{3,2,1,0:T(2,128)(2,1)} %param.9) | data formatting | bytes 16777216 | tf_op args[2]
  13.0 7.8 %sort_it.1 = (s32[12]{0:T(128)}, s32[12]{0:T(128)}, s32[12]{0:T(128)}, bf16[3,2,512,256]{3,2,1,0:T(8,128)(2,1)}, bf16[3,2,512,256]{3,2,1,0:T(8,128)(2,1)}, /*ind...) custom-call(s32[8,24]{1,0:T(8,128)} %bitcast.16, s32[128]{0:T(128)} %pslot_ref.1, s32[24]{0:T(128)} %qslot_ref.1, ...), custom_call_target="tpu_custom_call" | custom-call | bytes 12582912 | tf_op jit(solution)/shard_map/sort_it/pallas_call | solution.py:437
  20.8 2.6 collective-permute-start.7
  23.4 14.3 %collective-permute-done.2.refs_3_ = bf16[384,2048]{1,0:T(8,128)(2,1)} collective-permute-done((bf16[384,2048]{1,0:T(8,128)(2,1)}, bf16[384,2048]{1,0:T(8,128)(2,1)}, u32[]{:S(2)}, u32[]{:S(2)}) %collective-permute-start.2) | collective-permute-done | bytes 1572896 | tf_op jit(solution)/shard_map/ppermute | solution.py:751
  43.7 9.2 %collective-permute-start.22 = (bf16[2048,512]{1,0:T(8,128)(2,1)}, bf16[2048,512]{1,0:T(8,128)(2,1)}, u32[]{:S(2)}, u32[]{:S(2)}) collective-permute-start(bf16[2048,512]{1,0:T(8,128)(2,1)} %refs_6_.1), channel_id=1, source_target_pairs={{0,16},{4,20},{24,8},{28,12},{1,17},{5,21},{25,9},{29,13},{2,18},{... | collective-permute-start | bytes 6291464 | tf_op jit(solution)/shard_map/ppermute | solution.py:751
  52.9 16.2 %collective-permute-done.20.refs_5_.refs_7_ = bf16[512,512]{1,0:T(8,128)(2,1)} collective-permute-done((bf16[512,512]{1,0:T(8,128)(2,1)S(1)}, bf16[512,512]{1,0:T(8,128)(2,1)}, u32[]{:S(2)}, u32[]{:S(2)}) %collective-permute-start.20) | collective-permute-done | bytes 524320 | tf_op jit(solution)/shard_map/ppermute | solution.py:751
  72.4 5.4 %collective-permute-done.6.refs_4_ = bf16[384,2048]{1,0:T(8,128)(2,1)} collective-permute-done((bf16[384,2048]{1,0:T(8,128)(2,1)}, bf16[384,2048]{1,0:T(8,128)(2,1)}, u32[]{:S(2)}, u32[]{:S(2)}) %collective-permute-start.6) | collective-permute-done | bytes 1572896 | tf_op jit(solution)/shard_map/ppermute | solution.py:751
  79.1 15.5 %shard_map.75.refs_0_ = bf16[3,136,2048]{2,1,0:T(8,128)(2,1)} custom-call(s32[12]{0:T(128)} %get-tuple-element.13.refs_0_, s32[12]{0:T(128)} %get-tuple-element.14.refs_1_, s32[12]{0:T(128)} %get-tuple-element.15.refs_2_, bf16[384,2048]{1,0:T(8,128)(2,1)} %collective-permute-done.3.refs_3_, bf16[384,2048]{1,0:T(8,128)(2,1)} %collective-permute-done.6.refs_4_, ...), custom_call_target="tpu_custom_call" | custom-call | flops 3221225472 | bytes 3145728 | tf_op jit(solution)/shard_map/pallas_call | solution.py:631
  94.7 12.0 %collective-permute-done.refs_6_ = bf16[3,2,512,256]{3,2,1,0:T(8,128)(2,1)} collective-permute-done((bf16[3,2,512,256]{3,2,1,0:T(8,128)(2,1)}, bf16[3,2,512,256]{3,2,1,0:T(8,128)(2,1)}, u32[]{:S(2)}, u32[]{:S(2)}) %collective-permute-start) | collective-permute-done | bytes 1572896 | tf_op jit(solution)/shard_map/ppermute | solution.py:751
  106.7 39.0 %collective-permute-start.8 = (bf16[3,136,2048]{2,1,0:T(8,128)(2,1)}, bf16[3,136,2048]{2,1,0:T(8,128)(2,1)}, u32[]{:S(2)}, u32[]{:S(2)}) collective-permute-start(bf16[3,136,2048]{2,1,0:T(8,128)(2,1)} %shard_map.75.refs_0_), channel_id=1, source_target_pairs={{0,8},{4,12},{24,16},{28,20},{1,9},{5,13},{25,17},{29,21},{2,10},{... | collective-permute-start | bytes 5013512 | tf_op jit(solution)/shard_map/ppermute | solution.py:751
  145.7 2.6 slice.7
  149.8 51.3 %collective-permute-done.4.refs_4_ = bf16[384,2048]{1,0:T(8,128)(2,1)} collective-permute-done((bf16[384,2048]{1,0:T(8,128)(2,1)}, bf16[384,2048]{1,0:T(8,128)(2,1)}, u32[]{:S(2)}, u32[]{:S(2)}) %collective-permute-start.4) | collective-permute-done | bytes 1572896 | tf_op jit(solution)/shard_map/ppermute | solution.py:751
  202.6 15.5 %shard_map.74.refs_0_ = bf16[3,136,2048]{2,1,0:T(8,128)(2,1)} custom-call(s32[12]{0:T(128)} %get-tuple-element.13.refs_0_, s32[12]{0:T(128)} %get-tuple-element.14.refs_1_, s32[12]{0:T(128)} %get-tuple-element.15.refs_2_, bf16[384,2048]{1,0:T(8,128)(2,1)} %collective-permute-done.1.refs_3_, bf16[384,2048]{1,0:T(8,128)(2,1)} %collective-permute-done.4.refs_4_, ...), custom_call_target="tpu_custom_call" | custom-call | flops 3221225472 | bytes 3145728 | tf_op jit(solution)/shard_map/pallas_call | solution.py:631
  218.2 2.6 collective-permute-start.11
  222.8 2.4 collective-permute-start.25
  230.8 7.9 %collective-permute-done.21.refs_6_.refs_8_ = bf16[1536,512]{1,0:T(8,128)(2,1)} collective-permute-done((bf16[1536,512]{1,0:T(8,128)(2,1)}, bf16[1536,512]{1,0:T(8,128)(2,1)}, u32[]{:S(2)}, u32[]{:S(2)}) %collective-permute-start.21) | collective-permute-done | bytes 1572896 | tf_op jit(solution)/shard_map/ppermute | solution.py:751
  242.2 11.0 %collective-permute-done.11.refs_1_ = bf16[3,136,2048]{2,1,0:T(8,128)(2,1)} collective-permute-done((bf16[3,136,2048]{2,1,0:T(8,128)(2,1)}, bf16[3,136,2048]{2,1,0:T(8,128)(2,1)}, u32[]{:S(2)}, u32[]{:S(2)}) %collective-permute-start.11) | collective-permute-done | bytes 1671200 | tf_op jit(solution)/shard_map/ppermute | solution.py:751
  267.1 20.3 %shard_map.73.refs_0_ = bf16[3,136,2048]{2,1,0:T(8,128)(2,1)} custom-call(s32[12]{0:T(128)} %get-tuple-element.13.refs_0_, s32[12]{0:T(128)} %get-tuple-element.14.refs_1_, s32[12]{0:T(128)} %get-tuple-element.15.refs_2_, bf16[3,2,128,256]{3,2,1,0:T(8,128)(2,1)} %bitcast.14, bf16[384,2048]{1,0:T(8,128)(2,1)} %refs_4_.2, bf16[16,2,512,256]{3,2,1,0:T(8,128)(2,1)} %bitcast.11, ...), custom_call_target="tpu_custom_call" | custom-call | flops 3221225472 | bytes 3145728 | tf_op jit(solution)/shard_map/pallas_call | solution.py:631
  291.6 12.7 %collective-permute-start.26 = (bf16[1,136,2048]{2,1,0:T(8,128)(2,1)}, bf16[1,136,2048]{2,1,0:T(8,128)(2,1)}, u32[]{:S(2)}, u32[]{:S(2)}) collective-permute-start(bf16[1,136,2048]{2,1,0:T(8,128)(2,1)} %shard_map.77.refs_0_), channel_id=1, source_target_pairs={{0,8},{4,12},{8,0},{12,4},{16,24},{20,28},{24,16},{28,20},{1,9},{5... | collective-permute-start | bytes 1671176 | tf_op jit(solution)/shard_map/ppermute | solution.py:751
  306.4 2.4 collective-permute-start.28
  308.8 10.2 %shard_map.78.refs_0_ = bf16[3,136,2048]{2,1,0:T(8,128)(2,1)} custom-call(s32[12]{0:T(128)} %get-tuple-element.13.refs_0_, s32[12]{0:T(128)} %get-tuple-element.14.refs_1_, s32[12]{0:T(128)} %get-tuple-element.15.refs_2_, bf16[384,2048]{1,0:T(8,128)(2,1)} %collective-permute-done.2.refs_3_, bf16[16,2,512,256]{3,2,1,0:T(8,128)(2,1)} %bitcast.12), custom_call_target="tpu_custom_call" | custom-call | flops 1610612736 | bytes 1572864 | tf_op jit(solution)/shard_map/pallas_call | solution.py:631
  319.0 10.2 %shard_map.79.refs_1_ = bf16[3,136,2048]{2,1,0:T(8,128)(2,1)} custom-call(s32[12]{0:T(128)} %get-tuple-element.13.refs_0_, s32[12]{0:T(128)} %get-tuple-element.14.refs_1_, s32[12]{0:T(128)} %get-tuple-element.15.refs_2_, bf16[384,2048]{1,0:T(8,128)(2,1)} %collective-permute-done.2.refs_3_, bf16[16,2,512,256]{3,2,1,0:T(8,128)(2,1)} %bitcast.13, ...), custom_call_target="tpu_custom_call" | custom-call | flops 1610612736 | bytes 1572864 | tf_op jit(solution)/shard_map/pallas_call | solution.py:631
  329.2 2.7 shard_map.81.a_ref
  331.9 2.6 shard_map.85.a_ref
  334.5 2.6 shard_map.89.refs_2_
  340.0 2.5 shard_map.90.refs_0_
  342.5 2.5 shard_map.91.refs_1_
  344.9 10.3 %pf.1.refs_13_ = bf16[2,384,512]{2,1,0:T(8,128)(2,1)} custom-call(bf16[128,2048]{1,0:T(8,128)(2,1)} %shard_map.90.refs_0_, bf16[128,2048]{1,0:T(8,128)(2,1)} %shard_map.91.refs_1_, bf16[1,136,2048]{2,1,0:T(8,128)(2,1)} %shard_map.89.refs_2_, bf16[1,136,2048]{2,1,0:T(8,128)(2,1)} %collective-permute-done.28.refs_3_, bf16[2048,512]{1,0:T(8,128)(2,1)} %refs_6_.1, ...), custom_call_target="tpu_custom_call" | custom-call | flops 3221225472 | bytes 8388608 | tf_op jit(solution)/shard_map/pf/pallas_call | solution.py:991
  355.3 9.1 %collective-permute-done.16.refs_3_ = bf16[1,136,2048]{2,1,0:T(8,128)(2,1)} collective-permute-done((bf16[1,136,2048]{2,1,0:T(8,128)(2,1)}, bf16[1,136,2048]{2,1,0:T(8,128)(2,1)}, u32[]{:S(2)}, u32[]{:S(2)}) %collective-permute-start.16) | collective-permute-done | bytes 557088 | tf_op jit(solution)/shard_map/ppermute | solution.py:751
  364.4 6.0 %collective-permute-done.19.refs_5_ = bf16[1,136,2048]{2,1,0:T(8,128)(2,1)} collective-permute-done((bf16[1,136,2048]{2,1,0:T(8,128)(2,1)}, bf16[1,136,2048]{2,1,0:T(8,128)(2,1)}, u32[]{:S(2)}, u32[]{:S(2)}) %collective-permute-start.19) | collective-permute-done | bytes 557088 | tf_op jit(solution)/shard_map/ppermute | solution.py:751
  370.4 21.3 %ph.1 = bf16[384,1024]{1,0:T(8,128)(2,1)} custom-call(bf16[1,136,2048]{2,1,0:T(8,128)(2,1)} %shard_map.77.refs_0_, bf16[1,136,2048]{2,1,0:T(8,128)(2,1)} %collective-permute-done.13.refs_1_, bf16[1,136,2048]{2,1,0:T(8,128)(2,1)} %shard_map.83.refs_2_, bf16[1,136,2048]{2,1,0:T(8,128)(2,1)} %collective-permute-done.16.refs_3_, ...), custom_call_target="tpu_custom_call" | custom-call | flops 3221225472 | bytes 8388608 | tf_op jit(solution)/shard_map/ph/pallas_call | solution.py:991
  (53 shorter events, 51.5 us)
Async XLA Ops:
  0.0 37.8 %collective-permute-start.2 = (bf16[384,2048]{1,0:T(8,128)(2,1)}, bf16[384,2048]{1,0:T(8,128)(2,1)}, u32[]{:S(2)}, u32[]{:S(2)}) collective-permute-start(bf16[384,2048]{1,0:T(8,128)(2,1)} %refs_4_.2), channel_id=1, source_target_pairs={{0,8},{4,12},{8,0},{12,4},{16,24},{20,28},{24,16},{28,20},{1,9},{5... | collective-permute-start | bytes 4718600 | tf_op jit(solution)/shard_map/ppermute | solution.py:751
  3.1 36.6 %collective-permute-start.1 = (bf16[384,2048]{1,0:T(8,128)(2,1)}, bf16[384,2048]{1,0:T(8,128)(2,1)}, u32[]{:S(2)}, u32[]{:S(2)}) collective-permute-start(bf16[384,2048]{1,0:T(8,128)(2,1)} %refs_4_.2), channel_id=1, source_target_pairs={{8,16},{12,20},{16,8},{20,12},{9,17},{13,21},{17,9},{21,13},{10,18... | collective-permute-start | bytes 4718600 | tf_op jit(solution)/shard_map/ppermute | solution.py:751
  20.8 50.0 %collective-permute-start.7 = (bf16[3,2,512,256]{3,2,1,0:T(8,128)(2,1)}, bf16[3,2,512,256]{3,2,1,0:T(8,128)(2,1)}, u32[]{:S(2)}, u32[]{:S(2)}) collective-permute-start(bf16[3,2,512,256]{3,2,1,0:T(8,128)(2,1)} %get-tuple-element.18), channel_id=1, source_target_pairs={{0,4},{4,0},{8,12},{12,8},{16,20},{20,16},{24,28},{28,24},{1,5},{5... | collective-permute-start | bytes 4718600 | tf_op jit(solution)/shard_map/ppermute | solution.py:751
  37.8 33.4 %collective-permute-start.3 = (bf16[384,2048]{1,0:T(8,128)(2,1)}, bf16[384,2048]{1,0:T(8,128)(2,1)}, u32[]{:S(2)}, u32[]{:S(2)}) collective-permute-start(bf16[384,2048]{1,0:T(8,128)(2,1)} %collective-permute-done.2.refs_3_), channel_id=1, source_target_pairs={{8,16},{12,20},{16,8},{20,12},{9,17},{13,21},{17,9},{21,13},{10,18... | collective-permute-start | bytes 4718600 | tf_op jit(solution)/shard_map/ppermute | solution.py:751
  39.6 38.2 %collective-permute-start.6 = (bf16[384,2048]{1,0:T(8,128)(2,1)}, bf16[384,2048]{1,0:T(8,128)(2,1)}, u32[]{:S(2)}, u32[]{:S(2)}) collective-permute-start(bf16[384,2048]{1,0:T(8,128)(2,1)} %collective-permute-done.1.refs_3_), channel_id=1, source_target_pairs={{8,0},{12,4},{16,24},{20,28},{9,1},{13,5},{17,25},{21,29},{10,2},{... | collective-permute-start | bytes 4718600 | tf_op jit(solution)/shard_map/ppermute | solution.py:751
  42.0 27.1 %collective-permute-start.20 = (bf16[512,512]{1,0:T(8,128)(2,1)S(1)}, bf16[512,512]{1,0:T(8,128)(2,1)}, u32[]{:S(2)}, u32[]{:S(2)}) collective-permute-start(bf16[512,512]{1,0:T(8,128)(2,1)S(1)} %slice.6), channel_id=1, source_target_pairs={{0,4},{4,0},{8,12},{12,8},{16,20},{20,16},{24,28},{28,24},{1,5},{5... | collective-permute-start | bytes 1572872 | tf_op jit(solution)/shard_map/ppermute | solution.py:751
  43.7 174.4 %collective-permute-start.22 = (bf16[2048,512]{1,0:T(8,128)(2,1)}, bf16[2048,512]{1,0:T(8,128)(2,1)}, u32[]{:S(2)}, u32[]{:S(2)}) collective-permute-start(bf16[2048,512]{1,0:T(8,128)(2,1)} %refs_6_.1), channel_id=1, source_target_pairs={{0,16},{4,20},{24,8},{28,12},{1,17},{5,21},{25,9},{29,13},{2,18},{... | collective-permute-start | bytes 6291464 | tf_op jit(solution)/shard_map/ppermute | solution.py:751
  69.1 37.6 %collective-permute-start = (bf16[3,2,512,256]{3,2,1,0:T(8,128)(2,1)}, bf16[3,2,512,256]{3,2,1,0:T(8,128)(2,1)}, u32[]{:S(2)}, u32[]{:S(2)}) collective-permute-start(bf16[3,2,512,256]{3,2,1,0:T(8,128)(2,1)} %get-tuple-element.16), channel_id=1, source_target_pairs={{0,4},{4,0},{8,12},{12,8},{16,20},{20,16},{24,28},{28,24},{1,5},{5... | collective-permute-start | bytes 4718600 | tf_op jit(solution)/shard_map/ppermute | solution.py:751
  70.9 77.5 %collective-permute-start.5 = (bf16[3,2,512,256]{3,2,1,0:T(8,128)(2,1)}, bf16[3,2,512,256]{3,2,1,0:T(8,128)(2,1)}, u32[]{:S(2)}, u32[]{:S(2)}) collective-permute-start(bf16[3,2,512,256]{3,2,1,0:T(8,128)(2,1)} %get-tuple-element.17), channel_id=1, source_target_pairs={{0,4},{4,0},{8,12},{12,8},{16,20},{20,16},{24,28},{28,24},{1,5},{5... | collective-permute-start | bytes 4718600 | tf_op jit(solution)/shard_map/ppermute | solution.py:751
  71.1 130.0 %collective-permute-start.4 = (bf16[384,2048]{1,0:T(8,128)(2,1)}, bf16[384,2048]{1,0:T(8,128)(2,1)}, u32[]{:S(2)}, u32[]{:S(2)}) collective-permute-start(bf16[384,2048]{1,0:T(8,128)(2,1)} %collective-permute-done.3.refs_3_), channel_id=1, source_target_pairs={{8,0},{12,4},{16,24},{20,28},{9,1},{13,5},{17,25},{21,29},{10,2},{... | collective-permute-start | bytes 4718600 | tf_op jit(solution)/shard_map/ppermute | solution.py:751
  77.8 143.0 %collective-permute-start.24 = (bf16[2048,512]{1,0:T(8,128)(2,1)}, bf16[2048,512]{1,0:T(8,128)(2,1)}, u32[]{:S(2)}, u32[]{:S(2)}) collective-permute-start(bf16[2048,512]{1,0:T(8,128)(2,1)} %refs_6_.1), channel_id=1, source_target_pairs={{8,24},{12,28},{16,0},{20,4},{9,25},{13,29},{17,1},{21,5},{10,26},... | collective-permute-start | bytes 6291464 | tf_op jit(solution)/shard_map/ppermute | solution.py:751
  106.7 116.1 %collective-permute-start.8 = (bf16[3,136,2048]{2,1,0:T(8,128)(2,1)}, bf16[3,136,2048]{2,1,0:T(8,128)(2,1)}, u32[]{:S(2)}, u32[]{:S(2)}) collective-permute-start(bf16[3,136,2048]{2,1,0:T(8,128)(2,1)} %shard_map.75.refs_0_), channel_id=1, source_target_pairs={{0,8},{4,12},{24,16},{28,20},{1,9},{5,13},{25,17},{29,21},{2,10},{... | collective-permute-start | bytes 5013512 | tf_op jit(solution)/shard_map/ppermute | solution.py:751
  148.3 81.1 %collective-permute-start.10 = (bf16[3,2,512,256]{3,2,1,0:T(8,128)(2,1)}, bf16[3,2,512,256]{3,2,1,0:T(8,128)(2,1)}, u32[]{:S(2)}, u32[]{:S(2)}) collective-permute-start(bf16[3,2,512,256]{3,2,1,0:T(8,128)(2,1)} %get-tuple-element.19), channel_id=1, source_target_pairs={{0,4},{4,0},{8,12},{12,8},{16,20},{20,16},{24,28},{28,24},{1,5},{5... | collective-permute-start | bytes 4718600 | tf_op jit(solution)/shard_map/ppermute | solution.py:751
  201.1 37.6 %collective-permute-start.21 = (bf16[1536,512]{1,0:T(8,128)(2,1)}, bf16[1536,512]{1,0:T(8,128)(2,1)}, u32[]{:S(2)}, u32[]{:S(2)}) collective-permute-start(bf16[1536,512]{1,0:T(8,128)(2,1)} %slice.7), channel_id=1, source_target_pairs={{0,4},{4,0},{8,12},{12,8},{16,20},{20,16},{24,28},{28,24},{1,5},{5... | collective-permute-start | bytes 4718600 | tf_op jit(solution)/shard_map/ppermute | solution.py:751
  218.2 35.1 %collective-permute-start.11 = (bf16[3,136,2048]{2,1,0:T(8,128)(2,1)}, bf16[3,136,2048]{2,1,0:T(8,128)(2,1)}, u32[]{:S(2)}, u32[]{:S(2)}) collective-permute-start(bf16[3,136,2048]{2,1,0:T(8,128)(2,1)} %shard_map.74.refs_0_), channel_id=1, source_target_pairs={{0,8},{4,12},{24,16},{28,20},{1,9},{5,13},{25,17},{29,21},{2,10},{... | collective-permute-start | bytes 5013512 | tf_op jit(solution)/shard_map/ppermute | solution.py:751
  220.8 116.3 %collective-permute-start.23 = (bf16[2048,512]{1,0:T(8,128)(2,1)}, bf16[2048,512]{1,0:T(8,128)(2,1)}, u32[]{:S(2)}, u32[]{:S(2)}) collective-permute-start(bf16[2048,512]{1,0:T(8,128)(2,1)} %collective-permute-done.22.refs_7_.refs_9_), channel_id=1, source_target_pairs={{8,12},{12,8},{16,20},{20,16},{9,13},{13,9},{17,21},{21,17},{10,14... | collective-permute-start | bytes 6291464 | tf_op jit(solution)/shard_map/ppermute | solution.py:751
  222.8 122.1 %collective-permute-start.25 = (bf16[2048,512]{1,0:T(8,128)(2,1)}, bf16[2048,512]{1,0:T(8,128)(2,1)}, u32[]{:S(2)}, u32[]{:S(2)}) collective-permute-start(bf16[2048,512]{1,0:T(8,128)(2,1)} %collective-permute-done.24.refs_9_.refs_11_), channel_id=1, source_target_pairs={{0,4},{4,0},{24,28},{28,24},{1,5},{5,1},{25,29},{29,25},{2,6},{6,2... | collective-permute-start | bytes 6291464 | tf_op jit(solution)/shard_map/ppermute | solution.py:751
  229.4 29.5 %collective-permute-start.9 = (bf16[1,136,2048]{2,1,0:T(8,128)(2,1)}, bf16[1,136,2048]{2,1,0:T(8,128)(2,1)}, u32[]{:S(2)}, u32[]{:S(2)}) collective-permute-start(bf16[1,136,2048]{2,1,0:T(8,128)(2,1)} %shard_map.76), channel_id=1, source_target_pairs={{8,16},{12,20},{16,8},{20,12},{9,17},{13,21},{17,9},{21,13},{10,18... | collective-permute-start | bytes 1671176 | tf_op jit(solution)/shard_map/ppermute | solution.py:751
  238.7 21.6 %collective-permute-start.14 = (bf16[1,136,2048]{2,1,0:T(8,128)(2,1)}, bf16[1,136,2048]{2,1,0:T(8,128)(2,1)}, u32[]{:S(2)}, u32[]{:S(2)}) collective-permute-start(bf16[1,136,2048]{2,1,0:T(8,128)(2,1)} %shard_map.82), channel_id=1, source_target_pairs={{8,16},{12,20},{16,8},{20,12},{9,17},{13,21},{17,9},{21,13},{10,18... | collective-permute-start | bytes 1671176 | tf_op jit(solution)/shard_map/ppermute | solution.py:751
  253.2 10.6 %collective-permute-start.17 = (bf16[1,136,2048]{2,1,0:T(8,128)(2,1)}, bf16[1,136,2048]{2,1,0:T(8,128)(2,1)}, u32[]{:S(2)}, u32[]{:S(2)}) collective-permute-start(bf16[1,136,2048]{2,1,0:T(8,128)(2,1)} %shard_map.86), channel_id=1, source_target_pairs={{8,16},{12,20},{16,8},{20,12},{9,17},{13,21},{17,9},{21,13},{10,18... | collective-permute-start | bytes 1671176 | tf_op jit(solution)/shard_map/ppermute | solution.py:751
  258.8 32.8 %collective-permute-start.12 = (bf16[1,136,2048]{2,1,0:T(8,128)(2,1)}, bf16[1,136,2048]{2,1,0:T(8,128)(2,1)}, u32[]{:S(2)}, u32[]{:S(2)}) collective-permute-start(bf16[1,136,2048]{2,1,0:T(8,128)(2,1)} %shard_map.80), channel_id=1, source_target_pairs={{8,16},{12,20},{16,8},{20,12},{9,17},{13,21},{17,9},{21,13},{10,18... | collective-permute-start | bytes 1671176 | tf_op jit(solution)/shard_map/ppermute | solution.py:751
  260.3 43.9 %collective-permute-start.15 = (bf16[1,136,2048]{2,1,0:T(8,128)(2,1)}, bf16[1,136,2048]{2,1,0:T(8,128)(2,1)}, u32[]{:S(2)}, u32[]{:S(2)}) collective-permute-start(bf16[1,136,2048]{2,1,0:T(8,128)(2,1)} %shard_map.84), channel_id=1, source_target_pairs={{8,16},{12,20},{16,8},{20,12},{9,17},{13,21},{17,9},{21,13},{10,18... | collective-permute-start | bytes 1671176 | tf_op jit(solution)/shard_map/ppermute | solution.py:751
  263.9 42.5 %collective-permute-start.18 = (bf16[1,136,2048]{2,1,0:T(8,128)(2,1)}, bf16[1,136,2048]{2,1,0:T(8,128)(2,1)}, u32[]{:S(2)}, u32[]{:S(2)}) collective-permute-start(bf16[1,136,2048]{2,1,0:T(8,128)(2,1)} %shard_map.88), channel_id=1, source_target_pairs={{8,16},{12,20},{16,8},{20,12},{9,17},{13,21},{17,9},{21,13},{10,18... | collective-permute-start | bytes 1671176 | tf_op jit(solution)/shard_map/ppermute | solution.py:751
  291.6 46.4 %collective-permute-start.26 = (bf16[1,136,2048]{2,1,0:T(8,128)(2,1)}, bf16[1,136,2048]{2,1,0:T(8,128)(2,1)}, u32[]{:S(2)}, u32[]{:S(2)}) collective-permute-start(bf16[1,136,2048]{2,1,0:T(8,128)(2,1)} %shard_map.77.refs_0_), channel_id=1, source_target_pairs={{0,8},{4,12},{8,0},{12,4},{16,24},{20,28},{24,16},{28,20},{1,9},{5... | collective-permute-start | bytes 1671176 | tf_op jit(solution)/shard_map/ppermute | solution.py:751
  304.3 34.9 %collective-permute-start.27 = (bf16[1,136,2048]{2,1,0:T(8,128)(2,1)}, bf16[1,136,2048]{2,1,0:T(8,128)(2,1)}, u32[]{:S(2)}, u32[]{:S(2)}) collective-permute-start(bf16[1,136,2048]{2,1,0:T(8,128)(2,1)} %shard_map.83.refs_2_), channel_id=1, source_target_pairs={{0,8},{4,12},{8,0},{12,4},{16,24},{20,28},{24,16},{28,20},{1,9},{5... | collective-permute-start | bytes 1671176 | tf_op jit(solution)/shard_map/ppermute | solution.py:751
  306.4 38.5 %collective-permute-start.28 = (bf16[1,136,2048]{2,1,0:T(8,128)(2,1)}, bf16[1,136,2048]{2,1,0:T(8,128)(2,1)}, u32[]{:S(2)}, u32[]{:S(2)}) collective-permute-start(bf16[1,136,2048]{2,1,0:T(8,128)(2,1)} %shard_map.87.refs_4_), channel_id=1, source_target_pairs={{0,8},{4,12},{8,0},{12,4},{16,24},{20,28},{24,16},{28,20},{1,9},{5... | collective-permute-start | bytes 1671176 | tf_op jit(solution)/shard_map/ppermute | solution.py:751
  337.2 18.1 %collective-permute-start.13 = (bf16[1,136,2048]{2,1,0:T(8,128)(2,1)}, bf16[1,136,2048]{2,1,0:T(8,128)(2,1)}, u32[]{:S(2)}, u32[]{:S(2)}) collective-permute-start(bf16[1,136,2048]{2,1,0:T(8,128)(2,1)} %shard_map.81.a_ref), channel_id=1, source_target_pairs={{0,8},{4,12},{8,0},{12,4},{16,24},{20,28},{24,16},{28,20},{1,9},{5... | collective-permute-start | bytes 1671176 | tf_op jit(solution)/shard_map/ppermute | solution.py:751
  338.0 26.5 %collective-permute-start.16 = (bf16[1,136,2048]{2,1,0:T(8,128)(2,1)}, bf16[1,136,2048]{2,1,0:T(8,128)(2,1)}, u32[]{:S(2)}, u32[]{:S(2)}) collective-permute-start(bf16[1,136,2048]{2,1,0:T(8,128)(2,1)} %shard_map.85.a_ref), channel_id=1, source_target_pairs={{0,8},{4,12},{8,0},{12,4},{16,24},{20,28},{24,16},{28,20},{1,9},{5... | collective-permute-start | bytes 1671176 | tf_op jit(solution)/shard_map/ppermute | solution.py:751
  339.2 31.2 %collective-permute-start.19 = (bf16[1,136,2048]{2,1,0:T(8,128)(2,1)}, bf16[1,136,2048]{2,1,0:T(8,128)(2,1)}, u32[]{:S(2)}, u32[]{:S(2)}) collective-permute-start(bf16[1,136,2048]{2,1,0:T(8,128)(2,1)} %shard_map.89.refs_2_), channel_id=1, source_target_pairs={{0,8},{4,12},{8,0},{12,4},{16,24},{20,28},{24,16},{28,20},{1,9},{5... | collective-permute-start | bytes 1671176 | tf_op jit(solution)/shard_map/ppermute | solution.py:751
